TPU v7x, 512 devices: a whole 4x8x8 slice. The times are simulated.
512 devices in a mesh: tile: 64 (over z_hi, y, x), section: 8 (over z_lo, core).
Axes of the slice: x: 4, y: 8, z: 8 (z_hi: 2, z_lo: 4; z = z_hi * 4 + z_lo), core: 2. Of those that a mesh axis runs over, the one named last changes fastest.
Arguments:
- fields: bfloat16 [4, 2, 18, 147456], P(None, None, None, 'tile'), may hold values from -6 to 6, as said below
- land_mask: int32 [18, 768], P(None, 'tile'), may hold values 0 or 1
- land_vector: float32 [192], replicated, may hold values from -4 to 4
- w_qkv: bfloat16 [8, 192, 576], P('section'), may hold values from -3 to 3, as said below
- w_proj: bfloat16 [8, 192, 192], P('section'), may hold values from -0.4375 to 0.4375
- w_up: bfloat16 [8, 192, 768], P('section'), may hold values from -0.4375 to 0.4375
- w_down: bfloat16 [8, 768, 192], P('section'), may hold values from -0.21875 to 0.21875
Outputs:
- streams: bfloat16 [8, 4, 2, 18, 147456], P('section', None, None, None, 'tile')
Inputs may be any that keep to these rules, and one draw needn't show every extreme that they name: `fields`: finite values. `w_qkv`: finite values.
All inputs are finite; a program needn't handle non-finite values. No bound on the sum of `land_mask` on one device may be relied on, other than what follows from the above.
Results may differ from a plain program's by a relative error of at most 0.02.
Values may be sent and summed in bfloat16 or wider, within the bound.
No kernel may reach another device: no remote copies, remote signals or barrier semaphores. Data moves between devices by JAX's collectives and lax.ppermute only.
A program may use at most 64 MiB of HBM per device.

v0:
```python
import jax
import jax.numpy as jnp
from jax import lax
from jax.sharding import PartitionSpec as P

HEADS = 6
WZ = 2
WLAT = 6
WLON = 12


def shifted_2(value, axis, steps):
    count = lax.axis_size(axis)
    pairs = [(source, (source + steps) % count) for source in range(count)]
    return lax.ppermute(value, axis, pairs)


def shifted_3(block, axis, distance):
    devices = range(lax.axis_size(axis))
    route = [(i - distance, i) for i in devices if i - distance in devices]
    return lax.ppermute(block, axis, route)


def normalize(values):
    center = values - jnp.mean(values, axis=-1, keepdims=True)
    spread = jnp.mean(center * center, axis=-1, keepdims=True)
    return center * lax.rsqrt(spread + 1e-05)


def region_ids(length, window, shifted):
    places = jnp.arange(length)
    labels = jnp.where(places < length - window, 0, jnp.where(places < length - window // 2, 1, 2))
    return labels * shifted


def window_attend(normed, weight_qkv, weight_proj, shifted):
    levels, rows, columns, width = normed.shape
    head_size = width // HEADS
    lev_blocks, lat_blocks, lon_blocks = (levels // WZ, rows // WLAT, columns // WLON)
    points = WZ * WLAT * WLON
    qkv = jnp.einsum(
        "zlwc,cd->zlwd", normed, weight_qkv, preferred_element_type=jnp.float32
    ).astype(jnp.bfloat16)
    parts = qkv.reshape(lev_blocks, WZ, lat_blocks, WLAT, lon_blocks, WLON, 3, HEADS, head_size)
    parts = parts.transpose(6, 0, 2, 4, 7, 1, 3, 5, 8).reshape(
        3, lev_blocks, lat_blocks, lon_blocks, HEADS, points, head_size
    )
    level_ids = region_ids(levels, WZ, shifted).reshape(lev_blocks, WZ)
    row_ids = region_ids(rows, WLAT, shifted).reshape(lat_blocks, WLAT)
    labels = level_ids[:, None, :, None] * 3 + row_ids[None, :, None, :]
    labels = jnp.broadcast_to(labels[..., None], (lev_blocks, lat_blocks, WZ, WLAT, WLON)).reshape(
        lev_blocks, lat_blocks, points
    )
    allowed = labels[:, :, None, None, :, None] == labels[:, :, None, None, None, :]
    scores = jnp.einsum(
        "abcdqe,abcdke->abcdqk", parts[0], parts[1], preferred_element_type=jnp.float32
    ) * head_size ** (-0.5)
    scores = jnp.where(allowed, scores, -1e30)
    highest = jnp.max(scores, axis=-1, keepdims=True)
    raised = jnp.exp(scores - highest)
    probs = (raised / jnp.sum(raised, axis=-1, keepdims=True)).astype(jnp.bfloat16)
    attended = jnp.einsum(
        "abcdqk,abcdke->abcdqe", probs, parts[2], preferred_element_type=jnp.float32
    ).astype(jnp.bfloat16)
    attended = attended.reshape(
        lev_blocks, lat_blocks, lon_blocks, HEADS, WZ, WLAT, WLON, head_size
    )
    attended = attended.transpose(0, 4, 1, 5, 2, 6, 3, 7).reshape(levels, rows, columns, width)
    return jnp.einsum("zlwc,cd->zlwd", attended, weight_proj, preferred_element_type=jnp.float32)


def run_block(tokens, weight_qkv, weight_proj, weight_up, weight_down, shifted):
    levels, rows, lon_dev, width = tokens.shape
    half_window = WLON // 2
    level_move = WZ // 2 * shifted
    row_move = WLAT // 2 * shifted
    column_move = half_window * shifted
    values = tokens.astype(jnp.float32)
    normed = normalize(values).astype(jnp.bfloat16)
    normed = jnp.roll(jnp.roll(normed, -level_move, 0), -row_move, 1)
    column_strip = shifted_2(normed[:, :, :half_window], "tile", -1)
    extended = jnp.concatenate([normed, column_strip], 2)
    window_cols = lax.dynamic_slice_in_dim(extended, column_move, lon_dev, 2)
    projected = window_attend(window_cols, weight_qkv, weight_proj, shifted)
    spread_out = jnp.zeros((levels, rows, lon_dev + half_window, width), jnp.float32)
    spread_out = lax.dynamic_update_slice_in_dim(spread_out, projected, column_move, 2)
    spill_over = shifted_2(spread_out[:, :, lon_dev:].astype(jnp.bfloat16), "tile", 1).astype(
        jnp.float32
    )
    projected = spread_out[:, :, :lon_dev] + jnp.pad(
        spill_over, ((0, 0), (0, 0), (0, lon_dev - half_window), (0, 0))
    )
    projected = jnp.roll(jnp.roll(projected, level_move, 0), row_move, 1)
    residual = values + projected
    normed_two = normalize(residual).astype(jnp.bfloat16)
    hidden = jax.nn.gelu(
        jnp.einsum("zlwc,cf->zlwf", normed_two, weight_up, preferred_element_type=jnp.float32),
        approximate=False,
    ).astype(jnp.bfloat16)
    output = residual + jnp.einsum(
        "zlwf,fc->zlwc", hidden, weight_down, preferred_element_type=jnp.float32
    )
    return output.astype(jnp.bfloat16)


def on_device(fields, land_mask, land_vector, w_qkv, w_proj, w_up, w_down):
    micro_count, levels, rows, flat_width = fields.shape
    width = land_vector.shape[0]
    lon_dev = flat_width // width
    section_index = lax.axis_index("section")
    section_count = lax.axis_size("section")
    tick_count = micro_count + section_count - 1
    shifted = section_index % 2
    inputs_grid = fields.reshape(micro_count, levels, rows, lon_dev, width).astype(jnp.float32)
    inputs_grid = (
        inputs_grid
        + land_mask.astype(jnp.float32)[None, None, :, :, None]
        * land_vector[None, None, None, None, :]
    )
    inputs_grid = inputs_grid.astype(jnp.bfloat16)
    weight_qkv, weight_proj, weight_up, weight_down = (w_qkv[0], w_proj[0], w_up[0], w_down[0])

    def hand_off(output):
        return shifted_3(output, "section", 1)

    def one_tick(step_index, state_pair):
        inbox, saved = state_pair
        incoming = lax.dynamic_index_in_dim(
            inputs_grid, jnp.minimum(step_index, micro_count - 1), 0, keepdims=False
        )
        tokens = jnp.where(section_index == 0, incoming, inbox)
        output = run_block(tokens, weight_qkv, weight_proj, weight_up, weight_down, shifted)
        batch_index = step_index - section_index
        valid = (batch_index >= 0) & (batch_index < micro_count)
        slot_index = jnp.clip(batch_index, 0, micro_count - 1)
        current = lax.dynamic_slice_in_dim(saved, slot_index, 1, 0)
        flat_output = output.reshape(1, levels, rows, lon_dev * width)
        saved = lax.dynamic_update_slice_in_dim(
            saved, jnp.where(valid, flat_output, current), slot_index, 0
        )
        inbox = hand_off(output)
        return (inbox, saved)

    start_inbox = jnp.zeros((levels, rows, lon_dev, width), jnp.bfloat16)
    start_saved = jnp.zeros((micro_count, levels, rows, lon_dev * width), jnp.bfloat16)
    final_inbox, saved = lax.fori_loop(0, tick_count, one_tick, (start_inbox, start_saved))
    return saved[None]


def solution(mesh):
    in_specs = (
        P(None, None, None, "tile"),
        P(None, "tile"),
        P(),
        P("section", None, None),
        P("section", None, None),
        P("section", None, None),
        P("section", None, None),
    )
    out_specs = P("section", None, None, None, "tile")
    return jax.shard_map(
        on_device, mesh=mesh, in_specs=in_specs, out_specs=out_specs, check_vma=False
    )
```

profile of v0, /device:TPU:1, one launch (start us, length us, event | category | flops | bytes accessed | tf_op | source)
XLA Modules:
  0.0 696.0 jit_solution(14568358222501834179)
XLA Ops:
  5.3 690.6 %while.18 = (s32[]{:T(128)}, bf16[2,18,12,192]{3,2,1,0:T(8,128)(2,1)S(1)}, bf16[4,2,18,2304]{3,1,2,0:T(2,128)(2,1)}, pred[]{:T(512)}, bf16[4,2,18,12,192]{4,3,1,...) while((s32[]{:T(128)}, ...), condition=%wide.region_7.8_spmd, body=%wide.region_0.7_spmd.sunk | while | flops 461526944 | bytes 30496268 | solution.py:146
  7.6 16.6 %collective-permute-start = (bf16[2,18,6,192]{3,2,1,0:T(8,128)(2,1)S(1)}, bf16[2,18,6,192]{3,2,1,0:T(8,128)(2,1)S(1)}, u32[]{:S(2)}, u32[]{:S(2)}) collective-permute-start(bf16[2,18,6,192]{3,2,1,0:T(8,128)(2,1)S(1)} %slice.92), channel_id=1, source_target_pairs={{0,504},{8,0},{16,8},{24,16},{32,24},{40,32},{48,40},{56,48},{64,5... | collective-permute-start | bytes 248840 | tf_op jit(solution)/shard_map/while/body/eval_jaxpr/ppermute | solution.py:15
  42.3 6.0 dynamic_update_slice.26
  50.2 16.2 %collective-permute-done.1 = bf16[2,18,6,192]{3,2,1,0:T(8,128)(2,1)S(1)} collective-permute-done((bf16[2,18,6,192]{3,2,1,0:T(8,128)(2,1)S(1)}, bf16[2,18,6,192]{3,2,1,0:T(8,128)(2,1)S(1)}, u32[]{:S(2)}, u32[]{:S(2)}) %collective-permute-start.1) | collective-permute-done | bytes 82976 | tf_op jit(solution)/shard_map/while/body/eval_jaxpr/ppermute | solution.py:15
  68.4 4.2 fusion.129
  72.9 4.7 collective-permute-start.2
  105.2 6.0 dynamic_update_slice.26
  113.1 16.2 %collective-permute-done.1 = bf16[2,18,6,192]{3,2,1,0:T(8,128)(2,1)S(1)} collective-permute-done((bf16[2,18,6,192]{3,2,1,0:T(8,128)(2,1)S(1)}, bf16[2,18,6,192]{3,2,1,0:T(8,128)(2,1)S(1)}, u32[]{:S(2)}, u32[]{:S(2)}) %collective-permute-start.1) | collective-permute-done | bytes 82976 | tf_op jit(solution)/shard_map/while/body/eval_jaxpr/ppermute | solution.py:15
  131.4 4.2 fusion.129
  144.4 3.1 collective-permute-start
  165.9 6.0 dynamic_update_slice.26
  173.8 15.0 %collective-permute-done.1 = bf16[2,18,6,192]{3,2,1,0:T(8,128)(2,1)S(1)} collective-permute-done((bf16[2,18,6,192]{3,2,1,0:T(8,128)(2,1)S(1)}, bf16[2,18,6,192]{3,2,1,0:T(8,128)(2,1)S(1)}, u32[]{:S(2)}, u32[]{:S(2)}) %collective-permute-start.1) | collective-permute-done | bytes 82976 | tf_op jit(solution)/shard_map/while/body/eval_jaxpr/ppermute | solution.py:15
  190.9 4.2 fusion.129
  195.4 7.4 %collective-permute-start.2 = (bf16[2,18,12,192]{3,2,1,0:T(8,128)(2,1)S(1)}, bf16[2,18,12,192]{3,2,1,0:T(8,128)(2,1)S(1)}, u32[]{:S(2)}, u32[]{:S(2)}) collective-permute-start(bf16[2,18,12,192]{3,2,1,0:T(8,128)(2,1)S(1)} %fusion.129), channel_id=1, source_target_pairs={{0,1},{1,2},{2,3},{3,4},{4,5},{5,6},{6,7},{8,9},{9,10},{10,11},{11... | collective-permute-start | bytes 497672 | tf_op jit(solution)/shard_map/while/body/eval_jaxpr/ppermute | solution.py:21
  211.4 2.9 collective-permute-done
  230.0 6.0 dynamic_update_slice.26
  237.9 13.8 %collective-permute-done.1 = bf16[2,18,6,192]{3,2,1,0:T(8,128)(2,1)S(1)} collective-permute-done((bf16[2,18,6,192]{3,2,1,0:T(8,128)(2,1)S(1)}, bf16[2,18,6,192]{3,2,1,0:T(8,128)(2,1)S(1)}, u32[]{:S(2)}, u32[]{:S(2)}) %collective-permute-start.1) | collective-permute-done | bytes 82976 | tf_op jit(solution)/shard_map/while/body/eval_jaxpr/ppermute | solution.py:15
  253.7 4.2 fusion.129
  258.2 6.3 collective-permute-start.2
  273.2 2.9 collective-permute-done
  291.8 6.0 dynamic_update_slice.26
  299.7 13.8 %collective-permute-done.1 = bf16[2,18,6,192]{3,2,1,0:T(8,128)(2,1)S(1)} collective-permute-done((bf16[2,18,6,192]{3,2,1,0:T(8,128)(2,1)S(1)}, bf16[2,18,6,192]{3,2,1,0:T(8,128)(2,1)S(1)}, u32[]{:S(2)}, u32[]{:S(2)}) %collective-permute-start.1) | collective-permute-done | bytes 82976 | tf_op jit(solution)/shard_map/while/body/eval_jaxpr/ppermute | solution.py:15
  315.5 4.2 fusion.129
  319.9 6.2 collective-permute-start.2
  353.4 6.0 dynamic_update_slice.26
  361.4 14.2 %collective-permute-done.1 = bf16[2,18,6,192]{3,2,1,0:T(8,128)(2,1)S(1)} collective-permute-done((bf16[2,18,6,192]{3,2,1,0:T(8,128)(2,1)S(1)}, bf16[2,18,6,192]{3,2,1,0:T(8,128)(2,1)S(1)}, u32[]{:S(2)}, u32[]{:S(2)}) %collective-permute-start.1) | collective-permute-done | bytes 82976 | tf_op jit(solution)/shard_map/while/body/eval_jaxpr/ppermute | solution.py:15
  377.6 4.2 fusion.129
  382.1 5.6 collective-permute-start.2
  414.9 6.0 dynamic_update_slice.26
  422.9 13.8 %collective-permute-done.1 = bf16[2,18,6,192]{3,2,1,0:T(8,128)(2,1)S(1)} collective-permute-done((bf16[2,18,6,192]{3,2,1,0:T(8,128)(2,1)S(1)}, bf16[2,18,6,192]{3,2,1,0:T(8,128)(2,1)S(1)}, u32[]{:S(2)}, u32[]{:S(2)}) %collective-permute-start.1) | collective-permute-done | bytes 82976 | tf_op jit(solution)/shard_map/while/body/eval_jaxpr/ppermute | solution.py:15
  438.7 4.2 fusion.129
  443.2 5.8 collective-permute-start.2
  476.3 6.0 dynamic_update_slice.26
  484.2 13.8 %collective-permute-done.1 = bf16[2,18,6,192]{3,2,1,0:T(8,128)(2,1)S(1)} collective-permute-done((bf16[2,18,6,192]{3,2,1,0:T(8,128)(2,1)S(1)}, bf16[2,18,6,192]{3,2,1,0:T(8,128)(2,1)S(1)}, u32[]{:S(2)}, u32[]{:S(2)}) %collective-permute-start.1) | collective-permute-done | bytes 82976 | tf_op jit(solution)/shard_map/while/body/eval_jaxpr/ppermute | solution.py:15
  500.0 4.2 fusion.129
  504.5 5.6 collective-permute-start.2
  537.4 6.0 dynamic_update_slice.26
  545.4 12.7 %collective-permute-done.1 = bf16[2,18,6,192]{3,2,1,0:T(8,128)(2,1)S(1)} collective-permute-done((bf16[2,18,6,192]{3,2,1,0:T(8,128)(2,1)S(1)}, bf16[2,18,6,192]{3,2,1,0:T(8,128)(2,1)S(1)}, u32[]{:S(2)}, u32[]{:S(2)}) %collective-permute-start.1) | collective-permute-done | bytes 82976 | tf_op jit(solution)/shard_map/while/body/eval_jaxpr/ppermute | solution.py:15
  560.1 4.2 fusion.129
  564.6 6.5 collective-permute-start.2
  598.3 6.0 dynamic_update_slice.26
  606.2 13.8 %collective-permute-done.1 = bf16[2,18,6,192]{3,2,1,0:T(8,128)(2,1)S(1)} collective-permute-done((bf16[2,18,6,192]{3,2,1,0:T(8,128)(2,1)S(1)}, bf16[2,18,6,192]{3,2,1,0:T(8,128)(2,1)S(1)}, u32[]{:S(2)}, u32[]{:S(2)}) %collective-permute-start.1) | collective-permute-done | bytes 82976 | tf_op jit(solution)/shard_map/while/body/eval_jaxpr/ppermute | solution.py:15
  622.0 4.2 fusion.129
  626.5 5.1 collective-permute-start.2
  658.9 6.0 dynamic_update_slice.26
  666.9 14.0 %collective-permute-done.1 = bf16[2,18,6,192]{3,2,1,0:T(8,128)(2,1)S(1)} collective-permute-done((bf16[2,18,6,192]{3,2,1,0:T(8,128)(2,1)S(1)}, bf16[2,18,6,192]{3,2,1,0:T(8,128)(2,1)S(1)}, u32[]{:S(2)}, u32[]{:S(2)}) %collective-permute-start.1) | collective-permute-done | bytes 82976 | tf_op jit(solution)/shard_map/while/body/eval_jaxpr/ppermute | solution.py:15
  682.8 4.2 fusion.129
  687.3 5.0 collective-permute-start.2
  (714 shorter events, 339.5 us)
Async XLA Ops:
  0.0 2.4 copy-start.8
  0.0 2.6 copy-start.9
  2.7 2.6 copy-start.4
  7.6 19.1 %collective-permute-start = (bf16[2,18,6,192]{3,2,1,0:T(8,128)(2,1)S(1)}, bf16[2,18,6,192]{3,2,1,0:T(8,128)(2,1)S(1)}, u32[]{:S(2)}, u32[]{:S(2)}) collective-permute-start(bf16[2,18,6,192]{3,2,1,0:T(8,128)(2,1)S(1)} %slice.92), channel_id=1, source_target_pairs={{0,504},{8,0},{16,8},{24,16},{32,24},{40,32},{48,40},{56,48},{64,5... | collective-permute-start | bytes 248840 | tf_op jit(solution)/shard_map/while/body/eval_jaxpr/ppermute | solution.py:15
  31.5 1.4 copy-start.1
  48.3 18.1 %collective-permute-start.1 = (bf16[2,18,6,192]{3,2,1,0:T(8,128)(2,1)S(1)}, bf16[2,18,6,192]{3,2,1,0:T(8,128)(2,1)S(1)}, u32[]{:S(2)}, u32[]{:S(2)}) collective-permute-start(bf16[2,18,6,192]{3,2,1,0:T(8,128)(2,1)S(1)} %slice.93), channel_id=1, source_target_pairs={{0,8},{8,16},{16,24},{24,32},{32,40},{40,48},{48,56},{56,64},{64,7... | collective-permute-start | bytes 248840 | tf_op jit(solution)/shard_map/while/body/eval_jaxpr/ppermute | solution.py:15
  68.4 12.8 %copy-start.5 = (bf16[1,192,576]{2,1,0:T(8,128)(2,1)S(1)}, bf16[1,192,576]{2,1,0:T(8,128)(2,1)}, u32[]{:S(2)}) copy-start(bf16[1,192,576]{2,1,0:T(8,128)(2,1)} %get-tuple-element.732) | copy-start | bytes 663556 | tf_op jit(solution)/shard_map/while
  72.9 8.3 %collective-permute-start.2 = (bf16[2,18,12,192]{3,2,1,0:T(8,128)(2,1)S(1)}, bf16[2,18,12,192]{3,2,1,0:T(8,128)(2,1)S(1)}, u32[]{:S(2)}, u32[]{:S(2)}) collective-permute-start(bf16[2,18,12,192]{3,2,1,0:T(8,128)(2,1)S(1)} %fusion.129), channel_id=1, source_target_pairs={{0,1},{1,2},{2,3},{3,4},{4,5},{5,6},{6,7},{8,9},{9,10},{10,11},{11... | collective-permute-start | bytes 497672 | tf_op jit(solution)/shard_map/while/body/eval_jaxpr/ppermute | solution.py:21
  83.3 6.2 collective-permute-start
  111.2 18.2 %collective-permute-start.1 = (bf16[2,18,6,192]{3,2,1,0:T(8,128)(2,1)S(1)}, bf16[2,18,6,192]{3,2,1,0:T(8,128)(2,1)S(1)}, u32[]{:S(2)}, u32[]{:S(2)}) collective-permute-start(bf16[2,18,6,192]{3,2,1,0:T(8,128)(2,1)S(1)} %slice.93), channel_id=1, source_target_pairs={{0,8},{8,16},{16,24},{24,32},{32,40},{40,48},{48,56},{56,64},{64,7... | collective-permute-start | bytes 248840 | tf_op jit(solution)/shard_map/while/body/eval_jaxpr/ppermute | solution.py:15
  131.3 10.9 %copy-start.5 = (bf16[1,192,576]{2,1,0:T(8,128)(2,1)S(1)}, bf16[1,192,576]{2,1,0:T(8,128)(2,1)}, u32[]{:S(2)}) copy-start(bf16[1,192,576]{2,1,0:T(8,128)(2,1)} %get-tuple-element.732) | copy-start | bytes 663556 | tf_op jit(solution)/shard_map/while
  135.8 6.5 collective-permute-start.2
  144.4 5.9 collective-permute-start
  171.9 17.0 %collective-permute-start.1 = (bf16[2,18,6,192]{3,2,1,0:T(8,128)(2,1)S(1)}, bf16[2,18,6,192]{3,2,1,0:T(8,128)(2,1)S(1)}, u32[]{:S(2)}, u32[]{:S(2)}) collective-permute-start(bf16[2,18,6,192]{3,2,1,0:T(8,128)(2,1)S(1)} %slice.93), channel_id=1, source_target_pairs={{0,8},{8,16},{16,24},{24,32},{32,40},{40,48},{48,56},{56,64},{64,7... | collective-permute-start | bytes 248840 | tf_op jit(solution)/shard_map/while/body/eval_jaxpr/ppermute | solution.py:15
  190.9 15.5 %copy-start.5 = (bf16[1,192,576]{2,1,0:T(8,128)(2,1)S(1)}, bf16[1,192,576]{2,1,0:T(8,128)(2,1)}, u32[]{:S(2)}) copy-start(bf16[1,192,576]{2,1,0:T(8,128)(2,1)} %get-tuple-element.732) | copy-start | bytes 663556 | tf_op jit(solution)/shard_map/while
  195.4 11.0 %collective-permute-start.2 = (bf16[2,18,12,192]{3,2,1,0:T(8,128)(2,1)S(1)}, bf16[2,18,12,192]{3,2,1,0:T(8,128)(2,1)S(1)}, u32[]{:S(2)}, u32[]{:S(2)}) collective-permute-start(bf16[2,18,12,192]{3,2,1,0:T(8,128)(2,1)S(1)} %fusion.129), channel_id=1, source_target_pairs={{0,1},{1,2},{2,3},{3,4},{4,5},{5,6},{6,7},{8,9},{9,10},{10,11},{11... | collective-permute-start | bytes 497672 | tf_op jit(solution)/shard_map/while/body/eval_jaxpr/ppermute | solution.py:21
  208.5 5.9 collective-permute-start
  236.0 15.7 %collective-permute-start.1 = (bf16[2,18,6,192]{3,2,1,0:T(8,128)(2,1)S(1)}, bf16[2,18,6,192]{3,2,1,0:T(8,128)(2,1)S(1)}, u32[]{:S(2)}, u32[]{:S(2)}) collective-permute-start(bf16[2,18,6,192]{3,2,1,0:T(8,128)(2,1)S(1)} %slice.93), channel_id=1, source_target_pairs={{0,8},{8,16},{16,24},{24,32},{32,40},{40,48},{48,56},{56,64},{64,7... | collective-permute-start | bytes 248840 | tf_op jit(solution)/shard_map/while/body/eval_jaxpr/ppermute | solution.py:15
  253.7 14.4 %copy-start.5 = (bf16[1,192,576]{2,1,0:T(8,128)(2,1)S(1)}, bf16[1,192,576]{2,1,0:T(8,128)(2,1)}, u32[]{:S(2)}) copy-start(bf16[1,192,576]{2,1,0:T(8,128)(2,1)} %get-tuple-element.732) | copy-start | bytes 663556 | tf_op jit(solution)/shard_map/while
  258.2 10.0 %collective-permute-start.2 = (bf16[2,18,12,192]{3,2,1,0:T(8,128)(2,1)S(1)}, bf16[2,18,12,192]{3,2,1,0:T(8,128)(2,1)S(1)}, u32[]{:S(2)}, u32[]{:S(2)}) collective-permute-start(bf16[2,18,12,192]{3,2,1,0:T(8,128)(2,1)S(1)} %fusion.129), channel_id=1, source_target_pairs={{0,1},{1,2},{2,3},{3,4},{4,5},{5,6},{6,7},{8,9},{9,10},{10,11},{11... | collective-permute-start | bytes 497672 | tf_op jit(solution)/shard_map/while/body/eval_jaxpr/ppermute | solution.py:21
  270.2 5.9 collective-permute-start
  297.8 15.7 %collective-permute-start.1 = (bf16[2,18,6,192]{3,2,1,0:T(8,128)(2,1)S(1)}, bf16[2,18,6,192]{3,2,1,0:T(8,128)(2,1)S(1)}, u32[]{:S(2)}, u32[]{:S(2)}) collective-permute-start(bf16[2,18,6,192]{3,2,1,0:T(8,128)(2,1)S(1)} %slice.93), channel_id=1, source_target_pairs={{0,8},{8,16},{16,24},{24,32},{32,40},{40,48},{48,56},{56,64},{64,7... | collective-permute-start | bytes 248840 | tf_op jit(solution)/shard_map/while/body/eval_jaxpr/ppermute | solution.py:15
  315.5 14.4 %copy-start.5 = (bf16[1,192,576]{2,1,0:T(8,128)(2,1)S(1)}, bf16[1,192,576]{2,1,0:T(8,128)(2,1)}, u32[]{:S(2)}) copy-start(bf16[1,192,576]{2,1,0:T(8,128)(2,1)} %get-tuple-element.732) | copy-start | bytes 663556 | tf_op jit(solution)/shard_map/while
  319.9 9.9 %collective-permute-start.2 = (bf16[2,18,12,192]{3,2,1,0:T(8,128)(2,1)S(1)}, bf16[2,18,12,192]{3,2,1,0:T(8,128)(2,1)S(1)}, u32[]{:S(2)}, u32[]{:S(2)}) collective-permute-start(bf16[2,18,12,192]{3,2,1,0:T(8,128)(2,1)S(1)} %fusion.129), channel_id=1, source_target_pairs={{0,1},{1,2},{2,3},{3,4},{4,5},{5,6},{6,7},{8,9},{9,10},{10,11},{11... | collective-permute-start | bytes 497672 | tf_op jit(solution)/shard_map/while/body/eval_jaxpr/ppermute | solution.py:21
  331.9 5.9 collective-permute-start
  359.5 16.2 %collective-permute-start.1 = (bf16[2,18,6,192]{3,2,1,0:T(8,128)(2,1)S(1)}, bf16[2,18,6,192]{3,2,1,0:T(8,128)(2,1)S(1)}, u32[]{:S(2)}, u32[]{:S(2)}) collective-permute-start(bf16[2,18,6,192]{3,2,1,0:T(8,128)(2,1)S(1)} %slice.93), channel_id=1, source_target_pairs={{0,8},{8,16},{16,24},{24,32},{32,40},{40,48},{48,56},{56,64},{64,7... | collective-permute-start | bytes 248840 | tf_op jit(solution)/shard_map/while/body/eval_jaxpr/ppermute | solution.py:15
  377.6 13.7 %copy-start.5 = (bf16[1,192,576]{2,1,0:T(8,128)(2,1)S(1)}, bf16[1,192,576]{2,1,0:T(8,128)(2,1)}, u32[]{:S(2)}) copy-start(bf16[1,192,576]{2,1,0:T(8,128)(2,1)} %get-tuple-element.732) | copy-start | bytes 663556 | tf_op jit(solution)/shard_map/while
  382.1 9.2 %collective-permute-start.2 = (bf16[2,18,12,192]{3,2,1,0:T(8,128)(2,1)S(1)}, bf16[2,18,12,192]{3,2,1,0:T(8,128)(2,1)S(1)}, u32[]{:S(2)}, u32[]{:S(2)}) collective-permute-start(bf16[2,18,12,192]{3,2,1,0:T(8,128)(2,1)S(1)} %fusion.129), channel_id=1, source_target_pairs={{0,1},{1,2},{2,3},{3,4},{4,5},{5,6},{6,7},{8,9},{9,10},{10,11},{11... | collective-permute-start | bytes 497672 | tf_op jit(solution)/shard_map/while/body/eval_jaxpr/ppermute | solution.py:21
  393.4 5.9 collective-permute-start
  420.9 15.8 %collective-permute-start.1 = (bf16[2,18,6,192]{3,2,1,0:T(8,128)(2,1)S(1)}, bf16[2,18,6,192]{3,2,1,0:T(8,128)(2,1)S(1)}, u32[]{:S(2)}, u32[]{:S(2)}) collective-permute-start(bf16[2,18,6,192]{3,2,1,0:T(8,128)(2,1)S(1)} %slice.93), channel_id=1, source_target_pairs={{0,8},{8,16},{16,24},{24,32},{32,40},{40,48},{48,56},{56,64},{64,7... | collective-permute-start | bytes 248840 | tf_op jit(solution)/shard_map/while/body/eval_jaxpr/ppermute | solution.py:15
  438.7 14.0 %copy-start.5 = (bf16[1,192,576]{2,1,0:T(8,128)(2,1)S(1)}, bf16[1,192,576]{2,1,0:T(8,128)(2,1)}, u32[]{:S(2)}) copy-start(bf16[1,192,576]{2,1,0:T(8,128)(2,1)} %get-tuple-element.732) | copy-start | bytes 663556 | tf_op jit(solution)/shard_map/while
  443.2 9.5 %collective-permute-start.2 = (bf16[2,18,12,192]{3,2,1,0:T(8,128)(2,1)S(1)}, bf16[2,18,12,192]{3,2,1,0:T(8,128)(2,1)S(1)}, u32[]{:S(2)}, u32[]{:S(2)}) collective-permute-start(bf16[2,18,12,192]{3,2,1,0:T(8,128)(2,1)S(1)} %fusion.129), channel_id=1, source_target_pairs={{0,1},{1,2},{2,3},{3,4},{4,5},{5,6},{6,7},{8,9},{9,10},{10,11},{11... | collective-permute-start | bytes 497672 | tf_op jit(solution)/shard_map/while/body/eval_jaxpr/ppermute | solution.py:21
  454.8 5.9 collective-permute-start
  482.3 15.8 %collective-permute-start.1 = (bf16[2,18,6,192]{3,2,1,0:T(8,128)(2,1)S(1)}, bf16[2,18,6,192]{3,2,1,0:T(8,128)(2,1)S(1)}, u32[]{:S(2)}, u32[]{:S(2)}) collective-permute-start(bf16[2,18,6,192]{3,2,1,0:T(8,128)(2,1)S(1)} %slice.93), channel_id=1, source_target_pairs={{0,8},{8,16},{16,24},{24,32},{32,40},{40,48},{48,56},{56,64},{64,7... | collective-permute-start | bytes 248840 | tf_op jit(solution)/shard_map/while/body/eval_jaxpr/ppermute | solution.py:15
  500.0 13.8 %copy-start.5 = (bf16[1,192,576]{2,1,0:T(8,128)(2,1)S(1)}, bf16[1,192,576]{2,1,0:T(8,128)(2,1)}, u32[]{:S(2)}) copy-start(bf16[1,192,576]{2,1,0:T(8,128)(2,1)} %get-tuple-element.732) | copy-start | bytes 663556 | tf_op jit(solution)/shard_map/while
  504.5 9.3 %collective-permute-start.2 = (bf16[2,18,12,192]{3,2,1,0:T(8,128)(2,1)S(1)}, bf16[2,18,12,192]{3,2,1,0:T(8,128)(2,1)S(1)}, u32[]{:S(2)}, u32[]{:S(2)}) collective-permute-start(bf16[2,18,12,192]{3,2,1,0:T(8,128)(2,1)S(1)} %fusion.129), channel_id=1, source_target_pairs={{0,1},{1,2},{2,3},{3,4},{4,5},{5,6},{6,7},{8,9},{9,10},{10,11},{11... | collective-permute-start | bytes 497672 | tf_op jit(solution)/shard_map/while/body/eval_jaxpr/ppermute | solution.py:21
  515.9 5.9 collective-permute-start
  543.4 14.7 %collective-permute-start.1 = (bf16[2,18,6,192]{3,2,1,0:T(8,128)(2,1)S(1)}, bf16[2,18,6,192]{3,2,1,0:T(8,128)(2,1)S(1)}, u32[]{:S(2)}, u32[]{:S(2)}) collective-permute-start(bf16[2,18,6,192]{3,2,1,0:T(8,128)(2,1)S(1)} %slice.93), channel_id=1, source_target_pairs={{0,8},{8,16},{16,24},{24,32},{32,40},{40,48},{48,56},{56,64},{64,7... | collective-permute-start | bytes 248840 | tf_op jit(solution)/shard_map/while/body/eval_jaxpr/ppermute | solution.py:15
  560.1 14.6 %copy-start.5 = (bf16[1,192,576]{2,1,0:T(8,128)(2,1)S(1)}, bf16[1,192,576]{2,1,0:T(8,128)(2,1)}, u32[]{:S(2)}) copy-start(bf16[1,192,576]{2,1,0:T(8,128)(2,1)} %get-tuple-element.732) | copy-start | bytes 663556 | tf_op jit(solution)/shard_map/while
  564.6 10.1 %collective-permute-start.2 = (bf16[2,18,12,192]{3,2,1,0:T(8,128)(2,1)S(1)}, bf16[2,18,12,192]{3,2,1,0:T(8,128)(2,1)S(1)}, u32[]{:S(2)}, u32[]{:S(2)}) collective-permute-start(bf16[2,18,12,192]{3,2,1,0:T(8,128)(2,1)S(1)} %fusion.129), channel_id=1, source_target_pairs={{0,1},{1,2},{2,3},{3,4},{4,5},{5,6},{6,7},{8,9},{9,10},{10,11},{11... | collective-permute-start | bytes 497672 | tf_op jit(solution)/shard_map/while/body/eval_jaxpr/ppermute | solution.py:21
  576.7 5.9 collective-permute-start
  604.3 15.7 %collective-permute-start.1 = (bf16[2,18,6,192]{3,2,1,0:T(8,128)(2,1)S(1)}, bf16[2,18,6,192]{3,2,1,0:T(8,128)(2,1)S(1)}, u32[]{:S(2)}, u32[]{:S(2)}) collective-permute-start(bf16[2,18,6,192]{3,2,1,0:T(8,128)(2,1)S(1)} %slice.93), channel_id=1, source_target_pairs={{0,8},{8,16},{16,24},{24,32},{32,40},{40,48},{48,56},{56,64},{64,7... | collective-permute-start | bytes 248840 | tf_op jit(solution)/shard_map/while/body/eval_jaxpr/ppermute | solution.py:15
  622.0 13.3 %copy-start.5 = (bf16[1,192,576]{2,1,0:T(8,128)(2,1)S(1)}, bf16[1,192,576]{2,1,0:T(8,128)(2,1)}, u32[]{:S(2)}) copy-start(bf16[1,192,576]{2,1,0:T(8,128)(2,1)} %get-tuple-element.732) | copy-start | bytes 663556 | tf_op jit(solution)/shard_map/while
  626.5 8.8 %collective-permute-start.2 = (bf16[2,18,12,192]{3,2,1,0:T(8,128)(2,1)S(1)}, bf16[2,18,12,192]{3,2,1,0:T(8,128)(2,1)S(1)}, u32[]{:S(2)}, u32[]{:S(2)}) collective-permute-start(bf16[2,18,12,192]{3,2,1,0:T(8,128)(2,1)S(1)} %fusion.129), channel_id=1, source_target_pairs={{0,1},{1,2},{2,3},{3,4},{4,5},{5,6},{6,7},{8,9},{9,10},{10,11},{11... | collective-permute-start | bytes 497672 | tf_op jit(solution)/shard_map/while/body/eval_jaxpr/ppermute | solution.py:21
  637.4 5.9 collective-permute-start
  664.9 15.9 %collective-permute-start.1 = (bf16[2,18,6,192]{3,2,1,0:T(8,128)(2,1)S(1)}, bf16[2,18,6,192]{3,2,1,0:T(8,128)(2,1)S(1)}, u32[]{:S(2)}, u32[]{:S(2)}) collective-permute-start(bf16[2,18,6,192]{3,2,1,0:T(8,128)(2,1)S(1)} %slice.93), channel_id=1, source_target_pairs={{0,8},{8,16},{16,24},{24,32},{32,40},{40,48},{48,56},{56,64},{64,7... | collective-permute-start | bytes 248840 | tf_op jit(solution)/shard_map/while/body/eval_jaxpr/ppermute | solution.py:15
  682.8 13.1 %copy-start.5 = (bf16[1,192,576]{2,1,0:T(8,128)(2,1)S(1)}, bf16[1,192,576]{2,1,0:T(8,128)(2,1)}, u32[]{:S(2)}) copy-start(bf16[1,192,576]{2,1,0:T(8,128)(2,1)} %get-tuple-element.732) | copy-start | bytes 663556 | tf_op jit(solution)/shard_map/while
  687.3 8.6 %collective-permute-start.2 = (bf16[2,18,12,192]{3,2,1,0:T(8,128)(2,1)S(1)}, bf16[2,18,12,192]{3,2,1,0:T(8,128)(2,1)S(1)}, u32[]{:S(2)}, u32[]{:S(2)}) collective-permute-start(bf16[2,18,12,192]{3,2,1,0:T(8,128)(2,1)S(1)} %fusion.129), channel_id=1, source_target_pairs={{0,1},{1,2},{2,3},{3,4},{4,5},{5,6},{6,7},{8,9},{9,10},{10,11},{11... | collective-permute-start | bytes 497672 | tf_op jit(solution)/shard_map/while/body/eval_jaxpr/ppermute | solution.py:21
  (87 other events, 102.3 us)
where the time goes:
time: 699 us; the launch traced here: 696 us
  waiting for transfers between devices  208 us (30%)
  local copies, waits for them, and re-layouts  188 us (27%)
  starting transfers between devices  119 us (17%)
  matrix products  116 us (17%)
  other arithmetic  60.6 us (9%)
    ppermute x22, waiting for transfers between devices, shifted_2(): return lax.ppermute(value, axis, pairs)  187 us
    dynamic_update_slice x11, local copies, waits for them, and re-layouts, run_block(): lax.dynamic_update_slice_in_dim(spread_out, projected, column_move, 2)  65.5 us
    ppermute x11, starting transfers between devices, shifted_3(): return lax.ppermute(block, axis, route)  61 us
    ppermute x22, starting transfers between devices, shifted_2(): return lax.ppermute(value, axis, pairs)  58.4 us
    dot_general x11, matrix products, run_block(): jnp.einsum('zlwf,fc->zlwc', hidden, weight_down, preferred_element_type=j...  46 us
    another operation x44, local copies, waits for them, and re-layouts  29.9 us
    sub x11, matrix products, window_attend(): raised = jnp.exp(scores - highest)  28.6 us
    reshape x11, local copies, waits for them, and re-layouts, window_attend(): qkv.reshape(lev_blocks, WZ, lat_blocks, WLAT, lon_blocks, WLON, 3, HEADS,...  23.8 us
  transfers between devices with their start and end apart: 33, of which 33 were waited for; matrix products, arithmetic and copies ran while one was open for 4% of the time, Pallas kernels for 0%

commit v1 on v0

v1 whole, which is shorter than its diff:
```python
import functools

import jax
import jax.numpy as jnp
import numpy as np
from jax import lax
from jax.experimental import pallas as pl
from jax.experimental.pallas import tpu as pltpu
from jax.sharding import PartitionSpec as P

HEADS = 6
WZ = 2
WLAT = 6
WLON = 12
HALF = WLON // 2
LOG2E = 1.4426950408889634


def normalize(values):
    center = values - jnp.mean(values, axis=-1, keepdims=True)
    spread = jnp.mean(center * center, axis=-1, keepdims=True)
    return center * lax.rsqrt(spread + 1e-05)


def window_bias(levels, rows):
    lat_blocks = rows // WLAT
    index = np.arange(WLAT * levels * HALF)
    row, level = index // (levels * HALF), index // HALF % levels
    row = row[None] + WLAT * np.arange(lat_blocks)[:, None]

    def label(place, length, window):
        return np.where(place < length - window, 0, np.where(place < length - window // 2, 1, 2))

    labels = label(level, levels, WZ)[None] * 3 + label(row, rows, WLAT)
    keys = np.concatenate([labels, labels], 1)
    return np.where(labels[:, :, None] == keys[:, None, :], 0.0, -1e30).astype(np.float32)


def block_kernel(shifted, own_ref, par_ref, wqkv_ref, wproj_ref, wup_ref, wdown_ref, bias_ref, out_ref):
    tokens, width = own_ref.shape
    head_size = width // HEADS
    piece = bias_ref.shape[1]
    move = piece // 2
    x = own_ref[...].astype(jnp.float32)
    y = par_ref[...].astype(jnp.float32)
    if shifted:
        x = pltpu.roll(x, tokens - move, 0)
        y = pltpu.roll(y, tokens - move, 0)
    nx = normalize(x).astype(jnp.bfloat16)
    ny = normalize(y).astype(jnp.bfloat16)
    f32 = jnp.float32
    qkv = jnp.dot(nx, wqkv_ref[...], preferred_element_type=f32)
    kv = jnp.dot(ny, wqkv_ref[:, 256:], preferred_element_type=f32)
    channel_head = lax.broadcasted_iota(jnp.int32, (1, width), 1) // head_size
    attended = []
    scale = head_size ** (-0.5) * LOG2E
    for w in range(tokens // piece):
        at = slice(w * piece, (w + 1) * piece)
        q = qkv[at, :width]
        qm = jnp.concatenate([jnp.where(channel_head == h, q, 0.0) for h in range(HEADS)], 0).astype(jnp.bfloat16)
        k = jnp.concatenate([qkv[at, 256 : 256 + width], kv[at, :width]], 0).astype(jnp.bfloat16)
        v = jnp.concatenate([qkv[at, 512 : 512 + width], kv[at, 256 : 256 + width]], 0).astype(jnp.bfloat16)
        s = lax.dot_general(qm, k, (((1,), (1,)), ((), ())), preferred_element_type=f32)
        s = s * scale
        if shifted:
            s = (s.reshape(HEADS, piece, 2 * piece) + bias_ref[w][None]).reshape(HEADS * piece, 2 * piece)
        e = jnp.exp2(s - jnp.max(s, axis=-1, keepdims=True))
        r = 1.0 / jnp.sum(e, axis=-1, keepdims=True)
        o = jnp.dot(e.astype(jnp.bfloat16), v, preferred_element_type=f32) * r
        total = jnp.zeros((piece, width), f32)
        for h in range(HEADS):
            total = jnp.where(channel_head == h, o[h * piece : (h + 1) * piece], total)
        attended.append(total)
    a = jnp.concatenate(attended, 0).astype(jnp.bfloat16)
    residual = x + jnp.dot(a, wproj_ref[...], preferred_element_type=f32)
    n2 = normalize(residual).astype(jnp.bfloat16)
    u = jnp.dot(n2, wup_ref[...], preferred_element_type=f32)
    hidden = (0.5 * u * (1.0 + lax.erf(u * (0.5**0.5)))).astype(jnp.bfloat16)
    result = residual + jnp.dot(hidden, wdown_ref[...], preferred_element_type=f32)
    if shifted:
        result = pltpu.roll(result, move, 0)
    out_ref[...] = result.astype(jnp.bfloat16)


def run_block(own, partner, weights, bias, shifted, interpret=False):
    return pl.pallas_call(
        functools.partial(block_kernel, shifted),
        out_shape=jax.ShapeDtypeStruct(own.shape, jnp.bfloat16),
        compiler_params=pltpu.CompilerParams(vmem_limit_bytes=40 * 2**20),
        interpret=interpret,
        name="odd_block" if shifted else "even_block",
    )(own, partner, *weights, bias)


def on_device(fields, land_mask, land_vector, w_qkv, w_proj, w_up, w_down):
    micro_count, levels, rows, flat_width = fields.shape
    width = land_vector.shape[0]
    tile_count, section_count = lax.axis_size("tile"), lax.axis_size("section")
    section = lax.axis_index("section")
    core, chip = section % 2, section // 2
    chips = section_count // 2
    tokens = rows * levels * HALF

    mates = [(s, s ^ 1) for s in range(section_count)]
    onward = [(s, s + 2) for s in range(section_count - 2)]
    across = []
    for t in range(tile_count):
        for c in range(chips):
            west, east = t * section_count + 2 * c + 1, (t + 1) % tile_count * section_count + 2 * c
            across += [(west, east), (east, west)]

    pack = jnp.concatenate([jnp.concatenate([w_qkv[0], w_proj[0]], 1), w_up[0], w_down[0].T], 0)
    other = lax.ppermute(pack, "section", mates)

    def unpack(p):
        qkvp, up, down = p[:width], p[width : 2 * width], p[2 * width :].T
        parts = [jnp.pad(qkvp[:, i * width : (i + 1) * width], ((0, 0), (0, 256 - width))) for i in range(3)]
        return jnp.concatenate(parts, 1), qkvp[:, 3 * width :], up, down

    even_weights = unpack(jnp.where(core == 0, pack, other))
    odd_weights = unpack(jnp.where(core == 0, other, pack))
    bias = jnp.asarray(window_bias(levels, rows))

    grid = fields.reshape(micro_count, levels, rows, WLON, width).astype(jnp.float32)
    grid = grid + land_mask.astype(jnp.float32)[None, None, :, :, None] * land_vector
    grid = grid.astype(jnp.bfloat16).reshape(micro_count, levels, rows, 2, HALF, width)
    grid = grid.transpose(0, 3, 2, 1, 4, 5).reshape(micro_count, 2, tokens, width)
    start_own = jnp.where(core == 0, grid[:, 0], grid[:, 1])
    start_partner = jnp.where(core == 0, grid[:, 1], grid[:, 0])

    evens, odds = [], []
    own, partner = start_own[0], start_partner[0]
    for tick in range(micro_count + chips - 1):
        even = run_block(own, partner, even_weights, bias, False)
        odd = run_block(even, lax.ppermute(even, ("tile", "section"), across), odd_weights, bias, True)
        evens.append(even)
        odds.append(odd)
        if tick == micro_count + chips - 2:
            break
        own = lax.ppermute(odd, "section", onward)
        partner = lax.ppermute(own, "section", mates)
        if tick + 1 < micro_count:
            own = jnp.where(chip == 0, start_own[tick + 1], own)
            partner = jnp.where(chip == 0, start_partner[tick + 1], partner)

    evens = lax.dynamic_slice_in_dim(jnp.stack(evens), chip, micro_count, 0)
    odds = lax.dynamic_slice_in_dim(jnp.stack(odds), chip, micro_count, 0)
    mine = jnp.where(core == 0, evens, odds)
    theirs = lax.ppermute(jnp.where(core == 0, odds, evens), "section", mates)
    halves = jnp.stack([jnp.where(core == 0, mine, theirs), jnp.where(core == 0, theirs, mine)], 1)
    out = halves.reshape(micro_count, 2, rows, levels, HALF, width).transpose(0, 3, 2, 1, 4, 5)
    return out.reshape(1, micro_count, levels, rows, flat_width)


def solution(mesh):
    in_specs = (
        P(None, None, None, "tile"),
        P(None, "tile"),
        P(),
        P("section", None, None),
        P("section", None, None),
        P("section", None, None),
        P("section", None, None),
    )
    out_specs = P("section", None, None, None, "tile")
    return jax.shard_map(on_device, mesh=mesh, in_specs=in_specs, out_specs=out_specs, check_vma=False)
```

time: 699 us -> 220 us (0.31)
  waiting for transfers between devices: 208 us -> 38.9 us
  local copies, waits for them, and re-layouts: 188 us -> 20.5 us
  matrix products: 116 us -> 0 us
  other arithmetic: 60.6 us -> 6.87 us
  Pallas kernels: 0 us -> 24 us
  starting transfers between devices: 119 us -> 128 us
    ppermute x33 -> x21, waiting for transfers between devices: 208 us -> 38.9 us  [the longest x7 24.6 us: on_device(): lax.ppermute(even, ('tile', 'section'), across)]
    dot_general x55 -> x0, matrix products: 87.5 us -> none  [the longest x11 46 us: run_block(): jnp.einsum('zlwf,fc->zlwc', hidden, weight_down, preferred_element_type=j...]
    dynamic_update_slice x11 -> x0, local copies, waits for them, and re-layouts: 65.5 us -> none  [run_block(): lax.dynamic_update_slice_in_dim(spread_out, projected, column_move, 2)]
    reshape x55 -> x1, local copies, waits for them, and re-layouts: 40.2 us -> 1.96 us  [on_device(): return out.reshape(1, micro_count, levels, rows, flat_width)]
    another operation x44 -> x1, local copies, waits for them, and re-layouts: 29.9 us -> 0.01 us  [on_device(): evens = lax.dynamic_slice_in_dim(jnp.stack(evens), chip, micro_count, 0)]
    sub x11 -> x0, matrix products: 28.6 us -> none  [window_attend(): raised = jnp.exp(scores - highest)]
    pallas_call x0 -> x13, Pallas kernels: none -> 24 us  [run_block(): pl.pallas_call(functools.partial(block_kernel, shifted), out_shape=jax.Sh...]
    slice x66 -> x6, local copies, waits for them, and re-layouts: 26.3 us -> 3.42 us  [the longest x2 1.3 us: unpack(): qkvp, up, down = (p[:width], p[width:2 * width], p[2 * width:].T)]
  transfers between devices with their start and end apart: 33 -> 21, of which waited for: 33 -> 16; matrix products, arithmetic and copies ran while one was open for 4% -> 5% of each run, Pallas kernels for 0% -> 0%
where the time goes in v1:
time: 220 us; the launch traced here: 219 us
  starting transfers between devices  128 us (58%)
  waiting for transfers between devices  38.9 us (18%)
  Pallas kernels  24 us (11%)
  local copies, waits for them, and re-layouts  20.5 us (9%)
  other arithmetic  6.87 us (3%)
    ppermute x6, starting transfers between devices, on_device(): partner = lax.ppermute(own, 'section', mates)  73.1 us
    ppermute x7, waiting for transfers between devices, on_device(): lax.ppermute(even, ('tile', 'section'), across)  24.6 us
    pallas_call x13, Pallas kernels, run_block(): pl.pallas_call(functools.partial(block_kernel, shifted), out_shape=jax.Sh...  24 us
    ppermute x6, starting transfers between devices, on_device(): own = lax.ppermute(odd, 'section', onward)  21.5 us
    ppermute x7, starting transfers between devices, on_device(): lax.ppermute(even, ('tile', 'section'), across)  13.6 us
    ppermute x1, starting transfers between devices, on_device(): theirs = lax.ppermute(jnp.where(core == 0, odds, evens), 'section', mates)  11 us
    ppermute x6, waiting for transfers between devices, on_device(): own = lax.ppermute(odd, 'section', onward)  10.3 us
    ppermute x1, starting transfers between devices, on_device(): other = lax.ppermute(pack, 'section', mates)  8.79 us
  transfers between devices with their start and end apart: 21, of which 16 were waited for; matrix products, arithmetic and copies ran while one was open for 5% of the time, Pallas kernels for 0%

profile of v1, /device:TPU:1, one launch (start us, length us, event | category | flops | bytes accessed | tf_op | source)
XLA Modules:
  0.0 219.2 jit_solution(10758604884292004387)
XLA Ops:
  6.4 8.8 %collective-permute-start = (bf16[576,768]{1,0:T(8,128)(2,1)}, bf16[576,768]{1,0:T(8,128)(2,1)}, u32[]{:S(2)}, u32[]{:S(2)}) collective-permute-start(bf16[576,768]{1,0:T(8,128)(2,1)} %copy.119), channel_id=1, source_target_pairs={{0,1},{1,0},{2,3},{3,2},{4,5},{5,4},{6,7},{7,6},{8,9},{9,8},{10,11... | collective-permute-start | bytes 2654216 | tf_op jit(solution)/shard_map/ppermute | solution.py:113
  24.3 1.8 even_block.7.own_ref
  26.1 1.9 collective-permute-start.1
  28.0 1.7 fusion.11
  32.2 1.9 odd_block.7
  35.4 1.7 collective-permute-done.2
  37.1 13.4 %collective-permute-start.3 = (bf16[216,192]{1,0:T(8,128)(2,1)S(1)}, bf16[216,192]{1,0:T(8,128)(2,1)S(1)}, u32[]{:S(2)}, u32[]{:S(2)}) collective-permute-start(bf16[216,192]{1,0:T(8,128)(2,1)S(1)} %collective-permute-done.2), channel_id=1, source_target_pairs={{0,1},{1,0},{2,3},{3,2},{4,5},{5,4},{6,7},{7,6},{8,9},{9,8},{10,11... | collective-permute-start | bytes 248840 | tf_op jit(solution)/shard_map/ppermute | solution.py:141
  51.4 1.8 even_block.8.own_ref
  53.3 2.1 collective-permute-start.4
  55.4 4.0 %collective-permute-done.4.par_ref = bf16[216,192]{1,0:T(8,128)(2,1)S(1)} collective-permute-done((bf16[216,192]{1,0:T(8,128)(2,1)S(1)}, bf16[216,192]{1,0:T(8,128)(2,1)S(1)}, u32[]{:S(2)}, u32[]{:S(2)}) %collective-permute-start.4) | collective-permute-done | bytes 82976 | tf_op jit(solution)/shard_map/ppermute | solution.py:135
  59.3 1.9 odd_block.8
  61.2 4.0 %collective-permute-start.5 = (bf16[216,192]{1,0:T(8,128)(2,1)S(1)}, bf16[216,192]{1,0:T(8,128)(2,1)S(1)}, u32[]{:S(2)}, u32[]{:S(2)}) collective-permute-start(bf16[216,192]{1,0:T(8,128)(2,1)S(1)} %odd_block.8), channel_id=1, source_target_pairs={{0,2},{1,3},{2,4},{3,5},{4,6},{5,7},{8,10},{9,11},{10,12},{11,13},... | collective-permute-start | bytes 248840 | tf_op jit(solution)/shard_map/ppermute | solution.py:140
  65.3 1.7 collective-permute-done.5
  67.0 11.9 %collective-permute-start.6 = (bf16[216,192]{1,0:T(8,128)(2,1)S(1)}, bf16[216,192]{1,0:T(8,128)(2,1)S(1)}, u32[]{:S(2)}, u32[]{:S(2)}) collective-permute-start(bf16[216,192]{1,0:T(8,128)(2,1)S(1)} %collective-permute-done.5), channel_id=1, source_target_pairs={{0,1},{1,0},{2,3},{3,2},{4,5},{5,4},{6,7},{7,6},{8,9},{9,8},{10,11... | collective-permute-start | bytes 248840 | tf_op jit(solution)/shard_map/ppermute | solution.py:141
  79.9 1.8 even_block.9.own_ref
  81.7 1.9 collective-permute-start.7
  83.7 4.1 %collective-permute-done.7.par_ref = bf16[216,192]{1,0:T(8,128)(2,1)S(1)} collective-permute-done((bf16[216,192]{1,0:T(8,128)(2,1)S(1)}, bf16[216,192]{1,0:T(8,128)(2,1)S(1)}, u32[]{:S(2)}, u32[]{:S(2)}) %collective-permute-start.7) | collective-permute-done | bytes 82976 | tf_op jit(solution)/shard_map/ppermute | solution.py:135
  87.8 1.9 odd_block.9
  89.6 4.0 %collective-permute-start.8 = (bf16[216,192]{1,0:T(8,128)(2,1)S(1)}, bf16[216,192]{1,0:T(8,128)(2,1)S(1)}, u32[]{:S(2)}, u32[]{:S(2)}) collective-permute-start(bf16[216,192]{1,0:T(8,128)(2,1)S(1)} %odd_block.9), channel_id=1, source_target_pairs={{0,2},{1,3},{2,4},{3,5},{4,6},{5,7},{8,10},{9,11},{10,12},{11,13},... | collective-permute-start | bytes 248840 | tf_op jit(solution)/shard_map/ppermute | solution.py:140
  93.7 1.7 collective-permute-done.8
  95.4 11.9 %collective-permute-start.9 = (bf16[216,192]{1,0:T(8,128)(2,1)S(1)}, bf16[216,192]{1,0:T(8,128)(2,1)S(1)}, u32[]{:S(2)}, u32[]{:S(2)}) collective-permute-start(bf16[216,192]{1,0:T(8,128)(2,1)S(1)} %collective-permute-done.8), channel_id=1, source_target_pairs={{0,1},{1,0},{2,3},{3,2},{4,5},{5,4},{6,7},{7,6},{8,9},{9,8},{10,11... | collective-permute-start | bytes 248840 | tf_op jit(solution)/shard_map/ppermute | solution.py:141
  108.3 1.8 even_block.10.own_ref
  110.2 1.9 collective-permute-start.10
  112.1 4.1 %collective-permute-done.10.par_ref = bf16[216,192]{1,0:T(8,128)(2,1)S(1)} collective-permute-done((bf16[216,192]{1,0:T(8,128)(2,1)S(1)}, bf16[216,192]{1,0:T(8,128)(2,1)S(1)}, u32[]{:S(2)}, u32[]{:S(2)}) %collective-permute-start.10) | collective-permute-done | bytes 82976 | tf_op jit(solution)/shard_map/ppermute | solution.py:135
  116.2 1.9 odd_block.10
  118.1 4.0 %collective-permute-start.11 = (bf16[216,192]{1,0:T(8,128)(2,1)S(1)}, bf16[216,192]{1,0:T(8,128)(2,1)S(1)}, u32[]{:S(2)}, u32[]{:S(2)}) collective-permute-start(bf16[216,192]{1,0:T(8,128)(2,1)S(1)} %odd_block.10), channel_id=1, source_target_pairs={{0,2},{1,3},{2,4},{3,5},{4,6},{5,7},{8,10},{9,11},{10,12},{11,13},... | collective-permute-start | bytes 248840 | tf_op jit(solution)/shard_map/ppermute | solution.py:140
  122.2 1.7 collective-permute-done.11.own_ref
  123.9 11.9 %collective-permute-start.12 = (bf16[216,192]{1,0:T(8,128)(2,1)S(1)}, bf16[216,192]{1,0:T(8,128)(2,1)S(1)}, u32[]{:S(2)}, u32[]{:S(2)}) collective-permute-start(bf16[216,192]{1,0:T(8,128)(2,1)S(1)} %collective-permute-done.11.own_ref), channel_id=1, source_target_pairs={{0,1},{1,0},{2,3},{3,2},{4,5},{5,4},{6,7},{7,6},{8,9},{9,8},{10,11... | collective-permute-start | bytes 248840 | tf_op jit(solution)/shard_map/ppermute | solution.py:141
  136.7 1.8 even_block.11.own_ref
  138.6 1.9 collective-permute-start.13
  140.5 4.1 %collective-permute-done.13.par_ref = bf16[216,192]{1,0:T(8,128)(2,1)S(1)} collective-permute-done((bf16[216,192]{1,0:T(8,128)(2,1)S(1)}, bf16[216,192]{1,0:T(8,128)(2,1)S(1)}, u32[]{:S(2)}, u32[]{:S(2)}) %collective-permute-start.13) | collective-permute-done | bytes 82976 | tf_op jit(solution)/shard_map/ppermute | solution.py:135
  144.6 1.9 odd_block.11
  146.5 4.0 %collective-permute-start.14 = (bf16[216,192]{1,0:T(8,128)(2,1)S(1)}, bf16[216,192]{1,0:T(8,128)(2,1)S(1)}, u32[]{:S(2)}, u32[]{:S(2)}) collective-permute-start(bf16[216,192]{1,0:T(8,128)(2,1)S(1)} %odd_block.11), channel_id=1, source_target_pairs={{0,2},{1,3},{2,4},{3,5},{4,6},{5,7},{8,10},{9,11},{10,12},{11,13},... | collective-permute-start | bytes 248840 | tf_op jit(solution)/shard_map/ppermute | solution.py:140
  150.6 1.7 collective-permute-done.14.own_ref
  152.3 12.1 %collective-permute-start.15 = (bf16[216,192]{1,0:T(8,128)(2,1)S(1)}, bf16[216,192]{1,0:T(8,128)(2,1)S(1)}, u32[]{:S(2)}, u32[]{:S(2)}) collective-permute-start(bf16[216,192]{1,0:T(8,128)(2,1)S(1)} %collective-permute-done.14.own_ref), channel_id=1, source_target_pairs={{0,1},{1,0},{2,3},{3,2},{4,5},{5,4},{6,7},{7,6},{8,9},{9,8},{10,11... | collective-permute-start | bytes 248840 | tf_op jit(solution)/shard_map/ppermute | solution.py:141
  165.1 1.8 even_block.12.own_ref
  167.0 1.9 collective-permute-start.16
  168.9 4.1 %collective-permute-done.16.par_ref = bf16[216,192]{1,0:T(8,128)(2,1)S(1)} collective-permute-done((bf16[216,192]{1,0:T(8,128)(2,1)S(1)}, bf16[216,192]{1,0:T(8,128)(2,1)S(1)}, u32[]{:S(2)}, u32[]{:S(2)}) %collective-permute-start.16) | collective-permute-done | bytes 82976 | tf_op jit(solution)/shard_map/ppermute | solution.py:135
  173.0 1.9 odd_block.12
  174.9 4.0 %collective-permute-start.17 = (bf16[216,192]{1,0:T(8,128)(2,1)S(1)}, bf16[216,192]{1,0:T(8,128)(2,1)S(1)}, u32[]{:S(2)}, u32[]{:S(2)}) collective-permute-start(bf16[216,192]{1,0:T(8,128)(2,1)S(1)} %odd_block.12), channel_id=1, source_target_pairs={{0,2},{1,3},{2,4},{3,5},{4,6},{5,7},{8,10},{9,11},{10,12},{11,13},... | collective-permute-start | bytes 248840 | tf_op jit(solution)/shard_map/ppermute | solution.py:140
  179.0 1.7 collective-permute-done.17.own_ref
  180.7 11.9 %collective-permute-start.18 = (bf16[216,192]{1,0:T(8,128)(2,1)S(1)}, bf16[216,192]{1,0:T(8,128)(2,1)S(1)}, u32[]{:S(2)}, u32[]{:S(2)}) collective-permute-start(bf16[216,192]{1,0:T(8,128)(2,1)S(1)} %collective-permute-done.17.own_ref), channel_id=1, source_target_pairs={{0,1},{1,0},{2,3},{3,2},{4,5},{5,4},{6,7},{7,6},{8,9},{9,8},{10,11... | collective-permute-start | bytes 248840 | tf_op jit(solution)/shard_map/ppermute | solution.py:141
  193.5 1.8 even_block.13
  195.4 1.9 collective-permute-start.19
  197.3 4.1 %collective-permute-done.19 = bf16[216,192]{1,0:T(8,128)(2,1)S(1)} collective-permute-done((bf16[216,192]{1,0:T(8,128)(2,1)S(1)}, bf16[216,192]{1,0:T(8,128)(2,1)S(1)}, u32[]{:S(2)}, u32[]{:S(2)}) %collective-permute-start.19) | collective-permute-done | bytes 82976 | tf_op jit(solution)/shard_map/ppermute | solution.py:135
  201.4 1.9 odd_block.13
  203.4 11.0 %collective-permute-start.20 = (bf16[4,216,192]{2,1,0:T(8,128)(2,1)S(1)}, bf16[4,216,192]{2,1,0:T(8,128)(2,1)S(1)}, u32[]{:S(2)}, u32[]{:S(2)}) collective-permute-start(bf16[4,216,192]{2,1,0:T(8,128)(2,1)S(1)} %broadcast_select_fusion.6), channel_id=1, source_target_pairs={{0,1},{1,0},{2,3},{3,2},{4,5},{5,4},{6,7},{7,6},{8,9},{9,8},{10,11... | collective-permute-start | bytes 995336 | tf_op jit(solution)/shard_map/ppermute | solution.py:149
  217.3 2.0 reshape.48
  (89 shorter events, 27.2 us)
Async XLA Ops:
  1.1 5.2 %copy-start.1 = (bf16[1,768,192]{2,1,0:T(8,128)(2,1)}, bf16[1,768,192]{2,1,0:T(8,128)(2,1)S(1)}, u32[]{:S(2)}) copy-start(bf16[1,768,192]{2,1,0:T(8,128)(2,1)S(1)} %copy.118) | copy-start | bytes 884740
  2.4 3.9 %copy-start.3 = (bf16[1,192,768]{1,2,0:T(8,128)(2,1)}, bf16[1,192,768]{1,2,0:T(8,128)(2,1)S(1)}, u32[]{:S(2)}) copy-start(bf16[1,192,768]{1,2,0:T(8,128)(2,1)S(1)} %copy.117) | copy-start | bytes 884740
  3.5 2.8 %copy-start.8 = (bf16[1,192,192]{1,2,0:T(8,128)(2,1)}, bf16[1,192,192]{1,2,0:T(8,128)(2,1)S(1)}, u32[]{:S(2)}) copy-start(bf16[1,192,192]{1,2,0:T(8,128)(2,1)S(1)} %copy.116) | copy-start | bytes 221188
  4.7 1.7 copy-start.5
  4.7 10.5 %copy-start.10 = (bf16[4,2,18,2304]{3,1,2,0:T(2,128)(2,1)S(1)}, bf16[4,2,18,2304]{3,1,2,0:T(2,128)(2,1)}, u32[]{:S(2)}) copy-start(bf16[4,2,18,2304]{3,1,2,0:T(2,128)(2,1)} %param.8) | copy-start | bytes 1990660
  6.4 9.8 %copy-start.11 = (s32[18,12]{0,1:T(8,128)S(1)}, s32[18,12]{0,1:T(8,128)}, u32[]{:S(2)}) copy-start(s32[18,12]{0,1:T(8,128)} %param.9) | copy-start | bytes 2596
  6.4 10.0 %copy-start.12 = (f32[192]{0:T(256)S(1)}, f32[192]{0:T(256)}, u32[]{:S(2)}) copy-start(f32[192]{0:T(256)} %param.10) | copy-start | bytes 2308
  6.4 13.4 %collective-permute-start = (bf16[576,768]{1,0:T(8,128)(2,1)}, bf16[576,768]{1,0:T(8,128)(2,1)}, u32[]{:S(2)}, u32[]{:S(2)}) collective-permute-start(bf16[576,768]{1,0:T(8,128)(2,1)} %copy.119), channel_id=1, source_target_pairs={{0,1},{1,0},{2,3},{3,2},{4,5},{5,4},{6,7},{7,6},{8,9},{9,8},{10,11... | collective-permute-start | bytes 2654216 | tf_op jit(solution)/shard_map/ppermute | solution.py:113
  18.9 2.5 %copy-start.2 = (bf16[1,768,192]{2,1,0:T(8,128)(2,1)S(1)}, bf16[1,768,192]{2,1,0:T(8,128)(2,1)}, u32[]{:S(2)}) copy-start(bf16[1,768,192]{2,1,0:T(8,128)(2,1)} %copy-done.1) | copy-start | bytes 884740
  18.9 2.5 %copy-start.4 = (bf16[1,192,768]{1,2,0:T(8,128)(2,1)S(1)}, bf16[1,192,768]{1,2,0:T(8,128)(2,1)}, u32[]{:S(2)}) copy-start(bf16[1,192,768]{1,2,0:T(8,128)(2,1)} %copy-done.3) | copy-start | bytes 884740
  18.9 2.5 %copy-start.6 = (bf16[1,192,576]{1,2,0:T(8,128)(2,1)S(1)}, bf16[1,192,576]{1,2,0:T(8,128)(2,1)}, u32[]{:S(2)}) copy-start(bf16[1,192,576]{1,2,0:T(8,128)(2,1)} %copy-done.5) | copy-start | bytes 663556
  18.9 2.5 %copy-start.9 = (bf16[1,192,192]{1,2,0:T(8,128)(2,1)S(1)}, bf16[1,192,192]{1,2,0:T(8,128)(2,1)}, u32[]{:S(2)}) copy-start(bf16[1,192,192]{1,2,0:T(8,128)(2,1)} %copy-done.8) | copy-start | bytes 221188
  19.1 0.8 copy-start.7
  22.8 1.4 copy-start
  26.1 6.1 %collective-permute-start.1 = (bf16[216,192]{1,0:T(8,128)(2,1)S(1)}, bf16[216,192]{1,0:T(8,128)(2,1)S(1)}, u32[]{:S(2)}, u32[]{:S(2)}) collective-permute-start(bf16[216,192]{1,0:T(8,128)(2,1)S(1)} %even_block.7.own_ref), channel_id=1, source_target_pairs={{1,8},{8,1},{3,10},{10,3},{5,12},{12,5},{7,14},{14,7},{9,16},{16,9... | collective-permute-start | bytes 248840 | tf_op jit(solution)/shard_map/ppermute | solution.py:135
  34.0 3.0 %collective-permute-start.2 = (bf16[216,192]{1,0:T(8,128)(2,1)S(1)}, bf16[216,192]{1,0:T(8,128)(2,1)S(1)}, u32[]{:S(2)}, u32[]{:S(2)}) collective-permute-start(bf16[216,192]{1,0:T(8,128)(2,1)S(1)} %odd_block.7), channel_id=1, source_target_pairs={{0,2},{1,3},{2,4},{3,5},{4,6},{5,7},{8,10},{9,11},{10,12},{11,13},... | collective-permute-start | bytes 248840 | tf_op jit(solution)/shard_map/ppermute | solution.py:140
  37.1 14.3 %collective-permute-start.3 = (bf16[216,192]{1,0:T(8,128)(2,1)S(1)}, bf16[216,192]{1,0:T(8,128)(2,1)S(1)}, u32[]{:S(2)}, u32[]{:S(2)}) collective-permute-start(bf16[216,192]{1,0:T(8,128)(2,1)S(1)} %collective-permute-done.2), channel_id=1, source_target_pairs={{0,1},{1,0},{2,3},{3,2},{4,5},{5,4},{6,7},{7,6},{8,9},{9,8},{10,11... | collective-permute-start | bytes 248840 | tf_op jit(solution)/shard_map/ppermute | solution.py:141
  53.3 6.1 %collective-permute-start.4 = (bf16[216,192]{1,0:T(8,128)(2,1)S(1)}, bf16[216,192]{1,0:T(8,128)(2,1)S(1)}, u32[]{:S(2)}, u32[]{:S(2)}) collective-permute-start(bf16[216,192]{1,0:T(8,128)(2,1)S(1)} %even_block.8.own_ref), channel_id=1, source_target_pairs={{1,8},{8,1},{3,10},{10,3},{5,12},{12,5},{7,14},{14,7},{9,16},{16,9... | collective-permute-start | bytes 248840 | tf_op jit(solution)/shard_map/ppermute | solution.py:135
  61.2 5.8 %collective-permute-start.5 = (bf16[216,192]{1,0:T(8,128)(2,1)S(1)}, bf16[216,192]{1,0:T(8,128)(2,1)S(1)}, u32[]{:S(2)}, u32[]{:S(2)}) collective-permute-start(bf16[216,192]{1,0:T(8,128)(2,1)S(1)} %odd_block.8), channel_id=1, source_target_pairs={{0,2},{1,3},{2,4},{3,5},{4,6},{5,7},{8,10},{9,11},{10,12},{11,13},... | collective-permute-start | bytes 248840 | tf_op jit(solution)/shard_map/ppermute | solution.py:140
  67.0 12.9 %collective-permute-start.6 = (bf16[216,192]{1,0:T(8,128)(2,1)S(1)}, bf16[216,192]{1,0:T(8,128)(2,1)S(1)}, u32[]{:S(2)}, u32[]{:S(2)}) collective-permute-start(bf16[216,192]{1,0:T(8,128)(2,1)S(1)} %collective-permute-done.5), channel_id=1, source_target_pairs={{0,1},{1,0},{2,3},{3,2},{4,5},{5,4},{6,7},{7,6},{8,9},{9,8},{10,11... | collective-permute-start | bytes 248840 | tf_op jit(solution)/shard_map/ppermute | solution.py:141
  81.7 6.1 %collective-permute-start.7 = (bf16[216,192]{1,0:T(8,128)(2,1)S(1)}, bf16[216,192]{1,0:T(8,128)(2,1)S(1)}, u32[]{:S(2)}, u32[]{:S(2)}) collective-permute-start(bf16[216,192]{1,0:T(8,128)(2,1)S(1)} %even_block.9.own_ref), channel_id=1, source_target_pairs={{1,8},{8,1},{3,10},{10,3},{5,12},{12,5},{7,14},{14,7},{9,16},{16,9... | collective-permute-start | bytes 248840 | tf_op jit(solution)/shard_map/ppermute | solution.py:135
  89.6 5.8 %collective-permute-start.8 = (bf16[216,192]{1,0:T(8,128)(2,1)S(1)}, bf16[216,192]{1,0:T(8,128)(2,1)S(1)}, u32[]{:S(2)}, u32[]{:S(2)}) collective-permute-start(bf16[216,192]{1,0:T(8,128)(2,1)S(1)} %odd_block.9), channel_id=1, source_target_pairs={{0,2},{1,3},{2,4},{3,5},{4,6},{5,7},{8,10},{9,11},{10,12},{11,13},... | collective-permute-start | bytes 248840 | tf_op jit(solution)/shard_map/ppermute | solution.py:140
  95.4 12.8 %collective-permute-start.9 = (bf16[216,192]{1,0:T(8,128)(2,1)S(1)}, bf16[216,192]{1,0:T(8,128)(2,1)S(1)}, u32[]{:S(2)}, u32[]{:S(2)}) collective-permute-start(bf16[216,192]{1,0:T(8,128)(2,1)S(1)} %collective-permute-done.8), channel_id=1, source_target_pairs={{0,1},{1,0},{2,3},{3,2},{4,5},{5,4},{6,7},{7,6},{8,9},{9,8},{10,11... | collective-permute-start | bytes 248840 | tf_op jit(solution)/shard_map/ppermute | solution.py:141
  110.2 6.1 %collective-permute-start.10 = (bf16[216,192]{1,0:T(8,128)(2,1)S(1)}, bf16[216,192]{1,0:T(8,128)(2,1)S(1)}, u32[]{:S(2)}, u32[]{:S(2)}) collective-permute-start(bf16[216,192]{1,0:T(8,128)(2,1)S(1)} %even_block.10.own_ref), channel_id=1, source_target_pairs={{1,8},{8,1},{3,10},{10,3},{5,12},{12,5},{7,14},{14,7},{9,16},{16,9... | collective-permute-start | bytes 248840 | tf_op jit(solution)/shard_map/ppermute | solution.py:135
  118.1 5.8 %collective-permute-start.11 = (bf16[216,192]{1,0:T(8,128)(2,1)S(1)}, bf16[216,192]{1,0:T(8,128)(2,1)S(1)}, u32[]{:S(2)}, u32[]{:S(2)}) collective-permute-start(bf16[216,192]{1,0:T(8,128)(2,1)S(1)} %odd_block.10), channel_id=1, source_target_pairs={{0,2},{1,3},{2,4},{3,5},{4,6},{5,7},{8,10},{9,11},{10,12},{11,13},... | collective-permute-start | bytes 248840 | tf_op jit(solution)/shard_map/ppermute | solution.py:140
  123.9 12.8 %collective-permute-start.12 = (bf16[216,192]{1,0:T(8,128)(2,1)S(1)}, bf16[216,192]{1,0:T(8,128)(2,1)S(1)}, u32[]{:S(2)}, u32[]{:S(2)}) collective-permute-start(bf16[216,192]{1,0:T(8,128)(2,1)S(1)} %collective-permute-done.11.own_ref), channel_id=1, source_target_pairs={{0,1},{1,0},{2,3},{3,2},{4,5},{5,4},{6,7},{7,6},{8,9},{9,8},{10,11... | collective-permute-start | bytes 248840 | tf_op jit(solution)/shard_map/ppermute | solution.py:141
  138.6 6.1 %collective-permute-start.13 = (bf16[216,192]{1,0:T(8,128)(2,1)S(1)}, bf16[216,192]{1,0:T(8,128)(2,1)S(1)}, u32[]{:S(2)}, u32[]{:S(2)}) collective-permute-start(bf16[216,192]{1,0:T(8,128)(2,1)S(1)} %even_block.11.own_ref), channel_id=1, source_target_pairs={{1,8},{8,1},{3,10},{10,3},{5,12},{12,5},{7,14},{14,7},{9,16},{16,9... | collective-permute-start | bytes 248840 | tf_op jit(solution)/shard_map/ppermute | solution.py:135
  146.5 5.8 %collective-permute-start.14 = (bf16[216,192]{1,0:T(8,128)(2,1)S(1)}, bf16[216,192]{1,0:T(8,128)(2,1)S(1)}, u32[]{:S(2)}, u32[]{:S(2)}) collective-permute-start(bf16[216,192]{1,0:T(8,128)(2,1)S(1)} %odd_block.11), channel_id=1, source_target_pairs={{0,2},{1,3},{2,4},{3,5},{4,6},{5,7},{8,10},{9,11},{10,12},{11,13},... | collective-permute-start | bytes 248840 | tf_op jit(solution)/shard_map/ppermute | solution.py:140
  152.3 12.8 %collective-permute-start.15 = (bf16[216,192]{1,0:T(8,128)(2,1)S(1)}, bf16[216,192]{1,0:T(8,128)(2,1)S(1)}, u32[]{:S(2)}, u32[]{:S(2)}) collective-permute-start(bf16[216,192]{1,0:T(8,128)(2,1)S(1)} %collective-permute-done.14.own_ref), channel_id=1, source_target_pairs={{0,1},{1,0},{2,3},{3,2},{4,5},{5,4},{6,7},{7,6},{8,9},{9,8},{10,11... | collective-permute-start | bytes 248840 | tf_op jit(solution)/shard_map/ppermute | solution.py:141
  167.0 6.1 %collective-permute-start.16 = (bf16[216,192]{1,0:T(8,128)(2,1)S(1)}, bf16[216,192]{1,0:T(8,128)(2,1)S(1)}, u32[]{:S(2)}, u32[]{:S(2)}) collective-permute-start(bf16[216,192]{1,0:T(8,128)(2,1)S(1)} %even_block.12.own_ref), channel_id=1, source_target_pairs={{1,8},{8,1},{3,10},{10,3},{5,12},{12,5},{7,14},{14,7},{9,16},{16,9... | collective-permute-start | bytes 248840 | tf_op jit(solution)/shard_map/ppermute | solution.py:135
  174.9 5.8 %collective-permute-start.17 = (bf16[216,192]{1,0:T(8,128)(2,1)S(1)}, bf16[216,192]{1,0:T(8,128)(2,1)S(1)}, u32[]{:S(2)}, u32[]{:S(2)}) collective-permute-start(bf16[216,192]{1,0:T(8,128)(2,1)S(1)} %odd_block.12), channel_id=1, source_target_pairs={{0,2},{1,3},{2,4},{3,5},{4,6},{5,7},{8,10},{9,11},{10,12},{11,13},... | collective-permute-start | bytes 248840 | tf_op jit(solution)/shard_map/ppermute | solution.py:140
  180.7 12.8 %collective-permute-start.18 = (bf16[216,192]{1,0:T(8,128)(2,1)S(1)}, bf16[216,192]{1,0:T(8,128)(2,1)S(1)}, u32[]{:S(2)}, u32[]{:S(2)}) collective-permute-start(bf16[216,192]{1,0:T(8,128)(2,1)S(1)} %collective-permute-done.17.own_ref), channel_id=1, source_target_pairs={{0,1},{1,0},{2,3},{3,2},{4,5},{5,4},{6,7},{7,6},{8,9},{9,8},{10,11... | collective-permute-start | bytes 248840 | tf_op jit(solution)/shard_map/ppermute | solution.py:141
  195.4 6.1 %collective-permute-start.19 = (bf16[216,192]{1,0:T(8,128)(2,1)S(1)}, bf16[216,192]{1,0:T(8,128)(2,1)S(1)}, u32[]{:S(2)}, u32[]{:S(2)}) collective-permute-start(bf16[216,192]{1,0:T(8,128)(2,1)S(1)} %even_block.13), channel_id=1, source_target_pairs={{1,8},{8,1},{3,10},{10,3},{5,12},{12,5},{7,14},{14,7},{9,16},{16,9... | collective-permute-start | bytes 248840 | tf_op jit(solution)/shard_map/ppermute | solution.py:135
  203.4 12.5 %collective-permute-start.20 = (bf16[4,216,192]{2,1,0:T(8,128)(2,1)S(1)}, bf16[4,216,192]{2,1,0:T(8,128)(2,1)S(1)}, u32[]{:S(2)}, u32[]{:S(2)}) collective-permute-start(bf16[4,216,192]{2,1,0:T(8,128)(2,1)S(1)} %broadcast_select_fusion.6), channel_id=1, source_target_pairs={{0,1},{1,0},{2,3},{3,2},{4,5},{5,4},{6,7},{7,6},{8,9},{9,8},{10,11... | collective-permute-start | bytes 995336 | tf_op jit(solution)/shard_map/ppermute | solution.py:149

commit v2 on v1

v2 whole, which is shorter than its diff:
```python
import functools

import jax
import jax.numpy as jnp
import numpy as np
from jax import lax
from jax.experimental import pallas as pl
from jax.experimental.pallas import tpu as pltpu
from jax.sharding import PartitionSpec as P

HEADS = 6
WZ = 2
WLAT = 6
WLON = 12
HALF = WLON // 2
STAGE = 4
REACH = 2
LOG2E = 1.4426950408889634
LANES = 128
VMEM_LIMIT = 56 * 2**20


def normalize(values):
    center = values - jnp.mean(values, axis=-1, keepdims=True)
    spread = jnp.mean(center * center, axis=-1, keepdims=True)
    return center * lax.rsqrt(spread + 1e-05)


def window_bias(levels, rows):
    lat_blocks = rows // WLAT
    index = np.arange(WLAT * levels * HALF)
    row, level = index // (levels * HALF), index // HALF % levels
    row = row[None] + WLAT * np.arange(lat_blocks)[:, None]

    def label(place, length, window):
        return np.where(place < length - window, 0, np.where(place < length - window // 2, 1, 2))

    labels = label(level, levels, WZ)[None] * 3 + label(row, rows, WLAT)
    keys = np.concatenate([labels, labels], 1)
    return np.where(labels[:, :, None] == keys[:, None, :], 0.0, -1e30).astype(np.float32)


def pack_tile(west, east):
    return jnp.concatenate(
        [west[:, :LANES], east[:, :LANES], jnp.concatenate([west[:, LANES:], east[:, LANES:]], 1)], 0
    )


def unpack_tile(packed):
    tokens = packed.shape[0] // 3
    last = packed[2 * tokens :]
    side = last.shape[1] // 2
    west = jnp.concatenate([packed[:tokens], last[:, :side]], 1)
    east = jnp.concatenate([packed[tokens : 2 * tokens], last[:, side:]], 1)
    return west, east


def prepare_kernel(micro_ref, fields_ref, mask_ref, vector_ref, wqkv_ref, wproj_ref, wup_ref, wdown_ref,
                   tile_ref, pack_ref, grid_ref):
    _, levels, rows, _ = fields_ref.shape
    width = vector_ref.shape[1]
    mask = mask_ref[...].astype(jnp.float32)
    vector = vector_ref[...]
    step = levels * HALF
    for level in range(levels):
        for column in range(WLON):
            piece = fields_ref[0, level, :, column * width : (column + 1) * width].astype(jnp.float32)
            piece = piece + mask[:, column : column + 1] * vector
            half, inside = divmod(column, HALF)
            at = pl.ds(level * HALF + inside, rows, stride=step)
            grid_ref[2 * half, at, :] = piece[:, :LANES]
            grid_ref[2 * half + 1, at, :] = jnp.concatenate([piece[:, LANES:]] * 2, 1)
    tokens, side = rows * step, width - LANES
    tile_ref[:tokens] = grid_ref[0].astype(jnp.bfloat16)
    tile_ref[tokens : 2 * tokens] = grid_ref[2].astype(jnp.bfloat16)
    lane = lax.broadcasted_iota(jnp.int32, (1, LANES), 1)
    tile_ref[2 * tokens :] = jnp.where(lane < side, grid_ref[1], grid_ref[3]).astype(jnp.bfloat16)
    side = 256 - width
    for i in range(3):
        pack_ref[:, 256 * i : 256 * i + 256] = jnp.concatenate(
            [wqkv_ref[0, :, i * width : (i + 1) * width], wproj_ref[0, :, i * side : (i + 1) * side]], 1
        )
    hidden = wup_ref.shape[2]
    pack_ref[:, 768 : 768 + hidden] = wup_ref[0]
    at = 768 + hidden
    for i in range(hidden // width):
        pack_ref[:, at + LANES * i : at + LANES * (i + 1)] = wdown_ref[0, i * width : (i + 1) * width, :LANES]
    at += hidden // width * LANES
    for i in range(0, hidden // width, 2):
        pack_ref[:, at + side * i : at + side * (i + 2)] = jnp.concatenate(
            [wdown_ref[0, (i + j) * width : (i + j + 1) * width, LANES:] for j in range(2)], 1
        )


def prepare(micro, fields, land_mask, land_vector, weights):
    _, levels, rows, flat = fields.shape
    width = land_vector.shape[1]
    tokens = rows * levels * HALF
    whole = lambda a: pl.BlockSpec(a.shape, lambda i, m: (0,) * a.ndim)
    return pl.pallas_call(
        prepare_kernel,
        out_shape=(
            jax.ShapeDtypeStruct((3 * tokens, LANES), jnp.bfloat16),
            jax.ShapeDtypeStruct((width, 2304), jnp.bfloat16),
        ),
        grid_spec=pltpu.PrefetchScalarGridSpec(
            num_scalar_prefetch=1,
            grid=(1,),
            in_specs=[pl.BlockSpec((1, levels, rows, flat), lambda i, m: (m[0], 0, 0, 0))]
            + [whole(a) for a in (land_mask, land_vector, *weights)],
            out_specs=(
                pl.BlockSpec((3 * tokens, LANES), lambda i, m: (0, 0)),
                pl.BlockSpec((width, 2304), lambda i, m: (0, 0)),
            ),
            scratch_shapes=[pltpu.VMEM((4, tokens, LANES), jnp.float32)],
        ),
        compiler_params=pltpu.CompilerParams(vmem_limit_bytes=VMEM_LIMIT),
        name="prepare",
    )(micro, fields, land_mask, land_vector, *weights)


def stage_kernel(place_ref, t0, t1, t2, t3, t4, w0, w1, w2, w3, bias_ref, last_ref, outs_ref,
                 xa, xb, q_ref, k_ref, v_ref, wqkv_ref, wproj_ref, wup_ref, wdown_ref):
    f32, bf16 = jnp.float32, jnp.bfloat16
    halves, tokens, width = xa.shape
    head_size = width // HEADS
    windows, piece, _ = bias_ref.shape
    move = piece // 2
    place = place_ref[0]
    side = 256 - width
    hidden = wup_ref.shape[2]

    for i, ref in enumerate((t0, t1, t2, t3, t4)):
        west, east = unpack_tile(ref[...].astype(f32))
        xa[2 * i] = west.astype(bf16)
        xa[2 * i + 1] = east.astype(bf16)
    for i, ref in enumerate((w0, w1, w2, w3)):
        at = place ^ i
        wqkv_ref[at] = ref[:, :768]
        wproj_ref[at] = jnp.concatenate([ref[:, 256 * j + width : 256 * j + 256] for j in range(3)], 1)
        wup_ref[at] = ref[:, 768 : 768 + hidden]
        base = 768 + hidden
        rest = base + hidden // width * LANES
        for j in range(hidden // width):
            wdown_ref[at, j * width : (j + 1) * width, :] = jnp.concatenate(
                [ref[:, base + LANES * j : base + LANES * (j + 1)], ref[:, rest + side * j : rest + side * (j + 1)]], 1
            )

    channel_head = lax.broadcasted_iota(jnp.int32, (1, width), 1) // head_size
    scale = head_size ** (-0.5) * LOG2E
    ones = jnp.ones((2 * piece, side), f32)

    for b in range(STAGE):
        shifted = b % 2 == 1
        source, target = (xa, xb) if b % 2 == 0 else (xb, xa)

        def load(h, source=source, shifted=shifted):
            x = source[h].astype(f32)
            return pltpu.roll(x, tokens - move, 0) if shifted else x

        def pair(i, carry, b=b, load=load):
            kv = []
            for j in range(2):
                h = b + 2 * i + j
                qkv = jnp.dot(normalize(load(h)).astype(bf16), wqkv_ref[b], preferred_element_type=f32)
                q_ref[h] = qkv[:, :width] * scale
                kv.append((qkv[:, 256 : 256 + width], qkv[:, 512 : 512 + width]))
            for w in range(windows):
                at = slice(w * piece, (w + 1) * piece)
                k_ref[i, w] = jnp.concatenate([kv[0][0][at], kv[1][0][at]], 0).astype(bf16)
                v = jnp.concatenate([kv[0][1][at], kv[1][1][at]], 0)
                v_ref[i, w] = jnp.concatenate([v, ones], 1).astype(bf16)
            return carry

        def attend(h, carry, b=b, load=load, target=target, shifted=shifted):
            i = (h - b) // 2
            x = load(h)
            attended = []
            for w in range(windows):
                q = q_ref[h, w * piece : (w + 1) * piece, :]
                qm = jnp.concatenate([jnp.where(channel_head == n, q, 0.0) for n in range(HEADS)], 0).astype(bf16)
                s = lax.dot_general(qm, k_ref[i, w], (((1,), (1,)), ((), ())), preferred_element_type=f32)
                if shifted:
                    s = (s.reshape(HEADS, piece, 2 * piece) + bias_ref[w][None]).reshape(HEADS * piece, 2 * piece)
                e = jnp.exp2(s - jnp.max(s, axis=-1, keepdims=True)).astype(bf16)
                o = jnp.dot(e, v_ref[i, w], preferred_element_type=f32)
                o = o[:, :width] * (1.0 / o[:, width : width + 1])
                total = o[:piece]
                for n in range(1, HEADS):
                    total = jnp.where(channel_head == n, o[n * piece : (n + 1) * piece], total)
                attended.append(total)
            a = jnp.concatenate(attended, 0).astype(bf16)
            residual = x + jnp.dot(a, wproj_ref[b], preferred_element_type=f32)
            n2 = normalize(residual).astype(bf16)
            u = jnp.dot(n2, wup_ref[b], preferred_element_type=f32)
            g = (0.5 * u * (1.0 + lax.erf(u * (0.5**0.5)))).astype(bf16)
            y = residual + jnp.dot(g, wdown_ref[b], preferred_element_type=f32)
            if shifted:
                y = pltpu.roll(y, move, 0)
            target[h] = y.astype(bf16)
            return carry

        lax.fori_loop(0, halves // 2 - b, pair, 0)
        lax.fori_loop(1 + b, halves - 1 - b, attend, 0)
        west, east = target[halves // 2 - 1].astype(f32), target[halves // 2].astype(f32)
        packed = pack_tile(west, east).astype(bf16)
        outs_ref[place ^ b] = packed
        if b == STAGE - 1:
            last_ref[...] = packed


def run_stage(place, tiles, weights, bias):
    packed_tokens = tiles[0].shape[0]
    tokens = packed_tokens // 3
    width = weights[0].shape[0]
    halves = 2 * len(tiles)
    windows, piece, _ = bias.shape
    vmem = pl.BlockSpec(memory_space=pltpu.VMEM)
    bf16, f32 = jnp.bfloat16, jnp.float32
    return pl.pallas_call(
        stage_kernel,
        out_shape=(
            jax.ShapeDtypeStruct((packed_tokens, LANES), bf16),
            jax.ShapeDtypeStruct((STAGE, packed_tokens, LANES), bf16),
        ),
        in_specs=[pl.BlockSpec(memory_space=pltpu.SMEM)] + [vmem] * (len(tiles) + len(weights) + 1),
        out_specs=(vmem, vmem),
        scratch_shapes=[
            pltpu.VMEM((halves, tokens, width), bf16),
            pltpu.VMEM((halves, tokens, width), bf16),
            pltpu.VMEM((halves, tokens, width), f32),
            pltpu.VMEM((halves // 2, windows, 2 * piece, width), bf16),
            pltpu.VMEM((halves // 2, windows, 2 * piece, 256), bf16),
            pltpu.VMEM((STAGE, width, 768), bf16),
            pltpu.VMEM((STAGE, width, width), bf16),
            pltpu.VMEM((STAGE, width, 768), bf16),
            pltpu.VMEM((STAGE, 768, width), bf16),
        ],
        compiler_params=pltpu.CompilerParams(vmem_limit_bytes=VMEM_LIMIT),
        name="stage",
    )(place, *tiles, *weights, bias)


def finish_kernel(place_ref, o0, o1, o2, o3, out_ref, grid_ref):
    _, _, levels, rows, _ = out_ref.shape
    tokens = grid_ref.shape[1]
    step = levels * HALF
    width = out_ref.shape[4] // WLON
    side = width - LANES
    for i, ref in enumerate((o0, o1, o2, o3)):
        packed = ref[...].astype(jnp.float32)
        for part in range(3):
            grid_ref[part] = packed[part * tokens : (part + 1) * tokens]
        micro = place_ref[0] ^ i
        for level in range(levels):
            for column in range(WLON):
                half, inside = divmod(column, HALF)
                at = pl.ds(level * HALF + inside, rows, stride=step)
                rest = grid_ref[2, at, :][:, half * side : (half + 1) * side]
                piece = jnp.concatenate([grid_ref[half, at, :], rest], 1)
                out_ref[0, micro, level, :, column * width : (column + 1) * width] = piece.astype(jnp.bfloat16)


def finish(place, pieces, shape):
    tokens = pieces[0].shape[0] // 3
    vmem = pl.BlockSpec(memory_space=pltpu.VMEM)
    return pl.pallas_call(
        finish_kernel,
        out_shape=jax.ShapeDtypeStruct(shape, jnp.bfloat16),
        in_specs=[pl.BlockSpec(memory_space=pltpu.SMEM)] + [vmem] * len(pieces),
        out_specs=vmem,
        scratch_shapes=[pltpu.VMEM((3, tokens, LANES), jnp.float32)],
        compiler_params=pltpu.CompilerParams(vmem_limit_bytes=VMEM_LIMIT),
        name="finish",
    )(place, *pieces)


def on_device(fields, land_mask, land_vector, w_qkv, w_proj, w_up, w_down):
    micro_count, levels, rows, flat_width = fields.shape
    width = land_vector.shape[0]
    tile_count, section_count = lax.axis_size("tile"), lax.axis_size("section")
    section = lax.axis_index("section")
    place = (section % STAGE).astype(jnp.int32).reshape(1)
    axes = ("tile", "section")

    def exchange(value, bit):
        return lax.ppermute(value, "section", [(s, s ^ bit) for s in range(section_count)])

    def shift(value, tiles, stages):
        pairs = [
            (t * section_count + s, (t + tiles) % tile_count * section_count + s + stages * STAGE)
            for t in range(tile_count)
            for s in range(STAGE)
        ]
        return lax.ppermute(value, axes, pairs)

    tile, pack = prepare(place, fields, land_mask, land_vector.reshape(1, width), (w_qkv, w_proj, w_up, w_down))
    bias = jnp.asarray(window_bias(levels, rows))

    far = exchange(pack, 2)
    offsets = range(-REACH, REACH + 1)
    tiles = [tile if d == 0 else shift(tile, -d, 0) for d in offsets]
    weights = (pack, exchange(pack, 1), far, exchange(far, 1))

    last, early = run_stage(place, tiles, weights, bias)
    tiles = [shift(last, -d, 1) for d in offsets]
    _, late = run_stage(place, tiles, weights, bias)
    outs = jnp.where(section < STAGE, early, late)

    pieces = [outs[0]] + [exchange(outs[i], i) for i in range(1, STAGE)]
    return finish(place, pieces, (1, micro_count, levels, rows, flat_width))


def solution(mesh):
    in_specs = (
        P(None, None, None, "tile"),
        P(None, "tile"),
        P(),
        P("section", None, None),
        P("section", None, None),
        P("section", None, None),
        P("section", None, None),
    )
    out_specs = P("section", None, None, None, "tile")
    return jax.shard_map(on_device, mesh=mesh, in_specs=in_specs, out_specs=out_specs, check_vma=False)
```

time: 220 us -> 221 us (level)
  the two profiles are of different devices: /device:TPU:1 before, /device:TPU:134 now
where the time goes in v2:
time: 221 us; the launch traced here: 220 us
  Pallas kernels  101 us (46%)
  waiting for transfers between devices  67.3 us (30%)
  starting transfers between devices  40.2 us (18%)
  local copies, waits for them, and re-layouts  10.9 us (5%)
    pallas_call x2, Pallas kernels, run_stage(): pl.pallas_call(stage_kernel, out_shape=(jax.ShapeDtypeStruct((packed_toke...  94.5 us
    ppermute x9, waiting for transfers between devices, shift(): return lax.ppermute(value, axes, pairs)  45.1 us
    ppermute x6, starting transfers between devices, exchange(): lax.ppermute(value, 'section', [(s, s ^ bit) for s in range(section_count)])  30.8 us
    ppermute x6, waiting for transfers between devices, exchange(): lax.ppermute(value, 'section', [(s, s ^ bit) for s in range(section_count)])  22.1 us
    ppermute x9, starting transfers between devices, shift(): return lax.ppermute(value, axes, pairs)  9.32 us
    unnamed x37, local copies, waits for them, and re-layouts  7.67 us
  transfers between devices with their start and end apart: 15, of which 7 were waited for; matrix products, arithmetic and copies ran while one was open for 0% of the time, Pallas kernels for 0%

profile of v2, /device:TPU:134, one launch (start us, length us, event | category | flops | bytes accessed | tf_op | source)
XLA Modules:
  0.0 220.3 jit_solution(9208286342240350488)
XLA Ops:
  0.0 1.4 copy.10.mask_ref
  1.4 1.9 copy.11.wdown_ref
  3.3 1.0 copy.9.fields_ref
  4.3 2.9 %prepare.1 = (bf16[648,128]{1,0:T(8,128)(2,1)}, bf16[192,2304]{1,0:T(8,128)(2,1)}) custom-call(s32[1]{0:T(128)} %bitcast.micro_ref.place_ref, bf16[4,2,18,2304]{3,2,1,0:T(8,128)(2,1)} %copy.9.fields_ref, s32[18,12]{1,0:T(8,128)} %copy.10.mask_ref, f32[1,192]{1,0:T(1,128)} %bitcast.10, bf16[1,192,576]{2,1,0:T(8,128)(2,1)} %wqkv_ref.1, ...), custom_call_target="tpu_custom_call" | custom-call | tf_op jit(solution)/shard_map/prepare/pallas_call | solution.py:100
  7.3 4.3 %collective-permute-start.5 = (bf16[192,2304]{1,0:T(8,128)(2,1)}, bf16[192,2304]{1,0:T(8,128)(2,1)S(1)}, u32[]{:S(2)}, u32[]{:S(2)}) collective-permute-start(bf16[192,2304]{1,0:T(8,128)(2,1)} %get-tuple-element.11.w0), channel_id=1, source_target_pairs={{0,2},{1,3},{2,0},{3,1},{4,6},{5,7},{6,4},{7,5},{8,10},{9,11},{10,... | collective-permute-start | bytes 2654216 | tf_op jit(solution)/shard_map/ppermute | solution.py:287
  11.5 1.9 collective-permute-start.4
  13.5 17.9 %collective-permute-done.5.w2 = bf16[192,2304]{1,0:T(8,128)(2,1)S(1)} collective-permute-done((bf16[192,2304]{1,0:T(8,128)(2,1)}, bf16[192,2304]{1,0:T(8,128)(2,1)S(1)}, u32[]{:S(2)}, u32[]{:S(2)}) %collective-permute-start.5) | collective-permute-done | bytes 884768 | tf_op jit(solution)/shard_map/ppermute | solution.py:287
  31.4 1.9 collective-permute-start.6
  33.3 0.7 collective-permute-start.3
  34.0 0.7 collective-permute-start.2
  34.7 0.7 collective-permute-start.1
  35.3 0.0 collective-permute-done.3.t4
  35.4 0.7 collective-permute-start
  36.0 0.0 collective-permute-done.2.t3
  36.1 0.0 collective-permute-done.1.t1
  36.1 0.0 collective-permute-done.t0
  36.1 0.0 collective-permute-done.4.w1
  36.1 0.6 copy-done.10
  36.7 0.1 copy-done.12
  36.8 0.1 copy-done.13
  36.8 0.3 copy-done.1
  37.1 0.9 copy-done.2
  38.1 47.2 %stage.2 = (bf16[648,128]{1,0:T(8,128)(2,1)}, bf16[4,648,128]{2,1,0:T(8,128)(2,1)}) custom-call(s32[1]{0:T(128)} %bitcast.micro_ref.place_ref, bf16[648,128]{1,0:T(8,128)(2,1)} %copy-done.13, bf16[648,128]{1,0:T(8,128)(2,1)} %copy-done.12, bf16[648,128]{1,0:T(8,128)(2,1)} %get-tuple-element.10.t2, bf16[648,128]{1,0:T(8,128)(2,1)} %copy-done.10, ...), custom_call_target="tpu_custom_call" | custom-call | tf_op jit(solution)/shard_map/stage/pallas_call | solution.py:220
  85.3 1.3 collective-permute-start.11
  86.6 1.3 collective-permute-start.10
  87.9 1.3 collective-permute-start.9
  89.2 1.3 collective-permute-start.8
  90.5 1.5 collective-permute-start.7
  91.9 0.0 copy-start.4
  92.0 19.7 %collective-permute-done.11.t4 = bf16[648,128]{1,0:T(8,128)(2,1)S(1)} collective-permute-done((bf16[648,128]{1,0:T(8,128)(2,1)}, bf16[648,128]{1,0:T(8,128)(2,1)S(1)}, u32[]{:S(2)}, u32[]{:S(2)}) %collective-permute-start.11) | collective-permute-done | bytes 165920 | tf_op jit(solution)/shard_map/ppermute | solution.py:295
  111.7 14.0 %collective-permute-done.10.t3 = bf16[648,128]{1,0:T(8,128)(2,1)S(1)} collective-permute-done((bf16[648,128]{1,0:T(8,128)(2,1)}, bf16[648,128]{1,0:T(8,128)(2,1)S(1)}, u32[]{:S(2)}, u32[]{:S(2)}) %collective-permute-start.10) | collective-permute-done | bytes 165920 | tf_op jit(solution)/shard_map/ppermute | solution.py:295
  125.7 0.0 collective-permute-done.9.t2
  125.7 3.9 %collective-permute-done.8.t1 = bf16[648,128]{1,0:T(8,128)(2,1)S(1)} collective-permute-done((bf16[648,128]{1,0:T(8,128)(2,1)}, bf16[648,128]{1,0:T(8,128)(2,1)S(1)}, u32[]{:S(2)}, u32[]{:S(2)}) %collective-permute-start.8) | collective-permute-done | bytes 165920 | tf_op jit(solution)/shard_map/ppermute | solution.py:295
  129.6 7.5 %collective-permute-done.7.t0 = bf16[648,128]{1,0:T(8,128)(2,1)S(1)} collective-permute-done((bf16[648,128]{1,0:T(8,128)(2,1)}, bf16[648,128]{1,0:T(8,128)(2,1)S(1)}, u32[]{:S(2)}, u32[]{:S(2)}) %collective-permute-start.7) | collective-permute-done | bytes 165920 | tf_op jit(solution)/shard_map/ppermute | solution.py:295
  137.1 0.7 copy-done.11
  137.8 47.2 %stage.3 = (bf16[648,128]{1,0:T(8,128)(2,1)}, bf16[4,648,128]{2,1,0:T(8,128)(2,1)}) custom-call(s32[1]{0:T(128)} %bitcast.micro_ref.place_ref, bf16[648,128]{1,0:T(8,128)(2,1)} %copy-done.11, bf16[648,128]{1,0:T(8,128)(2,1)} %copy-done.9, bf16[648,128]{1,0:T(8,128)(2,1)} %copy-done.7, bf16[648,128]{1,0:T(8,128)(2,1)} %copy-done.6, ...), custom_call_target="tpu_custom_call" | custom-call | tf_op jit(solution)/shard_map/stage/pallas_call | solution.py:220
  185.1 1.2 broadcast_select_fusion
  186.2 0.7 slice_bitcast_fusion
  186.9 18.4 %collective-permute-start.14 = (bf16[648,128]{1,0:T(8,128)(2,1)S(1)}, bf16[648,128]{1,0:T(8,128)(2,1)S(1)}, u32[]{:S(2)}, u32[]{:S(2)}) collective-permute-start(bf16[648,128]{1,0:T(8,128)(2,1)S(1)} %get-tuple-element.15), channel_id=1, source_target_pairs={{0,3},{1,2},{2,1},{3,0},{4,7},{5,6},{6,5},{7,4},{8,11},{9,10},{10,... | collective-permute-start | bytes 497672 | tf_op jit(solution)/shard_map/ppermute | solution.py:287
  205.3 2.3 %collective-permute-start.13 = (bf16[648,128]{1,0:T(8,128)(2,1)S(1)}, bf16[648,128]{1,0:T(8,128)(2,1)S(1)}, u32[]{:S(2)}, u32[]{:S(2)}) collective-permute-start(bf16[648,128]{1,0:T(8,128)(2,1)S(1)} %get-tuple-element.16), channel_id=1, source_target_pairs={{0,2},{1,3},{2,0},{3,1},{4,6},{5,7},{6,4},{7,5},{8,10},{9,11},{10,... | collective-permute-start | bytes 497672 | tf_op jit(solution)/shard_map/ppermute | solution.py:287
  207.7 2.0 collective-permute-start.12
  209.7 0.2 collective-permute-done.14.o3
  209.9 4.0 %collective-permute-done.13.o2 = bf16[648,128]{1,0:T(8,128)(2,1)S(1)} collective-permute-done((bf16[648,128]{1,0:T(8,128)(2,1)S(1)}, bf16[648,128]{1,0:T(8,128)(2,1)S(1)}, u32[]{:S(2)}, u32[]{:S(2)}) %collective-permute-start.13) | collective-permute-done | bytes 165920 | tf_op jit(solution)/shard_map/ppermute | solution.py:287
  213.9 0.0 collective-permute-done.12.o1
  213.9 0.7 copy-done.15
  214.6 0.1 copy-done.16
  214.6 3.1 %finish.1 = bf16[1,4,2,18,2304]{4,3,2,1,0:T(8,128)(2,1)} custom-call(s32[1]{0:T(128)} %bitcast.micro_ref.place_ref, bf16[648,128]{1,0:T(8,128)(2,1)} %get-tuple-element.18.o0, bf16[648,128]{1,0:T(8,128)(2,1)} %copy-done.16, bf16[648,128]{1,0:T(8,128)(2,1)} %copy-done.15, bf16[648,128]{1,0:T(8,128)(2,1)} %copy-done.14), custom_call_target="tpu_custom_call" | custom-call | tf_op jit(solution)/shard_map/finish/pallas_call | solution.py:267
  217.8 2.5 %copy.12 = bf16[1,4,2,18,2304]{4,2,3,1,0:T(2,128)(2,1)} copy(bf16[1,4,2,18,2304]{4,3,2,1,0:T(8,128)(2,1)} %finish.1) | data formatting | bytes 1327104 | tf_op jit(solution)/shard_map/finish/pallas_call | solution.py:267
  (26 shorter events, 0.0 us)
Async XLA Ops:
  0.0 3.3 %copy-start.3 = (bf16[4,2,18,2304]{3,1,2,0:T(2,128)(2,1)S(1)}, bf16[4,2,18,2304]{3,1,2,0:T(2,128)(2,1)}, u32[]{:S(2)}) copy-start(bf16[4,2,18,2304]{3,1,2,0:T(2,128)(2,1)} %param.8) | copy-start | bytes 1990660
  7.3 24.1 %collective-permute-start.5 = (bf16[192,2304]{1,0:T(8,128)(2,1)}, bf16[192,2304]{1,0:T(8,128)(2,1)S(1)}, u32[]{:S(2)}, u32[]{:S(2)}) collective-permute-start(bf16[192,2304]{1,0:T(8,128)(2,1)} %get-tuple-element.11.w0), channel_id=1, source_target_pairs={{0,2},{1,3},{2,0},{3,1},{4,6},{5,7},{6,4},{7,5},{8,10},{9,11},{10,... | collective-permute-start | bytes 2654216 | tf_op jit(solution)/shard_map/ppermute | solution.py:287
  11.5 24.6 %collective-permute-start.4 = (bf16[192,2304]{1,0:T(8,128)(2,1)}, bf16[192,2304]{1,0:T(8,128)(2,1)S(1)}, u32[]{:S(2)}, u32[]{:S(2)}) collective-permute-start(bf16[192,2304]{1,0:T(8,128)(2,1)} %get-tuple-element.11.w0), channel_id=1, source_target_pairs={{0,1},{1,0},{2,3},{3,2},{4,5},{5,4},{6,7},{7,6},{8,9},{9,8},{10,11... | collective-permute-start | bytes 2654216 | tf_op jit(solution)/shard_map/ppermute | solution.py:287
  31.4 4.8 %copy-start = (bf16[192,2304]{1,0:T(8,128)(2,1)}, bf16[192,2304]{1,0:T(8,128)(2,1)S(1)}, u32[]{:S(2)}) copy-start(bf16[192,2304]{1,0:T(8,128)(2,1)S(1)} %collective-permute-done.5.w2) | copy-start | bytes 2654212
  31.4 4.7 %collective-permute-start.6 = (bf16[192,2304]{1,0:T(8,128)(2,1)S(1)}, bf16[192,2304]{1,0:T(8,128)(2,1)S(1)}, u32[]{:S(2)}, u32[]{:S(2)}) collective-permute-start(bf16[192,2304]{1,0:T(8,128)(2,1)S(1)} %collective-permute-done.5.w2), channel_id=1, source_target_pairs={{0,1},{1,0},{2,3},{3,2},{4,5},{5,4},{6,7},{7,6},{8,9},{9,8},{10,11... | collective-permute-start | bytes 2654216 | tf_op jit(solution)/shard_map/ppermute | solution.py:287
  33.3 2.0 collective-permute-start.3
  34.0 2.1 collective-permute-start.2
  34.7 1.4 collective-permute-start.1
  35.3 0.8 copy-start.8
  35.4 0.7 collective-permute-start
  36.0 0.7 copy-start.10
  36.1 0.7 copy-start.12
  36.1 0.8 copy-start.13
  36.1 1.0 copy-start.1
  37.1 0.9 copy-start.2
  85.3 26.4 %collective-permute-start.11 = (bf16[648,128]{1,0:T(8,128)(2,1)}, bf16[648,128]{1,0:T(8,128)(2,1)S(1)}, u32[]{:S(2)}, u32[]{:S(2)}) collective-permute-start(bf16[648,128]{1,0:T(8,128)(2,1)} %get-tuple-element.13), channel_id=1, source_target_pairs={{0,500},{1,501},{2,502},{3,503},{8,508},{9,509},{10,510},{11,511},... | collective-permute-start | bytes 497672 | tf_op jit(solution)/shard_map/ppermute | solution.py:295
  86.6 39.1 %collective-permute-start.10 = (bf16[648,128]{1,0:T(8,128)(2,1)}, bf16[648,128]{1,0:T(8,128)(2,1)S(1)}, u32[]{:S(2)}, u32[]{:S(2)}) collective-permute-start(bf16[648,128]{1,0:T(8,128)(2,1)} %get-tuple-element.13), channel_id=1, source_target_pairs={{0,508},{1,509},{2,510},{3,511},{8,4},{9,5},{10,6},{11,7},{16,12},... | collective-permute-start | bytes 497672 | tf_op jit(solution)/shard_map/ppermute | solution.py:295
  87.9 37.8 %collective-permute-start.9 = (bf16[648,128]{1,0:T(8,128)(2,1)}, bf16[648,128]{1,0:T(8,128)(2,1)S(1)}, u32[]{:S(2)}, u32[]{:S(2)}) collective-permute-start(bf16[648,128]{1,0:T(8,128)(2,1)} %get-tuple-element.13), channel_id=1, source_target_pairs={{0,4},{1,5},{2,6},{3,7},{8,12},{9,13},{10,14},{11,15},{16,20},{17,... | collective-permute-start | bytes 497672 | tf_op jit(solution)/shard_map/ppermute | solution.py:295
  89.2 40.4 %collective-permute-start.8 = (bf16[648,128]{1,0:T(8,128)(2,1)}, bf16[648,128]{1,0:T(8,128)(2,1)S(1)}, u32[]{:S(2)}, u32[]{:S(2)}) collective-permute-start(bf16[648,128]{1,0:T(8,128)(2,1)} %get-tuple-element.13), channel_id=1, source_target_pairs={{0,12},{1,13},{2,14},{3,15},{8,20},{9,21},{10,22},{11,23},{16,28},... | collective-permute-start | bytes 497672 | tf_op jit(solution)/shard_map/ppermute | solution.py:295
  90.5 46.6 %collective-permute-start.7 = (bf16[648,128]{1,0:T(8,128)(2,1)}, bf16[648,128]{1,0:T(8,128)(2,1)S(1)}, u32[]{:S(2)}, u32[]{:S(2)}) collective-permute-start(bf16[648,128]{1,0:T(8,128)(2,1)} %get-tuple-element.13), channel_id=1, source_target_pairs={{0,20},{1,21},{2,22},{3,23},{8,28},{9,29},{10,30},{11,31},{16,36},... | collective-permute-start | bytes 497672 | tf_op jit(solution)/shard_map/ppermute | solution.py:295
  91.9 93.1 %copy-start.4 = (bf16[4,648,128]{2,1,0:T(8,128)(2,1)S(1)}, bf16[4,648,128]{2,1,0:T(8,128)(2,1)}, u32[]{:S(2)}) copy-start(bf16[4,648,128]{2,1,0:T(8,128)(2,1)} %get-tuple-element.12) | copy-start | bytes 1990660
  111.7 25.4 %copy-start.5 = (bf16[648,128]{1,0:T(8,128)(2,1)}, bf16[648,128]{1,0:T(8,128)(2,1)S(1)}, u32[]{:S(2)}) copy-start(bf16[648,128]{1,0:T(8,128)(2,1)S(1)} %collective-permute-done.11.t4) | copy-start | bytes 497668
  125.7 11.4 %copy-start.6 = (bf16[648,128]{1,0:T(8,128)(2,1)}, bf16[648,128]{1,0:T(8,128)(2,1)S(1)}, u32[]{:S(2)}) copy-start(bf16[648,128]{1,0:T(8,128)(2,1)S(1)} %collective-permute-done.10.t3) | copy-start | bytes 497668
  125.7 11.4 %copy-start.7 = (bf16[648,128]{1,0:T(8,128)(2,1)}, bf16[648,128]{1,0:T(8,128)(2,1)S(1)}, u32[]{:S(2)}) copy-start(bf16[648,128]{1,0:T(8,128)(2,1)S(1)} %collective-permute-done.9.t2) | copy-start | bytes 497668
  129.6 7.5 %copy-start.9 = (bf16[648,128]{1,0:T(8,128)(2,1)}, bf16[648,128]{1,0:T(8,128)(2,1)S(1)}, u32[]{:S(2)}) copy-start(bf16[648,128]{1,0:T(8,128)(2,1)S(1)} %collective-permute-done.8.t1) | copy-start | bytes 497668
  137.1 0.7 copy-start.11
  186.9 23.0 %collective-permute-start.14 = (bf16[648,128]{1,0:T(8,128)(2,1)S(1)}, bf16[648,128]{1,0:T(8,128)(2,1)S(1)}, u32[]{:S(2)}, u32[]{:S(2)}) collective-permute-start(bf16[648,128]{1,0:T(8,128)(2,1)S(1)} %get-tuple-element.15), channel_id=1, source_target_pairs={{0,3},{1,2},{2,1},{3,0},{4,7},{5,6},{6,5},{7,4},{8,11},{9,10},{10,... | collective-permute-start | bytes 497672 | tf_op jit(solution)/shard_map/ppermute | solution.py:287
  205.3 8.6 %collective-permute-start.13 = (bf16[648,128]{1,0:T(8,128)(2,1)S(1)}, bf16[648,128]{1,0:T(8,128)(2,1)S(1)}, u32[]{:S(2)}, u32[]{:S(2)}) collective-permute-start(bf16[648,128]{1,0:T(8,128)(2,1)S(1)} %get-tuple-element.16), channel_id=1, source_target_pairs={{0,2},{1,3},{2,0},{3,1},{4,6},{5,7},{6,4},{7,5},{8,10},{9,11},{10,... | collective-permute-start | bytes 497672 | tf_op jit(solution)/shard_map/ppermute | solution.py:287
  207.7 6.2 %collective-permute-start.12 = (bf16[648,128]{1,0:T(8,128)(2,1)S(1)}, bf16[648,128]{1,0:T(8,128)(2,1)S(1)}, u32[]{:S(2)}, u32[]{:S(2)}) collective-permute-start(bf16[648,128]{1,0:T(8,128)(2,1)S(1)} %get-tuple-element.17), channel_id=1, source_target_pairs={{0,1},{1,0},{2,3},{3,2},{4,5},{5,4},{6,7},{7,6},{8,9},{9,8},{10,11... | collective-permute-start | bytes 497672 | tf_op jit(solution)/shard_map/ppermute | solution.py:287
  209.9 4.0 %copy-start.14 = (bf16[648,128]{1,0:T(8,128)(2,1)}, bf16[648,128]{1,0:T(8,128)(2,1)S(1)}, u32[]{:S(2)}) copy-start(bf16[648,128]{1,0:T(8,128)(2,1)S(1)} %collective-permute-done.14.o3) | copy-start | bytes 497668
  213.9 0.7 copy-start.15
  213.9 0.7 copy-start.16

commit v3 on v2

--- a/solution.py
+++ b/solution.py
@@ -82,14 +82,7 @@
         )
     hidden = wup_ref.shape[2]
     pack_ref[:, 768 : 768 + hidden] = wup_ref[0]
-    at = 768 + hidden
-    for i in range(hidden // width):
-        pack_ref[:, at + LANES * i : at + LANES * (i + 1)] = wdown_ref[0, i * width : (i + 1) * width, :LANES]
-    at += hidden // width * LANES
-    for i in range(0, hidden // width, 2):
-        pack_ref[:, at + side * i : at + side * (i + 2)] = jnp.concatenate(
-            [wdown_ref[0, (i + j) * width : (i + j + 1) * width, LANES:] for j in range(2)], 1
-        )
+    pack_ref[:, 768 + hidden :] = wdown_ref[0]
 
 
 def prepare(micro, fields, land_mask, land_vector, weights):
@@ -120,7 +113,7 @@
 
 
 def stage_kernel(place_ref, t0, t1, t2, t3, t4, w0, w1, w2, w3, bias_ref, last_ref, outs_ref,
-                 xa, xb, q_ref, k_ref, v_ref, wqkv_ref, wproj_ref, wup_ref, wdown_ref):
+                 xa, xb, q_ref, k_ref, v_ref, w_ref, wproj_ref, low_ref, high_ref):
     f32, bf16 = jnp.float32, jnp.bfloat16
     halves, tokens, width = xa.shape
     head_size = width // HEADS
@@ -128,41 +121,69 @@
     move = piece // 2
     place = place_ref[0]
     side = 256 - width
-    hidden = wup_ref.shape[2]
-
-    for i, ref in enumerate((t0, t1, t2, t3, t4)):
-        west, east = unpack_tile(ref[...].astype(f32))
-        xa[2 * i] = west.astype(bf16)
-        xa[2 * i + 1] = east.astype(bf16)
+    hidden = (w_ref.shape[2] - 768) // 2
+
     for i, ref in enumerate((w0, w1, w2, w3)):
         at = place ^ i
-        wqkv_ref[at] = ref[:, :768]
+        w_ref[at] = ref[...]
         wproj_ref[at] = jnp.concatenate([ref[:, 256 * j + width : 256 * j + 256] for j in range(3)], 1)
-        wup_ref[at] = ref[:, 768 : 768 + hidden]
-        base = 768 + hidden
-        rest = base + hidden // width * LANES
-        for j in range(hidden // width):
-            wdown_ref[at, j * width : (j + 1) * width, :] = jnp.concatenate(
-                [ref[:, base + LANES * j : base + LANES * (j + 1)], ref[:, rest + side * j : rest + side * (j + 1)]], 1
-            )
 
     channel_head = lax.broadcasted_iota(jnp.int32, (1, width), 1) // head_size
     scale = head_size ** (-0.5) * LOG2E
-    ones = jnp.ones((2 * piece, side), f32)
-
-    for b in range(STAGE):
-        shifted = b % 2 == 1
-        source, target = (xa, xb) if b % 2 == 0 else (xb, xa)
-
-        def load(h, source=source, shifted=shifted):
+    ones = jnp.ones((2 * piece, 256 - width), f32)
+
+    def load_tiles():
+        for i, ref in enumerate((t0, t1, t2, t3, t4)):
+            west, east = unpack_tile(ref[...].astype(f32))
+            xa[2 * i] = west.astype(bf16)
+            xa[2 * i + 1] = east.astype(bf16)
+
+    def select_heads(parts, first, lanes):
+        total = parts[0]
+        for n in range(1, len(parts)):
+            total = jnp.where(channel_head[:, first : first + lanes] == first // head_size + n, parts[n], total)
+        return total
+
+    def window_attention(h, i, w, shifted, exact):
+        q = q_ref[h, w * piece : (w + 1) * piece, :]
+        qm = jnp.concatenate([jnp.where(channel_head == n, q, 0.0) for n in range(HEADS)], 0).astype(bf16)
+        s = lax.dot_general(qm, k_ref[i, w], (((1,), (1,)), ((), ())), preferred_element_type=f32)
+        if shifted:
+            s = (s.reshape(HEADS, piece, 2 * piece) + bias_ref[w][None]).reshape(HEADS * piece, 2 * piece)
+        if exact:
+            s = s - jnp.max(s, axis=-1, keepdims=True)
+        o = jnp.dot(jnp.exp2(s).astype(bf16), v_ref[i, w], preferred_element_type=f32)
+        heads = [o[n * piece : (n + 1) * piece] for n in range(HEADS)]
+        full = LANES // head_size
+        tops = [select_heads([x[:, :LANES] for x in heads[:full]], 0, LANES),
+                select_heads([x[:, LANES:width] for x in heads[full:]], LANES, width - LANES)]
+        side = 256 - width
+        ends = [x[:, LANES:] for x in heads]
+        odd = channel_head[:, :LANES] % 2 == 1
+        couples = [jnp.where(odd, ends[n + 1], ends[n]) for n in range(0, HEADS, 2)]
+        lane = lax.broadcasted_iota(jnp.int32, (1, LANES), 1)
+        sums = [jnp.where(lane < side, pltpu.roll(couples[0], side, 1), couples[1]),
+                pltpu.roll(couples[2], side, 1)[:, :side]]
+        if not exact:
+            low_ref[...] = jnp.minimum(low_ref[...], jnp.min(sums[0].reshape(-1, 8, LANES), axis=0))
+            high_ref[...] = jnp.maximum(high_ref[...], jnp.max(sums[0].reshape(-1, 8, LANES), axis=0))
+            rest = slice(0, width - LANES)
+            low_ref[:, rest] = jnp.minimum(low_ref[:, rest], jnp.min(sums[1].reshape(-1, 8, width - LANES), axis=0))
+            high_ref[:, rest] = jnp.maximum(high_ref[:, rest], jnp.max(sums[1].reshape(-1, 8, width - LANES), axis=0))
+        return jnp.concatenate([top / total for top, total in zip(tops, sums)], 1)
+
+    def block(b, shifted, exact, together):
+        source, target = (xb, xa) if shifted else (xa, xb)
+
+        def load(h):
             x = source[h].astype(f32)
             return pltpu.roll(x, tokens - move, 0) if shifted else x
 
-        def pair(i, carry, b=b, load=load):
+        def pair(i, carry):
             kv = []
             for j in range(2):
                 h = b + 2 * i + j
-                qkv = jnp.dot(normalize(load(h)).astype(bf16), wqkv_ref[b], preferred_element_type=f32)
+                qkv = jnp.dot(normalize(load(h)).astype(bf16), w_ref[b, :, :768], preferred_element_type=f32)
                 q_ref[h] = qkv[:, :width] * scale
                 kv.append((qkv[:, 256 : 256 + width], qkv[:, 512 : 512 + width]))
             for w in range(windows):
@@ -172,41 +193,51 @@
                 v_ref[i, w] = jnp.concatenate([v, ones], 1).astype(bf16)
             return carry
 
-        def attend(h, carry, b=b, load=load, target=target, shifted=shifted):
-            i = (h - b) // 2
-            x = load(h)
-            attended = []
-            for w in range(windows):
-                q = q_ref[h, w * piece : (w + 1) * piece, :]
-                qm = jnp.concatenate([jnp.where(channel_head == n, q, 0.0) for n in range(HEADS)], 0).astype(bf16)
-                s = lax.dot_general(qm, k_ref[i, w], (((1,), (1,)), ((), ())), preferred_element_type=f32)
-                if shifted:
-                    s = (s.reshape(HEADS, piece, 2 * piece) + bias_ref[w][None]).reshape(HEADS * piece, 2 * piece)
-                e = jnp.exp2(s - jnp.max(s, axis=-1, keepdims=True)).astype(bf16)
-                o = jnp.dot(e, v_ref[i, w], preferred_element_type=f32)
-                o = o[:, :width] * (1.0 / o[:, width : width + 1])
-                total = o[:piece]
-                for n in range(1, HEADS):
-                    total = jnp.where(channel_head == n, o[n * piece : (n + 1) * piece], total)
-                attended.append(total)
-            a = jnp.concatenate(attended, 0).astype(bf16)
+        def attend(c, carry):
+            own = [1 + b + together * c + j for j in range(together)]
+            x = jnp.concatenate([load(h) for h in own], 0)
+            a = jnp.concatenate(
+                [window_attention(h, (h - b) // 2, w, shifted, exact) for h in own for w in range(windows)], 0
+            ).astype(bf16)
             residual = x + jnp.dot(a, wproj_ref[b], preferred_element_type=f32)
             n2 = normalize(residual).astype(bf16)
-            u = jnp.dot(n2, wup_ref[b], preferred_element_type=f32)
+            u = jnp.dot(n2, w_ref[b, :, 768 : 768 + hidden], preferred_element_type=f32)
             g = (0.5 * u * (1.0 + lax.erf(u * (0.5**0.5)))).astype(bf16)
-            y = residual + jnp.dot(g, wdown_ref[b], preferred_element_type=f32)
-            if shifted:
-                y = pltpu.roll(y, move, 0)
-            target[h] = y.astype(bf16)
+            y = residual + lax.dot_general(
+                g, w_ref[b, :, 768 + hidden :], (((1,), (1,)), ((), ())), preferred_element_type=f32
+            )
+            for j, h in enumerate(own):
+                part = y[j * tokens : (j + 1) * tokens]
+                if shifted:
+                    part = pltpu.roll(part, move, 0)
+                target[h] = part.astype(bf16)
             return carry
 
         lax.fori_loop(0, halves // 2 - b, pair, 0)
-        lax.fori_loop(1 + b, halves - 1 - b, attend, 0)
+        lax.fori_loop(0, (halves - 2 - 2 * b) // together, attend, 0)
         west, east = target[halves // 2 - 1].astype(f32), target[halves // 2].astype(f32)
-        packed = pack_tile(west, east).astype(bf16)
-        outs_ref[place ^ b] = packed
-        if b == STAGE - 1:
-            last_ref[...] = packed
+        outs_ref[place ^ b] = pack_tile(west, east).astype(bf16)
+
+    def compute(exact, together):
+        load_tiles()
+
+        def two_blocks(n, carry):
+            block(2 * n, False, exact, together)
+            block(2 * n + 1, True, exact, together)
+            return carry
+
+        lax.fori_loop(0, STAGE // 2, two_blocks, 0)
+
+    low_ref[...] = jnp.ones_like(low_ref)
+    high_ref[...] = jnp.ones_like(high_ref)
+    compute(False, 2)
+    safe = (jnp.min(low_ref[...]) >= 2.0**-90) & (jnp.max(high_ref[...]) <= 2.0**90)
+
+    @pl.when(jnp.logical_not(safe))
+    def _():
+        compute(True, 1)
+
+    last_ref[...] = outs_ref[place ^ (STAGE - 1)]
 
 
 def run_stage(place, tiles, weights, bias):
@@ -231,10 +262,10 @@
             pltpu.VMEM((halves, tokens, width), f32),
             pltpu.VMEM((halves // 2, windows, 2 * piece, width), bf16),
             pltpu.VMEM((halves // 2, windows, 2 * piece, 256), bf16),
-            pltpu.VMEM((STAGE, width, 768), bf16),
+            pltpu.VMEM((STAGE,) + weights[0].shape, bf16),
             pltpu.VMEM((STAGE, width, width), bf16),
-            pltpu.VMEM((STAGE, width, 768), bf16),
-            pltpu.VMEM((STAGE, 768, width), bf16),
+            pltpu.VMEM((8, LANES), f32),
+            pltpu.VMEM((8, LANES), f32),
         ],
         compiler_params=pltpu.CompilerParams(vmem_limit_bytes=VMEM_LIMIT),
         name="stage",
@@ -294,13 +325,12 @@
         ]
         return lax.ppermute(value, axes, pairs)
 
-    tile, pack = prepare(place, fields, land_mask, land_vector.reshape(1, width), (w_qkv, w_proj, w_up, w_down))
+    tile, pack = prepare(place, fields, land_mask, land_vector.reshape(1, width), (w_qkv, w_proj, w_up, w_down.transpose(0, 2, 1)))
     bias = jnp.asarray(window_bias(levels, rows))
 
-    far = exchange(pack, 2)
     offsets = range(-REACH, REACH + 1)
     tiles = [tile if d == 0 else shift(tile, -d, 0) for d in offsets]
-    weights = (pack, exchange(pack, 1), far, exchange(far, 1))
+    weights = [pack] + [exchange(pack, i) for i in range(1, STAGE)]
 
     last, early = run_stage(place, tiles, weights, bias)
     tiles = [shift(last, -d, 1) for d in offsets]

time: 221 us -> 273 us (1.24)
  Pallas kernels: 101 us -> 153 us
    pallas_call x2, Pallas kernels: 94.5 us -> 147 us  [run_stage(): pl.pallas_call(stage_kernel, out_shape=(jax.ShapeDtypeStruct((packed_toke...]
    ppermute x9, waiting for transfers between devices: 45.1 us -> 23.6 us  [shift(): return lax.ppermute(value, axes, pairs)]
    ppermute x6, waiting for transfers between devices: 22.1 us -> 43.4 us  [exchange(): lax.ppermute(value, 'section', [(s, s ^ bit) for s in range(section_count)])]
    unnamed x37 -> x36, local copies, waits for them, and re-layouts: 7.67 us -> 6.71 us
where the time goes in v3:
time: 273 us; the launch traced here: 272 us
  Pallas kernels  153 us (56%)
  waiting for transfers between devices  67 us (25%)
  starting transfers between devices  40.6 us (15%)
  local copies, waits for them, and re-layouts  9.94 us (4%)
    pallas_call x2, Pallas kernels, run_stage(): pl.pallas_call(stage_kernel, out_shape=(jax.ShapeDtypeStruct((packed_toke...  147 us
    ppermute x6, waiting for transfers between devices, exchange(): lax.ppermute(value, 'section', [(s, s ^ bit) for s in range(section_count)])  43.4 us
    ppermute x6, starting transfers between devices, exchange(): lax.ppermute(value, 'section', [(s, s ^ bit) for s in range(section_count)])  31.3 us
    ppermute x9, waiting for transfers between devices, shift(): return lax.ppermute(value, axes, pairs)  23.6 us
    ppermute x9, starting transfers between devices, shift(): return lax.ppermute(value, axes, pairs)  9.32 us
    unnamed x36, local copies, waits for them, and re-layouts  6.71 us
  transfers between devices with their start and end apart: 15, of which 7 were waited for; matrix products, arithmetic and copies ran while one was open for 0% of the time, Pallas kernels for 0%

profile of v3, /device:TPU:134, one launch (start us, length us, event | category | flops | bytes accessed | tf_op | source)
XLA Modules:
  0.0 272.2 jit_solution(5930810860209426116)
XLA Ops:
  0.0 0.7 copy-done.16
  0.7 0.7 copy.10.mask_ref
  1.4 2.1 copy.9.fields_ref
  3.5 2.9 %prepare.1 = (bf16[648,128]{1,0:T(8,128)(2,1)}, bf16[192,2304]{1,0:T(8,128)(2,1)}) custom-call(s32[1]{0:T(128)} %bitcast.micro_ref.place_ref, bf16[4,2,18,2304]{3,2,1,0:T(8,128)(2,1)} %copy.9.fields_ref, s32[18,12]{1,0:T(8,128)} %copy.10.mask_ref, f32[1,192]{1,0:T(1,128)} %bitcast.12, bf16[1,192,576]{2,1,0:T(8,128)(2,1)} %wqkv_ref.1, ...), custom_call_target="tpu_custom_call" | custom-call | tf_op jit(solution)/shard_map/prepare/pallas_call | solution.py:93
  6.4 3.7 %collective-permute-start.6 = (bf16[192,2304]{1,0:T(8,128)(2,1)}, bf16[192,2304]{1,0:T(8,128)(2,1)S(1)}, u32[]{:S(2)}, u32[]{:S(2)}) collective-permute-start(bf16[192,2304]{1,0:T(8,128)(2,1)} %get-tuple-element.11.w0), channel_id=1, source_target_pairs={{0,3},{1,2},{2,1},{3,0},{4,7},{5,6},{6,5},{7,4},{8,11},{9,10},{10,... | collective-permute-start | bytes 2654216 | tf_op jit(solution)/shard_map/ppermute | solution.py:318
  10.1 2.5 collective-permute-start.5
  12.6 2.0 collective-permute-start.4
  14.6 0.7 collective-permute-start.3
  15.3 0.7 collective-permute-start.2
  16.0 0.0 collective-permute-done.3.t4
  16.0 0.0 copy-start.6
  16.0 0.7 collective-permute-start.1
  16.7 0.0 collective-permute-done.2.t3
  16.7 0.7 collective-permute-start
  17.4 0.0 collective-permute-done.1.t1
  17.4 0.0 collective-permute-done.t0
  17.4 13.0 %collective-permute-done.6.w3 = bf16[192,2304]{1,0:T(8,128)(2,1)S(1)} collective-permute-done((bf16[192,2304]{1,0:T(8,128)(2,1)}, bf16[192,2304]{1,0:T(8,128)(2,1)S(1)}, u32[]{:S(2)}, u32[]{:S(2)}) %collective-permute-start.6) | collective-permute-done | bytes 884768 | tf_op jit(solution)/shard_map/ppermute | solution.py:318
  30.4 26.1 %collective-permute-done.5.w2 = bf16[192,2304]{1,0:T(8,128)(2,1)S(1)} collective-permute-done((bf16[192,2304]{1,0:T(8,128)(2,1)}, bf16[192,2304]{1,0:T(8,128)(2,1)S(1)}, u32[]{:S(2)}, u32[]{:S(2)}) %collective-permute-start.5) | collective-permute-done | bytes 884768 | tf_op jit(solution)/shard_map/ppermute | solution.py:318
  56.5 0.0 collective-permute-done.4.w1
  56.6 0.9 copy-done.1
  57.5 0.9 copy-done.2
  58.4 73.6 %stage.2 = (bf16[648,128]{1,0:T(8,128)(2,1)}, bf16[4,648,128]{2,1,0:T(8,128)(2,1)}) custom-call(s32[1]{0:T(128)} %bitcast.micro_ref.place_ref, bf16[648,128]{1,0:T(8,128)(2,1)} %copy-done.12, bf16[648,128]{1,0:T(8,128)(2,1)} %copy-done.11, bf16[648,128]{1,0:T(8,128)(2,1)} %get-tuple-element.10.t2, bf16[648,128]{1,0:T(8,128)(2,1)} %copy-done.8, ...), custom_call_target="tpu_custom_call" | custom-call | tf_op jit(solution)/shard_map/stage/pallas_call | solution.py:251
  132.0 1.3 collective-permute-start.11
  133.3 1.3 collective-permute-start.10
  134.6 1.3 collective-permute-start.9
  135.9 1.3 collective-permute-start.8
  137.2 1.5 collective-permute-start.7
  138.7 0.0 copy-start.3
  138.7 8.6 %collective-permute-done.11.t4 = bf16[648,128]{1,0:T(8,128)(2,1)S(1)} collective-permute-done((bf16[648,128]{1,0:T(8,128)(2,1)}, bf16[648,128]{1,0:T(8,128)(2,1)S(1)}, u32[]{:S(2)}, u32[]{:S(2)}) %collective-permute-start.11) | collective-permute-done | bytes 165920 | tf_op jit(solution)/shard_map/ppermute | solution.py:326
  147.3 2.7 collective-permute-done.10.t3
  149.9 0.0 collective-permute-done.9.t2
  149.9 0.0 collective-permute-done.8.t1
  149.9 12.4 %collective-permute-done.7.t0 = bf16[648,128]{1,0:T(8,128)(2,1)S(1)} collective-permute-done((bf16[648,128]{1,0:T(8,128)(2,1)}, bf16[648,128]{1,0:T(8,128)(2,1)S(1)}, u32[]{:S(2)}, u32[]{:S(2)}) %collective-permute-start.7) | collective-permute-done | bytes 165920 | tf_op jit(solution)/shard_map/ppermute | solution.py:326
  162.3 0.0 copy-done.7
  162.3 0.7 copy-done.10
  163.0 73.6 %stage.3 = (bf16[648,128]{1,0:T(8,128)(2,1)}, bf16[4,648,128]{2,1,0:T(8,128)(2,1)}) custom-call(s32[1]{0:T(128)} %bitcast.micro_ref.place_ref, bf16[648,128]{1,0:T(8,128)(2,1)} %copy-done.10, bf16[648,128]{1,0:T(8,128)(2,1)} %copy-done.9, bf16[648,128]{1,0:T(8,128)(2,1)} %copy-done.7, bf16[648,128]{1,0:T(8,128)(2,1)} %copy-done.5, ...), custom_call_target="tpu_custom_call" | custom-call | tf_op jit(solution)/shard_map/stage/pallas_call | solution.py:251
  236.7 1.2 broadcast_select_fusion
  237.8 0.7 slice_bitcast_fusion
  238.5 18.7 %collective-permute-start.14 = (bf16[648,128]{1,0:T(8,128)(2,1)S(1)}, bf16[648,128]{1,0:T(8,128)(2,1)S(1)}, u32[]{:S(2)}, u32[]{:S(2)}) collective-permute-start(bf16[648,128]{1,0:T(8,128)(2,1)S(1)} %get-tuple-element.15), channel_id=1, source_target_pairs={{0,3},{1,2},{2,1},{3,0},{4,7},{5,6},{6,5},{7,4},{8,11},{9,10},{10,... | collective-permute-start | bytes 497672 | tf_op jit(solution)/shard_map/ppermute | solution.py:318
  257.2 2.3 collective-permute-start.13
  259.6 2.0 collective-permute-start.12
  261.6 0.2 collective-permute-done.14.o3
  261.8 4.0 %collective-permute-done.13.o2 = bf16[648,128]{1,0:T(8,128)(2,1)S(1)} collective-permute-done((bf16[648,128]{1,0:T(8,128)(2,1)S(1)}, bf16[648,128]{1,0:T(8,128)(2,1)S(1)}, u32[]{:S(2)}, u32[]{:S(2)}) %collective-permute-start.13) | collective-permute-done | bytes 165920 | tf_op jit(solution)/shard_map/ppermute | solution.py:318
  265.8 0.0 collective-permute-done.12.o1
  265.8 0.7 copy-done.14
  266.5 0.1 copy-done.15
  266.5 3.1 %finish.1 = bf16[1,4,2,18,2304]{4,3,2,1,0:T(8,128)(2,1)} custom-call(s32[1]{0:T(128)} %bitcast.micro_ref.place_ref, bf16[648,128]{1,0:T(8,128)(2,1)} %get-tuple-element.18.o0, bf16[648,128]{1,0:T(8,128)(2,1)} %copy-done.15, bf16[648,128]{1,0:T(8,128)(2,1)} %copy-done.14, bf16[648,128]{1,0:T(8,128)(2,1)} %copy-done.13), custom_call_target="tpu_custom_call" | custom-call | tf_op jit(solution)/shard_map/finish/pallas_call | solution.py:298
  269.6 2.5 copy.11
  (25 shorter events, 0.0 us)
Async XLA Ops:
  0.0 0.7 copy-start.16
  6.4 24.0 %collective-permute-start.6 = (bf16[192,2304]{1,0:T(8,128)(2,1)}, bf16[192,2304]{1,0:T(8,128)(2,1)S(1)}, u32[]{:S(2)}, u32[]{:S(2)}) collective-permute-start(bf16[192,2304]{1,0:T(8,128)(2,1)} %get-tuple-element.11.w0), channel_id=1, source_target_pairs={{0,3},{1,2},{2,1},{3,0},{4,7},{5,6},{6,5},{7,4},{8,11},{9,10},{10,... | collective-permute-start | bytes 2654216 | tf_op jit(solution)/shard_map/ppermute | solution.py:318
  10.1 46.5 %collective-permute-start.5 = (bf16[192,2304]{1,0:T(8,128)(2,1)}, bf16[192,2304]{1,0:T(8,128)(2,1)S(1)}, u32[]{:S(2)}, u32[]{:S(2)}) collective-permute-start(bf16[192,2304]{1,0:T(8,128)(2,1)} %get-tuple-element.11.w0), channel_id=1, source_target_pairs={{0,2},{1,3},{2,0},{3,1},{4,6},{5,7},{6,4},{7,5},{8,10},{9,11},{10,... | collective-permute-start | bytes 2654216 | tf_op jit(solution)/shard_map/ppermute | solution.py:318
  12.6 44.0 %collective-permute-start.4 = (bf16[192,2304]{1,0:T(8,128)(2,1)}, bf16[192,2304]{1,0:T(8,128)(2,1)S(1)}, u32[]{:S(2)}, u32[]{:S(2)}) collective-permute-start(bf16[192,2304]{1,0:T(8,128)(2,1)} %get-tuple-element.11.w0), channel_id=1, source_target_pairs={{0,1},{1,0},{2,3},{3,2},{4,5},{5,4},{6,7},{7,6},{8,9},{9,8},{10,11... | collective-permute-start | bytes 2654216 | tf_op jit(solution)/shard_map/ppermute | solution.py:318
  14.6 1.4 collective-permute-start.3
  15.3 1.4 collective-permute-start.2
  16.0 40.6 %copy-start.6 = (bf16[648,128]{1,0:T(8,128)(2,1)}, bf16[648,128]{1,0:T(8,128)(2,1)S(1)}, u32[]{:S(2)}) copy-start(bf16[648,128]{1,0:T(8,128)(2,1)S(1)} %collective-permute-done.3.t4) | copy-start | bytes 497668
  16.0 1.4 collective-permute-start.1
  16.7 39.9 %copy-start.8 = (bf16[648,128]{1,0:T(8,128)(2,1)}, bf16[648,128]{1,0:T(8,128)(2,1)S(1)}, u32[]{:S(2)}) copy-start(bf16[648,128]{1,0:T(8,128)(2,1)S(1)} %collective-permute-done.2.t3) | copy-start | bytes 497668
  16.7 0.7 collective-permute-start
  17.4 39.2 %copy-start.11 = (bf16[648,128]{1,0:T(8,128)(2,1)}, bf16[648,128]{1,0:T(8,128)(2,1)S(1)}, u32[]{:S(2)}) copy-start(bf16[648,128]{1,0:T(8,128)(2,1)S(1)} %collective-permute-done.1.t1) | copy-start | bytes 497668
  17.4 39.2 %copy-start.12 = (bf16[648,128]{1,0:T(8,128)(2,1)}, bf16[648,128]{1,0:T(8,128)(2,1)S(1)}, u32[]{:S(2)}) copy-start(bf16[648,128]{1,0:T(8,128)(2,1)S(1)} %collective-permute-done.t0) | copy-start | bytes 497668
  30.4 26.2 %copy-start = (bf16[192,2304]{1,0:T(8,128)(2,1)}, bf16[192,2304]{1,0:T(8,128)(2,1)S(1)}, u32[]{:S(2)}) copy-start(bf16[192,2304]{1,0:T(8,128)(2,1)S(1)} %collective-permute-done.6.w3) | copy-start | bytes 2654212
  56.5 0.9 copy-start.1
  57.5 0.9 copy-start.2
  132.0 15.3 %collective-permute-start.11 = (bf16[648,128]{1,0:T(8,128)(2,1)}, bf16[648,128]{1,0:T(8,128)(2,1)S(1)}, u32[]{:S(2)}, u32[]{:S(2)}) collective-permute-start(bf16[648,128]{1,0:T(8,128)(2,1)} %get-tuple-element.13), channel_id=1, source_target_pairs={{0,500},{1,501},{2,502},{3,503},{8,508},{9,509},{10,510},{11,511},... | collective-permute-start | bytes 497672 | tf_op jit(solution)/shard_map/ppermute | solution.py:326
  133.3 16.7 %collective-permute-start.10 = (bf16[648,128]{1,0:T(8,128)(2,1)}, bf16[648,128]{1,0:T(8,128)(2,1)S(1)}, u32[]{:S(2)}, u32[]{:S(2)}) collective-permute-start(bf16[648,128]{1,0:T(8,128)(2,1)} %get-tuple-element.13), channel_id=1, source_target_pairs={{0,508},{1,509},{2,510},{3,511},{8,4},{9,5},{10,6},{11,7},{16,12},... | collective-permute-start | bytes 497672 | tf_op jit(solution)/shard_map/ppermute | solution.py:326
  134.6 15.4 %collective-permute-start.9 = (bf16[648,128]{1,0:T(8,128)(2,1)}, bf16[648,128]{1,0:T(8,128)(2,1)S(1)}, u32[]{:S(2)}, u32[]{:S(2)}) collective-permute-start(bf16[648,128]{1,0:T(8,128)(2,1)} %get-tuple-element.13), channel_id=1, source_target_pairs={{0,4},{1,5},{2,6},{3,7},{8,12},{9,13},{10,14},{11,15},{16,20},{17,... | collective-permute-start | bytes 497672 | tf_op jit(solution)/shard_map/ppermute | solution.py:326
  135.9 14.1 %collective-permute-start.8 = (bf16[648,128]{1,0:T(8,128)(2,1)}, bf16[648,128]{1,0:T(8,128)(2,1)S(1)}, u32[]{:S(2)}, u32[]{:S(2)}) collective-permute-start(bf16[648,128]{1,0:T(8,128)(2,1)} %get-tuple-element.13), channel_id=1, source_target_pairs={{0,12},{1,13},{2,14},{3,15},{8,20},{9,21},{10,22},{11,23},{16,28},... | collective-permute-start | bytes 497672 | tf_op jit(solution)/shard_map/ppermute | solution.py:326
  137.2 25.1 %collective-permute-start.7 = (bf16[648,128]{1,0:T(8,128)(2,1)}, bf16[648,128]{1,0:T(8,128)(2,1)S(1)}, u32[]{:S(2)}, u32[]{:S(2)}) collective-permute-start(bf16[648,128]{1,0:T(8,128)(2,1)} %get-tuple-element.13), channel_id=1, source_target_pairs={{0,20},{1,21},{2,22},{3,23},{8,28},{9,29},{10,30},{11,31},{16,36},... | collective-permute-start | bytes 497672 | tf_op jit(solution)/shard_map/ppermute | solution.py:326
  138.7 98.0 %copy-start.3 = (bf16[4,648,128]{2,1,0:T(8,128)(2,1)S(1)}, bf16[4,648,128]{2,1,0:T(8,128)(2,1)}, u32[]{:S(2)}) copy-start(bf16[4,648,128]{2,1,0:T(8,128)(2,1)} %get-tuple-element.12) | copy-start | bytes 1990660
  147.3 15.1 %copy-start.4 = (bf16[648,128]{1,0:T(8,128)(2,1)}, bf16[648,128]{1,0:T(8,128)(2,1)S(1)}, u32[]{:S(2)}) copy-start(bf16[648,128]{1,0:T(8,128)(2,1)S(1)} %collective-permute-done.11.t4) | copy-start | bytes 497668
  149.9 12.4 %copy-start.5 = (bf16[648,128]{1,0:T(8,128)(2,1)}, bf16[648,128]{1,0:T(8,128)(2,1)S(1)}, u32[]{:S(2)}) copy-start(bf16[648,128]{1,0:T(8,128)(2,1)S(1)} %collective-permute-done.10.t3) | copy-start | bytes 497668
  149.9 12.4 %copy-start.7 = (bf16[648,128]{1,0:T(8,128)(2,1)}, bf16[648,128]{1,0:T(8,128)(2,1)S(1)}, u32[]{:S(2)}) copy-start(bf16[648,128]{1,0:T(8,128)(2,1)S(1)} %collective-permute-done.9.t2) | copy-start | bytes 497668
  149.9 12.4 %copy-start.9 = (bf16[648,128]{1,0:T(8,128)(2,1)}, bf16[648,128]{1,0:T(8,128)(2,1)S(1)}, u32[]{:S(2)}) copy-start(bf16[648,128]{1,0:T(8,128)(2,1)S(1)} %collective-permute-done.8.t1) | copy-start | bytes 497668
  162.3 0.7 copy-start.10
  238.5 23.3 %collective-permute-start.14 = (bf16[648,128]{1,0:T(8,128)(2,1)S(1)}, bf16[648,128]{1,0:T(8,128)(2,1)S(1)}, u32[]{:S(2)}, u32[]{:S(2)}) collective-permute-start(bf16[648,128]{1,0:T(8,128)(2,1)S(1)} %get-tuple-element.15), channel_id=1, source_target_pairs={{0,3},{1,2},{2,1},{3,0},{4,7},{5,6},{6,5},{7,4},{8,11},{9,10},{10,... | collective-permute-start | bytes 497672 | tf_op jit(solution)/shard_map/ppermute | solution.py:318
  257.2 8.6 %collective-permute-start.13 = (bf16[648,128]{1,0:T(8,128)(2,1)S(1)}, bf16[648,128]{1,0:T(8,128)(2,1)S(1)}, u32[]{:S(2)}, u32[]{:S(2)}) collective-permute-start(bf16[648,128]{1,0:T(8,128)(2,1)S(1)} %get-tuple-element.16), channel_id=1, source_target_pairs={{0,2},{1,3},{2,0},{3,1},{4,6},{5,7},{6,4},{7,5},{8,10},{9,11},{10,... | collective-permute-start | bytes 497672 | tf_op jit(solution)/shard_map/ppermute | solution.py:318
  259.6 6.2 %collective-permute-start.12 = (bf16[648,128]{1,0:T(8,128)(2,1)S(1)}, bf16[648,128]{1,0:T(8,128)(2,1)S(1)}, u32[]{:S(2)}, u32[]{:S(2)}) collective-permute-start(bf16[648,128]{1,0:T(8,128)(2,1)S(1)} %get-tuple-element.17), channel_id=1, source_target_pairs={{0,1},{1,0},{2,3},{3,2},{4,5},{5,4},{6,7},{7,6},{8,9},{9,8},{10,11... | collective-permute-start | bytes 497672 | tf_op jit(solution)/shard_map/ppermute | solution.py:318
  261.8 4.0 %copy-start.13 = (bf16[648,128]{1,0:T(8,128)(2,1)}, bf16[648,128]{1,0:T(8,128)(2,1)S(1)}, u32[]{:S(2)}) copy-start(bf16[648,128]{1,0:T(8,128)(2,1)S(1)} %collective-permute-done.14.o3) | copy-start | bytes 497668
  265.8 0.7 copy-start.14
  265.8 0.7 copy-start.15

commit v4 on v3

--- a/solution.py
+++ b/solution.py
@@ -42,17 +42,17 @@
 
 def pack_tile(west, east):
     return jnp.concatenate(
-        [west[:, :LANES], east[:, :LANES], jnp.concatenate([west[:, LANES:], east[:, LANES:]], 1)], 0
+        [west[:, :LANES], jnp.concatenate([west[:, LANES:], east[:, LANES:]], 1), east[:, :LANES]], 0
     )
 
 
-def unpack_tile(packed):
-    tokens = packed.shape[0] // 3
-    last = packed[2 * tokens :]
-    side = last.shape[1] // 2
-    west = jnp.concatenate([packed[:tokens], last[:, :side]], 1)
-    east = jnp.concatenate([packed[tokens : 2 * tokens], last[:, side:]], 1)
-    return west, east
+def west_of(packed, tokens):
+    return jnp.concatenate([packed[:tokens], packed[tokens : 2 * tokens, : LANES // 2]], 1)
+
+
+def east_of(packed, tokens):
+    end = packed.shape[0]
+    return jnp.concatenate([packed[end - tokens :], packed[end - 2 * tokens : end - tokens, LANES // 2 :]], 1)
 
 
 def prepare_kernel(micro_ref, fields_ref, mask_ref, vector_ref, wqkv_ref, wproj_ref, wup_ref, wdown_ref,
@@ -72,9 +72,9 @@
             grid_ref[2 * half + 1, at, :] = jnp.concatenate([piece[:, LANES:]] * 2, 1)
     tokens, side = rows * step, width - LANES
     tile_ref[:tokens] = grid_ref[0].astype(jnp.bfloat16)
-    tile_ref[tokens : 2 * tokens] = grid_ref[2].astype(jnp.bfloat16)
+    tile_ref[2 * tokens :] = grid_ref[2].astype(jnp.bfloat16)
     lane = lax.broadcasted_iota(jnp.int32, (1, LANES), 1)
-    tile_ref[2 * tokens :] = jnp.where(lane < side, grid_ref[1], grid_ref[3]).astype(jnp.bfloat16)
+    tile_ref[tokens : 2 * tokens] = jnp.where(lane < side, grid_ref[1], grid_ref[3]).astype(jnp.bfloat16)
     side = 256 - width
     for i in range(3):
         pack_ref[:, 256 * i : 256 * i + 256] = jnp.concatenate(
@@ -112,31 +112,29 @@
     )(micro, fields, land_mask, land_vector, *weights)
 
 
-def stage_kernel(place_ref, t0, t1, t2, t3, t4, w0, w1, w2, w3, bias_ref, last_ref, outs_ref,
-                 xa, xb, q_ref, k_ref, v_ref, w_ref, wproj_ref, low_ref, high_ref):
+def compute_stage(mode, tile_refs, bias_ref, w_ref, wproj_ref, store, scratch):
+    xa, xb, q_ref, k_ref, v_ref, low_ref, high_ref = scratch
     f32, bf16 = jnp.float32, jnp.bfloat16
     halves, tokens, width = xa.shape
     head_size = width // HEADS
     windows, piece, _ = bias_ref.shape
     move = piece // 2
-    place = place_ref[0]
-    side = 256 - width
     hidden = (w_ref.shape[2] - 768) // 2
-
-    for i, ref in enumerate((w0, w1, w2, w3)):
-        at = place ^ i
-        w_ref[at] = ref[...]
-        wproj_ref[at] = jnp.concatenate([ref[:, 256 * j + width : 256 * j + 256] for j in range(3)], 1)
+    middle = halves // 2
 
     channel_head = lax.broadcasted_iota(jnp.int32, (1, width), 1) // head_size
     scale = head_size ** (-0.5) * LOG2E
     ones = jnp.ones((2 * piece, 256 - width), f32)
 
     def load_tiles():
-        for i, ref in enumerate((t0, t1, t2, t3, t4)):
-            west, east = unpack_tile(ref[...].astype(f32))
-            xa[2 * i] = west.astype(bf16)
-            xa[2 * i + 1] = east.astype(bf16)
+        into = xb if mode == "rest" else xa
+        first = middle - len(tile_refs)
+        for i, ref in enumerate(tile_refs):
+            packed = ref[...].astype(f32)
+            for j, part in enumerate((west_of, east_of)):
+                h = first + 2 * i + j
+                if mode != "rest" or 0 < h < halves - 1:
+                    into[h] = part(packed, tokens).astype(bf16)
 
     def select_heads(parts, first, lanes):
         total = parts[0]
@@ -172,7 +170,7 @@
             high_ref[:, rest] = jnp.maximum(high_ref[:, rest], jnp.max(sums[1].reshape(-1, 8, width - LANES), axis=0))
         return jnp.concatenate([top / total for top, total in zip(tops, sums)], 1)
 
-    def block(b, shifted, exact, together):
+    def block(b, shifted, exact, together, alone=False):
         source, target = (xb, xa) if shifted else (xa, xb)
 
         def load(h):
@@ -194,7 +192,7 @@
             return carry
 
         def attend(c, carry):
-            own = [1 + b + together * c + j for j in range(together)]
+            own = [(middle - 1 if alone else 1 + b) + together * c + j for j in range(together)]
             x = jnp.concatenate([load(h) for h in own], 0)
             a = jnp.concatenate(
                 [window_attention(h, (h - b) // 2, w, shifted, exact) for h in own for w in range(windows)], 0
@@ -213,10 +211,13 @@
                 target[h] = part.astype(bf16)
             return carry
 
-        lax.fori_loop(0, halves // 2 - b, pair, 0)
-        lax.fori_loop(0, (halves - 2 - 2 * b) // together, attend, 0)
-        west, east = target[halves // 2 - 1].astype(f32), target[halves // 2].astype(f32)
-        outs_ref[place ^ b] = pack_tile(west, east).astype(bf16)
+        if alone:
+            pair(middle // 2, 0)
+            lax.fori_loop(0, 2 // together, attend, 0)
+        else:
+            lax.fori_loop(0, middle - b, pair, 0)
+            lax.fori_loop(0, (halves - 2 - 2 * b) // together, attend, 0)
+        store(b, pack_tile(target[middle - 1].astype(f32), target[middle].astype(f32)).astype(bf16))
 
     def compute(exact, together):
         load_tiles()
@@ -226,7 +227,13 @@
             block(2 * n + 1, True, exact, together)
             return carry
 
-        lax.fori_loop(0, STAGE // 2, two_blocks, 0)
+        if mode == "whole":
+            lax.fori_loop(0, STAGE // 2, two_blocks, 0)
+        elif mode == "first":
+            block(0, False, exact, together, True)
+        else:
+            for b in range(1, STAGE):
+                block(b, b % 2 == 1, exact, together)
 
     low_ref[...] = jnp.ones_like(low_ref)
     high_ref[...] = jnp.ones_like(high_ref)
@@ -237,39 +244,90 @@
     def _():
         compute(True, 1)
 
+
+def unpack_projection(ref, width):
+    return jnp.concatenate([ref[:, 256 * j + width : 256 * j + 256] for j in range(3)], 1)
+
+
+def gather_weights(place, refs, w_ref, wproj_ref):
+    for i, ref in enumerate(refs):
+        w_ref[place ^ i] = ref[...]
+        wproj_ref[place ^ i] = unpack_projection(ref, wproj_ref.shape[1])
+
+
+def whole_kernel(place_ref, t0, t1, t2, t3, t4, w0, w1, w2, w3, bias_ref, last_ref, outs_ref,
+                 w_ref, wproj_ref, *scratch):
+    place = place_ref[0]
+    gather_weights(place, (w0, w1, w2, w3), w_ref, wproj_ref)
+
+    def store(b, packed):
+        outs_ref[place ^ b] = packed
+
+    compute_stage("whole", (t0, t1, t2, t3, t4), bias_ref, w_ref, wproj_ref, store, scratch)
     last_ref[...] = outs_ref[place ^ (STAGE - 1)]
 
 
-def run_stage(place, tiles, weights, bias):
-    packed_tokens = tiles[0].shape[0]
-    tokens = packed_tokens // 3
-    width = weights[0].shape[0]
-    halves = 2 * len(tiles)
-    windows, piece, _ = bias.shape
+def first_kernel(tile_in, w_in, bias_ref, tile_ref, west_ref, east_ref, w_ref, wproj_ref, *scratch):
+    w_ref[0] = w_in[...]
+    wproj_ref[0] = unpack_projection(w_in, wproj_ref.shape[1])
+
+    def store(b, packed):
+        tile_ref[...] = packed
+
+    compute_stage("first", (tile_in,), bias_ref, w_ref, wproj_ref, store, scratch)
+    west_ref[...] = tile_ref[: west_ref.shape[0]]
+    east_ref[...] = tile_ref[tile_ref.shape[0] - east_ref.shape[0] :]
+
+
+def rest_kernel(place_ref, t0, t1, t2, t3, t4, w0, w1, w2, w3, bias_ref, early_ref, o0, o1, o2, o3,
+                outs_ref, w_ref, wproj_ref, *scratch):
+    place = place_ref[0]
+    late = place_ref[1] == 1
+
+    @pl.when(late)
+    def _():
+        gather_weights(place, (w0, w1, w2, w3), w_ref, wproj_ref)
+
+        def store(b, packed):
+            outs_ref[place ^ b] = packed
+
+        store(0, t2[...])
+        compute_stage("rest", (t0, t1, t2, t3, t4), bias_ref, w_ref, wproj_ref, store, scratch)
+        for i, ref in enumerate((o0, o1, o2, o3)):
+            ref[...] = outs_ref[i]
+
+    @pl.when(jnp.logical_not(late))
+    def _():
+        for i, ref in enumerate((o0, o1, o2, o3)):
+            ref[...] = early_ref[i]
+
+
+def run_stage(kernel, place, operands, outs, extra, blocks, tokens, width, bias_shape):
+    halves = 2 * (2 * REACH + 1)
+    windows, piece, _ = bias_shape
     vmem = pl.BlockSpec(memory_space=pltpu.VMEM)
     bf16, f32 = jnp.bfloat16, jnp.float32
+    places = [] if place is None else [place]
     return pl.pallas_call(
-        stage_kernel,
-        out_shape=(
-            jax.ShapeDtypeStruct((packed_tokens, LANES), bf16),
-            jax.ShapeDtypeStruct((STAGE, packed_tokens, LANES), bf16),
-        ),
-        in_specs=[pl.BlockSpec(memory_space=pltpu.SMEM)] + [vmem] * (len(tiles) + len(weights) + 1),
-        out_specs=(vmem, vmem),
-        scratch_shapes=[
+        kernel,
+        out_shape=tuple(jax.ShapeDtypeStruct(shape, bf16) for shape in outs),
+        in_specs=[pl.BlockSpec(memory_space=pltpu.SMEM)] * len(places) + [vmem] * len(operands),
+        out_specs=(vmem,) * len(outs),
+        scratch_shapes=[pltpu.VMEM(shape, bf16) for shape in extra]
+        + [
+            pltpu.VMEM((blocks, width, 2304), bf16),
+            pltpu.VMEM((blocks, width, width), bf16),
             pltpu.VMEM((halves, tokens, width), bf16),
             pltpu.VMEM((halves, tokens, width), bf16),
             pltpu.VMEM((halves, tokens, width), f32),
             pltpu.VMEM((halves // 2, windows, 2 * piece, width), bf16),
             pltpu.VMEM((halves // 2, windows, 2 * piece, 256), bf16),
-            pltpu.VMEM((STAGE,) + weights[0].shape, bf16),
-            pltpu.VMEM((STAGE, width, width), bf16),
             pltpu.VMEM((8, LANES), f32),
             pltpu.VMEM((8, LANES), f32),
         ],
         compiler_params=pltpu.CompilerParams(vmem_limit_bytes=VMEM_LIMIT),
-        name="stage",
-    )(place, *tiles, *weights, bias)
+        name=kernel.__name__,
+    )(*places, *operands)
 
 
 def finish_kernel(place_ref, o0, o1, o2, o3, out_ref, grid_ref):
@@ -287,8 +345,8 @@
             for column in range(WLON):
                 half, inside = divmod(column, HALF)
                 at = pl.ds(level * HALF + inside, rows, stride=step)
-                rest = grid_ref[2, at, :][:, half * side : (half + 1) * side]
-                piece = jnp.concatenate([grid_ref[half, at, :], rest], 1)
+                rest = grid_ref[1, at, :][:, half * side : (half + 1) * side]
+                piece = jnp.concatenate([grid_ref[2 * half, at, :], rest], 1)
                 out_ref[0, micro, level, :, column * width : (column + 1) * width] = piece.astype(jnp.bfloat16)
 
 
@@ -311,31 +369,43 @@
     width = land_vector.shape[0]
     tile_count, section_count = lax.axis_size("tile"), lax.axis_size("section")
     section = lax.axis_index("section")
-    place = (section % STAGE).astype(jnp.int32).reshape(1)
+    place = jnp.stack([section % STAGE, section // STAGE]).astype(jnp.int32)
     axes = ("tile", "section")
 
     def exchange(value, bit):
         return lax.ppermute(value, "section", [(s, s ^ bit) for s in range(section_count)])
 
-    def shift(value, tiles, stages):
+    def shift(value, tiles, first, stages=0):
         pairs = [
             (t * section_count + s, (t + tiles) % tile_count * section_count + s + stages * STAGE)
             for t in range(tile_count)
-            for s in range(STAGE)
+            for s in range(first, first + STAGE)
         ]
         return lax.ppermute(value, axes, pairs)
 
-    tile, pack = prepare(place, fields, land_mask, land_vector.reshape(1, width), (w_qkv, w_proj, w_up, w_down.transpose(0, 2, 1)))
+    tokens = rows * levels * HALF
+    tile_shape, half_shape = (3 * tokens, LANES), (2 * tokens, LANES)
     bias = jnp.asarray(window_bias(levels, rows))
-
-    offsets = range(-REACH, REACH + 1)
-    tiles = [tile if d == 0 else shift(tile, -d, 0) for d in offsets]
-    weights = [pack] + [exchange(pack, i) for i in range(1, STAGE)]
-
-    last, early = run_stage(place, tiles, weights, bias)
-    tiles = [shift(last, -d, 1) for d in offsets]
-    _, late = run_stage(place, tiles, weights, bias)
-    outs = jnp.where(section < STAGE, early, late)
+    sizes = (tokens, width, bias.shape)
+
+    tile, pack = prepare(
+        place, fields, land_mask, land_vector.reshape(1, width), (w_qkv, w_proj, w_up, w_down.transpose(0, 2, 1))
+    )
+    tiles = [tile if d == 0 else shift(tile, -d, 0) for d in range(-REACH, REACH + 1)]
+    near, far = exchange(pack, 1), exchange(pack, 2)
+    far, tiles = lax.optimization_barrier((far, tiles))
+    weights = [pack, near, far, exchange(far, 1)]
+
+    last, early = run_stage(
+        whole_kernel, place, (*tiles, *weights, bias), (tile_shape, (STAGE,) + tile_shape), (), STAGE, *sizes
+    )
+    own = shift(last, 0, 0, 1)
+    first = lax.select_n(place[0], *weights)
+    own, west, east = run_stage(first_kernel, None, (own, first, bias), (tile_shape, half_shape, half_shape), (), 1, *sizes)
+    tiles = [shift(east, 2, STAGE), shift(own, 1, STAGE), own, shift(own, -1, STAGE), shift(west, -2, STAGE)]
+    outs = run_stage(
+        rest_kernel, place, (*tiles, *weights, bias, early), (tile_shape,) * STAGE, ((STAGE,) + tile_shape,), STAGE, *sizes
+    )
 
     pieces = [outs[0]] + [exchange(outs[i], i) for i in range(1, STAGE)]
     return finish(place, pieces, (1, micro_count, levels, rows, flat_width))

time: 273 us -> 237 us (0.87)
  the two profiles are of different devices: /device:TPU:134 before, /device:TPU:129 now
where the time goes in v4:
time: 237 us; the launch traced here: 236 us
  Pallas kernels  136 us (57%)
  starting transfers between devices  45.3 us (19%)
  waiting for transfers between devices  42.5 us (18%)
  local copies, waits for them, and re-layouts  9.04 us (4%)
  other arithmetic  3.18 us (1%)
    pallas_call x3, Pallas kernels, run_stage(): pl.pallas_call(kernel, out_shape=tuple((jax.ShapeDtypeStruct(shape, bf16)...  129 us
    ppermute x9, starting transfers between devices, shift(): return lax.ppermute(value, axes, pairs)  23.1 us
    ppermute x6, waiting for transfers between devices, exchange(): lax.ppermute(value, 'section', [(s, s ^ bit) for s in range(section_count)])  22.2 us
    ppermute x6, starting transfers between devices, exchange(): lax.ppermute(value, 'section', [(s, s ^ bit) for s in range(section_count)])  22.1 us
    ppermute x9, waiting for transfers between devices, shift(): return lax.ppermute(value, axes, pairs)  20.3 us
    unnamed x36, local copies, waits for them, and re-layouts  6.53 us
  transfers between devices with their start and end apart: 15, of which 7 were waited for; matrix products, arithmetic and copies ran while one was open for 1% of the time, Pallas kernels for 0%

profile of v4, /device:TPU:129, one launch (start us, length us, event | category | flops | bytes accessed | tf_op | source)
XLA Modules:
  0.0 236.2 jit_solution(1142971403652919940)
XLA Ops:
  0.0 0.7 copy-done.16
  0.7 0.7 copy.10.mask_ref
  1.4 2.1 copy.9.fields_ref
  3.5 0.7 pad_add_fusion.micro_ref.place_ref
  4.1 3.5 %prepare.1 = (bf16[648,128]{1,0:T(8,128)(2,1)}, bf16[192,2304]{1,0:T(8,128)(2,1)}) custom-call(s32[2]{0:T(128)} %pad_add_fusion.micro_ref.place_ref, bf16[4,2,18,2304]{3,2,1,0:T(8,128)(2,1)} %copy.9.fields_ref, s32[18,12]{1,0:T(8,128)} %copy.10.mask_ref, f32[1,192]{1,0:T(1,128)} %bitcast.5, bf16[1,192,576]{2,1,0:T(8,128)(2,1)} %wqkv_ref.1, ...), custom_call_target="tpu_custom_call" | custom-call | tf_op jit(solution)/shard_map/prepare/pallas_call | solution.py:93
  7.7 4.0 %collective-permute-start = (bf16[192,2304]{1,0:T(8,128)(2,1)}, bf16[192,2304]{1,0:T(8,128)(2,1)S(1)}, u32[]{:S(2)}, u32[]{:S(2)}) collective-permute-start(bf16[192,2304]{1,0:T(8,128)(2,1)} %get-tuple-element.22.w0), channel_id=1, source_target_pairs={{0,2},{1,3},{2,0},{3,1},{4,6},{5,7},{6,4},{7,5},{8,10},{9,11},{10,... | collective-permute-start | bytes 2654216 | tf_op jit(solution)/shard_map/ppermute | solution.py:376
  11.7 0.7 collective-permute-start.4
  12.4 0.7 collective-permute-start.3
  13.0 0.7 collective-permute-start.2
  13.7 0.7 collective-permute-start.1
  14.4 0.0 collective-permute-done.4.t4
  14.4 2.9 %collective-permute-start.5 = (bf16[192,2304]{1,0:T(8,128)(2,1)}, bf16[192,2304]{1,0:T(8,128)(2,1)S(1)}, u32[]{:S(2)}, u32[]{:S(2)}) collective-permute-start(bf16[192,2304]{1,0:T(8,128)(2,1)} %get-tuple-element.22.w0), channel_id=1, source_target_pairs={{0,1},{1,0},{2,3},{3,2},{4,5},{5,4},{6,7},{7,6},{8,9},{9,8},{10,11... | collective-permute-start | bytes 2654216 | tf_op jit(solution)/shard_map/ppermute | solution.py:376
  17.3 0.0 collective-permute-done.3.t3
  17.3 0.0 collective-permute-done.2.t1
  17.3 0.0 collective-permute-done.1.t0
  17.4 13.9 %collective-permute-done.w2 = bf16[192,2304]{1,0:T(8,128)(2,1)S(1)} collective-permute-done((bf16[192,2304]{1,0:T(8,128)(2,1)}, bf16[192,2304]{1,0:T(8,128)(2,1)S(1)}, u32[]{:S(2)}, u32[]{:S(2)}) %collective-permute-start) | collective-permute-done | bytes 884768 | tf_op jit(solution)/shard_map/ppermute | solution.py:376
  31.3 3.1 %collective-permute-start.6 = (bf16[192,2304]{1,0:T(8,128)(2,1)S(1)}, bf16[192,2304]{1,0:T(8,128)(2,1)S(1)}, u32[]{:S(2)}, u32[]{:S(2)}) collective-permute-start(bf16[192,2304]{1,0:T(8,128)(2,1)S(1)} %collective-permute-done.w2), channel_id=1, source_target_pairs={{0,1},{1,0},{2,3},{3,2},{4,5},{5,4},{6,7},{7,6},{8,9},{9,8},{10,11... | collective-permute-start | bytes 2654216 | tf_op jit(solution)/shard_map/ppermute | solution.py:376
  34.4 0.0 collective-permute-done.5.w1
  34.4 2.0 collective-permute-done.6.w3
  36.5 0.9 copy-done.3
  37.4 73.7 %whole_kernel.1 = (bf16[648,128]{1,0:T(8,128)(2,1)}, bf16[4,648,128]{2,1,0:T(8,128)(2,1)}) custom-call(s32[2]{0:T(128)} %pad_add_fusion.micro_ref.place_ref, bf16[648,128]{1,0:T(8,128)(2,1)} %copy-done.7, bf16[648,128]{1,0:T(8,128)(2,1)} %copy-done.6, bf16[648,128]{1,0:T(8,128)(2,1)} %get-tuple-element.26.t2, bf16[648,128]{1,0:T(8,128)(2,1)} %copy-done.5, ...), custom_call_target="tpu_custom_call" | custom-call | tf_op jit(solution)/shard_map/whole_kernel/pallas_call | solution.py:311
  111.1 1.5 collective-permute-start.7
  112.6 2.5 %select_select_fusion.w_in = bf16[192,2304]{1,0:T(8,128)(2,1)} fusion(bf16[192,2304]{1,0:T(8,128)(2,1)} %copy-done.1, bf16[192,2304]{1,0:T(8,128)(2,1)} %copy-done.3, bf16[192,2304]{1,0:T(8,128)(2,1)S(1)} %copy-done, bf16[192,2304]{1,0:T(8,128)(2,1)} %copy-done.2, pred[]{:T(512)S(6)} %select_n.45, pred[]{:T(512)S(6)} %select_n.42, pred[]{:T(512)S(6)} %select_n.40), kind=kLoop, calls=%fused_computation | loop fusion | flops 1327104 | bytes 4423683 | tf_op jit(solution)/shard_map/select_n | solution.py:403
  115.1 18.2 %collective-permute-done.7.tile_in = bf16[648,128]{1,0:T(8,128)(2,1)S(1)} collective-permute-done((bf16[648,128]{1,0:T(8,128)(2,1)}, bf16[648,128]{1,0:T(8,128)(2,1)S(1)}, u32[]{:S(2)}, u32[]{:S(2)}) %collective-permute-start.7) | collective-permute-done | bytes 165920 | tf_op jit(solution)/shard_map/ppermute | solution.py:384
  133.3 0.7 copy-done.10
  134.0 8.7 %first_kernel.1 = (bf16[648,128]{1,0:T(8,128)(2,1)}, bf16[432,128]{1,0:T(8,128)(2,1)}, bf16[432,128]{1,0:T(8,128)(2,1)}) custom-call(bf16[648,128]{1,0:T(8,128)(2,1)} %copy-done.10, bf16[192,2304]{1,0:T(8,128)(2,1)} %select_select_fusion.w_in, f32[3,72,144]{2,1,0:T(8,128)} %constant.35.clone.bias_ref), custom_call_target="tpu_custom_call" | custom-call | tf_op jit(solution)/shard_map/first_kernel/pallas_call | solution.py:311
  142.7 3.3 %collective-permute-start.10 = (bf16[648,128]{1,0:T(8,128)(2,1)}, bf16[648,128]{1,0:T(8,128)(2,1)S(1)}, u32[]{:S(2)}, u32[]{:S(2)}) collective-permute-start(bf16[648,128]{1,0:T(8,128)(2,1)} %get-tuple-element.32.t2), channel_id=1, source_target_pairs={{4,508},{5,509},{6,510},{7,511},{12,4},{13,5},{14,6},{15,7},{20,12... | collective-permute-start | bytes 497672 | tf_op jit(solution)/shard_map/ppermute | solution.py:384
  146.0 1.9 collective-permute-start.9
  147.9 2.7 %collective-permute-start.8 = (bf16[432,128]{1,0:T(8,128)(2,1)}, bf16[432,128]{1,0:T(8,128)(2,1)S(1)}, u32[]{:S(2)}, u32[]{:S(2)}) collective-permute-start(bf16[432,128]{1,0:T(8,128)(2,1)} %get-tuple-element.31), channel_id=1, source_target_pairs={{4,20},{5,21},{6,22},{7,23},{12,28},{13,29},{14,30},{15,31},{20,36... | collective-permute-start | bytes 331784 | tf_op jit(solution)/shard_map/ppermute | solution.py:384
  150.6 11.1 %collective-permute-start.11 = (bf16[432,128]{1,0:T(8,128)(2,1)}, bf16[432,128]{1,0:T(8,128)(2,1)S(1)}, u32[]{:S(2)}, u32[]{:S(2)}) collective-permute-start(bf16[432,128]{1,0:T(8,128)(2,1)} %get-tuple-element.33), channel_id=1, source_target_pairs={{4,500},{5,501},{6,502},{7,503},{12,508},{13,509},{14,510},{15,511... | collective-permute-start | bytes 331784 | tf_op jit(solution)/shard_map/ppermute | solution.py:384
  161.7 2.0 collective-permute-done.8.t0
  163.6 0.1 collective-permute-done.11.t4
  163.7 0.0 collective-permute-done.10.t3
  163.7 0.0 collective-permute-done.9.t1
  163.7 0.5 copy-done.14
  164.3 0.1 copy-done.15
  164.4 0.0 copy-done.8
  164.4 0.1 copy-done.9
  164.5 46.8 %rest_kernel.1 = (bf16[648,128]{1,0:T(8,128)(2,1)}, bf16[648,128]{1,0:T(8,128)(2,1)}, bf16[648,128]{1,0:T(8,128)(2,1)}, bf16[648,128]{1,0:T(8,128)(2,1)}) custom-call(s32[2]{0:T(128)} %pad_add_fusion.micro_ref.place_ref, bf16[432,128]{1,0:T(8,128)(2,1)} %copy-done.14, bf16[648,128]{1,0:T(8,128)(2,1)} %copy-done.9, bf16[648,128]{1,0:T(8,128)(2,1)} %get-tuple-element.32.t2, ...), custom_call_target="tpu_custom_call" | custom-call | tf_op jit(solution)/shard_map/rest_kernel/pallas_call | solution.py:311
  211.3 4.6 %collective-permute-start.12 = (bf16[648,128]{1,0:T(8,128)(2,1)}, bf16[648,128]{1,0:T(8,128)(2,1)S(1)}, u32[]{:S(2)}, u32[]{:S(2)}) collective-permute-start(bf16[648,128]{1,0:T(8,128)(2,1)} %get-tuple-element.36), channel_id=1, source_target_pairs={{0,1},{1,0},{2,3},{3,2},{4,5},{5,4},{6,7},{7,6},{8,9},{9,8},{10,11... | collective-permute-start | bytes 497672 | tf_op jit(solution)/shard_map/ppermute | solution.py:376
  215.9 5.6 %collective-permute-start.13 = (bf16[648,128]{1,0:T(8,128)(2,1)}, bf16[648,128]{1,0:T(8,128)(2,1)S(1)}, u32[]{:S(2)}, u32[]{:S(2)}) collective-permute-start(bf16[648,128]{1,0:T(8,128)(2,1)} %get-tuple-element.37), channel_id=1, source_target_pairs={{0,2},{1,3},{2,0},{3,1},{4,6},{5,7},{6,4},{7,5},{8,10},{9,11},{10,... | collective-permute-start | bytes 497672 | tf_op jit(solution)/shard_map/ppermute | solution.py:376
  221.6 1.9 collective-permute-start.14
  223.5 0.0 copy-start.11
  223.5 2.9 %collective-permute-done.13.o2 = bf16[648,128]{1,0:T(8,128)(2,1)S(1)} collective-permute-done((bf16[648,128]{1,0:T(8,128)(2,1)}, bf16[648,128]{1,0:T(8,128)(2,1)S(1)}, u32[]{:S(2)}, u32[]{:S(2)}) %collective-permute-start.13) | collective-permute-done | bytes 165920 | tf_op jit(solution)/shard_map/ppermute | solution.py:376
  226.4 3.5 %collective-permute-done.14.o3 = bf16[648,128]{1,0:T(8,128)(2,1)S(1)} collective-permute-done((bf16[648,128]{1,0:T(8,128)(2,1)}, bf16[648,128]{1,0:T(8,128)(2,1)S(1)}, u32[]{:S(2)}, u32[]{:S(2)}) %collective-permute-start.14) | collective-permute-done | bytes 165920 | tf_op jit(solution)/shard_map/ppermute | solution.py:376
  229.8 0.7 copy-done.13
  230.5 3.2 %finish.1 = bf16[1,4,2,18,2304]{4,3,2,1,0:T(8,128)(2,1)} custom-call(s32[2]{0:T(128)} %pad_add_fusion.micro_ref.place_ref, bf16[648,128]{1,0:T(8,128)(2,1)} %get-tuple-element.35.o0, bf16[648,128]{1,0:T(8,128)(2,1)} %copy-done.11, bf16[648,128]{1,0:T(8,128)(2,1)} %copy-done.12, bf16[648,128]{1,0:T(8,128)(2,1)} %copy-done.13), custom_call_target="tpu_custom_call" | custom-call | tf_op jit(solution)/shard_map/finish/pallas_call | solution.py:356
  233.7 2.5 %copy.11 = bf16[1,4,2,18,2304]{4,2,3,1,0:T(2,128)(2,1)} copy(bf16[1,4,2,18,2304]{4,3,2,1,0:T(8,128)(2,1)} %finish.1) | data formatting | bytes 1327104 | tf_op jit(solution)/shard_map/finish/pallas_call | solution.py:356
  (26 shorter events, 0.1 us)
Async XLA Ops:
  0.0 0.7 copy-start.16
  7.7 23.6 %collective-permute-start = (bf16[192,2304]{1,0:T(8,128)(2,1)}, bf16[192,2304]{1,0:T(8,128)(2,1)S(1)}, u32[]{:S(2)}, u32[]{:S(2)}) collective-permute-start(bf16[192,2304]{1,0:T(8,128)(2,1)} %get-tuple-element.22.w0), channel_id=1, source_target_pairs={{0,2},{1,3},{2,0},{3,1},{4,6},{5,7},{6,4},{7,5},{8,10},{9,11},{10,... | collective-permute-start | bytes 2654216 | tf_op jit(solution)/shard_map/ppermute | solution.py:376
  11.7 2.7 %collective-permute-start.4 = (bf16[648,128]{1,0:T(8,128)(2,1)}, bf16[648,128]{1,0:T(8,128)(2,1)S(1)}, u32[]{:S(2)}, u32[]{:S(2)}) collective-permute-start(bf16[648,128]{1,0:T(8,128)(2,1)} %get-tuple-element.26.t2), channel_id=1, source_target_pairs={{0,496},{1,497},{2,498},{3,499},{8,504},{9,505},{10,506},{11,507},... | collective-permute-start | bytes 497672 | tf_op jit(solution)/shard_map/ppermute | solution.py:384
  12.4 4.9 %collective-permute-start.3 = (bf16[648,128]{1,0:T(8,128)(2,1)}, bf16[648,128]{1,0:T(8,128)(2,1)S(1)}, u32[]{:S(2)}, u32[]{:S(2)}) collective-permute-start(bf16[648,128]{1,0:T(8,128)(2,1)} %get-tuple-element.26.t2), channel_id=1, source_target_pairs={{0,504},{1,505},{2,506},{3,507},{8,0},{9,1},{10,2},{11,3},{16,8},{... | collective-permute-start | bytes 497672 | tf_op jit(solution)/shard_map/ppermute | solution.py:384
  13.0 4.3 %collective-permute-start.2 = (bf16[648,128]{1,0:T(8,128)(2,1)}, bf16[648,128]{1,0:T(8,128)(2,1)S(1)}, u32[]{:S(2)}, u32[]{:S(2)}) collective-permute-start(bf16[648,128]{1,0:T(8,128)(2,1)} %get-tuple-element.26.t2), channel_id=1, source_target_pairs={{0,8},{1,9},{2,10},{3,11},{8,16},{9,17},{10,18},{11,19},{16,24},{1... | collective-permute-start | bytes 497672 | tf_op jit(solution)/shard_map/ppermute | solution.py:384
  13.7 3.6 %collective-permute-start.1 = (bf16[648,128]{1,0:T(8,128)(2,1)}, bf16[648,128]{1,0:T(8,128)(2,1)S(1)}, u32[]{:S(2)}, u32[]{:S(2)}) collective-permute-start(bf16[648,128]{1,0:T(8,128)(2,1)} %get-tuple-element.26.t2), channel_id=1, source_target_pairs={{0,16},{1,17},{2,18},{3,19},{8,24},{9,25},{10,26},{11,27},{16,32},... | collective-permute-start | bytes 497672 | tf_op jit(solution)/shard_map/ppermute | solution.py:384
  14.4 22.0 %copy-start.4 = (bf16[648,128]{1,0:T(8,128)(2,1)}, bf16[648,128]{1,0:T(8,128)(2,1)S(1)}, u32[]{:S(2)}) copy-start(bf16[648,128]{1,0:T(8,128)(2,1)S(1)} %collective-permute-done.4.t4) | copy-start | bytes 497668
  14.4 20.0 %collective-permute-start.5 = (bf16[192,2304]{1,0:T(8,128)(2,1)}, bf16[192,2304]{1,0:T(8,128)(2,1)S(1)}, u32[]{:S(2)}, u32[]{:S(2)}) collective-permute-start(bf16[192,2304]{1,0:T(8,128)(2,1)} %get-tuple-element.22.w0), channel_id=1, source_target_pairs={{0,1},{1,0},{2,3},{3,2},{4,5},{5,4},{6,7},{7,6},{8,9},{9,8},{10,11... | collective-permute-start | bytes 2654216 | tf_op jit(solution)/shard_map/ppermute | solution.py:376
  17.3 19.1 %copy-start.5 = (bf16[648,128]{1,0:T(8,128)(2,1)}, bf16[648,128]{1,0:T(8,128)(2,1)S(1)}, u32[]{:S(2)}) copy-start(bf16[648,128]{1,0:T(8,128)(2,1)S(1)} %collective-permute-done.3.t3) | copy-start | bytes 497668
  17.3 19.1 %copy-start.6 = (bf16[648,128]{1,0:T(8,128)(2,1)}, bf16[648,128]{1,0:T(8,128)(2,1)S(1)}, u32[]{:S(2)}) copy-start(bf16[648,128]{1,0:T(8,128)(2,1)S(1)} %collective-permute-done.2.t1) | copy-start | bytes 497668
  17.3 19.1 %copy-start.7 = (bf16[648,128]{1,0:T(8,128)(2,1)}, bf16[648,128]{1,0:T(8,128)(2,1)S(1)}, u32[]{:S(2)}) copy-start(bf16[648,128]{1,0:T(8,128)(2,1)S(1)} %collective-permute-done.1.t0) | copy-start | bytes 497668
  31.2 5.2 %copy-start.1 = (bf16[192,2304]{1,0:T(8,128)(2,1)}, bf16[192,2304]{1,0:T(8,128)(2,1)S(1)}, u32[]{:S(2)}) copy-start(bf16[192,2304]{1,0:T(8,128)(2,1)S(1)} %collective-permute-done.w2) | copy-start | bytes 2654212
  31.3 5.2 %collective-permute-start.6 = (bf16[192,2304]{1,0:T(8,128)(2,1)S(1)}, bf16[192,2304]{1,0:T(8,128)(2,1)S(1)}, u32[]{:S(2)}, u32[]{:S(2)}) collective-permute-start(bf16[192,2304]{1,0:T(8,128)(2,1)S(1)} %collective-permute-done.w2), channel_id=1, source_target_pairs={{0,1},{1,0},{2,3},{3,2},{4,5},{5,4},{6,7},{7,6},{8,9},{9,8},{10,11... | collective-permute-start | bytes 2654216 | tf_op jit(solution)/shard_map/ppermute | solution.py:376
  34.4 78.2 %copy-start = (bf16[192,2304]{1,0:T(8,128)(2,1)S(1)}, bf16[192,2304]{1,0:T(8,128)(2,1)}, u32[]{:S(2)}) copy-start(bf16[192,2304]{1,0:T(8,128)(2,1)} %get-tuple-element.22.w0) | copy-start | bytes 2654212
  34.4 2.0 copy-start.2
  36.4 0.9 copy-start.3
  111.1 22.2 %collective-permute-start.7 = (bf16[648,128]{1,0:T(8,128)(2,1)}, bf16[648,128]{1,0:T(8,128)(2,1)S(1)}, u32[]{:S(2)}, u32[]{:S(2)}) collective-permute-start(bf16[648,128]{1,0:T(8,128)(2,1)} %get-tuple-element.30), channel_id=1, source_target_pairs={{0,4},{1,5},{2,6},{3,7},{8,12},{9,13},{10,14},{11,15},{16,20},{17,... | collective-permute-start | bytes 497672 | tf_op jit(solution)/shard_map/ppermute | solution.py:384
  133.3 0.7 copy-start.10
  142.7 21.1 %collective-permute-start.10 = (bf16[648,128]{1,0:T(8,128)(2,1)}, bf16[648,128]{1,0:T(8,128)(2,1)S(1)}, u32[]{:S(2)}, u32[]{:S(2)}) collective-permute-start(bf16[648,128]{1,0:T(8,128)(2,1)} %get-tuple-element.32.t2), channel_id=1, source_target_pairs={{4,508},{5,509},{6,510},{7,511},{12,4},{13,5},{14,6},{15,7},{20,12... | collective-permute-start | bytes 497672 | tf_op jit(solution)/shard_map/ppermute | solution.py:384
  146.0 17.7 %collective-permute-start.9 = (bf16[648,128]{1,0:T(8,128)(2,1)}, bf16[648,128]{1,0:T(8,128)(2,1)S(1)}, u32[]{:S(2)}, u32[]{:S(2)}) collective-permute-start(bf16[648,128]{1,0:T(8,128)(2,1)} %get-tuple-element.32.t2), channel_id=1, source_target_pairs={{4,12},{5,13},{6,14},{7,15},{12,20},{13,21},{14,22},{15,23},{20,28... | collective-permute-start | bytes 497672 | tf_op jit(solution)/shard_map/ppermute | solution.py:384
  147.9 15.7 %collective-permute-start.8 = (bf16[432,128]{1,0:T(8,128)(2,1)}, bf16[432,128]{1,0:T(8,128)(2,1)S(1)}, u32[]{:S(2)}, u32[]{:S(2)}) collective-permute-start(bf16[432,128]{1,0:T(8,128)(2,1)} %get-tuple-element.31), channel_id=1, source_target_pairs={{4,20},{5,21},{6,22},{7,23},{12,28},{13,29},{14,30},{15,31},{20,36... | collective-permute-start | bytes 331784 | tf_op jit(solution)/shard_map/ppermute | solution.py:384
  150.6 13.1 %collective-permute-start.11 = (bf16[432,128]{1,0:T(8,128)(2,1)}, bf16[432,128]{1,0:T(8,128)(2,1)S(1)}, u32[]{:S(2)}, u32[]{:S(2)}) collective-permute-start(bf16[432,128]{1,0:T(8,128)(2,1)} %get-tuple-element.33), channel_id=1, source_target_pairs={{4,500},{5,501},{6,502},{7,503},{12,508},{13,509},{14,510},{15,511... | collective-permute-start | bytes 331784 | tf_op jit(solution)/shard_map/ppermute | solution.py:384
  163.6 0.6 copy-start.14
  163.7 0.7 copy-start.15
  163.7 0.7 copy-start.8
  163.7 0.8 copy-start.9
  211.3 12.2 %collective-permute-start.12 = (bf16[648,128]{1,0:T(8,128)(2,1)}, bf16[648,128]{1,0:T(8,128)(2,1)S(1)}, u32[]{:S(2)}, u32[]{:S(2)}) collective-permute-start(bf16[648,128]{1,0:T(8,128)(2,1)} %get-tuple-element.36), channel_id=1, source_target_pairs={{0,1},{1,0},{2,3},{3,2},{4,5},{5,4},{6,7},{7,6},{8,9},{9,8},{10,11... | collective-permute-start | bytes 497672 | tf_op jit(solution)/shard_map/ppermute | solution.py:376
  215.9 10.4 %collective-permute-start.13 = (bf16[648,128]{1,0:T(8,128)(2,1)}, bf16[648,128]{1,0:T(8,128)(2,1)S(1)}, u32[]{:S(2)}, u32[]{:S(2)}) collective-permute-start(bf16[648,128]{1,0:T(8,128)(2,1)} %get-tuple-element.37), channel_id=1, source_target_pairs={{0,2},{1,3},{2,0},{3,1},{4,6},{5,7},{6,4},{7,5},{8,10},{9,11},{10,... | collective-permute-start | bytes 497672 | tf_op jit(solution)/shard_map/ppermute | solution.py:376
  221.6 8.3 %collective-permute-start.14 = (bf16[648,128]{1,0:T(8,128)(2,1)}, bf16[648,128]{1,0:T(8,128)(2,1)S(1)}, u32[]{:S(2)}, u32[]{:S(2)}) collective-permute-start(bf16[648,128]{1,0:T(8,128)(2,1)} %get-tuple-element.38), channel_id=1, source_target_pairs={{0,3},{1,2},{2,1},{3,0},{4,7},{5,6},{6,5},{7,4},{8,11},{9,10},{10,... | collective-permute-start | bytes 497672 | tf_op jit(solution)/shard_map/ppermute | solution.py:376
  223.5 6.3 %copy-start.11 = (bf16[648,128]{1,0:T(8,128)(2,1)}, bf16[648,128]{1,0:T(8,128)(2,1)S(1)}, u32[]{:S(2)}) copy-start(bf16[648,128]{1,0:T(8,128)(2,1)S(1)} %collective-permute-done.12.o1) | copy-start | bytes 497668
  226.4 3.5 %copy-start.12 = (bf16[648,128]{1,0:T(8,128)(2,1)}, bf16[648,128]{1,0:T(8,128)(2,1)S(1)}, u32[]{:S(2)}) copy-start(bf16[648,128]{1,0:T(8,128)(2,1)S(1)} %collective-permute-done.13.o2) | copy-start | bytes 497668
  229.8 0.7 copy-start.13

commit v5 on v4

--- a/solution.py
+++ b/solution.py
@@ -55,8 +55,7 @@
     return jnp.concatenate([packed[end - tokens :], packed[end - 2 * tokens : end - tokens, LANES // 2 :]], 1)
 
 
-def prepare_kernel(micro_ref, fields_ref, mask_ref, vector_ref, wqkv_ref, wproj_ref, wup_ref, wdown_ref,
-                   tile_ref, pack_ref, grid_ref):
+def embed_kernel(micro_ref, fields_ref, mask_ref, vector_ref, tile_ref, grid_ref):
     _, levels, rows, _ = fields_ref.shape
     width = vector_ref.shape[1]
     mask = mask_ref[...].astype(jnp.float32)
@@ -75,6 +74,30 @@
     tile_ref[2 * tokens :] = grid_ref[2].astype(jnp.bfloat16)
     lane = lax.broadcasted_iota(jnp.int32, (1, LANES), 1)
     tile_ref[tokens : 2 * tokens] = jnp.where(lane < side, grid_ref[1], grid_ref[3]).astype(jnp.bfloat16)
+
+
+def embed(micro, fields, land_mask, land_vector):
+    _, levels, rows, flat = fields.shape
+    tokens = rows * levels * HALF
+    whole = lambda a: pl.BlockSpec(a.shape, lambda i, m: (0,) * a.ndim)
+    return pl.pallas_call(
+        embed_kernel,
+        out_shape=jax.ShapeDtypeStruct((3 * tokens, LANES), jnp.bfloat16),
+        grid_spec=pltpu.PrefetchScalarGridSpec(
+            num_scalar_prefetch=1,
+            grid=(1,),
+            in_specs=[pl.BlockSpec((1, levels, rows, flat), lambda i, m: (m[0], 0, 0, 0)),
+                      whole(land_mask), whole(land_vector)],
+            out_specs=pl.BlockSpec((3 * tokens, LANES), lambda i, m: (0, 0)),
+            scratch_shapes=[pltpu.VMEM((4, tokens, LANES), jnp.float32)],
+        ),
+        compiler_params=pltpu.CompilerParams(vmem_limit_bytes=VMEM_LIMIT),
+        name="embed",
+    )(micro, fields, land_mask, land_vector)
+
+
+def pack_kernel(wqkv_ref, wproj_ref, wup_ref, wdown_ref, pack_ref):
+    width = wproj_ref.shape[1]
     side = 256 - width
     for i in range(3):
         pack_ref[:, 256 * i : 256 * i + 256] = jnp.concatenate(
@@ -85,31 +108,17 @@
     pack_ref[:, 768 + hidden :] = wdown_ref[0]
 
 
-def prepare(micro, fields, land_mask, land_vector, weights):
-    _, levels, rows, flat = fields.shape
-    width = land_vector.shape[1]
-    tokens = rows * levels * HALF
-    whole = lambda a: pl.BlockSpec(a.shape, lambda i, m: (0,) * a.ndim)
+def pack_weights(*weights):
+    vmem = pl.BlockSpec(memory_space=pltpu.VMEM)
+    width = weights[0].shape[1]
     return pl.pallas_call(
-        prepare_kernel,
-        out_shape=(
-            jax.ShapeDtypeStruct((3 * tokens, LANES), jnp.bfloat16),
-            jax.ShapeDtypeStruct((width, 2304), jnp.bfloat16),
-        ),
-        grid_spec=pltpu.PrefetchScalarGridSpec(
-            num_scalar_prefetch=1,
-            grid=(1,),
-            in_specs=[pl.BlockSpec((1, levels, rows, flat), lambda i, m: (m[0], 0, 0, 0))]
-            + [whole(a) for a in (land_mask, land_vector, *weights)],
-            out_specs=(
-                pl.BlockSpec((3 * tokens, LANES), lambda i, m: (0, 0)),
-                pl.BlockSpec((width, 2304), lambda i, m: (0, 0)),
-            ),
-            scratch_shapes=[pltpu.VMEM((4, tokens, LANES), jnp.float32)],
-        ),
+        pack_kernel,
+        out_shape=jax.ShapeDtypeStruct((width, 2304), jnp.bfloat16),
+        in_specs=[vmem] * len(weights),
+        out_specs=vmem,
         compiler_params=pltpu.CompilerParams(vmem_limit_bytes=VMEM_LIMIT),
-        name="prepare",
-    )(micro, fields, land_mask, land_vector, *weights)
+        name="pack_weights",
+    )(*weights)
 
 
 def compute_stage(mode, tile_refs, bias_ref, w_ref, wproj_ref, store, scratch):
@@ -223,17 +232,17 @@
         load_tiles()
 
         def two_blocks(n, carry):
-            block(2 * n, False, exact, together)
+            @pl.when(n > 0)
+            def _():
+                block(2 * n, False, exact, together)
+
             block(2 * n + 1, True, exact, together)
             return carry
 
-        if mode == "whole":
-            lax.fori_loop(0, STAGE // 2, two_blocks, 0)
-        elif mode == "first":
+        if mode == "first":
             block(0, False, exact, together, True)
         else:
-            for b in range(1, STAGE):
-                block(b, b % 2 == 1, exact, together)
+            lax.fori_loop(0, STAGE // 2, two_blocks, 0)
 
     low_ref[...] = jnp.ones_like(low_ref)
     high_ref[...] = jnp.ones_like(high_ref)
@@ -255,21 +264,14 @@
         wproj_ref[place ^ i] = unpack_projection(ref, wproj_ref.shape[1])
 
 
-def whole_kernel(place_ref, t0, t1, t2, t3, t4, w0, w1, w2, w3, bias_ref, last_ref, outs_ref,
+def first_kernel(place_ref, tile_in, w0, w1, w2, w3, bias_ref, tile_ref, west_ref, east_ref,
                  w_ref, wproj_ref, *scratch):
-    place = place_ref[0]
-    gather_weights(place, (w0, w1, w2, w3), w_ref, wproj_ref)
-
-    def store(b, packed):
-        outs_ref[place ^ b] = packed
-
-    compute_stage("whole", (t0, t1, t2, t3, t4), bias_ref, w_ref, wproj_ref, store, scratch)
-    last_ref[...] = outs_ref[place ^ (STAGE - 1)]
-
-
-def first_kernel(tile_in, w_in, bias_ref, tile_ref, west_ref, east_ref, w_ref, wproj_ref, *scratch):
-    w_ref[0] = w_in[...]
-    wproj_ref[0] = unpack_projection(w_in, wproj_ref.shape[1])
+    for i, ref in enumerate((w0, w1, w2, w3)):
+
+        @pl.when(place_ref[0] == i)
+        def _(ref=ref):
+            w_ref[0] = ref[...]
+            wproj_ref[0] = unpack_projection(ref, wproj_ref.shape[1])
 
     def store(b, packed):
         tile_ref[...] = packed
@@ -279,20 +281,32 @@
     east_ref[...] = tile_ref[tile_ref.shape[0] - east_ref.shape[0] :]
 
 
-def rest_kernel(place_ref, t0, t1, t2, t3, t4, w0, w1, w2, w3, bias_ref, early_ref, o0, o1, o2, o3,
+def compute_rest(place, tiles, weights, bias_ref, outs_ref, w_ref, wproj_ref, scratch):
+    gather_weights(place, weights, w_ref, wproj_ref)
+
+    def store(b, packed):
+        outs_ref[place ^ b] = packed
+
+    store(0, tiles[REACH][...])
+    compute_stage("rest", tiles, bias_ref, w_ref, wproj_ref, store, scratch)
+
+
+def early_kernel(place_ref, t0, t1, t2, t3, t4, w0, w1, w2, w3, bias_ref, last_ref, outs_ref,
+                 w_ref, wproj_ref, *scratch):
+    place = place_ref[0]
+    compute_rest(place, (t0, t1, t2, t3, t4), (w0, w1, w2, w3), bias_ref, outs_ref, w_ref, wproj_ref, scratch)
+    last_ref[...] = outs_ref[place ^ (STAGE - 1)]
+
+
+def late_kernel(place_ref, t0, t1, t2, t3, t4, w0, w1, w2, w3, bias_ref, early_ref, o0, o1, o2, o3,
                 outs_ref, w_ref, wproj_ref, *scratch):
-    place = place_ref[0]
     late = place_ref[1] == 1
 
     @pl.when(late)
     def _():
-        gather_weights(place, (w0, w1, w2, w3), w_ref, wproj_ref)
-
-        def store(b, packed):
-            outs_ref[place ^ b] = packed
-
-        store(0, t2[...])
-        compute_stage("rest", (t0, t1, t2, t3, t4), bias_ref, w_ref, wproj_ref, store, scratch)
+        compute_rest(
+            place_ref[0], (t0, t1, t2, t3, t4), (w0, w1, w2, w3), bias_ref, outs_ref, w_ref, wproj_ref, scratch
+        )
         for i, ref in enumerate((o0, o1, o2, o3)):
             ref[...] = outs_ref[i]
 
@@ -307,11 +321,10 @@
     windows, piece, _ = bias_shape
     vmem = pl.BlockSpec(memory_space=pltpu.VMEM)
     bf16, f32 = jnp.bfloat16, jnp.float32
-    places = [] if place is None else [place]
     return pl.pallas_call(
         kernel,
         out_shape=tuple(jax.ShapeDtypeStruct(shape, bf16) for shape in outs),
-        in_specs=[pl.BlockSpec(memory_space=pltpu.SMEM)] * len(places) + [vmem] * len(operands),
+        in_specs=[pl.BlockSpec(memory_space=pltpu.SMEM)] + [vmem] * len(operands),
         out_specs=(vmem,) * len(outs),
         scratch_shapes=[pltpu.VMEM(shape, bf16) for shape in extra]
         + [
@@ -327,7 +340,7 @@
         ],
         compiler_params=pltpu.CompilerParams(vmem_limit_bytes=VMEM_LIMIT),
         name=kernel.__name__,
-    )(*places, *operands)
+    )(place, *operands)
 
 
 def finish_kernel(place_ref, o0, o1, o2, o3, out_ref, grid_ref):
@@ -388,23 +401,25 @@
     bias = jnp.asarray(window_bias(levels, rows))
     sizes = (tokens, width, bias.shape)
 
-    tile, pack = prepare(
-        place, fields, land_mask, land_vector.reshape(1, width), (w_qkv, w_proj, w_up, w_down.transpose(0, 2, 1))
+    pack = pack_weights(w_qkv, w_proj, w_up, w_down.transpose(0, 2, 1))
+    near, far = exchange(pack, 1), exchange(pack, 2)
+    weights = (pack, near, far, exchange(far, 1))
+    stack_shape = (STAGE,) + tile_shape
+
+    def even_then_halo(tile, first_section):
+        own, west, east = run_stage(
+            first_kernel, place, (tile, *weights, bias), (tile_shape, half_shape, half_shape), (), 1, *sizes
+        )
+        move = functools.partial(shift, first=first_section)
+        return move(east, 2), move(own, 1), own, move(own, -1), move(west, -2)
+
+    tiles = even_then_halo(embed(place, fields, land_mask, land_vector.reshape(1, width)), 0)
+    last, early = run_stage(
+        early_kernel, place, (*tiles, *weights, bias), (tile_shape, stack_shape), (), STAGE, *sizes
     )
-    tiles = [tile if d == 0 else shift(tile, -d, 0) for d in range(-REACH, REACH + 1)]
-    near, far = exchange(pack, 1), exchange(pack, 2)
-    far, tiles = lax.optimization_barrier((far, tiles))
-    weights = [pack, near, far, exchange(far, 1)]
-
-    last, early = run_stage(
-        whole_kernel, place, (*tiles, *weights, bias), (tile_shape, (STAGE,) + tile_shape), (), STAGE, *sizes
-    )
-    own = shift(last, 0, 0, 1)
-    first = lax.select_n(place[0], *weights)
-    own, west, east = run_stage(first_kernel, None, (own, first, bias), (tile_shape, half_shape, half_shape), (), 1, *sizes)
-    tiles = [shift(east, 2, STAGE), shift(own, 1, STAGE), own, shift(own, -1, STAGE), shift(west, -2, STAGE)]
+    tiles = even_then_halo(shift(last, 0, 0, 1), STAGE)
     outs = run_stage(
-        rest_kernel, place, (*tiles, *weights, bias, early), (tile_shape,) * STAGE, ((STAGE,) + tile_shape,), STAGE, *sizes
+        late_kernel, place, (*tiles, *weights, bias, early), (tile_shape,) * STAGE, (stack_shape,), STAGE, *sizes
     )
 
     pieces = [outs[0]] + [exchange(outs[i], i) for i in range(1, STAGE)]

time: 237 us -> 246 us (1.038)
  Pallas kernels: 136 us -> 121 us
  waiting for transfers between devices: 42.5 us -> 57 us
  starting transfers between devices: 45.3 us -> 55.5 us
  other arithmetic: 3.18 us -> 0.59 us
    pallas_call x3 -> x4, Pallas kernels: 129 us -> 113 us  [run_stage(): pl.pallas_call(kernel, out_shape=tuple((jax.ShapeDtypeStruct(shape, bf16)...]
    ppermute x9, waiting for transfers between devices: 20.3 us -> 34 us  [shift(): return lax.ppermute(value, axes, pairs)]
    ppermute x9, starting transfers between devices: 23.1 us -> 31.6 us  [shift(): return lax.ppermute(value, axes, pairs)]
    select_n x1 -> x0, other arithmetic: 2.52 us -> none  [on_device(): first = lax.select_n(place[0], *weights)]
    pallas_call x1 -> x2, Pallas kernels: 3.54 us -> 5.07 us  [the longest x1 2.75 us: embed(): pl.pallas_call(embed_kernel, out_shape=jax.ShapeDtypeStruct((3 * tokens,...]
  transfers between devices with their start and end apart: 15 -> 15, of which waited for: 7 -> 6; matrix products, arithmetic and copies ran while one was open for 1% -> 1% of each run, Pallas kernels for 0% -> 1%
where the time goes in v5:
time: 246 us; the launch traced here: 245 us
  Pallas kernels  121 us (49%)
  waiting for transfers between devices  57 us (23%)
  starting transfers between devices  55.5 us (23%)
  local copies, waits for them, and re-layouts  10.2 us (4%)
    pallas_call x4, Pallas kernels, run_stage(): pl.pallas_call(kernel, out_shape=tuple((jax.ShapeDtypeStruct(shape, bf16)...  113 us
    ppermute x9, waiting for transfers between devices, shift(): return lax.ppermute(value, axes, pairs)  34 us
    ppermute x9, starting transfers between devices, shift(): return lax.ppermute(value, axes, pairs)  31.6 us
    ppermute x6, starting transfers between devices, exchange(): lax.ppermute(value, 'section', [(s, s ^ bit) for s in range(section_count)])  23.9 us
    ppermute x6, waiting for transfers between devices, exchange(): lax.ppermute(value, 'section', [(s, s ^ bit) for s in range(section_count)])  23 us
    unnamed x36, local copies, waits for them, and re-layouts  7.63 us
  transfers between devices with their start and end apart: 15, of which 6 were waited for; matrix products, arithmetic and copies ran while one was open for 1% of the time, Pallas kernels for 1%

profile of v5, /device:TPU:129, one launch (start us, length us, event | category | flops | bytes accessed | tf_op | source)
XLA Modules:
  0.0 245.1 jit_solution(17308665071691318980)
XLA Ops:
  0.0 2.3 pack_weights.1.w0
  2.3 4.0 %collective-permute-start.1 = (bf16[192,2304]{1,0:T(8,128)(2,1)}, bf16[192,2304]{1,0:T(8,128)(2,1)S(1)}, u32[]{:S(2)}, u32[]{:S(2)}) collective-permute-start(bf16[192,2304]{1,0:T(8,128)(2,1)} %pack_weights.1.w0), channel_id=1, source_target_pairs={{0,2},{1,3},{2,0},{3,1},{4,6},{5,7},{6,4},{7,5},{8,10},{9,11},{10,... | collective-permute-start | bytes 2654216 | tf_op jit(solution)/shard_map/ppermute | solution.py:389
  6.3 2.9 %collective-permute-start = (bf16[192,2304]{1,0:T(8,128)(2,1)}, bf16[192,2304]{1,0:T(8,128)(2,1)S(1)}, u32[]{:S(2)}, u32[]{:S(2)}) collective-permute-start(bf16[192,2304]{1,0:T(8,128)(2,1)} %pack_weights.1.w0), channel_id=1, source_target_pairs={{0,1},{1,0},{2,3},{3,2},{4,5},{5,4},{6,7},{7,6},{8,9},{9,8},{10,11... | collective-permute-start | bytes 2654216 | tf_op jit(solution)/shard_map/ppermute | solution.py:389
  9.2 16.7 %collective-permute-done.1.w2 = bf16[192,2304]{1,0:T(8,128)(2,1)S(1)} collective-permute-done((bf16[192,2304]{1,0:T(8,128)(2,1)}, bf16[192,2304]{1,0:T(8,128)(2,1)S(1)}, u32[]{:S(2)}, u32[]{:S(2)}) %collective-permute-start.1) | collective-permute-done | bytes 884768 | tf_op jit(solution)/shard_map/ppermute | solution.py:389
  25.9 3.1 %collective-permute-start.2 = (bf16[192,2304]{1,0:T(8,128)(2,1)S(1)}, bf16[192,2304]{1,0:T(8,128)(2,1)S(1)}, u32[]{:S(2)}, u32[]{:S(2)}) collective-permute-start(bf16[192,2304]{1,0:T(8,128)(2,1)S(1)} %collective-permute-done.1.w2), channel_id=1, source_target_pairs={{0,1},{1,0},{2,3},{3,2},{4,5},{5,4},{6,7},{7,6},{8,9},{9,8},{10,11... | collective-permute-start | bytes 2654216 | tf_op jit(solution)/shard_map/ppermute | solution.py:389
  29.0 0.0 copy-start.16
  29.1 0.7 copy-done.16
  29.7 0.7 copy.10.mask_ref
  30.4 1.0 copy.9.fields_ref
  31.4 0.6 pad_add_fusion.micro_ref.place_ref
  32.0 2.8 %embed.1.tile_in = bf16[648,128]{1,0:T(8,128)(2,1)} custom-call(s32[2]{0:T(128)} %pad_add_fusion.micro_ref.place_ref, bf16[4,2,18,2304]{3,2,1,0:T(8,128)(2,1)} %copy.9.fields_ref, s32[18,12]{1,0:T(8,128)} %copy.10.mask_ref, f32[1,192]{1,0:T(1,128)} %bitcast.5), custom_call_target="tpu_custom_call" | custom-call | tf_op jit(solution)/shard_map/embed/pallas_call | solution.py:83
  34.8 0.0 collective-permute-done.w1
  34.8 0.9 copy-done.1
  35.7 0.9 copy-done.2
  36.6 9.6 %first_kernel.2 = (bf16[648,128]{1,0:T(8,128)(2,1)}, bf16[432,128]{1,0:T(8,128)(2,1)}, bf16[432,128]{1,0:T(8,128)(2,1)}) custom-call(s32[2]{0:T(128)} %pad_add_fusion.micro_ref.place_ref, bf16[648,128]{1,0:T(8,128)(2,1)} %embed.1.tile_in, bf16[192,2304]{1,0:T(8,128)(2,1)} %pack_weights.1.w0, bf16[192,2304]{1,0:T(8,128)(2,1)} %copy-done.1, ...), custom_call_target="tpu_custom_call" | custom-call | tf_op jit(solution)/shard_map/first_kernel/pallas_call | solution.py:324
  46.2 0.7 collective-permute-start.5
  46.9 0.7 collective-permute-start.4
  47.6 0.7 collective-permute-start.3
  48.2 0.7 collective-permute-start.6
  49.0 0.6 copy-done.12
  49.6 0.1 copy-done.13
  49.6 0.0 copy-done.4
  49.7 0.7 copy-done.5
  50.3 46.8 %early_kernel.1 = (bf16[648,128]{1,0:T(8,128)(2,1)}, bf16[4,648,128]{2,1,0:T(8,128)(2,1)}) custom-call(s32[2]{0:T(128)} %pad_add_fusion.micro_ref.place_ref, bf16[432,128]{1,0:T(8,128)(2,1)} %copy-done.12, bf16[648,128]{1,0:T(8,128)(2,1)} %copy-done.5, bf16[648,128]{1,0:T(8,128)(2,1)} %get-tuple-element.18.t2, bf16[648,128]{1,0:T(8,128)(2,1)} %copy-done.4, ...), custom_call_target="tpu_custom_call" | custom-call | tf_op jit(solution)/shard_map/early_kernel/pallas_call | solution.py:324
  97.2 1.3 collective-permute-start.7
  98.5 32.0 %collective-permute-done.7.tile_in = bf16[648,128]{1,0:T(8,128)(2,1)S(1)} collective-permute-done((bf16[648,128]{1,0:T(8,128)(2,1)}, bf16[648,128]{1,0:T(8,128)(2,1)S(1)}, u32[]{:S(2)}, u32[]{:S(2)}) %collective-permute-start.7) | collective-permute-done | bytes 165920 | tf_op jit(solution)/shard_map/ppermute | solution.py:397
  130.4 0.7 copy-done.8
  131.1 9.6 %first_kernel.3 = (bf16[648,128]{1,0:T(8,128)(2,1)}, bf16[432,128]{1,0:T(8,128)(2,1)}, bf16[432,128]{1,0:T(8,128)(2,1)}) custom-call(s32[2]{0:T(128)} %pad_add_fusion.micro_ref.place_ref, bf16[648,128]{1,0:T(8,128)(2,1)} %copy-done.8, bf16[192,2304]{1,0:T(8,128)(2,1)} %pack_weights.1.w0, bf16[192,2304]{1,0:T(8,128)(2,1)} %copy-done.1, ...), custom_call_target="tpu_custom_call" | custom-call | tf_op jit(solution)/shard_map/first_kernel/pallas_call | solution.py:324
  140.7 12.1 %collective-permute-start.10 = (bf16[648,128]{1,0:T(8,128)(2,1)}, bf16[648,128]{1,0:T(8,128)(2,1)S(1)}, u32[]{:S(2)}, u32[]{:S(2)}) collective-permute-start(bf16[648,128]{1,0:T(8,128)(2,1)} %get-tuple-element.22.t2), channel_id=1, source_target_pairs={{4,508},{5,509},{6,510},{7,511},{12,4},{13,5},{14,6},{15,7},{20,12... | collective-permute-start | bytes 497672 | tf_op jit(solution)/shard_map/ppermute | solution.py:397
  152.8 1.9 collective-permute-start.9
  154.7 1.9 collective-permute-start.8
  156.6 11.8 %collective-permute-start.11 = (bf16[432,128]{1,0:T(8,128)(2,1)}, bf16[432,128]{1,0:T(8,128)(2,1)S(1)}, u32[]{:S(2)}, u32[]{:S(2)}) collective-permute-start(bf16[432,128]{1,0:T(8,128)(2,1)} %get-tuple-element.23), channel_id=1, source_target_pairs={{4,500},{5,501},{6,502},{7,503},{12,508},{13,509},{14,510},{15,511... | collective-permute-start | bytes 331784 | tf_op jit(solution)/shard_map/ppermute | solution.py:397
  168.4 1.5 collective-permute-done.8.t0
  169.9 0.5 collective-permute-done.11.t4
  170.5 0.1 copy-done.14
  170.6 0.6 copy-done.15
  171.1 0.1 copy-done.6
  171.2 0.0 copy-done.7
  171.2 47.2 %late_kernel.1 = (bf16[648,128]{1,0:T(8,128)(2,1)}, bf16[648,128]{1,0:T(8,128)(2,1)}, bf16[648,128]{1,0:T(8,128)(2,1)}, bf16[648,128]{1,0:T(8,128)(2,1)}) custom-call(s32[2]{0:T(128)} %pad_add_fusion.micro_ref.place_ref, bf16[432,128]{1,0:T(8,128)(2,1)} %copy-done.14, bf16[648,128]{1,0:T(8,128)(2,1)} %copy-done.7, bf16[648,128]{1,0:T(8,128)(2,1)} %get-tuple-element.22.t2, ...), custom_call_target="tpu_custom_call" | custom-call | tf_op jit(solution)/shard_map/late_kernel/pallas_call | solution.py:324
  218.4 5.4 %collective-permute-start.12 = (bf16[648,128]{1,0:T(8,128)(2,1)}, bf16[648,128]{1,0:T(8,128)(2,1)S(1)}, u32[]{:S(2)}, u32[]{:S(2)}) collective-permute-start(bf16[648,128]{1,0:T(8,128)(2,1)} %get-tuple-element.26), channel_id=1, source_target_pairs={{0,1},{1,0},{2,3},{3,2},{4,5},{5,4},{6,7},{7,6},{8,9},{9,8},{10,11... | collective-permute-start | bytes 497672 | tf_op jit(solution)/shard_map/ppermute | solution.py:389
  223.9 6.6 %collective-permute-start.13 = (bf16[648,128]{1,0:T(8,128)(2,1)}, bf16[648,128]{1,0:T(8,128)(2,1)S(1)}, u32[]{:S(2)}, u32[]{:S(2)}) collective-permute-start(bf16[648,128]{1,0:T(8,128)(2,1)} %get-tuple-element.27), channel_id=1, source_target_pairs={{0,2},{1,3},{2,0},{3,1},{4,6},{5,7},{6,4},{7,5},{8,10},{9,11},{10,... | collective-permute-start | bytes 497672 | tf_op jit(solution)/shard_map/ppermute | solution.py:389
  230.4 1.9 collective-permute-start.14
  232.4 0.0 copy-start.9
  232.4 2.9 %collective-permute-done.13.o2 = bf16[648,128]{1,0:T(8,128)(2,1)S(1)} collective-permute-done((bf16[648,128]{1,0:T(8,128)(2,1)}, bf16[648,128]{1,0:T(8,128)(2,1)S(1)}, u32[]{:S(2)}, u32[]{:S(2)}) %collective-permute-start.13) | collective-permute-done | bytes 165920 | tf_op jit(solution)/shard_map/ppermute | solution.py:389
  235.2 3.5 %collective-permute-done.14.o3 = bf16[648,128]{1,0:T(8,128)(2,1)S(1)} collective-permute-done((bf16[648,128]{1,0:T(8,128)(2,1)}, bf16[648,128]{1,0:T(8,128)(2,1)S(1)}, u32[]{:S(2)}, u32[]{:S(2)}) %collective-permute-start.14) | collective-permute-done | bytes 165920 | tf_op jit(solution)/shard_map/ppermute | solution.py:389
  238.7 0.7 copy-done.11
  239.4 3.2 %finish.1 = bf16[1,4,2,18,2304]{4,3,2,1,0:T(8,128)(2,1)} custom-call(s32[2]{0:T(128)} %pad_add_fusion.micro_ref.place_ref, bf16[648,128]{1,0:T(8,128)(2,1)} %get-tuple-element.25.o0, bf16[648,128]{1,0:T(8,128)(2,1)} %copy-done.9, bf16[648,128]{1,0:T(8,128)(2,1)} %copy-done.10, bf16[648,128]{1,0:T(8,128)(2,1)} %copy-done.11), custom_call_target="tpu_custom_call" | custom-call | tf_op jit(solution)/shard_map/finish/pallas_call | solution.py:369
  242.5 2.5 %copy.11 = bf16[1,4,2,18,2304]{4,2,3,1,0:T(2,128)(2,1)} copy(bf16[1,4,2,18,2304]{4,3,2,1,0:T(8,128)(2,1)} %finish.1) | data formatting | bytes 1327104 | tf_op jit(solution)/shard_map/finish/pallas_call | solution.py:369
  (27 shorter events, 0.1 us)
Async XLA Ops:
  0.0 30.4 %copy-start.3 = (bf16[4,2,18,2304]{3,1,2,0:T(2,128)(2,1)S(1)}, bf16[4,2,18,2304]{3,1,2,0:T(2,128)(2,1)}, u32[]{:S(2)}) copy-start(bf16[4,2,18,2304]{3,1,2,0:T(2,128)(2,1)} %param.8) | copy-start | bytes 1990660
  2.3 23.6 %collective-permute-start.1 = (bf16[192,2304]{1,0:T(8,128)(2,1)}, bf16[192,2304]{1,0:T(8,128)(2,1)S(1)}, u32[]{:S(2)}, u32[]{:S(2)}) collective-permute-start(bf16[192,2304]{1,0:T(8,128)(2,1)} %pack_weights.1.w0), channel_id=1, source_target_pairs={{0,2},{1,3},{2,0},{3,1},{4,6},{5,7},{6,4},{7,5},{8,10},{9,11},{10,... | collective-permute-start | bytes 2654216 | tf_op jit(solution)/shard_map/ppermute | solution.py:389
  6.3 28.5 %collective-permute-start = (bf16[192,2304]{1,0:T(8,128)(2,1)}, bf16[192,2304]{1,0:T(8,128)(2,1)S(1)}, u32[]{:S(2)}, u32[]{:S(2)}) collective-permute-start(bf16[192,2304]{1,0:T(8,128)(2,1)} %pack_weights.1.w0), channel_id=1, source_target_pairs={{0,1},{1,0},{2,3},{3,2},{4,5},{5,4},{6,7},{7,6},{8,9},{9,8},{10,11... | collective-permute-start | bytes 2654216 | tf_op jit(solution)/shard_map/ppermute | solution.py:389
  25.9 8.9 %copy-start = (bf16[192,2304]{1,0:T(8,128)(2,1)}, bf16[192,2304]{1,0:T(8,128)(2,1)S(1)}, u32[]{:S(2)}) copy-start(bf16[192,2304]{1,0:T(8,128)(2,1)S(1)} %collective-permute-done.1.w2) | copy-start | bytes 2654212
  25.9 8.9 %collective-permute-start.2 = (bf16[192,2304]{1,0:T(8,128)(2,1)S(1)}, bf16[192,2304]{1,0:T(8,128)(2,1)S(1)}, u32[]{:S(2)}, u32[]{:S(2)}) collective-permute-start(bf16[192,2304]{1,0:T(8,128)(2,1)S(1)} %collective-permute-done.1.w2), channel_id=1, source_target_pairs={{0,1},{1,0},{2,3},{3,2},{4,5},{5,4},{6,7},{7,6},{8,9},{9,8},{10,11... | collective-permute-start | bytes 2654216 | tf_op jit(solution)/shard_map/ppermute | solution.py:389
  29.0 0.7 copy-start.16
  34.8 0.9 copy-start.1
  35.7 0.9 copy-start.2
  46.2 2.7 %collective-permute-start.5 = (bf16[648,128]{1,0:T(8,128)(2,1)}, bf16[648,128]{1,0:T(8,128)(2,1)S(1)}, u32[]{:S(2)}, u32[]{:S(2)}) collective-permute-start(bf16[648,128]{1,0:T(8,128)(2,1)} %get-tuple-element.18.t2), channel_id=1, source_target_pairs={{0,504},{1,505},{2,506},{3,507},{8,0},{9,1},{10,2},{11,3},{16,8},{... | collective-permute-start | bytes 497672 | tf_op jit(solution)/shard_map/ppermute | solution.py:397
  46.9 2.1 collective-permute-start.4
  47.6 1.4 collective-permute-start.3
  48.2 0.7 collective-permute-start.6
  48.9 0.6 copy-start.12
  48.9 0.7 copy-start.13
  49.0 0.7 copy-start.4
  49.7 0.7 copy-start.5
  97.2 33.3 %collective-permute-start.7 = (bf16[648,128]{1,0:T(8,128)(2,1)}, bf16[648,128]{1,0:T(8,128)(2,1)S(1)}, u32[]{:S(2)}, u32[]{:S(2)}) collective-permute-start(bf16[648,128]{1,0:T(8,128)(2,1)} %get-tuple-element.20), channel_id=1, source_target_pairs={{0,4},{1,5},{2,6},{3,7},{8,12},{9,13},{10,14},{11,15},{16,20},{17,... | collective-permute-start | bytes 497672 | tf_op jit(solution)/shard_map/ppermute | solution.py:397
  130.4 0.7 copy-start.8
  140.7 29.8 %collective-permute-start.10 = (bf16[648,128]{1,0:T(8,128)(2,1)}, bf16[648,128]{1,0:T(8,128)(2,1)S(1)}, u32[]{:S(2)}, u32[]{:S(2)}) collective-permute-start(bf16[648,128]{1,0:T(8,128)(2,1)} %get-tuple-element.22.t2), channel_id=1, source_target_pairs={{4,508},{5,509},{6,510},{7,511},{12,4},{13,5},{14,6},{15,7},{20,12... | collective-permute-start | bytes 497672 | tf_op jit(solution)/shard_map/ppermute | solution.py:397
  152.8 17.7 %collective-permute-start.9 = (bf16[648,128]{1,0:T(8,128)(2,1)}, bf16[648,128]{1,0:T(8,128)(2,1)S(1)}, u32[]{:S(2)}, u32[]{:S(2)}) collective-permute-start(bf16[648,128]{1,0:T(8,128)(2,1)} %get-tuple-element.22.t2), channel_id=1, source_target_pairs={{4,12},{5,13},{6,14},{7,15},{12,20},{13,21},{14,22},{15,23},{20,28... | collective-permute-start | bytes 497672 | tf_op jit(solution)/shard_map/ppermute | solution.py:397
  154.7 15.2 %collective-permute-start.8 = (bf16[432,128]{1,0:T(8,128)(2,1)}, bf16[432,128]{1,0:T(8,128)(2,1)S(1)}, u32[]{:S(2)}, u32[]{:S(2)}) collective-permute-start(bf16[432,128]{1,0:T(8,128)(2,1)} %get-tuple-element.21), channel_id=1, source_target_pairs={{4,20},{5,21},{6,22},{7,23},{12,28},{13,29},{14,30},{15,31},{20,36... | collective-permute-start | bytes 331784 | tf_op jit(solution)/shard_map/ppermute | solution.py:397
  156.6 13.8 %collective-permute-start.11 = (bf16[432,128]{1,0:T(8,128)(2,1)}, bf16[432,128]{1,0:T(8,128)(2,1)S(1)}, u32[]{:S(2)}, u32[]{:S(2)}) collective-permute-start(bf16[432,128]{1,0:T(8,128)(2,1)} %get-tuple-element.23), channel_id=1, source_target_pairs={{4,500},{5,501},{6,502},{7,503},{12,508},{13,509},{14,510},{15,511... | collective-permute-start | bytes 331784 | tf_op jit(solution)/shard_map/ppermute | solution.py:397
  169.9 0.6 copy-start.14
  170.5 0.7 copy-start.15
  170.5 0.7 copy-start.6
  170.5 0.8 copy-start.7
  218.4 13.9 %collective-permute-start.12 = (bf16[648,128]{1,0:T(8,128)(2,1)}, bf16[648,128]{1,0:T(8,128)(2,1)S(1)}, u32[]{:S(2)}, u32[]{:S(2)}) collective-permute-start(bf16[648,128]{1,0:T(8,128)(2,1)} %get-tuple-element.26), channel_id=1, source_target_pairs={{0,1},{1,0},{2,3},{3,2},{4,5},{5,4},{6,7},{7,6},{8,9},{9,8},{10,11... | collective-permute-start | bytes 497672 | tf_op jit(solution)/shard_map/ppermute | solution.py:389
  223.9 11.4 %collective-permute-start.13 = (bf16[648,128]{1,0:T(8,128)(2,1)}, bf16[648,128]{1,0:T(8,128)(2,1)S(1)}, u32[]{:S(2)}, u32[]{:S(2)}) collective-permute-start(bf16[648,128]{1,0:T(8,128)(2,1)} %get-tuple-element.27), channel_id=1, source_target_pairs={{0,2},{1,3},{2,0},{3,1},{4,6},{5,7},{6,4},{7,5},{8,10},{9,11},{10,... | collective-permute-start | bytes 497672 | tf_op jit(solution)/shard_map/ppermute | solution.py:389
  230.4 8.3 %collective-permute-start.14 = (bf16[648,128]{1,0:T(8,128)(2,1)}, bf16[648,128]{1,0:T(8,128)(2,1)S(1)}, u32[]{:S(2)}, u32[]{:S(2)}) collective-permute-start(bf16[648,128]{1,0:T(8,128)(2,1)} %get-tuple-element.28), channel_id=1, source_target_pairs={{0,3},{1,2},{2,1},{3,0},{4,7},{5,6},{6,5},{7,4},{8,11},{9,10},{10,... | collective-permute-start | bytes 497672 | tf_op jit(solution)/shard_map/ppermute | solution.py:389
  232.4 6.3 %copy-start.9 = (bf16[648,128]{1,0:T(8,128)(2,1)}, bf16[648,128]{1,0:T(8,128)(2,1)S(1)}, u32[]{:S(2)}) copy-start(bf16[648,128]{1,0:T(8,128)(2,1)S(1)} %collective-permute-done.12.o1) | copy-start | bytes 497668
  235.2 3.5 %copy-start.10 = (bf16[648,128]{1,0:T(8,128)(2,1)}, bf16[648,128]{1,0:T(8,128)(2,1)S(1)}, u32[]{:S(2)}) copy-start(bf16[648,128]{1,0:T(8,128)(2,1)S(1)} %collective-permute-done.13.o2) | copy-start | bytes 497668
  238.7 0.7 copy-start.11

commit v6 on v5

--- a/solution.py
+++ b/solution.py
@@ -46,13 +46,11 @@
     )
 
 
-def west_of(packed, tokens):
-    return jnp.concatenate([packed[:tokens], packed[tokens : 2 * tokens, : LANES // 2]], 1)
-
-
-def east_of(packed, tokens):
-    end = packed.shape[0]
-    return jnp.concatenate([packed[end - tokens :], packed[end - 2 * tokens : end - tokens, LANES // 2 :]], 1)
+def unpack_tile(packed, tokens):
+    side = packed[tokens : 2 * tokens]
+    middle = LANES // 2
+    west = jnp.concatenate([packed[:tokens], side[:, :middle]], 1)
+    return west, jnp.concatenate([packed[2 * tokens :], side[:, middle:]], 1)
 
 
 def embed_kernel(micro_ref, fields_ref, mask_ref, vector_ref, tile_ref, grid_ref):
@@ -121,7 +119,7 @@
     )(*weights)
 
 
-def compute_stage(mode, tile_refs, bias_ref, w_ref, wproj_ref, store, scratch):
+def compute_stage(mode, flags, tile_refs, bias_ref, w_ref, wproj_ref, store, scratch):
     xa, xb, q_ref, k_ref, v_ref, low_ref, high_ref = scratch
     f32, bf16 = jnp.float32, jnp.bfloat16
     halves, tokens, width = xa.shape
@@ -137,13 +135,17 @@
 
     def load_tiles():
         into = xb if mode == "rest" else xa
-        first = middle - len(tile_refs)
         for i, ref in enumerate(tile_refs):
-            packed = ref[...].astype(f32)
-            for j, part in enumerate((west_of, east_of)):
-                h = first + 2 * i + j
-                if mode != "rest" or 0 < h < halves - 1:
-                    into[h] = part(packed, tokens).astype(bf16)
+            distance = (0, 1, 1, 2, 2)[i]
+            east = flags[i] if i else 0
+            base = middle - 1 - 2 * distance + 4 * distance * east
+            if mode == "rest" and distance == REACH:
+                main, side = ref[:tokens].astype(f32), ref[tokens:].astype(f32)
+                last = jnp.where(east == 1, side[:, : LANES // 2], side[:, LANES // 2 :])
+                into[base + 1 - east] = jnp.concatenate([main, last], 1).astype(bf16)
+            else:
+                for j, part in enumerate(unpack_tile(ref[...].astype(f32), tokens)):
+                    into[base + j] = part.astype(bf16)
 
     def select_heads(parts, first, lanes):
         total = parts[0]
@@ -232,9 +234,13 @@
         load_tiles()
 
         def two_blocks(n, carry):
-            @pl.when(n > 0)
-            def _():
+            if mode == "whole":
                 block(2 * n, False, exact, together)
+            else:
+
+                @pl.when(n > 0)
+                def _():
+                    block(2 * n, False, exact, together)
 
             block(2 * n + 1, True, exact, together)
             return carry
@@ -264,8 +270,7 @@
         wproj_ref[place ^ i] = unpack_projection(ref, wproj_ref.shape[1])
 
 
-def first_kernel(place_ref, tile_in, w0, w1, w2, w3, bias_ref, tile_ref, west_ref, east_ref,
-                 w_ref, wproj_ref, *scratch):
+def first_kernel(place_ref, tile_in, w0, w1, w2, w3, bias_ref, tile_ref, p_ref, q_ref, w_ref, wproj_ref, *scratch):
     for i, ref in enumerate((w0, w1, w2, w3)):
 
         @pl.when(place_ref[0] == i)
@@ -276,37 +281,44 @@
     def store(b, packed):
         tile_ref[...] = packed
 
-    compute_stage("first", (tile_in,), bias_ref, w_ref, wproj_ref, store, scratch)
-    west_ref[...] = tile_ref[: west_ref.shape[0]]
-    east_ref[...] = tile_ref[tile_ref.shape[0] - east_ref.shape[0] :]
-
-
-def compute_rest(place, tiles, weights, bias_ref, outs_ref, w_ref, wproj_ref, scratch):
-    gather_weights(place, weights, w_ref, wproj_ref)
+    compute_stage("first", None, (tile_in,), bias_ref, w_ref, wproj_ref, store, scratch)
+    tokens = tile_ref.shape[0] // 3
+    for ref, flag in ((p_ref, place_ref[4]), (q_ref, place_ref[5])):
+        ref[:tokens] = jnp.where(flag == 1, tile_ref[2 * tokens :].astype(jnp.float32),
+                                 tile_ref[:tokens].astype(jnp.float32)).astype(jnp.bfloat16)
+        ref[tokens:] = tile_ref[tokens : 2 * tokens]
+
+
+def flags_of(place_ref):
+    return (0,) + tuple(place_ref[2 + i] for i in range(4))
+
+
+def whole_kernel(place_ref, t0, t1, t2, t3, t4, w0, w1, w2, w3, bias_ref, last_ref, outs_ref,
+                 w_ref, wproj_ref, *scratch):
+    place = place_ref[0]
+    gather_weights(place, (w0, w1, w2, w3), w_ref, wproj_ref)
 
     def store(b, packed):
         outs_ref[place ^ b] = packed
 
-    store(0, tiles[REACH][...])
-    compute_stage("rest", tiles, bias_ref, w_ref, wproj_ref, store, scratch)
-
-
-def early_kernel(place_ref, t0, t1, t2, t3, t4, w0, w1, w2, w3, bias_ref, last_ref, outs_ref,
-                 w_ref, wproj_ref, *scratch):
+    compute_stage("whole", flags_of(place_ref), (t0, t1, t2, t3, t4), bias_ref, w_ref, wproj_ref, store, scratch)
+    last_ref[...] = outs_ref[place ^ (STAGE - 1)]
+
+
+def rest_kernel(place_ref, t0, t1, t2, t3, t4, w0, w1, w2, w3, bias_ref, early_ref, o0, o1, o2, o3,
+                outs_ref, w_ref, wproj_ref, *scratch):
     place = place_ref[0]
-    compute_rest(place, (t0, t1, t2, t3, t4), (w0, w1, w2, w3), bias_ref, outs_ref, w_ref, wproj_ref, scratch)
-    last_ref[...] = outs_ref[place ^ (STAGE - 1)]
-
-
-def late_kernel(place_ref, t0, t1, t2, t3, t4, w0, w1, w2, w3, bias_ref, early_ref, o0, o1, o2, o3,
-                outs_ref, w_ref, wproj_ref, *scratch):
     late = place_ref[1] == 1
 
     @pl.when(late)
     def _():
-        compute_rest(
-            place_ref[0], (t0, t1, t2, t3, t4), (w0, w1, w2, w3), bias_ref, outs_ref, w_ref, wproj_ref, scratch
-        )
+        gather_weights(place, (w0, w1, w2, w3), w_ref, wproj_ref)
+
+        def store(b, packed):
+            outs_ref[place ^ b] = packed
+
+        store(0, t0[...])
+        compute_stage("rest", flags_of(place_ref), (t0, t1, t2, t3, t4), bias_ref, w_ref, wproj_ref, store, scratch)
         for i, ref in enumerate((o0, o1, o2, o3)):
             ref[...] = outs_ref[i]
 
@@ -382,19 +394,31 @@
     width = land_vector.shape[0]
     tile_count, section_count = lax.axis_size("tile"), lax.axis_size("section")
     section = lax.axis_index("section")
-    place = jnp.stack([section % STAGE, section // STAGE]).astype(jnp.int32)
+    tile_index = lax.axis_index("tile")
+    east_of_pair = tile_index % 2 == 0
+    east_of_four = tile_index % 4 < 2
+    place = jnp.stack(
+        [section % STAGE, section // STAGE, ~east_of_pair, east_of_pair, ~east_of_four, east_of_four]
+    ).astype(jnp.int32)
     axes = ("tile", "section")
 
     def exchange(value, bit):
         return lax.ppermute(value, "section", [(s, s ^ bit) for s in range(section_count)])
 
-    def shift(value, tiles, first, stages=0):
-        pairs = [
-            (t * section_count + s, (t + tiles) % tile_count * section_count + s + stages * STAGE)
-            for t in range(tile_count)
-            for s in range(first, first + STAGE)
-        ]
-        return lax.ppermute(value, axes, pairs)
+    def forward(value):
+        return lax.ppermute(value, "section", [(s, s + STAGE) for s in range(STAGE)])
+
+    def swap(values, first):
+        received = []
+        for value, distance, phase in zip(values, (1, 1, 2, 2), (1, 0, 1, 0)):
+            pairs = []
+            for t in range(tile_count):
+                if t // distance % 2 == phase:
+                    for s in range(first, first + STAGE):
+                        here, there = t * section_count + s, (t + distance) % tile_count * section_count + s
+                        pairs += [(here, there), (there, here)]
+            received.append(lax.ppermute(value, axes, pairs))
+        return received
 
     tokens = rows * levels * HALF
     tile_shape, half_shape = (3 * tokens, LANES), (2 * tokens, LANES)
@@ -403,23 +427,21 @@
 
     pack = pack_weights(w_qkv, w_proj, w_up, w_down.transpose(0, 2, 1))
     near, far = exchange(pack, 1), exchange(pack, 2)
+    tile = embed(place, fields, land_mask, land_vector.reshape(1, width))
+    halo = swap((tile,) * 4, 0)
+    far, halo = lax.optimization_barrier((far, halo))
     weights = (pack, near, far, exchange(far, 1))
     stack_shape = (STAGE,) + tile_shape
 
-    def even_then_halo(tile, first_section):
-        own, west, east = run_stage(
-            first_kernel, place, (tile, *weights, bias), (tile_shape, half_shape, half_shape), (), 1, *sizes
-        )
-        move = functools.partial(shift, first=first_section)
-        return move(east, 2), move(own, 1), own, move(own, -1), move(west, -2)
-
-    tiles = even_then_halo(embed(place, fields, land_mask, land_vector.reshape(1, width)), 0)
     last, early = run_stage(
-        early_kernel, place, (*tiles, *weights, bias), (tile_shape, stack_shape), (), STAGE, *sizes
+        whole_kernel, place, (tile, *halo, *weights, bias), (tile_shape, stack_shape), (), STAGE, *sizes
     )
-    tiles = even_then_halo(shift(last, 0, 0, 1), STAGE)
+    tile, p, q = run_stage(
+        first_kernel, place, (forward(last), *weights, bias), (tile_shape, half_shape, half_shape), (), 1, *sizes
+    )
+    halo = swap((tile, tile, p, q), STAGE)
     outs = run_stage(
-        late_kernel, place, (*tiles, *weights, bias, early), (tile_shape,) * STAGE, (stack_shape,), STAGE, *sizes
+        rest_kernel, place, (tile, *halo, *weights, bias, early), (tile_shape,) * STAGE, (stack_shape,), STAGE, *sizes
     )
 
     pieces = [outs[0]] + [exchange(outs[i], i) for i in range(1, STAGE)]

time: 246 us -> 239 us (0.972)
  the two profiles are of different devices: /device:TPU:129 before, /device:TPU:131 now
where the time goes in v6:
time: 239 us; the launch traced here: 238 us
  Pallas kernels  139 us (58%)
  starting transfers between devices  50.9 us (21%)
  waiting for transfers between devices  39.2 us (16%)
  local copies, waits for them, and re-layouts  8.53 us (4%)
    pallas_call x3, Pallas kernels, run_stage(): pl.pallas_call(kernel, out_shape=tuple((jax.ShapeDtypeStruct(shape, bf16)...  131 us
    ppermute x8, starting transfers between devices, swap(): received.append(lax.ppermute(value, axes, pairs))  28.3 us
    ppermute x6, starting transfers between devices, exchange(): lax.ppermute(value, 'section', [(s, s ^ bit) for s in range(section_count)])  21.3 us
    ppermute x1, waiting for transfers between devices, forward(): lax.ppermute(value, 'section', [(s, s + STAGE) for s in range(STAGE)])  16.7 us
    ppermute x6, waiting for transfers between devices, exchange(): lax.ppermute(value, 'section', [(s, s ^ bit) for s in range(section_count)])  16.4 us
    ppermute x8, waiting for transfers between devices, swap(): received.append(lax.ppermute(value, axes, pairs))  6.09 us
    unnamed x38, local copies, waits for them, and re-layouts  5.41 us
  transfers between devices with their start and end apart: 15, of which 7 were waited for; matrix products, arithmetic and copies ran while one was open for 1% of the time, Pallas kernels for 1%

profile of v6, /device:TPU:131, one launch (start us, length us, event | category | flops | bytes accessed | tf_op | source)
XLA Modules:
  0.0 238.0 jit_solution(11571446405451611604)
XLA Ops:
  0.0 2.3 pack_weights.1.w0
  2.3 4.0 %collective-permute-start = (bf16[192,2304]{1,0:T(8,128)(2,1)}, bf16[192,2304]{1,0:T(8,128)(2,1)S(1)}, u32[]{:S(2)}, u32[]{:S(2)}) collective-permute-start(bf16[192,2304]{1,0:T(8,128)(2,1)} %pack_weights.1.w0), channel_id=1, source_target_pairs={{0,2},{1,3},{2,0},{3,1},{4,6},{5,7},{6,4},{7,5},{8,10},{9,11},{10,... | collective-permute-start | bytes 2654216 | tf_op jit(solution)/shard_map/ppermute | solution.py:406
  6.4 0.0 copy-start.17
  6.4 0.7 copy-done.17
  7.1 0.7 copy.10.mask_ref
  7.7 1.0 copy.9.fields_ref
  8.8 0.6 stack.43.micro_ref.place_ref
  9.4 2.7 %embed.1.t0 = bf16[648,128]{1,0:T(8,128)(2,1)} custom-call(s32[6]{0:T(128)} %stack.43.micro_ref.place_ref, bf16[4,2,18,2304]{3,2,1,0:T(8,128)(2,1)} %copy.9.fields_ref, s32[18,12]{1,0:T(8,128)} %copy.10.mask_ref, f32[1,192]{1,0:T(1,128)} %bitcast.9), custom_call_target="tpu_custom_call" | custom-call | tf_op jit(solution)/shard_map/embed/pallas_call | solution.py:81
  12.1 0.7 collective-permute-start.4
  12.8 0.7 collective-permute-start.3
  13.5 0.7 collective-permute-start.2
  14.1 0.7 collective-permute-start.1
  14.8 0.0 collective-permute-done.4.t4
  14.8 2.9 %collective-permute-start.5 = (bf16[192,2304]{1,0:T(8,128)(2,1)S(1)}, bf16[192,2304]{1,0:T(8,128)(2,1)S(1)}, u32[]{:S(2)}, u32[]{:S(2)}) collective-permute-start(bf16[192,2304]{1,0:T(8,128)(2,1)S(1)} %copy-done), channel_id=1, source_target_pairs={{0,1},{1,0},{2,3},{3,2},{4,5},{5,4},{6,7},{7,6},{8,9},{9,8},{10,11... | collective-permute-start | bytes 2654216 | tf_op jit(solution)/shard_map/ppermute | solution.py:406
  17.7 0.0 collective-permute-done.3.t3
  17.7 0.0 collective-permute-done.2.t2
  17.8 8.1 %collective-permute-done.w2 = bf16[192,2304]{1,0:T(8,128)(2,1)S(1)} collective-permute-done((bf16[192,2304]{1,0:T(8,128)(2,1)}, bf16[192,2304]{1,0:T(8,128)(2,1)S(1)}, u32[]{:S(2)}, u32[]{:S(2)}) %collective-permute-start) | collective-permute-done | bytes 884768 | tf_op jit(solution)/shard_map/ppermute | solution.py:406
  25.9 3.1 %collective-permute-start.6 = (bf16[192,2304]{1,0:T(8,128)(2,1)S(1)}, bf16[192,2304]{1,0:T(8,128)(2,1)S(1)}, u32[]{:S(2)}, u32[]{:S(2)}) collective-permute-start(bf16[192,2304]{1,0:T(8,128)(2,1)S(1)} %collective-permute-done.w2), channel_id=1, source_target_pairs={{0,1},{1,0},{2,3},{3,2},{4,5},{5,4},{6,7},{7,6},{8,9},{9,8},{10,11... | collective-permute-start | bytes 2654216 | tf_op jit(solution)/shard_map/ppermute | solution.py:406
  29.0 0.0 collective-permute-done.5.w1
  29.0 2.0 collective-permute-done.6.w3
  31.1 0.9 copy-done.3
  32.0 73.8 %whole_kernel.1 = (bf16[648,128]{1,0:T(8,128)(2,1)}, bf16[4,648,128]{2,1,0:T(8,128)(2,1)}) custom-call(s32[6]{0:T(128)} %stack.43.micro_ref.place_ref, bf16[648,128]{1,0:T(8,128)(2,1)} %embed.1.t0, bf16[648,128]{1,0:T(8,128)(2,1)} %copy-done.10, bf16[648,128]{1,0:T(8,128)(2,1)} %copy-done.8, bf16[648,128]{1,0:T(8,128)(2,1)} %copy-done.6, ...), custom_call_target="tpu_custom_call" | custom-call | tf_op jit(solution)/shard_map/whole_kernel/pallas_call | solution.py:336
  105.8 1.3 collective-permute-start.7
  107.1 16.7 %collective-permute-done.7.tile_in = bf16[648,128]{1,0:T(8,128)(2,1)S(1)} collective-permute-done((bf16[648,128]{1,0:T(8,128)(2,1)}, bf16[648,128]{1,0:T(8,128)(2,1)S(1)}, u32[]{:S(2)}, u32[]{:S(2)}) %collective-permute-start.7) | collective-permute-done | bytes 165920 | tf_op jit(solution)/shard_map/ppermute | solution.py:409
  123.7 0.7 copy-done.11
  124.4 9.8 %first_kernel.1 = (bf16[648,128]{1,0:T(8,128)(2,1)}, bf16[432,128]{1,0:T(8,128)(2,1)}, bf16[432,128]{1,0:T(8,128)(2,1)}) custom-call(s32[6]{0:T(128)} %stack.43.micro_ref.place_ref, bf16[648,128]{1,0:T(8,128)(2,1)} %copy-done.11, bf16[192,2304]{1,0:T(8,128)(2,1)} %pack_weights.1.w0, bf16[192,2304]{1,0:T(8,128)(2,1)} %copy-done.2, ...), custom_call_target="tpu_custom_call" | custom-call | tf_op jit(solution)/shard_map/first_kernel/pallas_call | solution.py:336
  134.2 11.2 %collective-permute-start.9 = (bf16[648,128]{1,0:T(8,128)(2,1)}, bf16[648,128]{1,0:T(8,128)(2,1)S(1)}, u32[]{:S(2)}, u32[]{:S(2)}) collective-permute-start(bf16[648,128]{1,0:T(8,128)(2,1)} %get-tuple-element.25.t0), channel_id=1, source_target_pairs={{4,12},{12,4},{5,13},{13,5},{6,14},{14,6},{7,15},{15,7},{20,28},{2... | collective-permute-start | bytes 497672 | tf_op jit(solution)/shard_map/ppermute | solution.py:420
  145.4 1.9 collective-permute-start.8
  147.3 10.6 %collective-permute-start.10 = (bf16[432,128]{1,0:T(8,128)(2,1)}, bf16[432,128]{1,0:T(8,128)(2,1)S(1)}, u32[]{:S(2)}, u32[]{:S(2)}) collective-permute-start(bf16[432,128]{1,0:T(8,128)(2,1)} %get-tuple-element.26), channel_id=1, source_target_pairs={{20,36},{36,20},{21,37},{37,21},{22,38},{38,22},{23,39},{39,23},{2... | collective-permute-start | bytes 331784 | tf_op jit(solution)/shard_map/ppermute | solution.py:420
  158.0 1.9 collective-permute-start.11
  159.9 3.7 %collective-permute-done.10.t3 = bf16[432,128]{1,0:T(8,128)(2,1)S(1)} collective-permute-done((bf16[432,128]{1,0:T(8,128)(2,1)}, bf16[432,128]{1,0:T(8,128)(2,1)S(1)}, u32[]{:S(2)}, u32[]{:S(2)}) %collective-permute-start.10) | collective-permute-done | bytes 110624 | tf_op jit(solution)/shard_map/ppermute | solution.py:420
  163.6 2.4 collective-permute-done.11.t4
  166.0 0.0 collective-permute-done.9.t2
  166.0 0.0 collective-permute-done.8.t1
  166.0 0.6 copy-done.16
  166.6 0.1 copy-done.7
  166.7 0.0 copy-done.9
  166.7 47.3 %rest_kernel.1 = (bf16[648,128]{1,0:T(8,128)(2,1)}, bf16[648,128]{1,0:T(8,128)(2,1)}, bf16[648,128]{1,0:T(8,128)(2,1)}, bf16[648,128]{1,0:T(8,128)(2,1)}) custom-call(s32[6]{0:T(128)} %stack.43.micro_ref.place_ref, bf16[648,128]{1,0:T(8,128)(2,1)} %get-tuple-element.25.t0, bf16[648,128]{1,0:T(8,128)(2,1)} %copy-done.9, bf16[648,128]{1,0:T(8,128)(2,1)} %copy-done.7, ...), custom_call_target="tpu_custom_call" | custom-call | tf_op jit(solution)/shard_map/rest_kernel/pallas_call | solution.py:336
  214.0 3.7 %collective-permute-start.12 = (bf16[648,128]{1,0:T(8,128)(2,1)}, bf16[648,128]{1,0:T(8,128)(2,1)S(1)}, u32[]{:S(2)}, u32[]{:S(2)}) collective-permute-start(bf16[648,128]{1,0:T(8,128)(2,1)} %get-tuple-element.30), channel_id=1, source_target_pairs={{0,1},{1,0},{2,3},{3,2},{4,5},{5,4},{6,7},{7,6},{8,9},{9,8},{10,11... | collective-permute-start | bytes 497672 | tf_op jit(solution)/shard_map/ppermute | solution.py:406
  217.7 5.6 %collective-permute-start.13 = (bf16[648,128]{1,0:T(8,128)(2,1)}, bf16[648,128]{1,0:T(8,128)(2,1)S(1)}, u32[]{:S(2)}, u32[]{:S(2)}) collective-permute-start(bf16[648,128]{1,0:T(8,128)(2,1)} %get-tuple-element.31), channel_id=1, source_target_pairs={{0,2},{1,3},{2,0},{3,1},{4,6},{5,7},{6,4},{7,5},{8,10},{9,11},{10,... | collective-permute-start | bytes 497672 | tf_op jit(solution)/shard_map/ppermute | solution.py:406
  223.4 1.9 collective-permute-start.14
  225.3 0.0 collective-permute-done.12.o1
  225.3 0.0 copy-start.12
  225.3 2.9 %collective-permute-done.13.o2 = bf16[648,128]{1,0:T(8,128)(2,1)S(1)} collective-permute-done((bf16[648,128]{1,0:T(8,128)(2,1)}, bf16[648,128]{1,0:T(8,128)(2,1)S(1)}, u32[]{:S(2)}, u32[]{:S(2)}) %collective-permute-start.13) | collective-permute-done | bytes 165920 | tf_op jit(solution)/shard_map/ppermute | solution.py:406
  228.2 3.5 %collective-permute-done.14.o3 = bf16[648,128]{1,0:T(8,128)(2,1)S(1)} collective-permute-done((bf16[648,128]{1,0:T(8,128)(2,1)}, bf16[648,128]{1,0:T(8,128)(2,1)S(1)}, u32[]{:S(2)}, u32[]{:S(2)}) %collective-permute-start.14) | collective-permute-done | bytes 165920 | tf_op jit(solution)/shard_map/ppermute | solution.py:406
  231.6 0.7 copy-done.14
  232.3 3.2 %finish.1 = bf16[1,4,2,18,2304]{4,3,2,1,0:T(8,128)(2,1)} custom-call(s32[6]{0:T(128)} %stack.43.micro_ref.place_ref, bf16[648,128]{1,0:T(8,128)(2,1)} %get-tuple-element.29.o0, bf16[648,128]{1,0:T(8,128)(2,1)} %copy-done.12, bf16[648,128]{1,0:T(8,128)(2,1)} %copy-done.13, bf16[648,128]{1,0:T(8,128)(2,1)} %copy-done.14), custom_call_target="tpu_custom_call" | custom-call | tf_op jit(solution)/shard_map/finish/pallas_call | solution.py:381
  235.5 2.5 %copy.11 = bf16[1,4,2,18,2304]{4,2,3,1,0:T(2,128)(2,1)} copy(bf16[1,4,2,18,2304]{4,3,2,1,0:T(8,128)(2,1)} %finish.1) | data formatting | bytes 1327104 | tf_op jit(solution)/shard_map/finish/pallas_call | solution.py:381
  (28 shorter events, 0.1 us)
Async XLA Ops:
  0.0 7.7 %copy-start.4 = (bf16[4,2,18,2304]{3,1,2,0:T(2,128)(2,1)S(1)}, bf16[4,2,18,2304]{3,1,2,0:T(2,128)(2,1)}, u32[]{:S(2)}) copy-start(bf16[4,2,18,2304]{3,1,2,0:T(2,128)(2,1)} %param.8) | copy-start | bytes 1990660
  2.3 23.6 %collective-permute-start = (bf16[192,2304]{1,0:T(8,128)(2,1)}, bf16[192,2304]{1,0:T(8,128)(2,1)S(1)}, u32[]{:S(2)}, u32[]{:S(2)}) collective-permute-start(bf16[192,2304]{1,0:T(8,128)(2,1)} %pack_weights.1.w0), channel_id=1, source_target_pairs={{0,2},{1,3},{2,0},{3,1},{4,6},{5,7},{6,4},{7,5},{8,10},{9,11},{10,... | collective-permute-start | bytes 2654216 | tf_op jit(solution)/shard_map/ppermute | solution.py:406
  6.4 0.7 copy-start.17
  8.8 6.1 %copy-start = (bf16[192,2304]{1,0:T(8,128)(2,1)S(1)}, bf16[192,2304]{1,0:T(8,128)(2,1)}, u32[]{:S(2)}) copy-start(bf16[192,2304]{1,0:T(8,128)(2,1)} %pack_weights.1.w0) | copy-start | bytes 2654212
  12.1 2.7 %collective-permute-start.4 = (bf16[648,128]{1,0:T(8,128)(2,1)}, bf16[648,128]{1,0:T(8,128)(2,1)S(1)}, u32[]{:S(2)}, u32[]{:S(2)}) collective-permute-start(bf16[648,128]{1,0:T(8,128)(2,1)} %embed.1.t0), channel_id=1, source_target_pairs={{0,16},{16,0},{1,17},{17,1},{2,18},{18,2},{3,19},{19,3},{8,24},{24... | collective-permute-start | bytes 497672 | tf_op jit(solution)/shard_map/ppermute | solution.py:420
  12.8 4.9 %collective-permute-start.3 = (bf16[648,128]{1,0:T(8,128)(2,1)}, bf16[648,128]{1,0:T(8,128)(2,1)S(1)}, u32[]{:S(2)}, u32[]{:S(2)}) collective-permute-start(bf16[648,128]{1,0:T(8,128)(2,1)} %embed.1.t0), channel_id=1, source_target_pairs={{16,32},{32,16},{17,33},{33,17},{18,34},{34,18},{19,35},{35,19},{2... | collective-permute-start | bytes 497672 | tf_op jit(solution)/shard_map/ppermute | solution.py:420
  13.5 4.3 %collective-permute-start.2 = (bf16[648,128]{1,0:T(8,128)(2,1)}, bf16[648,128]{1,0:T(8,128)(2,1)S(1)}, u32[]{:S(2)}, u32[]{:S(2)}) collective-permute-start(bf16[648,128]{1,0:T(8,128)(2,1)} %embed.1.t0), channel_id=1, source_target_pairs={{0,8},{8,0},{1,9},{9,1},{2,10},{10,2},{3,11},{11,3},{16,24},{24,16... | collective-permute-start | bytes 497672 | tf_op jit(solution)/shard_map/ppermute | solution.py:420
  14.1 3.6 %collective-permute-start.1 = (bf16[648,128]{1,0:T(8,128)(2,1)}, bf16[648,128]{1,0:T(8,128)(2,1)S(1)}, u32[]{:S(2)}, u32[]{:S(2)}) collective-permute-start(bf16[648,128]{1,0:T(8,128)(2,1)} %embed.1.t0), channel_id=1, source_target_pairs={{8,16},{16,8},{9,17},{17,9},{10,18},{18,10},{11,19},{19,11},{24,32... | collective-permute-start | bytes 497672 | tf_op jit(solution)/shard_map/ppermute | solution.py:420
  14.8 16.2 %copy-start.5 = (bf16[648,128]{1,0:T(8,128)(2,1)}, bf16[648,128]{1,0:T(8,128)(2,1)S(1)}, u32[]{:S(2)}) copy-start(bf16[648,128]{1,0:T(8,128)(2,1)S(1)} %collective-permute-done.4.t4) | copy-start | bytes 497668
  14.8 14.2 %collective-permute-start.5 = (bf16[192,2304]{1,0:T(8,128)(2,1)S(1)}, bf16[192,2304]{1,0:T(8,128)(2,1)S(1)}, u32[]{:S(2)}, u32[]{:S(2)}) collective-permute-start(bf16[192,2304]{1,0:T(8,128)(2,1)S(1)} %copy-done), channel_id=1, source_target_pairs={{0,1},{1,0},{2,3},{3,2},{4,5},{5,4},{6,7},{7,6},{8,9},{9,8},{10,11... | collective-permute-start | bytes 2654216 | tf_op jit(solution)/shard_map/ppermute | solution.py:406
  17.7 13.3 %copy-start.6 = (bf16[648,128]{1,0:T(8,128)(2,1)}, bf16[648,128]{1,0:T(8,128)(2,1)S(1)}, u32[]{:S(2)}) copy-start(bf16[648,128]{1,0:T(8,128)(2,1)S(1)} %collective-permute-done.3.t3) | copy-start | bytes 497668
  17.8 13.3 %copy-start.8 = (bf16[648,128]{1,0:T(8,128)(2,1)}, bf16[648,128]{1,0:T(8,128)(2,1)S(1)}, u32[]{:S(2)}) copy-start(bf16[648,128]{1,0:T(8,128)(2,1)S(1)} %collective-permute-done.2.t2) | copy-start | bytes 497668
  17.8 13.3 %copy-start.10 = (bf16[648,128]{1,0:T(8,128)(2,1)}, bf16[648,128]{1,0:T(8,128)(2,1)S(1)}, u32[]{:S(2)}) copy-start(bf16[648,128]{1,0:T(8,128)(2,1)S(1)} %collective-permute-done.1.t1) | copy-start | bytes 497668
  25.9 5.2 %copy-start.1 = (bf16[192,2304]{1,0:T(8,128)(2,1)}, bf16[192,2304]{1,0:T(8,128)(2,1)S(1)}, u32[]{:S(2)}) copy-start(bf16[192,2304]{1,0:T(8,128)(2,1)S(1)} %collective-permute-done.w2) | copy-start | bytes 2654212
  25.9 5.2 %collective-permute-start.6 = (bf16[192,2304]{1,0:T(8,128)(2,1)S(1)}, bf16[192,2304]{1,0:T(8,128)(2,1)S(1)}, u32[]{:S(2)}, u32[]{:S(2)}) collective-permute-start(bf16[192,2304]{1,0:T(8,128)(2,1)S(1)} %collective-permute-done.w2), channel_id=1, source_target_pairs={{0,1},{1,0},{2,3},{3,2},{4,5},{5,4},{6,7},{7,6},{8,9},{9,8},{10,11... | collective-permute-start | bytes 2654216 | tf_op jit(solution)/shard_map/ppermute | solution.py:406
  29.0 2.0 copy-start.2
  31.1 0.9 copy-start.3
  105.8 17.9 %collective-permute-start.7 = (bf16[648,128]{1,0:T(8,128)(2,1)}, bf16[648,128]{1,0:T(8,128)(2,1)S(1)}, u32[]{:S(2)}, u32[]{:S(2)}) collective-permute-start(bf16[648,128]{1,0:T(8,128)(2,1)} %get-tuple-element.24), channel_id=1, source_target_pairs={{0,4},{1,5},{2,6},{3,7},{8,12},{9,13},{10,14},{11,15},{16,20},{17,... | collective-permute-start | bytes 497672 | tf_op jit(solution)/shard_map/ppermute | solution.py:409
  123.7 0.7 copy-start.11
  134.2 31.8 %collective-permute-start.9 = (bf16[648,128]{1,0:T(8,128)(2,1)}, bf16[648,128]{1,0:T(8,128)(2,1)S(1)}, u32[]{:S(2)}, u32[]{:S(2)}) collective-permute-start(bf16[648,128]{1,0:T(8,128)(2,1)} %get-tuple-element.25.t0), channel_id=1, source_target_pairs={{4,12},{12,4},{5,13},{13,5},{6,14},{14,6},{7,15},{15,7},{20,28},{2... | collective-permute-start | bytes 497672 | tf_op jit(solution)/shard_map/ppermute | solution.py:420
  145.4 20.6 %collective-permute-start.8 = (bf16[648,128]{1,0:T(8,128)(2,1)}, bf16[648,128]{1,0:T(8,128)(2,1)S(1)}, u32[]{:S(2)}, u32[]{:S(2)}) collective-permute-start(bf16[648,128]{1,0:T(8,128)(2,1)} %get-tuple-element.25.t0), channel_id=1, source_target_pairs={{12,20},{20,12},{13,21},{21,13},{14,22},{22,14},{15,23},{23,15},{2... | collective-permute-start | bytes 497672 | tf_op jit(solution)/shard_map/ppermute | solution.py:420
  147.3 16.3 %collective-permute-start.10 = (bf16[432,128]{1,0:T(8,128)(2,1)}, bf16[432,128]{1,0:T(8,128)(2,1)S(1)}, u32[]{:S(2)}, u32[]{:S(2)}) collective-permute-start(bf16[432,128]{1,0:T(8,128)(2,1)} %get-tuple-element.26), channel_id=1, source_target_pairs={{20,36},{36,20},{21,37},{37,21},{22,38},{38,22},{23,39},{39,23},{2... | collective-permute-start | bytes 331784 | tf_op jit(solution)/shard_map/ppermute | solution.py:420
  158.0 8.0 %collective-permute-start.11 = (bf16[432,128]{1,0:T(8,128)(2,1)}, bf16[432,128]{1,0:T(8,128)(2,1)S(1)}, u32[]{:S(2)}, u32[]{:S(2)}) collective-permute-start(bf16[432,128]{1,0:T(8,128)(2,1)} %get-tuple-element.27), channel_id=1, source_target_pairs={{4,20},{20,4},{5,21},{21,5},{6,22},{22,6},{7,23},{23,7},{12,28},{2... | collective-permute-start | bytes 331784 | tf_op jit(solution)/shard_map/ppermute | solution.py:420
  163.6 2.4 %copy-start.15 = (bf16[432,128]{1,0:T(8,128)(2,1)}, bf16[432,128]{1,0:T(8,128)(2,1)S(1)}, u32[]{:S(2)}) copy-start(bf16[432,128]{1,0:T(8,128)(2,1)S(1)} %collective-permute-done.10.t3) | copy-start | bytes 331780
  166.0 0.7 copy-start.16
  166.0 0.7 copy-start.7
  166.0 0.8 copy-start.9
  214.0 11.3 %collective-permute-start.12 = (bf16[648,128]{1,0:T(8,128)(2,1)}, bf16[648,128]{1,0:T(8,128)(2,1)S(1)}, u32[]{:S(2)}, u32[]{:S(2)}) collective-permute-start(bf16[648,128]{1,0:T(8,128)(2,1)} %get-tuple-element.30), channel_id=1, source_target_pairs={{0,1},{1,0},{2,3},{3,2},{4,5},{5,4},{6,7},{7,6},{8,9},{9,8},{10,11... | collective-permute-start | bytes 497672 | tf_op jit(solution)/shard_map/ppermute | solution.py:406
  217.7 10.4 %collective-permute-start.13 = (bf16[648,128]{1,0:T(8,128)(2,1)}, bf16[648,128]{1,0:T(8,128)(2,1)S(1)}, u32[]{:S(2)}, u32[]{:S(2)}) collective-permute-start(bf16[648,128]{1,0:T(8,128)(2,1)} %get-tuple-element.31), channel_id=1, source_target_pairs={{0,2},{1,3},{2,0},{3,1},{4,6},{5,7},{6,4},{7,5},{8,10},{9,11},{10,... | collective-permute-start | bytes 497672 | tf_op jit(solution)/shard_map/ppermute | solution.py:406
  223.4 8.3 %collective-permute-start.14 = (bf16[648,128]{1,0:T(8,128)(2,1)}, bf16[648,128]{1,0:T(8,128)(2,1)S(1)}, u32[]{:S(2)}, u32[]{:S(2)}) collective-permute-start(bf16[648,128]{1,0:T(8,128)(2,1)} %get-tuple-element.32), channel_id=1, source_target_pairs={{0,3},{1,2},{2,1},{3,0},{4,7},{5,6},{6,5},{7,4},{8,11},{9,10},{10,... | collective-permute-start | bytes 497672 | tf_op jit(solution)/shard_map/ppermute | solution.py:406
  225.3 6.3 %copy-start.12 = (bf16[648,128]{1,0:T(8,128)(2,1)}, bf16[648,128]{1,0:T(8,128)(2,1)S(1)}, u32[]{:S(2)}) copy-start(bf16[648,128]{1,0:T(8,128)(2,1)S(1)} %collective-permute-done.12.o1) | copy-start | bytes 497668
  228.2 3.5 %copy-start.13 = (bf16[648,128]{1,0:T(8,128)(2,1)}, bf16[648,128]{1,0:T(8,128)(2,1)S(1)}, u32[]{:S(2)}) copy-start(bf16[648,128]{1,0:T(8,128)(2,1)S(1)} %collective-permute-done.13.o2) | copy-start | bytes 497668
  231.6 0.7 copy-start.14

commit v7 on v6

--- a/solution.py
+++ b/solution.py
@@ -14,7 +14,6 @@
 WLON = 12
 HALF = WLON // 2
 STAGE = 4
-REACH = 2
 LOG2E = 1.4426950408889634
 LANES = 128
 VMEM_LIMIT = 56 * 2**20
@@ -119,7 +118,7 @@
     )(*weights)
 
 
-def compute_stage(mode, flags, tile_refs, bias_ref, w_ref, wproj_ref, store, scratch):
+def compute_blocks(mode, flags, tile_refs, bias_ref, w_ref, wproj_ref, store, scratch):
     xa, xb, q_ref, k_ref, v_ref, low_ref, high_ref = scratch
     f32, bf16 = jnp.float32, jnp.bfloat16
     halves, tokens, width = xa.shape
@@ -127,25 +126,22 @@
     windows, piece, _ = bias_ref.shape
     move = piece // 2
     hidden = (w_ref.shape[2] - 768) // 2
-    middle = halves // 2
-
     channel_head = lax.broadcasted_iota(jnp.int32, (1, width), 1) // head_size
     scale = head_size ** (-0.5) * LOG2E
     ones = jnp.ones((2 * piece, 256 - width), f32)
 
     def load_tiles():
-        into = xb if mode == "rest" else xa
+        into = xb if mode.startswith("odd") else xa
         for i, ref in enumerate(tile_refs):
-            distance = (0, 1, 1, 2, 2)[i]
-            east = flags[i] if i else 0
-            base = middle - 1 - 2 * distance + 4 * distance * east
-            if mode == "rest" and distance == REACH:
+            if ref.shape[0] == 3 * tokens:
+                base = 4 * flags[i - 1] if i else 2
+                for j, part in enumerate(unpack_tile(ref[...].astype(f32), tokens)):
+                    into[base + j] = part.astype(bf16)
+            else:
+                east = flags[i - 1]
                 main, side = ref[:tokens].astype(f32), ref[tokens:].astype(f32)
                 last = jnp.where(east == 1, side[:, : LANES // 2], side[:, LANES // 2 :])
-                into[base + 1 - east] = jnp.concatenate([main, last], 1).astype(bf16)
-            else:
-                for j, part in enumerate(unpack_tile(ref[...].astype(f32), tokens)):
-                    into[base + j] = part.astype(bf16)
+                into[1 + 3 * east] = jnp.concatenate([main, last], 1).astype(bf16)
 
     def select_heads(parts, first, lanes):
         total = parts[0]
@@ -181,7 +177,7 @@
             high_ref[:, rest] = jnp.maximum(high_ref[:, rest], jnp.max(sums[1].reshape(-1, 8, width - LANES), axis=0))
         return jnp.concatenate([top / total for top, total in zip(tops, sums)], 1)
 
-    def block(b, shifted, exact, together, alone=False):
+    def block(b, shifted, exact, together, first_pair, pairs, first_q, count):
         source, target = (xb, xa) if shifted else (xa, xb)
 
         def load(h):
@@ -191,7 +187,7 @@
         def pair(i, carry):
             kv = []
             for j in range(2):
-                h = b + 2 * i + j
+                h = first_pair + 2 * i + j
                 qkv = jnp.dot(normalize(load(h)).astype(bf16), w_ref[b, :, :768], preferred_element_type=f32)
                 q_ref[h] = qkv[:, :width] * scale
                 kv.append((qkv[:, 256 : 256 + width], qkv[:, 512 : 512 + width]))
@@ -203,10 +199,10 @@
             return carry
 
         def attend(c, carry):
-            own = [(middle - 1 if alone else 1 + b) + together * c + j for j in range(together)]
+            own = [first_q + together * c + j for j in range(together)]
             x = jnp.concatenate([load(h) for h in own], 0)
             a = jnp.concatenate(
-                [window_attention(h, (h - b) // 2, w, shifted, exact) for h in own for w in range(windows)], 0
+                [window_attention(h, (h - first_pair) // 2, w, shifted, exact) for h in own for w in range(windows)], 0
             ).astype(bf16)
             residual = x + jnp.dot(a, wproj_ref[b], preferred_element_type=f32)
             n2 = normalize(residual).astype(bf16)
@@ -222,33 +218,32 @@
                 target[h] = part.astype(bf16)
             return carry
 
-        if alone:
-            pair(middle // 2, 0)
-            lax.fori_loop(0, 2 // together, attend, 0)
-        else:
-            lax.fori_loop(0, middle - b, pair, 0)
-            lax.fori_loop(0, (halves - 2 - 2 * b) // together, attend, 0)
-        store(b, pack_tile(target[middle - 1].astype(f32), target[middle].astype(f32)).astype(bf16))
+        lax.fori_loop(0, pairs, pair, 0)
+        lax.fori_loop(0, count // together, attend, 0)
+        store(b, pack_tile(target[2].astype(f32), target[3].astype(f32)).astype(bf16))
 
     def compute(exact, together):
         load_tiles()
 
-        def two_blocks(n, carry):
-            if mode == "whole":
-                block(2 * n, False, exact, together)
-            else:
-
-                @pl.when(n > 0)
-                def _():
-                    block(2 * n, False, exact, together)
-
-            block(2 * n + 1, True, exact, together)
+        def odd(b):
+            block(b, True, exact, together, 1, 2, 2, 2)
+
+        def even(b):
+            block(b, False, exact, together, 2, 1, 2, 2)
+
+        def wide_even(n, carry):
+            block(2 * n, False, exact, together, 2 * n, 3 - 2 * n, 1 + n, 4 - 2 * n)
+            pl.when(n == 0)(lambda: odd(1))
             return carry
 
-        if mode == "first":
-            block(0, False, exact, together, True)
+        if mode == "wide even":
+            lax.fori_loop(0, 2, wide_even, 0)
+        elif mode == "even":
+            even(0)
         else:
-            lax.fori_loop(0, STAGE // 2, two_blocks, 0)
+            odd(0)
+            if mode == "odd even":
+                even(1)
 
     low_ref[...] = jnp.ones_like(low_ref)
     high_ref[...] = jnp.ones_like(high_ref)
@@ -264,72 +259,79 @@
     return jnp.concatenate([ref[:, 256 * j + width : 256 * j + 256] for j in range(3)], 1)
 
 
-def gather_weights(place, refs, w_ref, wproj_ref):
+def gather_weights(place, refs, blocks, w_ref, wproj_ref):
     for i, ref in enumerate(refs):
-        w_ref[place ^ i] = ref[...]
-        wproj_ref[place ^ i] = unpack_projection(ref, wproj_ref.shape[1])
-
-
-def first_kernel(place_ref, tile_in, w0, w1, w2, w3, bias_ref, tile_ref, p_ref, q_ref, w_ref, wproj_ref, *scratch):
-    for i, ref in enumerate((w0, w1, w2, w3)):
-
-        @pl.when(place_ref[0] == i)
-        def _(ref=ref):
-            w_ref[0] = ref[...]
-            wproj_ref[0] = unpack_projection(ref, wproj_ref.shape[1])
-
-    def store(b, packed):
-        tile_ref[...] = packed
-
-    compute_stage("first", None, (tile_in,), bias_ref, w_ref, wproj_ref, store, scratch)
+        b = place ^ i
+
+        @pl.when((b >= blocks[0]) & (b <= blocks[-1]))
+        def _(ref=ref, slot=b - blocks[0]):
+            w_ref[slot] = ref[...]
+            wproj_ref[slot] = unpack_projection(ref, wproj_ref.shape[1])
+
+
+def store_halves(place_ref, tile_ref, o_ref, e_ref):
     tokens = tile_ref.shape[0] // 3
-    for ref, flag in ((p_ref, place_ref[4]), (q_ref, place_ref[5])):
+    for ref, flag in ((o_ref, place_ref[2]), (e_ref, place_ref[3])):
         ref[:tokens] = jnp.where(flag == 1, tile_ref[2 * tokens :].astype(jnp.float32),
                                  tile_ref[:tokens].astype(jnp.float32)).astype(jnp.bfloat16)
         ref[tokens:] = tile_ref[tokens : 2 * tokens]
 
 
-def flags_of(place_ref):
-    return (0,) + tuple(place_ref[2 + i] for i in range(4))
-
-
-def whole_kernel(place_ref, t0, t1, t2, t3, t4, w0, w1, w2, w3, bias_ref, last_ref, outs_ref,
-                 w_ref, wproj_ref, *scratch):
+def part_kernel(mode, blocks, tile_count, place_ref, *refs):
+    tiles, refs = refs[:tile_count], refs[tile_count:]
+    weights, bias_ref, refs = refs[:STAGE], refs[STAGE], refs[STAGE + 1 :]
+    outs, refs = refs[: len(blocks)], refs[len(blocks) :]
+    halves = ()
+    if mode != "odd":
+        halves, refs = refs[:2], refs[2:]
+    w_ref, wproj_ref, stage_ref, *scratch = refs
+    gather_weights(place_ref[0], weights, blocks, w_ref, wproj_ref)
+
+    def store(slot, packed):
+        stage_ref[slot] = packed
+
+    flags = (place_ref[2], place_ref[3])
+    compute_blocks(mode, flags, tiles, bias_ref, w_ref, wproj_ref, store, scratch)
+    for i, ref in enumerate(outs):
+        ref[...] = stage_ref[i]
+    if halves:
+        store_halves(place_ref, outs[-1], *halves)
+
+
+def last_kernel(place_ref, *refs):
+    tiles, refs = refs[:3], refs[3:]
+    weights, bias_ref, refs = refs[:STAGE], refs[STAGE], refs[STAGE + 1 :]
+    early, late, refs = refs[:STAGE], refs[STAGE : 2 * STAGE - 1], refs[2 * STAGE - 1 :]
+    outs, refs = refs[:STAGE], refs[STAGE:]
+    w_ref, wproj_ref, stage_ref, *scratch = refs
     place = place_ref[0]
-    gather_weights(place, (w0, w1, w2, w3), w_ref, wproj_ref)
-
-    def store(b, packed):
-        outs_ref[place ^ b] = packed
-
-    compute_stage("whole", flags_of(place_ref), (t0, t1, t2, t3, t4), bias_ref, w_ref, wproj_ref, store, scratch)
-    last_ref[...] = outs_ref[place ^ (STAGE - 1)]
-
-
-def rest_kernel(place_ref, t0, t1, t2, t3, t4, w0, w1, w2, w3, bias_ref, early_ref, o0, o1, o2, o3,
-                outs_ref, w_ref, wproj_ref, *scratch):
-    place = place_ref[0]
-    late = place_ref[1] == 1
-
-    @pl.when(late)
+
+    def route(sources):
+        for i, ref in enumerate(outs):
+            for b, source in enumerate(sources):
+
+                @pl.when((place ^ i) == b)
+                def _(ref=ref, source=source):
+                    ref[...] = source[...]
+
+    @pl.when(place_ref[1] == 1)
     def _():
-        gather_weights(place, (w0, w1, w2, w3), w_ref, wproj_ref)
-
-        def store(b, packed):
-            outs_ref[place ^ b] = packed
-
-        store(0, t0[...])
-        compute_stage("rest", flags_of(place_ref), (t0, t1, t2, t3, t4), bias_ref, w_ref, wproj_ref, store, scratch)
-        for i, ref in enumerate((o0, o1, o2, o3)):
-            ref[...] = outs_ref[i]
-
-    @pl.when(jnp.logical_not(late))
+        gather_weights(place, weights, (STAGE - 1,), w_ref, wproj_ref)
+
+        def store(slot, packed):
+            stage_ref[slot] = packed
+
+        flags = (place_ref[2], place_ref[3])
+        compute_blocks("odd", flags, tiles, bias_ref, w_ref, wproj_ref, store, scratch)
+        route((*late, stage_ref.at[0]))
+
+    @pl.when(place_ref[1] == 0)
     def _():
-        for i, ref in enumerate((o0, o1, o2, o3)):
-            ref[...] = early_ref[i]
-
-
-def run_stage(kernel, place, operands, outs, extra, blocks, tokens, width, bias_shape):
-    halves = 2 * (2 * REACH + 1)
+        route(early)
+
+
+def run_part(kernel, name, place, operands, outs, blocks, tokens, width, bias_shape):
+    halves = 6
     windows, piece, _ = bias_shape
     vmem = pl.BlockSpec(memory_space=pltpu.VMEM)
     bf16, f32 = jnp.bfloat16, jnp.float32
@@ -338,10 +340,10 @@
         out_shape=tuple(jax.ShapeDtypeStruct(shape, bf16) for shape in outs),
         in_specs=[pl.BlockSpec(memory_space=pltpu.SMEM)] + [vmem] * len(operands),
         out_specs=(vmem,) * len(outs),
-        scratch_shapes=[pltpu.VMEM(shape, bf16) for shape in extra]
-        + [
+        scratch_shapes=[
             pltpu.VMEM((blocks, width, 2304), bf16),
             pltpu.VMEM((blocks, width, width), bf16),
+            pltpu.VMEM((blocks, 3 * tokens, LANES), bf16),
             pltpu.VMEM((halves, tokens, width), bf16),
             pltpu.VMEM((halves, tokens, width), bf16),
             pltpu.VMEM((halves, tokens, width), f32),
@@ -351,7 +353,7 @@
             pltpu.VMEM((8, LANES), f32),
         ],
         compiler_params=pltpu.CompilerParams(vmem_limit_bytes=VMEM_LIMIT),
-        name=kernel.__name__,
+        name=name,
     )(place, *operands)
 
 
@@ -395,11 +397,7 @@
     tile_count, section_count = lax.axis_size("tile"), lax.axis_size("section")
     section = lax.axis_index("section")
     tile_index = lax.axis_index("tile")
-    east_of_pair = tile_index % 2 == 0
-    east_of_four = tile_index % 4 < 2
-    place = jnp.stack(
-        [section % STAGE, section // STAGE, ~east_of_pair, east_of_pair, ~east_of_four, east_of_four]
-    ).astype(jnp.int32)
+    place = jnp.stack([section % STAGE, section // STAGE, tile_index % 2, 1 - tile_index % 2]).astype(jnp.int32)
     axes = ("tile", "section")
 
     def exchange(value, bit):
@@ -408,15 +406,14 @@
     def forward(value):
         return lax.ppermute(value, "section", [(s, s + STAGE) for s in range(STAGE)])
 
-    def swap(values, first):
+    def swap(odd_value, even_value, first):
         received = []
-        for value, distance, phase in zip(values, (1, 1, 2, 2), (1, 0, 1, 0)):
+        for value, phase in ((odd_value, 1), (even_value, 0)):
             pairs = []
-            for t in range(tile_count):
-                if t // distance % 2 == phase:
-                    for s in range(first, first + STAGE):
-                        here, there = t * section_count + s, (t + distance) % tile_count * section_count + s
-                        pairs += [(here, there), (there, here)]
+            for t in range(phase, tile_count, 2):
+                for s in range(first, first + STAGE):
+                    here, there = t * section_count + s, (t + 1) % tile_count * section_count + s
+                    pairs += [(here, there), (there, here)]
             received.append(lax.ppermute(value, axes, pairs))
         return received
 
@@ -428,21 +425,21 @@
     pack = pack_weights(w_qkv, w_proj, w_up, w_down.transpose(0, 2, 1))
     near, far = exchange(pack, 1), exchange(pack, 2)
     tile = embed(place, fields, land_mask, land_vector.reshape(1, width))
-    halo = swap((tile,) * 4, 0)
+    halo = swap(tile, tile, 0)
     far, halo = lax.optimization_barrier((far, halo))
     weights = (pack, near, far, exchange(far, 1))
-    stack_shape = (STAGE,) + tile_shape
-
-    last, early = run_stage(
-        whole_kernel, place, (tile, *halo, *weights, bias), (tile_shape, stack_shape), (), STAGE, *sizes
-    )
-    tile, p, q = run_stage(
-        first_kernel, place, (forward(last), *weights, bias), (tile_shape, half_shape, half_shape), (), 1, *sizes
-    )
-    halo = swap((tile, tile, p, q), STAGE)
-    outs = run_stage(
-        rest_kernel, place, (tile, *halo, *weights, bias, early), (tile_shape,) * STAGE, (stack_shape,), STAGE, *sizes
-    )
+
+    def part(mode, name, blocks, tiles):
+        shapes = (tile_shape,) * len(blocks) + (() if mode == "odd" else (half_shape,) * 2)
+        kernel = functools.partial(part_kernel, mode, blocks, len(tiles))
+        return run_part(kernel, name, place, (*tiles, *weights, bias), shapes, len(blocks), *sizes)
+
+    y0, y1, y2, o, e = part("wide even", "blocks_0_2", (0, 1, 2), (tile, *halo))
+    (y3,) = part("odd", "block_3", (3,), (y2, *swap(o, e, 0)))
+    y4, o, e = part("even", "block_4", (0,), (forward(y3),))
+    y5, y6, o, e = part("odd even", "blocks_5_6", (1, 2), (y4, *swap(o, e, STAGE)))
+    operands = (y6, *swap(o, e, STAGE), *weights, bias, y0, y1, y2, y3, y4, y5, y6)
+    outs = run_part(last_kernel, "block_7", place, operands, (tile_shape,) * STAGE, 1, *sizes)
 
     pieces = [outs[0]] + [exchange(outs[i], i) for i in range(1, STAGE)]
     return finish(place, pieces, (1, micro_count, levels, rows, flat_width))

time: 239 us -> 201 us (0.84)
  the two profiles are of different devices: /device:TPU:131 before, /device:TPU:129 now
where the time goes in v7:
time: 201 us
  Pallas kernels  90.6 us (45%)
  waiting for transfers between devices  51.6 us (26%)
  starting transfers between devices  48.3 us (24%)
  local copies, waits for them, and re-layouts  9.14 us (5%)
    pallas_call x5, Pallas kernels, run_part(): pl.pallas_call(kernel, out_shape=tuple((jax.ShapeDtypeStruct(shape, bf16)...  82.3 us
    ppermute x1, waiting for transfers between devices, forward(): lax.ppermute(value, 'section', [(s, s + STAGE) for s in range(STAGE)])  25.6 us
    ppermute x6, starting transfers between devices, exchange(): lax.ppermute(value, 'section', [(s, s ^ bit) for s in range(section_count)])  23.8 us
    ppermute x8, starting transfers between devices, swap(): received.append(lax.ppermute(value, axes, pairs))  23.2 us
    ppermute x6, waiting for transfers between devices, exchange(): lax.ppermute(value, 'section', [(s, s ^ bit) for s in range(section_count)])  17.8 us
    ppermute x8, waiting for transfers between devices, swap(): received.append(lax.ppermute(value, axes, pairs))  8.14 us
    unnamed x38, local copies, waits for them, and re-layouts  6.63 us
  transfers between devices with their start and end apart: 15, of which 9 were waited for; matrix products, arithmetic and copies ran while one was open for 1% of the time, Pallas kernels for 1%

profile of v7, /device:TPU:129, one launch (start us, length us, event | category | flops | bytes accessed | tf_op | source)
XLA Modules:
  0.0 200.5 jit_solution(8451936944644777523)
XLA Ops:
  0.0 2.3 %pack_weights.1.refs_3_.refs_1_ = bf16[192,2304]{1,0:T(8,128)(2,1)} custom-call(bf16[1,192,576]{2,1,0:T(8,128)(2,1)} %wqkv_ref.1, bf16[1,192,192]{2,1,0:T(8,128)(2,1)} %wproj_ref.1, bf16[1,192,768]{2,1,0:T(8,128)(2,1)} %wup_ref.1, bf16[1,192,768]{2,1,0:T(8,128)(2,1)} %bitcast.6), custom_call_target="tpu_custom_call" | custom-call | tf_op jit(solution)/shard_map/pack_weights/pallas_call | solution.py:111
  2.3 4.0 %collective-permute-start = (bf16[192,2304]{1,0:T(8,128)(2,1)}, bf16[192,2304]{1,0:T(8,128)(2,1)S(1)}, u32[]{:S(2)}, u32[]{:S(2)}) collective-permute-start(bf16[192,2304]{1,0:T(8,128)(2,1)} %pack_weights.1.refs_3_.refs_1_), channel_id=1, source_target_pairs={{0,2},{1,3},{2,0},{3,1},{4,6},{5,7},{6,4},{7,5},{8,10},{9,11},{10,... | collective-permute-start | bytes 2654216 | tf_op jit(solution)/shard_map/ppermute | solution.py:404
  6.4 0.0 copy-start.17
  6.4 0.7 copy-done.17
  7.1 0.7 copy.10.mask_ref
  7.7 1.0 copy.9.fields_ref
  8.8 0.6 pad_add_fusion.micro_ref.place_ref
  9.4 2.8 %embed.1.refs_0_ = bf16[648,128]{1,0:T(8,128)(2,1)} custom-call(s32[4]{0:T(128)} %pad_add_fusion.micro_ref.place_ref, bf16[4,2,18,2304]{3,2,1,0:T(8,128)(2,1)} %copy.9.fields_ref, s32[18,12]{1,0:T(8,128)} %copy.10.mask_ref, f32[1,192]{1,0:T(1,128)} %bitcast.7), custom_call_target="tpu_custom_call" | custom-call | tf_op jit(solution)/shard_map/embed/pallas_call | solution.py:80
  12.1 0.7 collective-permute-start.2
  12.8 0.7 collective-permute-start.1
  13.5 2.9 %collective-permute-start.3 = (bf16[192,2304]{1,0:T(8,128)(2,1)S(1)}, bf16[192,2304]{1,0:T(8,128)(2,1)S(1)}, u32[]{:S(2)}, u32[]{:S(2)}) collective-permute-start(bf16[192,2304]{1,0:T(8,128)(2,1)S(1)} %copy-done), channel_id=1, source_target_pairs={{0,1},{1,0},{2,3},{3,2},{4,5},{5,4},{6,7},{7,6},{8,9},{9,8},{10,11... | collective-permute-start | bytes 2654216 | tf_op jit(solution)/shard_map/ppermute | solution.py:404
  16.3 0.0 collective-permute-done.2.refs_2_
  16.4 9.5 %collective-permute-done.refs_5_.refs_3_ = bf16[192,2304]{1,0:T(8,128)(2,1)S(1)} collective-permute-done((bf16[192,2304]{1,0:T(8,128)(2,1)}, bf16[192,2304]{1,0:T(8,128)(2,1)S(1)}, u32[]{:S(2)}, u32[]{:S(2)}) %collective-permute-start) | collective-permute-done | bytes 884768 | tf_op jit(solution)/shard_map/ppermute | solution.py:404
  25.9 3.1 %collective-permute-start.4 = (bf16[192,2304]{1,0:T(8,128)(2,1)S(1)}, bf16[192,2304]{1,0:T(8,128)(2,1)S(1)}, u32[]{:S(2)}, u32[]{:S(2)}) collective-permute-start(bf16[192,2304]{1,0:T(8,128)(2,1)S(1)} %collective-permute-done.refs_5_.refs_3_), channel_id=1, source_target_pairs={{0,1},{1,0},{2,3},{3,2},{4,5},{5,4},{6,7},{7,6},{8,9},{9,8},{10,11... | collective-permute-start | bytes 2654216 | tf_op jit(solution)/shard_map/ppermute | solution.py:404
  29.1 2.0 %collective-permute-done.4.refs_6_.refs_4_ = bf16[192,2304]{1,0:T(8,128)(2,1)S(1)} collective-permute-done((bf16[192,2304]{1,0:T(8,128)(2,1)S(1)}, bf16[192,2304]{1,0:T(8,128)(2,1)S(1)}, u32[]{:S(2)}, u32[]{:S(2)}) %collective-permute-start.4) | collective-permute-done | bytes 884768 | tf_op jit(solution)/shard_map/ppermute | solution.py:404
  31.1 0.9 copy-done.3
  32.0 32.3 %blocks_0_2.1 = (bf16[648,128]{1,0:T(8,128)(2,1)}, bf16[648,128]{1,0:T(8,128)(2,1)}, bf16[648,128]{1,0:T(8,128)(2,1)}, bf16[432,128]{1,0:T(8,128)(2,1)}, bf16[432,128]{1,0:T(8,128)(2,1)}) custom-call(s32[4]{0:T(128)} %pad_add_fusion.micro_ref.place_ref, bf16[648,128]{1,0:T(8,128)(2,1)} %embed.1.refs_0_, bf16[648,128]{1,0:T(8,128)(2,1)} %copy-done.6, ...), custom_call_target="tpu_custom_call" | custom-call | tf_op jit(solution)/shard_map/blocks_0_2/pallas_call | solution.py:338
  64.3 0.7 collective-permute-start.5
  65.0 0.7 collective-permute-start.6
  65.7 0.6 copy-done.15
  66.3 0.0 copy-done.16
  66.3 11.1 %block_3.1.refs_11_ = bf16[648,128]{1,0:T(8,128)(2,1)} custom-call(s32[4]{0:T(128)} %pad_add_fusion.micro_ref.place_ref, bf16[648,128]{1,0:T(8,128)(2,1)} %get-tuple-element.27.refs_0_.refs_10_, bf16[432,128]{1,0:T(8,128)(2,1)} %copy-done.15, bf16[432,128]{1,0:T(8,128)(2,1)} %copy-done.16, bf16[192,2304]{1,0:T(8,128)(2,1)} %pack_weights.1.refs_3_.refs_1_, ...), custom_call_target="tpu_custom_call" | custom-call | tf_op jit(solution)/shard_map/block_3/pallas_call | solution.py:338
  77.5 1.3 collective-permute-start.7
  78.7 25.6 %collective-permute-done.7.refs_0_ = bf16[648,128]{1,0:T(8,128)(2,1)S(1)} collective-permute-done((bf16[648,128]{1,0:T(8,128)(2,1)}, bf16[648,128]{1,0:T(8,128)(2,1)S(1)}, u32[]{:S(2)}, u32[]{:S(2)}) %collective-permute-start.7) | collective-permute-done | bytes 165920 | tf_op jit(solution)/shard_map/ppermute | solution.py:407
  104.3 0.7 copy-done.7
  105.0 9.6 %block_4.1 = (bf16[648,128]{1,0:T(8,128)(2,1)}, bf16[432,128]{1,0:T(8,128)(2,1)}, bf16[432,128]{1,0:T(8,128)(2,1)}) custom-call(s32[4]{0:T(128)} %pad_add_fusion.micro_ref.place_ref, bf16[648,128]{1,0:T(8,128)(2,1)} %copy-done.7, bf16[192,2304]{1,0:T(8,128)(2,1)} %pack_weights.1.refs_3_.refs_1_, bf16[192,2304]{1,0:T(8,128)(2,1)} %copy-done.2, ...), custom_call_target="tpu_custom_call" | custom-call | tf_op jit(solution)/shard_map/block_4/pallas_call | solution.py:338
  114.6 8.8 %collective-permute-start.8 = (bf16[432,128]{1,0:T(8,128)(2,1)}, bf16[432,128]{1,0:T(8,128)(2,1)S(1)}, u32[]{:S(2)}, u32[]{:S(2)}) collective-permute-start(bf16[432,128]{1,0:T(8,128)(2,1)} %get-tuple-element.31), channel_id=1, source_target_pairs={{12,20},{20,12},{13,21},{21,13},{14,22},{22,14},{15,23},{23,15},{2... | collective-permute-start | bytes 331784 | tf_op jit(solution)/shard_map/ppermute | solution.py:417
  123.5 1.9 collective-permute-start.9
  125.4 3.2 %collective-permute-done.8.refs_1_ = bf16[432,128]{1,0:T(8,128)(2,1)S(1)} collective-permute-done((bf16[432,128]{1,0:T(8,128)(2,1)}, bf16[432,128]{1,0:T(8,128)(2,1)S(1)}, u32[]{:S(2)}, u32[]{:S(2)}) %collective-permute-start.8) | collective-permute-done | bytes 110624 | tf_op jit(solution)/shard_map/ppermute | solution.py:417
  128.6 0.9 collective-permute-done.9.refs_2_
  129.5 0.6 copy-done.14
  130.1 17.8 %blocks_5_6.1 = (bf16[648,128]{1,0:T(8,128)(2,1)}, bf16[648,128]{1,0:T(8,128)(2,1)}, bf16[432,128]{1,0:T(8,128)(2,1)}, bf16[432,128]{1,0:T(8,128)(2,1)}) custom-call(s32[4]{0:T(128)} %pad_add_fusion.micro_ref.place_ref, bf16[648,128]{1,0:T(8,128)(2,1)} %get-tuple-element.30.refs_0_.refs_12_, bf16[432,128]{1,0:T(8,128)(2,1)} %copy-done.13, ...), custom_call_target="tpu_custom_call" | custom-call | tf_op jit(solution)/shard_map/blocks_5_6/pallas_call | solution.py:338
  147.9 7.9 %collective-permute-start.10 = (bf16[432,128]{1,0:T(8,128)(2,1)}, bf16[432,128]{1,0:T(8,128)(2,1)S(1)}, u32[]{:S(2)}, u32[]{:S(2)}) collective-permute-start(bf16[432,128]{1,0:T(8,128)(2,1)} %get-tuple-element.34), channel_id=1, source_target_pairs={{12,20},{20,12},{13,21},{21,13},{14,22},{22,14},{15,23},{23,15},{2... | collective-permute-start | bytes 331784 | tf_op jit(solution)/shard_map/ppermute | solution.py:417
  155.8 1.9 collective-permute-start.11
  157.7 4.0 %collective-permute-done.10.refs_1_ = bf16[432,128]{1,0:T(8,128)(2,1)S(1)} collective-permute-done((bf16[432,128]{1,0:T(8,128)(2,1)}, bf16[432,128]{1,0:T(8,128)(2,1)S(1)}, u32[]{:S(2)}, u32[]{:S(2)}) %collective-permute-start.10) | collective-permute-done | bytes 110624 | tf_op jit(solution)/shard_map/ppermute | solution.py:417
  161.7 0.1 collective-permute-done.11.refs_2_
  161.8 0.6 copy-done.11
  162.3 0.1 copy-done.12
  162.4 11.5 %block_7.1 = (bf16[648,128]{1,0:T(8,128)(2,1)}, bf16[648,128]{1,0:T(8,128)(2,1)}, bf16[648,128]{1,0:T(8,128)(2,1)}, bf16[648,128]{1,0:T(8,128)(2,1)}) custom-call(s32[4]{0:T(128)} %pad_add_fusion.micro_ref.place_ref, bf16[648,128]{1,0:T(8,128)(2,1)} %get-tuple-element.33.refs_0_.refs_14_, bf16[432,128]{1,0:T(8,128)(2,1)} %copy-done.11, ...), custom_call_target="tpu_custom_call" | custom-call | tf_op jit(solution)/shard_map/block_7/pallas_call | solution.py:338
  174.0 6.0 %collective-permute-start.12 = (bf16[648,128]{1,0:T(8,128)(2,1)}, bf16[648,128]{1,0:T(8,128)(2,1)S(1)}, u32[]{:S(2)}, u32[]{:S(2)}) collective-permute-start(bf16[648,128]{1,0:T(8,128)(2,1)} %get-tuple-element.40), channel_id=1, source_target_pairs={{0,1},{1,0},{2,3},{3,2},{4,5},{5,4},{6,7},{7,6},{8,9},{9,8},{10,11... | collective-permute-start | bytes 497672 | tf_op jit(solution)/shard_map/ppermute | solution.py:404
  180.0 5.8 %collective-permute-start.13 = (bf16[648,128]{1,0:T(8,128)(2,1)}, bf16[648,128]{1,0:T(8,128)(2,1)S(1)}, u32[]{:S(2)}, u32[]{:S(2)}) collective-permute-start(bf16[648,128]{1,0:T(8,128)(2,1)} %get-tuple-element.41), channel_id=1, source_target_pairs={{0,2},{1,3},{2,0},{3,1},{4,6},{5,7},{6,4},{7,5},{8,10},{9,11},{10,... | collective-permute-start | bytes 497672 | tf_op jit(solution)/shard_map/ppermute | solution.py:404
  185.8 1.9 collective-permute-start.14
  187.8 0.0 copy-start.8
  187.8 2.9 %collective-permute-done.13.o2 = bf16[648,128]{1,0:T(8,128)(2,1)S(1)} collective-permute-done((bf16[648,128]{1,0:T(8,128)(2,1)}, bf16[648,128]{1,0:T(8,128)(2,1)S(1)}, u32[]{:S(2)}, u32[]{:S(2)}) %collective-permute-start.13) | collective-permute-done | bytes 165920 | tf_op jit(solution)/shard_map/ppermute | solution.py:404
  190.6 3.5 %collective-permute-done.14.o3 = bf16[648,128]{1,0:T(8,128)(2,1)S(1)} collective-permute-done((bf16[648,128]{1,0:T(8,128)(2,1)}, bf16[648,128]{1,0:T(8,128)(2,1)S(1)}, u32[]{:S(2)}, u32[]{:S(2)}) %collective-permute-start.14) | collective-permute-done | bytes 165920 | tf_op jit(solution)/shard_map/ppermute | solution.py:404
  194.1 0.7 copy-done.10
  194.8 3.2 %finish.1 = bf16[1,4,2,18,2304]{4,3,2,1,0:T(8,128)(2,1)} custom-call(s32[4]{0:T(128)} %pad_add_fusion.micro_ref.place_ref, bf16[648,128]{1,0:T(8,128)(2,1)} %get-tuple-element.39.o0, bf16[648,128]{1,0:T(8,128)(2,1)} %copy-done.8, bf16[648,128]{1,0:T(8,128)(2,1)} %copy-done.9, bf16[648,128]{1,0:T(8,128)(2,1)} %copy-done.10), custom_call_target="tpu_custom_call" | custom-call | tf_op jit(solution)/shard_map/finish/pallas_call | solution.py:383
  198.0 2.5 %copy.11 = bf16[1,4,2,18,2304]{4,2,3,1,0:T(2,128)(2,1)} copy(bf16[1,4,2,18,2304]{4,3,2,1,0:T(8,128)(2,1)} %finish.1) | data formatting | bytes 1327104 | tf_op jit(solution)/shard_map/finish/pallas_call | solution.py:383
  (30 shorter events, 0.1 us)
Async XLA Ops:
  0.0 7.7 %copy-start.4 = (bf16[4,2,18,2304]{3,1,2,0:T(2,128)(2,1)S(1)}, bf16[4,2,18,2304]{3,1,2,0:T(2,128)(2,1)}, u32[]{:S(2)}) copy-start(bf16[4,2,18,2304]{3,1,2,0:T(2,128)(2,1)} %param.8) | copy-start | bytes 1990660
  2.3 23.6 %collective-permute-start = (bf16[192,2304]{1,0:T(8,128)(2,1)}, bf16[192,2304]{1,0:T(8,128)(2,1)S(1)}, u32[]{:S(2)}, u32[]{:S(2)}) collective-permute-start(bf16[192,2304]{1,0:T(8,128)(2,1)} %pack_weights.1.refs_3_.refs_1_), channel_id=1, source_target_pairs={{0,2},{1,3},{2,0},{3,1},{4,6},{5,7},{6,4},{7,5},{8,10},{9,11},{10,... | collective-permute-start | bytes 2654216 | tf_op jit(solution)/shard_map/ppermute | solution.py:404
  6.4 0.7 copy-start.17
  8.8 4.7 %copy-start = (bf16[192,2304]{1,0:T(8,128)(2,1)S(1)}, bf16[192,2304]{1,0:T(8,128)(2,1)}, u32[]{:S(2)}) copy-start(bf16[192,2304]{1,0:T(8,128)(2,1)} %pack_weights.1.refs_3_.refs_1_) | copy-start | bytes 2654212
  12.1 4.2 %collective-permute-start.2 = (bf16[648,128]{1,0:T(8,128)(2,1)}, bf16[648,128]{1,0:T(8,128)(2,1)S(1)}, u32[]{:S(2)}, u32[]{:S(2)}) collective-permute-start(bf16[648,128]{1,0:T(8,128)(2,1)} %embed.1.refs_0_), channel_id=1, source_target_pairs={{0,8},{8,0},{1,9},{9,1},{2,10},{10,2},{3,11},{11,3},{16,24},{24,16... | collective-permute-start | bytes 497672 | tf_op jit(solution)/shard_map/ppermute | solution.py:417
  12.8 3.6 %collective-permute-start.1 = (bf16[648,128]{1,0:T(8,128)(2,1)}, bf16[648,128]{1,0:T(8,128)(2,1)S(1)}, u32[]{:S(2)}, u32[]{:S(2)}) collective-permute-start(bf16[648,128]{1,0:T(8,128)(2,1)} %embed.1.refs_0_), channel_id=1, source_target_pairs={{8,16},{16,8},{9,17},{17,9},{10,18},{18,10},{11,19},{19,11},{24,32... | collective-permute-start | bytes 497672 | tf_op jit(solution)/shard_map/ppermute | solution.py:417
  13.5 15.6 %collective-permute-start.3 = (bf16[192,2304]{1,0:T(8,128)(2,1)S(1)}, bf16[192,2304]{1,0:T(8,128)(2,1)S(1)}, u32[]{:S(2)}, u32[]{:S(2)}) collective-permute-start(bf16[192,2304]{1,0:T(8,128)(2,1)S(1)} %copy-done), channel_id=1, source_target_pairs={{0,1},{1,0},{2,3},{3,2},{4,5},{5,4},{6,7},{7,6},{8,9},{9,8},{10,11... | collective-permute-start | bytes 2654216 | tf_op jit(solution)/shard_map/ppermute | solution.py:404
  16.4 14.7 %copy-start.5 = (bf16[648,128]{1,0:T(8,128)(2,1)}, bf16[648,128]{1,0:T(8,128)(2,1)S(1)}, u32[]{:S(2)}) copy-start(bf16[648,128]{1,0:T(8,128)(2,1)S(1)} %collective-permute-done.2.refs_2_) | copy-start | bytes 497668
  16.4 14.7 %copy-start.6 = (bf16[648,128]{1,0:T(8,128)(2,1)}, bf16[648,128]{1,0:T(8,128)(2,1)S(1)}, u32[]{:S(2)}) copy-start(bf16[648,128]{1,0:T(8,128)(2,1)S(1)} %collective-permute-done.1.refs_1_) | copy-start | bytes 497668
  25.9 5.2 %copy-start.1 = (bf16[192,2304]{1,0:T(8,128)(2,1)}, bf16[192,2304]{1,0:T(8,128)(2,1)S(1)}, u32[]{:S(2)}) copy-start(bf16[192,2304]{1,0:T(8,128)(2,1)S(1)} %collective-permute-done.refs_5_.refs_3_) | copy-start | bytes 2654212
  25.9 5.2 %collective-permute-start.4 = (bf16[192,2304]{1,0:T(8,128)(2,1)S(1)}, bf16[192,2304]{1,0:T(8,128)(2,1)S(1)}, u32[]{:S(2)}, u32[]{:S(2)}) collective-permute-start(bf16[192,2304]{1,0:T(8,128)(2,1)S(1)} %collective-permute-done.refs_5_.refs_3_), channel_id=1, source_target_pairs={{0,1},{1,0},{2,3},{3,2},{4,5},{5,4},{6,7},{7,6},{8,9},{9,8},{10,11... | collective-permute-start | bytes 2654216 | tf_op jit(solution)/shard_map/ppermute | solution.py:404
  29.0 2.0 %copy-start.2 = (bf16[192,2304]{1,0:T(8,128)(2,1)}, bf16[192,2304]{1,0:T(8,128)(2,1)S(1)}, u32[]{:S(2)}) copy-start(bf16[192,2304]{1,0:T(8,128)(2,1)S(1)} %collective-permute-done.3.refs_4_.refs_2_) | copy-start | bytes 2654212
  31.1 0.9 copy-start.3
  64.3 1.3 collective-permute-start.5
  65.0 0.7 collective-permute-start.6
  65.6 0.7 copy-start.15
  65.7 0.7 copy-start.16
  77.5 26.9 %collective-permute-start.7 = (bf16[648,128]{1,0:T(8,128)(2,1)}, bf16[648,128]{1,0:T(8,128)(2,1)S(1)}, u32[]{:S(2)}, u32[]{:S(2)}) collective-permute-start(bf16[648,128]{1,0:T(8,128)(2,1)} %block_3.1.refs_11_), channel_id=1, source_target_pairs={{0,4},{1,5},{2,6},{3,7},{8,12},{9,13},{10,14},{11,15},{16,20},{17,... | collective-permute-start | bytes 497672 | tf_op jit(solution)/shard_map/ppermute | solution.py:407
  104.3 0.7 copy-start.7
  114.6 13.9 %collective-permute-start.8 = (bf16[432,128]{1,0:T(8,128)(2,1)}, bf16[432,128]{1,0:T(8,128)(2,1)S(1)}, u32[]{:S(2)}, u32[]{:S(2)}) collective-permute-start(bf16[432,128]{1,0:T(8,128)(2,1)} %get-tuple-element.31), channel_id=1, source_target_pairs={{12,20},{20,12},{13,21},{21,13},{14,22},{22,14},{15,23},{23,15},{2... | collective-permute-start | bytes 331784 | tf_op jit(solution)/shard_map/ppermute | solution.py:417
  123.5 6.0 %collective-permute-start.9 = (bf16[432,128]{1,0:T(8,128)(2,1)}, bf16[432,128]{1,0:T(8,128)(2,1)S(1)}, u32[]{:S(2)}, u32[]{:S(2)}) collective-permute-start(bf16[432,128]{1,0:T(8,128)(2,1)} %get-tuple-element.32), channel_id=1, source_target_pairs={{4,12},{12,4},{5,13},{13,5},{6,14},{14,6},{7,15},{15,7},{20,28},{2... | collective-permute-start | bytes 331784 | tf_op jit(solution)/shard_map/ppermute | solution.py:417
  128.6 0.9 copy-start.13
  129.5 0.6 copy-start.14
  147.9 13.8 %collective-permute-start.10 = (bf16[432,128]{1,0:T(8,128)(2,1)}, bf16[432,128]{1,0:T(8,128)(2,1)S(1)}, u32[]{:S(2)}, u32[]{:S(2)}) collective-permute-start(bf16[432,128]{1,0:T(8,128)(2,1)} %get-tuple-element.34), channel_id=1, source_target_pairs={{12,20},{20,12},{13,21},{21,13},{14,22},{22,14},{15,23},{23,15},{2... | collective-permute-start | bytes 331784 | tf_op jit(solution)/shard_map/ppermute | solution.py:417
  155.8 6.0 %collective-permute-start.11 = (bf16[432,128]{1,0:T(8,128)(2,1)}, bf16[432,128]{1,0:T(8,128)(2,1)S(1)}, u32[]{:S(2)}, u32[]{:S(2)}) collective-permute-start(bf16[432,128]{1,0:T(8,128)(2,1)} %get-tuple-element.35), channel_id=1, source_target_pairs={{4,12},{12,4},{5,13},{13,5},{6,14},{14,6},{7,15},{15,7},{20,28},{2... | collective-permute-start | bytes 331784 | tf_op jit(solution)/shard_map/ppermute | solution.py:417
  161.7 0.7 copy-start.11
  161.8 0.6 copy-start.12
  174.0 13.8 %collective-permute-start.12 = (bf16[648,128]{1,0:T(8,128)(2,1)}, bf16[648,128]{1,0:T(8,128)(2,1)S(1)}, u32[]{:S(2)}, u32[]{:S(2)}) collective-permute-start(bf16[648,128]{1,0:T(8,128)(2,1)} %get-tuple-element.40), channel_id=1, source_target_pairs={{0,1},{1,0},{2,3},{3,2},{4,5},{5,4},{6,7},{7,6},{8,9},{9,8},{10,11... | collective-permute-start | bytes 497672 | tf_op jit(solution)/shard_map/ppermute | solution.py:404
  180.0 10.6 %collective-permute-start.13 = (bf16[648,128]{1,0:T(8,128)(2,1)}, bf16[648,128]{1,0:T(8,128)(2,1)S(1)}, u32[]{:S(2)}, u32[]{:S(2)}) collective-permute-start(bf16[648,128]{1,0:T(8,128)(2,1)} %get-tuple-element.41), channel_id=1, source_target_pairs={{0,2},{1,3},{2,0},{3,1},{4,6},{5,7},{6,4},{7,5},{8,10},{9,11},{10,... | collective-permute-start | bytes 497672 | tf_op jit(solution)/shard_map/ppermute | solution.py:404
  185.8 8.3 %collective-permute-start.14 = (bf16[648,128]{1,0:T(8,128)(2,1)}, bf16[648,128]{1,0:T(8,128)(2,1)S(1)}, u32[]{:S(2)}, u32[]{:S(2)}) collective-permute-start(bf16[648,128]{1,0:T(8,128)(2,1)} %get-tuple-element.42), channel_id=1, source_target_pairs={{0,3},{1,2},{2,1},{3,0},{4,7},{5,6},{6,5},{7,4},{8,11},{9,10},{10,... | collective-permute-start | bytes 497672 | tf_op jit(solution)/shard_map/ppermute | solution.py:404
  187.8 6.3 %copy-start.8 = (bf16[648,128]{1,0:T(8,128)(2,1)}, bf16[648,128]{1,0:T(8,128)(2,1)S(1)}, u32[]{:S(2)}) copy-start(bf16[648,128]{1,0:T(8,128)(2,1)S(1)} %collective-permute-done.12.o1) | copy-start | bytes 497668
  190.6 3.5 %copy-start.9 = (bf16[648,128]{1,0:T(8,128)(2,1)}, bf16[648,128]{1,0:T(8,128)(2,1)S(1)}, u32[]{:S(2)}) copy-start(bf16[648,128]{1,0:T(8,128)(2,1)S(1)} %collective-permute-done.13.o2) | copy-start | bytes 497668
  194.1 0.7 copy-start.10

commit v8 on v7

--- a/solution.py
+++ b/solution.py
@@ -16,7 +16,11 @@
 STAGE = 4
 LOG2E = 1.4426950408889634
 LANES = 128
-VMEM_LIMIT = 56 * 2**20
+VMEM_LIMIT = 36 * 2**20
+
+
+def in_vmem(value):
+    return pltpu.with_memory_space_constraint(value, pltpu.VMEM)
 
 
 def normalize(values):
@@ -79,7 +83,7 @@
     whole = lambda a: pl.BlockSpec(a.shape, lambda i, m: (0,) * a.ndim)
     return pl.pallas_call(
         embed_kernel,
-        out_shape=jax.ShapeDtypeStruct((3 * tokens, LANES), jnp.bfloat16),
+        out_shape=pltpu.VMEM((3 * tokens, LANES), jnp.bfloat16),
         grid_spec=pltpu.PrefetchScalarGridSpec(
             num_scalar_prefetch=1,
             grid=(1,),
@@ -110,7 +114,7 @@
     width = weights[0].shape[1]
     return pl.pallas_call(
         pack_kernel,
-        out_shape=jax.ShapeDtypeStruct((width, 2304), jnp.bfloat16),
+        out_shape=pltpu.VMEM((width, 2304), jnp.bfloat16),
         in_specs=[vmem] * len(weights),
         out_specs=vmem,
         compiler_params=pltpu.CompilerParams(vmem_limit_bytes=VMEM_LIMIT),
@@ -149,8 +153,11 @@
             total = jnp.where(channel_head[:, first : first + lanes] == first // head_size + n, parts[n], total)
         return total
 
+    def rows_of(w):
+        return pl.ds(w * piece if isinstance(w, int) else pl.multiple_of(w * piece, 8), piece)
+
     def window_attention(h, i, w, shifted, exact):
-        q = q_ref[h, w * piece : (w + 1) * piece, :]
+        q = q_ref[h, rows_of(w), :]
         qm = jnp.concatenate([jnp.where(channel_head == n, q, 0.0) for n in range(HEADS)], 0).astype(bf16)
         s = lax.dot_general(qm, k_ref[i, w], (((1,), (1,)), ((), ())), preferred_element_type=f32)
         if shifted:
@@ -201,9 +208,20 @@
         def attend(c, carry):
             own = [first_q + together * c + j for j in range(together)]
             x = jnp.concatenate([load(h) for h in own], 0)
-            a = jnp.concatenate(
-                [window_attention(h, (h - first_pair) // 2, w, shifted, exact) for h in own for w in range(windows)], 0
-            ).astype(bf16)
+            if exact:
+
+                def one_window(w, carry):
+                    for h in own:
+                        q_ref[h, rows_of(w), :] = window_attention(h, (h - first_pair) // 2, w, shifted, exact)
+                    return carry
+
+                lax.fori_loop(0, windows, one_window, 0)
+                a = jnp.concatenate([q_ref[h] for h in own], 0).astype(bf16)
+            else:
+                parts = [
+                    window_attention(h, (h - first_pair) // 2, w, shifted, exact) for h in own for w in range(windows)
+                ]
+                a = jnp.concatenate(parts, 0).astype(bf16)
             residual = x + jnp.dot(a, wproj_ref[b], preferred_element_type=f32)
             n2 = normalize(residual).astype(bf16)
             u = jnp.dot(n2, w_ref[b, :, 768 : 768 + hidden], preferred_element_type=f32)
@@ -337,7 +355,7 @@
     bf16, f32 = jnp.bfloat16, jnp.float32
     return pl.pallas_call(
         kernel,
-        out_shape=tuple(jax.ShapeDtypeStruct(shape, bf16) for shape in outs),
+        out_shape=tuple(pltpu.VMEM(shape, bf16) for shape in outs),
         in_specs=[pl.BlockSpec(memory_space=pltpu.SMEM)] + [vmem] * len(operands),
         out_specs=(vmem,) * len(outs),
         scratch_shapes=[
@@ -354,11 +372,11 @@
         ],
         compiler_params=pltpu.CompilerParams(vmem_limit_bytes=VMEM_LIMIT),
         name=name,
-    )(place, *operands)
+    )(place, *[in_vmem(x) for x in operands])
 
 
 def finish_kernel(place_ref, o0, o1, o2, o3, out_ref, grid_ref):
-    _, _, levels, rows, _ = out_ref.shape
+    _, _, rows, levels, _ = out_ref.shape
     tokens = grid_ref.shape[1]
     step = levels * HALF
     width = out_ref.shape[4] // WLON
@@ -368,13 +386,12 @@
         for part in range(3):
             grid_ref[part] = packed[part * tokens : (part + 1) * tokens]
         micro = place_ref[0] ^ i
-        for level in range(levels):
-            for column in range(WLON):
-                half, inside = divmod(column, HALF)
-                at = pl.ds(level * HALF + inside, rows, stride=step)
-                rest = grid_ref[1, at, :][:, half * side : (half + 1) * side]
-                piece = jnp.concatenate([grid_ref[2 * half, at, :], rest], 1)
-                out_ref[0, micro, level, :, column * width : (column + 1) * width] = piece.astype(jnp.bfloat16)
+        for column in range(WLON):
+            half, inside = divmod(column, HALF)
+            at = pl.ds(inside, rows * levels, stride=HALF)
+            rest = grid_ref[1, at, :][:, half * side : (half + 1) * side]
+            piece = jnp.concatenate([grid_ref[2 * half, at, :], rest], 1).reshape(rows, levels, width)
+            out_ref[0, micro, :, :, column * width : (column + 1) * width] = piece.astype(jnp.bfloat16)
 
 
 def finish(place, pieces, shape):
@@ -388,7 +405,7 @@
         scratch_shapes=[pltpu.VMEM((3, tokens, LANES), jnp.float32)],
         compiler_params=pltpu.CompilerParams(vmem_limit_bytes=VMEM_LIMIT),
         name="finish",
-    )(place, *pieces)
+    )(place, *[in_vmem(x) for x in pieces])
 
 
 def on_device(fields, land_mask, land_vector, w_qkv, w_proj, w_up, w_down):
@@ -442,7 +459,7 @@
     outs = run_part(last_kernel, "block_7", place, operands, (tile_shape,) * STAGE, 1, *sizes)
 
     pieces = [outs[0]] + [exchange(outs[i], i) for i in range(1, STAGE)]
-    return finish(place, pieces, (1, micro_count, levels, rows, flat_width))
+    return finish(place, pieces, (1, micro_count, rows, levels, flat_width)).transpose(0, 1, 3, 2, 4)
 
 
 def solution(mesh):

time: 201 us -> 193 us (0.960)
  local copies, waits for them, and re-layouts: 9.14 us -> 5.31 us
  Pallas kernels: 90.6 us -> 87.7 us
    ppermute x1, waiting for transfers between devices: 25.6 us -> 22.2 us  [forward(): lax.ppermute(value, 'section', [(s, s + STAGE) for s in range(STAGE)])]
    pallas_call x7, Pallas kernels: 87.4 us -> 84.7 us  [the longest x5 83.6 us: run_part(): pl.pallas_call(kernel, out_shape=tuple((pltpu.VMEM(shape, bf16) for shape...]
    ppermute x6, waiting for transfers between devices: 17.8 us -> 20.6 us  [exchange(): lax.ppermute(value, 'section', [(s, s ^ bit) for s in range(section_count)])]
    pallas_call x1 -> x0, local copies, waits for them, and re-layouts: 2.52 us -> none  [finish(): pl.pallas_call(finish_kernel, out_shape=jax.ShapeDtypeStruct(shape, jnp.b...]
    unnamed x38 -> x18, local copies, waits for them, and re-layouts: 6.63 us -> 5.31 us
  transfers between devices with their start and end apart: 15 -> 15, of which waited for: 9 -> 9; matrix products, arithmetic and copies ran while one was open for 1% -> 0% of each run, Pallas kernels for 1% -> 1%
where the time goes in v8:
time: 193 us; the launch traced here: 192 us
  Pallas kernels  87.7 us (45%)
  waiting for transfers between devices  50.5 us (26%)
  starting transfers between devices  48.2 us (25%)
  local copies, waits for them, and re-layouts  5.31 us (3%)
    pallas_call x5, Pallas kernels, run_part(): pl.pallas_call(kernel, out_shape=tuple((pltpu.VMEM(shape, bf16) for shape...  83.6 us
    ppermute x6, starting transfers between devices, exchange(): lax.ppermute(value, 'section', [(s, s ^ bit) for s in range(section_count)])  23.6 us
    ppermute x8, starting transfers between devices, swap(): received.append(lax.ppermute(value, axes, pairs))  23.2 us
    ppermute x1, waiting for transfers between devices, forward(): lax.ppermute(value, 'section', [(s, s + STAGE) for s in range(STAGE)])  22.2 us
    ppermute x6, waiting for transfers between devices, exchange(): lax.ppermute(value, 'section', [(s, s ^ bit) for s in range(section_count)])  20.6 us
    ppermute x8, waiting for transfers between devices, swap(): received.append(lax.ppermute(value, axes, pairs))  7.73 us
    unnamed x18, local copies, waits for them, and re-layouts  5.31 us
  transfers between devices with their start and end apart: 15, of which 9 were waited for; matrix products, arithmetic and copies ran while one was open for 0% of the time, Pallas kernels for 1%

profile of v8, /device:TPU:129, one launch (start us, length us, event | category | flops | bytes accessed | tf_op | source)
XLA Modules:
  0.0 192.0 jit_solution(7487288125177872359)
XLA Ops:
  0.0 1.0 copy-done.1
  1.0 1.0 copy-done.2
  1.9 0.9 copy-done.3
  2.9 0.9 copy-done.4
  3.8 0.1 pack_weights.1.refs_3_.refs_1_
  3.9 4.1 %collective-permute-start = (bf16[192,2304]{1,0:T(8,128)(2,1)S(1)}, bf16[192,2304]{1,0:T(8,128)(2,1)S(1)}, u32[]{:S(2)}, u32[]{:S(2)}) collective-permute-start(bf16[192,2304]{1,0:T(8,128)(2,1)S(1)} %pack_weights.1.refs_3_.refs_1_), channel_id=1, source_target_pairs={{0,2},{1,3},{2,0},{3,1},{4,6},{5,7},{6,4},{7,5},{8,10},{9,11},{10,... | collective-permute-start | bytes 2654216 | tf_op jit(solution)/shard_map/ppermute | solution.py:421
  8.0 0.0 copy-start.7
  8.1 0.7 copy-done.7
  8.7 0.1 copy.10.mask_ref
  8.8 0.1 copy.9.fields_ref
  9.0 0.1 pad_add_fusion.micro_ref.place_ref
  9.0 0.7 copy-done.5
  9.7 1.0 embed.1.refs_0_
  10.7 0.7 collective-permute-start.2
  11.4 0.7 collective-permute-start.1
  12.1 2.9 %collective-permute-start.3 = (bf16[192,2304]{1,0:T(8,128)(2,1)S(1)}, bf16[192,2304]{1,0:T(8,128)(2,1)S(1)}, u32[]{:S(2)}, u32[]{:S(2)}) collective-permute-start(bf16[192,2304]{1,0:T(8,128)(2,1)S(1)} %pack_weights.1.refs_3_.refs_1_), channel_id=1, source_target_pairs={{0,1},{1,0},{2,3},{3,2},{4,5},{5,4},{6,7},{7,6},{8,9},{9,8},{10,11... | collective-permute-start | bytes 2654216 | tf_op jit(solution)/shard_map/ppermute | solution.py:421
  14.9 0.0 collective-permute-done.2.refs_2_
  15.0 0.0 collective-permute-done.1.refs_1_
  15.0 12.4 %collective-permute-done.refs_5_.refs_3_ = bf16[192,2304]{1,0:T(8,128)(2,1)S(1)} collective-permute-done((bf16[192,2304]{1,0:T(8,128)(2,1)S(1)}, bf16[192,2304]{1,0:T(8,128)(2,1)S(1)}, u32[]{:S(2)}, u32[]{:S(2)}) %collective-permute-start) | collective-permute-done | bytes 884768 | tf_op jit(solution)/shard_map/ppermute | solution.py:421
  27.4 3.1 %collective-permute-start.4 = (bf16[192,2304]{1,0:T(8,128)(2,1)S(1)}, bf16[192,2304]{1,0:T(8,128)(2,1)S(1)}, u32[]{:S(2)}, u32[]{:S(2)}) collective-permute-start(bf16[192,2304]{1,0:T(8,128)(2,1)S(1)} %collective-permute-done.refs_5_.refs_3_), channel_id=1, source_target_pairs={{0,1},{1,0},{2,3},{3,2},{4,5},{5,4},{6,7},{7,6},{8,9},{9,8},{10,11... | collective-permute-start | bytes 2654216 | tf_op jit(solution)/shard_map/ppermute | solution.py:421
  30.5 0.0 collective-permute-done.3.refs_4_.refs_2_
  30.5 2.0 %collective-permute-done.4.refs_6_.refs_4_ = bf16[192,2304]{1,0:T(8,128)(2,1)S(1)} collective-permute-done((bf16[192,2304]{1,0:T(8,128)(2,1)S(1)}, bf16[192,2304]{1,0:T(8,128)(2,1)S(1)}, u32[]{:S(2)}, u32[]{:S(2)}) %collective-permute-start.4) | collective-permute-done | bytes 884768 | tf_op jit(solution)/shard_map/ppermute | solution.py:421
  32.6 35.8 %blocks_0_2.1 = (bf16[648,128]{1,0:T(8,128)(2,1)S(1)}, bf16[648,128]{1,0:T(8,128)(2,1)S(1)}, bf16[648,128]{1,0:T(8,128)(2,1)S(1)}, bf16[432,128]{1,0:T(8,128)(2,1)S(1)}, bf16[432,128]{1,0:T(8,128)(2,1)S(1)}) custom-call(s32[4]{0:T(128)S(1)} %pad_add_fusion.micro_ref.place_ref, bf16[648,128]{1,0:T(8,128)(2,1)S(1)} %embed.1.refs_0_, ...), custom_call_target="tpu_custom_call" | custom-call | tf_op jit(solution)/shard_map/blocks_0_2/pallas_call | solution.py:356
  68.3 0.7 collective-permute-start.5
  69.0 0.7 collective-permute-start.6
  69.7 0.0 collective-permute-done.5.refs_1_
  69.7 0.0 collective-permute-done.6.refs_2_
  69.7 10.4 %block_3.1.refs_11_ = bf16[648,128]{1,0:T(8,128)(2,1)S(1)} custom-call(s32[4]{0:T(128)S(1)} %pad_add_fusion.micro_ref.place_ref, bf16[648,128]{1,0:T(8,128)(2,1)S(1)} %get-tuple-element.27.refs_0_.refs_10_, bf16[432,128]{1,0:T(8,128)(2,1)S(1)} %collective-permute-done.5.refs_1_, bf16[432,128]{1,0:T(8,128)(2,1)S(1)} %collective-permute-done.6.refs_2_, ...), custom_call_target="tpu_custom_call" | custom-call | tf_op jit(solution)/shard_map/block_3/pallas_call | solution.py:356
  80.1 1.3 collective-permute-start.7
  81.4 22.2 %collective-permute-done.7.refs_0_ = bf16[648,128]{1,0:T(8,128)(2,1)S(1)} collective-permute-done((bf16[648,128]{1,0:T(8,128)(2,1)S(1)}, bf16[648,128]{1,0:T(8,128)(2,1)S(1)}, u32[]{:S(2)}, u32[]{:S(2)}) %collective-permute-start.7) | collective-permute-done | bytes 165920 | tf_op jit(solution)/shard_map/ppermute | solution.py:424
  103.6 8.8 %block_4.1 = (bf16[648,128]{1,0:T(8,128)(2,1)S(1)}, bf16[432,128]{1,0:T(8,128)(2,1)S(1)}, bf16[432,128]{1,0:T(8,128)(2,1)S(1)}) custom-call(s32[4]{0:T(128)S(1)} %pad_add_fusion.micro_ref.place_ref, bf16[648,128]{1,0:T(8,128)(2,1)S(1)} %collective-permute-done.7.refs_0_, bf16[192,2304]{1,0:T(8,128)(2,1)S(1)} %pack_weights.1.refs_3_.refs_1_, ...), custom_call_target="tpu_custom_call" | custom-call | tf_op jit(solution)/shard_map/block_4/pallas_call | solution.py:356
  112.4 8.8 %collective-permute-start.8 = (bf16[432,128]{1,0:T(8,128)(2,1)S(1)}, bf16[432,128]{1,0:T(8,128)(2,1)S(1)}, u32[]{:S(2)}, u32[]{:S(2)}) collective-permute-start(bf16[432,128]{1,0:T(8,128)(2,1)S(1)} %get-tuple-element.31), channel_id=1, source_target_pairs={{12,20},{20,12},{13,21},{21,13},{14,22},{22,14},{15,23},{23,15},{2... | collective-permute-start | bytes 331784 | tf_op jit(solution)/shard_map/ppermute | solution.py:434
  121.2 1.9 %collective-permute-start.9 = (bf16[432,128]{1,0:T(8,128)(2,1)S(1)}, bf16[432,128]{1,0:T(8,128)(2,1)S(1)}, u32[]{:S(2)}, u32[]{:S(2)}) collective-permute-start(bf16[432,128]{1,0:T(8,128)(2,1)S(1)} %get-tuple-element.32), channel_id=1, source_target_pairs={{4,12},{12,4},{5,13},{13,5},{6,14},{14,6},{7,15},{15,7},{20,28},{2... | collective-permute-start | bytes 331784 | tf_op jit(solution)/shard_map/ppermute | solution.py:434
  123.2 3.0 %collective-permute-done.8.refs_1_ = bf16[432,128]{1,0:T(8,128)(2,1)S(1)} collective-permute-done((bf16[432,128]{1,0:T(8,128)(2,1)S(1)}, bf16[432,128]{1,0:T(8,128)(2,1)S(1)}, u32[]{:S(2)}, u32[]{:S(2)}) %collective-permute-start.8) | collective-permute-done | bytes 110624 | tf_op jit(solution)/shard_map/ppermute | solution.py:434
  126.2 0.8 collective-permute-done.9.refs_2_
  127.0 18.3 %blocks_5_6.1 = (bf16[648,128]{1,0:T(8,128)(2,1)S(1)}, bf16[648,128]{1,0:T(8,128)(2,1)S(1)}, bf16[432,128]{1,0:T(8,128)(2,1)S(1)}, bf16[432,128]{1,0:T(8,128)(2,1)S(1)}) custom-call(s32[4]{0:T(128)S(1)} %pad_add_fusion.micro_ref.place_ref, bf16[648,128]{1,0:T(8,128)(2,1)S(1)} %get-tuple-element.30.refs_0_.refs_12_, ...), custom_call_target="tpu_custom_call" | custom-call | tf_op jit(solution)/shard_map/blocks_5_6/pallas_call | solution.py:356
  145.3 7.9 %collective-permute-start.10 = (bf16[432,128]{1,0:T(8,128)(2,1)S(1)}, bf16[432,128]{1,0:T(8,128)(2,1)S(1)}, u32[]{:S(2)}, u32[]{:S(2)}) collective-permute-start(bf16[432,128]{1,0:T(8,128)(2,1)S(1)} %get-tuple-element.34), channel_id=1, source_target_pairs={{12,20},{20,12},{13,21},{21,13},{14,22},{22,14},{15,23},{23,15},{2... | collective-permute-start | bytes 331784 | tf_op jit(solution)/shard_map/ppermute | solution.py:434
  153.3 1.9 %collective-permute-start.11 = (bf16[432,128]{1,0:T(8,128)(2,1)S(1)}, bf16[432,128]{1,0:T(8,128)(2,1)S(1)}, u32[]{:S(2)}, u32[]{:S(2)}) collective-permute-start(bf16[432,128]{1,0:T(8,128)(2,1)S(1)} %get-tuple-element.35), channel_id=1, source_target_pairs={{4,12},{12,4},{5,13},{13,5},{6,14},{14,6},{7,15},{15,7},{20,28},{2... | collective-permute-start | bytes 331784 | tf_op jit(solution)/shard_map/ppermute | solution.py:434
  155.2 3.7 %collective-permute-done.10.refs_1_ = bf16[432,128]{1,0:T(8,128)(2,1)S(1)} collective-permute-done((bf16[432,128]{1,0:T(8,128)(2,1)S(1)}, bf16[432,128]{1,0:T(8,128)(2,1)S(1)}, u32[]{:S(2)}, u32[]{:S(2)}) %collective-permute-start.10) | collective-permute-done | bytes 110624 | tf_op jit(solution)/shard_map/ppermute | solution.py:434
  159.0 0.1 collective-permute-done.11.refs_2_
  159.1 10.3 %block_7.1 = (bf16[648,128]{1,0:T(8,128)(2,1)S(1)}, bf16[648,128]{1,0:T(8,128)(2,1)S(1)}, bf16[648,128]{1,0:T(8,128)(2,1)S(1)}, bf16[648,128]{1,0:T(8,128)(2,1)S(1)}) custom-call(s32[4]{0:T(128)S(1)} %pad_add_fusion.micro_ref.place_ref, bf16[648,128]{1,0:T(8,128)(2,1)S(1)} %get-tuple-element.33.refs_0_.refs_14_, ...), custom_call_target="tpu_custom_call" | custom-call | tf_op jit(solution)/shard_map/block_7/pallas_call | solution.py:356
  169.4 6.0 %collective-permute-start.12 = (bf16[648,128]{1,0:T(8,128)(2,1)S(1)}, bf16[648,128]{1,0:T(8,128)(2,1)S(1)}, u32[]{:S(2)}, u32[]{:S(2)}) collective-permute-start(bf16[648,128]{1,0:T(8,128)(2,1)S(1)} %get-tuple-element.40), channel_id=1, source_target_pairs={{0,1},{1,0},{2,3},{3,2},{4,5},{5,4},{6,7},{7,6},{8,9},{9,8},{10,11... | collective-permute-start | bytes 497672 | tf_op jit(solution)/shard_map/ppermute | solution.py:421
  175.4 5.6 %collective-permute-start.13 = (bf16[648,128]{1,0:T(8,128)(2,1)S(1)}, bf16[648,128]{1,0:T(8,128)(2,1)S(1)}, u32[]{:S(2)}, u32[]{:S(2)}) collective-permute-start(bf16[648,128]{1,0:T(8,128)(2,1)S(1)} %get-tuple-element.41), channel_id=1, source_target_pairs={{0,2},{1,3},{2,0},{3,1},{4,6},{5,7},{6,4},{7,5},{8,10},{9,11},{10,... | collective-permute-start | bytes 497672 | tf_op jit(solution)/shard_map/ppermute | solution.py:421
  181.0 1.9 %collective-permute-start.14 = (bf16[648,128]{1,0:T(8,128)(2,1)S(1)}, bf16[648,128]{1,0:T(8,128)(2,1)S(1)}, u32[]{:S(2)}, u32[]{:S(2)}) collective-permute-start(bf16[648,128]{1,0:T(8,128)(2,1)S(1)} %get-tuple-element.42), channel_id=1, source_target_pairs={{0,3},{1,2},{2,1},{3,0},{4,7},{5,6},{6,5},{7,4},{8,11},{9,10},{10,... | collective-permute-start | bytes 497672 | tf_op jit(solution)/shard_map/ppermute | solution.py:421
  182.9 0.0 collective-permute-done.12.o1
  182.9 2.7 %collective-permute-done.13.o2 = bf16[648,128]{1,0:T(8,128)(2,1)S(1)} collective-permute-done((bf16[648,128]{1,0:T(8,128)(2,1)S(1)}, bf16[648,128]{1,0:T(8,128)(2,1)S(1)}, u32[]{:S(2)}, u32[]{:S(2)}) %collective-permute-start.13) | collective-permute-done | bytes 165920 | tf_op jit(solution)/shard_map/ppermute | solution.py:421
  185.6 3.5 %collective-permute-done.14.o3 = bf16[648,128]{1,0:T(8,128)(2,1)S(1)} collective-permute-done((bf16[648,128]{1,0:T(8,128)(2,1)S(1)}, bf16[648,128]{1,0:T(8,128)(2,1)S(1)}, u32[]{:S(2)}, u32[]{:S(2)}) %collective-permute-start.14) | collective-permute-done | bytes 165920 | tf_op jit(solution)/shard_map/ppermute | solution.py:421
  189.0 3.0 %finish.1 = bf16[1,4,18,2,2304]{4,3,2,1,0:T(2,128)(2,1)} custom-call(s32[4]{0:T(128)S(1)} %pad_add_fusion.micro_ref.place_ref, bf16[648,128]{1,0:T(8,128)(2,1)S(1)} %get-tuple-element.39.o0, bf16[648,128]{1,0:T(8,128)(2,1)S(1)} %collective-permute-done.12.o1, bf16[648,128]{1,0:T(8,128)(2,1)S(1)} %collective-permute-done.13.o2, ...), custom_call_target="tpu_custom_call" | custom-call | tf_op jit(solution)/shard_map/finish/pallas_call | solution.py:400
  (9 shorter events, 0.0 us)
Async XLA Ops:
  0.0 1.0 copy-start.1
  1.0 1.0 copy-start.2
  1.9 0.9 copy-start.3
  2.9 0.9 copy-start.4
  3.8 5.1 %copy-start.6 = (bf16[4,2,18,2304]{3,1,2,0:T(2,128)(2,1)S(1)}, bf16[4,2,18,2304]{3,1,2,0:T(2,128)(2,1)}, u32[]{:S(2)}) copy-start(bf16[4,2,18,2304]{3,1,2,0:T(2,128)(2,1)} %param.8) | copy-start | bytes 1990660
  3.9 23.5 %collective-permute-start = (bf16[192,2304]{1,0:T(8,128)(2,1)S(1)}, bf16[192,2304]{1,0:T(8,128)(2,1)S(1)}, u32[]{:S(2)}, u32[]{:S(2)}) collective-permute-start(bf16[192,2304]{1,0:T(8,128)(2,1)S(1)} %pack_weights.1.refs_3_.refs_1_), channel_id=1, source_target_pairs={{0,2},{1,3},{2,0},{3,1},{4,6},{5,7},{6,4},{7,5},{8,10},{9,11},{10,... | collective-permute-start | bytes 2654216 | tf_op jit(solution)/shard_map/ppermute | solution.py:421
  8.0 0.7 copy-start.7
  9.0 0.7 copy-start.5
  9.7 22.8 %copy-start = (f32[3,72,144]{2,1,0:T(8,128)S(1)}, f32[3,72,144]{2,1,0:T(8,128)}, u32[]{:S(2)}) copy-start(f32[3,72,144]{2,1,0:T(8,128)} %constant.48.clone.refs_7_.refs_5_) | copy-start | bytes 373252
  10.7 4.2 %collective-permute-start.2 = (bf16[648,128]{1,0:T(8,128)(2,1)S(1)}, bf16[648,128]{1,0:T(8,128)(2,1)S(1)}, u32[]{:S(2)}, u32[]{:S(2)}) collective-permute-start(bf16[648,128]{1,0:T(8,128)(2,1)S(1)} %embed.1.refs_0_), channel_id=1, source_target_pairs={{0,8},{8,0},{1,9},{9,1},{2,10},{10,2},{3,11},{11,3},{16,24},{24,16... | collective-permute-start | bytes 497672 | tf_op jit(solution)/shard_map/ppermute | solution.py:434
  11.4 3.6 %collective-permute-start.1 = (bf16[648,128]{1,0:T(8,128)(2,1)S(1)}, bf16[648,128]{1,0:T(8,128)(2,1)S(1)}, u32[]{:S(2)}, u32[]{:S(2)}) collective-permute-start(bf16[648,128]{1,0:T(8,128)(2,1)S(1)} %embed.1.refs_0_), channel_id=1, source_target_pairs={{8,16},{16,8},{9,17},{17,9},{10,18},{18,10},{11,19},{19,11},{24,32... | collective-permute-start | bytes 497672 | tf_op jit(solution)/shard_map/ppermute | solution.py:434
  12.1 18.4 %collective-permute-start.3 = (bf16[192,2304]{1,0:T(8,128)(2,1)S(1)}, bf16[192,2304]{1,0:T(8,128)(2,1)S(1)}, u32[]{:S(2)}, u32[]{:S(2)}) collective-permute-start(bf16[192,2304]{1,0:T(8,128)(2,1)S(1)} %pack_weights.1.refs_3_.refs_1_), channel_id=1, source_target_pairs={{0,1},{1,0},{2,3},{3,2},{4,5},{5,4},{6,7},{7,6},{8,9},{9,8},{10,11... | collective-permute-start | bytes 2654216 | tf_op jit(solution)/shard_map/ppermute | solution.py:421
  27.4 5.2 %collective-permute-start.4 = (bf16[192,2304]{1,0:T(8,128)(2,1)S(1)}, bf16[192,2304]{1,0:T(8,128)(2,1)S(1)}, u32[]{:S(2)}, u32[]{:S(2)}) collective-permute-start(bf16[192,2304]{1,0:T(8,128)(2,1)S(1)} %collective-permute-done.refs_5_.refs_3_), channel_id=1, source_target_pairs={{0,1},{1,0},{2,3},{3,2},{4,5},{5,4},{6,7},{7,6},{8,9},{9,8},{10,11... | collective-permute-start | bytes 2654216 | tf_op jit(solution)/shard_map/ppermute | solution.py:421
  68.3 1.4 collective-permute-start.5
  69.0 0.7 collective-permute-start.6
  80.1 23.5 %collective-permute-start.7 = (bf16[648,128]{1,0:T(8,128)(2,1)S(1)}, bf16[648,128]{1,0:T(8,128)(2,1)S(1)}, u32[]{:S(2)}, u32[]{:S(2)}) collective-permute-start(bf16[648,128]{1,0:T(8,128)(2,1)S(1)} %block_3.1.refs_11_), channel_id=1, source_target_pairs={{0,4},{1,5},{2,6},{3,7},{8,12},{9,13},{10,14},{11,15},{16,20},{17,... | collective-permute-start | bytes 497672 | tf_op jit(solution)/shard_map/ppermute | solution.py:424
  112.4 13.7 %collective-permute-start.8 = (bf16[432,128]{1,0:T(8,128)(2,1)S(1)}, bf16[432,128]{1,0:T(8,128)(2,1)S(1)}, u32[]{:S(2)}, u32[]{:S(2)}) collective-permute-start(bf16[432,128]{1,0:T(8,128)(2,1)S(1)} %get-tuple-element.31), channel_id=1, source_target_pairs={{12,20},{20,12},{13,21},{21,13},{14,22},{22,14},{15,23},{23,15},{2... | collective-permute-start | bytes 331784 | tf_op jit(solution)/shard_map/ppermute | solution.py:434
  121.2 5.8 %collective-permute-start.9 = (bf16[432,128]{1,0:T(8,128)(2,1)S(1)}, bf16[432,128]{1,0:T(8,128)(2,1)S(1)}, u32[]{:S(2)}, u32[]{:S(2)}) collective-permute-start(bf16[432,128]{1,0:T(8,128)(2,1)S(1)} %get-tuple-element.32), channel_id=1, source_target_pairs={{4,12},{12,4},{5,13},{13,5},{6,14},{14,6},{7,15},{15,7},{20,28},{2... | collective-permute-start | bytes 331784 | tf_op jit(solution)/shard_map/ppermute | solution.py:434
  145.3 13.6 %collective-permute-start.10 = (bf16[432,128]{1,0:T(8,128)(2,1)S(1)}, bf16[432,128]{1,0:T(8,128)(2,1)S(1)}, u32[]{:S(2)}, u32[]{:S(2)}) collective-permute-start(bf16[432,128]{1,0:T(8,128)(2,1)S(1)} %get-tuple-element.34), channel_id=1, source_target_pairs={{12,20},{20,12},{13,21},{21,13},{14,22},{22,14},{15,23},{23,15},{2... | collective-permute-start | bytes 331784 | tf_op jit(solution)/shard_map/ppermute | solution.py:434
  153.3 5.8 %collective-permute-start.11 = (bf16[432,128]{1,0:T(8,128)(2,1)S(1)}, bf16[432,128]{1,0:T(8,128)(2,1)S(1)}, u32[]{:S(2)}, u32[]{:S(2)}) collective-permute-start(bf16[432,128]{1,0:T(8,128)(2,1)S(1)} %get-tuple-element.35), channel_id=1, source_target_pairs={{4,12},{12,4},{5,13},{13,5},{6,14},{14,6},{7,15},{15,7},{20,28},{2... | collective-permute-start | bytes 331784 | tf_op jit(solution)/shard_map/ppermute | solution.py:434
  169.4 13.5 %collective-permute-start.12 = (bf16[648,128]{1,0:T(8,128)(2,1)S(1)}, bf16[648,128]{1,0:T(8,128)(2,1)S(1)}, u32[]{:S(2)}, u32[]{:S(2)}) collective-permute-start(bf16[648,128]{1,0:T(8,128)(2,1)S(1)} %get-tuple-element.40), channel_id=1, source_target_pairs={{0,1},{1,0},{2,3},{3,2},{4,5},{5,4},{6,7},{7,6},{8,9},{9,8},{10,11... | collective-permute-start | bytes 497672 | tf_op jit(solution)/shard_map/ppermute | solution.py:421
  175.4 10.2 %collective-permute-start.13 = (bf16[648,128]{1,0:T(8,128)(2,1)S(1)}, bf16[648,128]{1,0:T(8,128)(2,1)S(1)}, u32[]{:S(2)}, u32[]{:S(2)}) collective-permute-start(bf16[648,128]{1,0:T(8,128)(2,1)S(1)} %get-tuple-element.41), channel_id=1, source_target_pairs={{0,2},{1,3},{2,0},{3,1},{4,6},{5,7},{6,4},{7,5},{8,10},{9,11},{10,... | collective-permute-start | bytes 497672 | tf_op jit(solution)/shard_map/ppermute | solution.py:421
  181.0 8.0 %collective-permute-start.14 = (bf16[648,128]{1,0:T(8,128)(2,1)S(1)}, bf16[648,128]{1,0:T(8,128)(2,1)S(1)}, u32[]{:S(2)}, u32[]{:S(2)}) collective-permute-start(bf16[648,128]{1,0:T(8,128)(2,1)S(1)} %get-tuple-element.42), channel_id=1, source_target_pairs={{0,3},{1,2},{2,1},{3,0},{4,7},{5,6},{6,5},{7,4},{8,11},{9,10},{10,... | collective-permute-start | bytes 497672 | tf_op jit(solution)/shard_map/ppermute | solution.py:421

commit v9 on v8

--- a/solution.py
+++ b/solution.py
@@ -119,7 +119,7 @@
         out_specs=vmem,
         compiler_params=pltpu.CompilerParams(vmem_limit_bytes=VMEM_LIMIT),
         name="pack_weights",
-    )(*weights)
+    )(*[pltpu.with_memory_space_constraint(w, pltpu.HBM) for w in weights])
 
 
 def compute_blocks(mode, flags, tile_refs, bias_ref, w_ref, wproj_ref, store, scratch):
@@ -375,37 +375,46 @@
     )(place, *[in_vmem(x) for x in operands])
 
 
-def finish_kernel(place_ref, o0, o1, o2, o3, out_ref, grid_ref):
+def finish_kernel(count, place_ref, *refs):
+    out_ref, grid_ref = refs[-2:]
     _, _, rows, levels, _ = out_ref.shape
     tokens = grid_ref.shape[1]
-    step = levels * HALF
     width = out_ref.shape[4] // WLON
     side = width - LANES
-    for i, ref in enumerate((o0, o1, o2, o3)):
-        packed = ref[...].astype(jnp.float32)
-        for part in range(3):
-            grid_ref[part] = packed[part * tokens : (part + 1) * tokens]
-        micro = place_ref[0] ^ i
-        for column in range(WLON):
-            half, inside = divmod(column, HALF)
-            at = pl.ds(inside, rows * levels, stride=HALF)
-            rest = grid_ref[1, at, :][:, half * side : (half + 1) * side]
-            piece = jnp.concatenate([grid_ref[2 * half, at, :], rest], 1).reshape(rows, levels, width)
-            out_ref[0, micro, :, :, column * width : (column + 1) * width] = piece.astype(jnp.bfloat16)
-
-
-def finish(place, pieces, shape):
+    for i, ref in enumerate(refs[:count]):
+
+        @pl.when(pl.program_id(0) == i)
+        def _(ref=ref):
+            packed = ref[...].astype(jnp.float32)
+            for part in range(3):
+                grid_ref[part] = packed[part * tokens : (part + 1) * tokens]
+            for column in range(WLON):
+                half, inside = divmod(column, HALF)
+                at = pl.ds(inside, rows * levels, stride=HALF)
+                rest = grid_ref[1, at, :][:, half * side : (half + 1) * side]
+                piece = jnp.concatenate([grid_ref[2 * half, at, :], rest], 1).reshape(rows, levels, width)
+                out_ref[0, 0, :, :, column * width : (column + 1) * width] = piece.astype(jnp.bfloat16)
+
+
+def finish(place, pieces, first, shape, buffer=None):
     tokens = pieces[0].shape[0] // 3
+    count = len(pieces)
     vmem = pl.BlockSpec(memory_space=pltpu.VMEM)
+    more = [] if buffer is None else [buffer]
     return pl.pallas_call(
-        finish_kernel,
+        functools.partial(finish_kernel, count),
         out_shape=jax.ShapeDtypeStruct(shape, jnp.bfloat16),
-        in_specs=[pl.BlockSpec(memory_space=pltpu.SMEM)] + [vmem] * len(pieces),
-        out_specs=vmem,
-        scratch_shapes=[pltpu.VMEM((3, tokens, LANES), jnp.float32)],
+        grid_spec=pltpu.PrefetchScalarGridSpec(
+            num_scalar_prefetch=1,
+            grid=(count,),
+            in_specs=[vmem] * count + [pl.BlockSpec(memory_space=pl.ANY)] * len(more),
+            out_specs=pl.BlockSpec((1, 1) + shape[2:], lambda i, m: (0, m[0] ^ (first + i), 0, 0, 0)),
+            scratch_shapes=[pltpu.VMEM((3, tokens, LANES), jnp.float32)],
+        ),
+        input_output_aliases={1 + count: 0} if more else {},
         compiler_params=pltpu.CompilerParams(vmem_limit_bytes=VMEM_LIMIT),
         name="finish",
-    )(place, *[in_vmem(x) for x in pieces])
+    )(place, *[in_vmem(x) for x in pieces], *more)
 
 
 def on_device(fields, land_mask, land_vector, w_qkv, w_proj, w_up, w_down):
@@ -458,8 +467,11 @@
     operands = (y6, *swap(o, e, STAGE), *weights, bias, y0, y1, y2, y3, y4, y5, y6)
     outs = run_part(last_kernel, "block_7", place, operands, (tile_shape,) * STAGE, 1, *sizes)
 
-    pieces = [outs[0]] + [exchange(outs[i], i) for i in range(1, STAGE)]
-    return finish(place, pieces, (1, micro_count, rows, levels, flat_width)).transpose(0, 1, 3, 2, 4)
+    across = [exchange(outs[i], i) for i in (2, 3)]
+    mate = exchange(outs[1], 1)
+    shape = (1, micro_count, rows, levels, flat_width)
+    result = finish(place, [outs[0], mate], 0, shape)
+    return finish(place, across, 2, shape, result).transpose(0, 1, 3, 2, 4)
 
 
 def solution(mesh):

time: 193 us -> 189 us (0.979)
  local copies, waits for them, and re-layouts: 5.31 us -> 1.55 us
  Pallas kernels: 87.7 us -> 89.7 us
    unnamed x18 -> x10, local copies, waits for them, and re-layouts: 5.31 us -> 1.55 us
  transfers between devices with their start and end apart: 15 -> 15, of which waited for: 9 -> 9; matrix products, arithmetic and copies ran while one was open for 0% -> 0% of each run, Pallas kernels for 1% -> 2%
where the time goes in v9:
time: 189 us; the launch traced here: 188 us
  Pallas kernels  89.7 us (47%)
  waiting for transfers between devices  48.7 us (26%)
  starting transfers between devices  47.9 us (25%)
    pallas_call x5, Pallas kernels, run_part(): pl.pallas_call(kernel, out_shape=tuple((pltpu.VMEM(shape, bf16) for shape...  83.6 us
    ppermute x6, starting transfers between devices, exchange(): lax.ppermute(value, 'section', [(s, s ^ bit) for s in range(section_count)])  23.3 us
    ppermute x8, starting transfers between devices, swap(): received.append(lax.ppermute(value, axes, pairs))  23.2 us
    ppermute x1, waiting for transfers between devices, forward(): lax.ppermute(value, 'section', [(s, s + STAGE) for s in range(STAGE)])  22.3 us
    ppermute x6, waiting for transfers between devices, exchange(): lax.ppermute(value, 'section', [(s, s ^ bit) for s in range(section_count)])  18.7 us
    ppermute x8, waiting for transfers between devices, swap(): received.append(lax.ppermute(value, axes, pairs))  7.73 us
  transfers between devices with their start and end apart: 15, of which 9 were waited for; matrix products, arithmetic and copies ran while one was open for 0% of the time, Pallas kernels for 2%

profile of v9, /device:TPU:129, one launch (start us, length us, event | category | flops | bytes accessed | tf_op | source)
XLA Modules:
  0.0 188.2 jit_solution(17289317500437723976)
XLA Ops:
  0.0 0.0 copy-start.2
  0.0 1.4 pack_weights.1.refs_3_.refs_1_
  1.4 4.0 %collective-permute-start = (bf16[192,2304]{1,0:T(8,128)(2,1)S(1)}, bf16[192,2304]{1,0:T(8,128)(2,1)S(1)}, u32[]{:S(2)}, u32[]{:S(2)}) collective-permute-start(bf16[192,2304]{1,0:T(8,128)(2,1)S(1)} %pack_weights.1.refs_3_.refs_1_), channel_id=1, source_target_pairs={{0,2},{1,3},{2,0},{3,1},{4,6},{5,7},{6,4},{7,5},{8,10},{9,11},{10,... | collective-permute-start | bytes 2654216 | tf_op jit(solution)/shard_map/ppermute | solution.py:430
  5.5 0.0 copy-start.3
  5.5 0.7 copy-done.3
  6.2 0.1 copy.11.mask_ref
  6.3 0.0 copy-done.2
  6.3 0.1 copy.10.fields_ref
  6.4 0.1 pad_add_fusion.micro_ref.place_ref
  6.5 0.7 copy-done.1
  7.1 1.0 embed.1.refs_0_
  8.1 0.7 collective-permute-start.2
  8.8 0.7 collective-permute-start.1
  9.5 2.9 %collective-permute-start.3 = (bf16[192,2304]{1,0:T(8,128)(2,1)S(1)}, bf16[192,2304]{1,0:T(8,128)(2,1)S(1)}, u32[]{:S(2)}, u32[]{:S(2)}) collective-permute-start(bf16[192,2304]{1,0:T(8,128)(2,1)S(1)} %pack_weights.1.refs_3_.refs_1_), channel_id=1, source_target_pairs={{0,1},{1,0},{2,3},{3,2},{4,5},{5,4},{6,7},{7,6},{8,9},{9,8},{10,11... | collective-permute-start | bytes 2654216 | tf_op jit(solution)/shard_map/ppermute | solution.py:430
  12.4 0.0 collective-permute-done.2.refs_2_
  12.4 0.0 collective-permute-done.1.refs_1_
  12.4 12.4 %collective-permute-done.refs_5_.refs_3_ = bf16[192,2304]{1,0:T(8,128)(2,1)S(1)} collective-permute-done((bf16[192,2304]{1,0:T(8,128)(2,1)S(1)}, bf16[192,2304]{1,0:T(8,128)(2,1)S(1)}, u32[]{:S(2)}, u32[]{:S(2)}) %collective-permute-start) | collective-permute-done | bytes 884768 | tf_op jit(solution)/shard_map/ppermute | solution.py:430
  24.8 3.1 %collective-permute-start.4 = (bf16[192,2304]{1,0:T(8,128)(2,1)S(1)}, bf16[192,2304]{1,0:T(8,128)(2,1)S(1)}, u32[]{:S(2)}, u32[]{:S(2)}) collective-permute-start(bf16[192,2304]{1,0:T(8,128)(2,1)S(1)} %collective-permute-done.refs_5_.refs_3_), channel_id=1, source_target_pairs={{0,1},{1,0},{2,3},{3,2},{4,5},{5,4},{6,7},{7,6},{8,9},{9,8},{10,11... | collective-permute-start | bytes 2654216 | tf_op jit(solution)/shard_map/ppermute | solution.py:430
  27.9 0.0 collective-permute-done.3.refs_4_.refs_2_
  28.0 2.0 %collective-permute-done.4.refs_6_.refs_4_ = bf16[192,2304]{1,0:T(8,128)(2,1)S(1)} collective-permute-done((bf16[192,2304]{1,0:T(8,128)(2,1)S(1)}, bf16[192,2304]{1,0:T(8,128)(2,1)S(1)}, u32[]{:S(2)}, u32[]{:S(2)}) %collective-permute-start.4) | collective-permute-done | bytes 884768 | tf_op jit(solution)/shard_map/ppermute | solution.py:430
  30.0 0.0 copy-done
  30.0 35.8 %blocks_0_2.1 = (bf16[648,128]{1,0:T(8,128)(2,1)S(1)}, bf16[648,128]{1,0:T(8,128)(2,1)S(1)}, bf16[648,128]{1,0:T(8,128)(2,1)S(1)}, bf16[432,128]{1,0:T(8,128)(2,1)S(1)}, bf16[432,128]{1,0:T(8,128)(2,1)S(1)}) custom-call(s32[4]{0:T(128)S(1)} %pad_add_fusion.micro_ref.place_ref, bf16[648,128]{1,0:T(8,128)(2,1)S(1)} %embed.1.refs_0_, ...), custom_call_target="tpu_custom_call" | custom-call | tf_op jit(solution)/shard_map/blocks_0_2/pallas_call | solution.py:356
  65.7 0.7 collective-permute-start.5
  66.4 0.7 collective-permute-start.6
  67.1 0.0 collective-permute-done.5.refs_1_
  67.1 0.0 collective-permute-done.6.refs_2_
  67.1 10.4 %block_3.1.refs_11_ = bf16[648,128]{1,0:T(8,128)(2,1)S(1)} custom-call(s32[4]{0:T(128)S(1)} %pad_add_fusion.micro_ref.place_ref, bf16[648,128]{1,0:T(8,128)(2,1)S(1)} %get-tuple-element.27.refs_0_.refs_10_, bf16[432,128]{1,0:T(8,128)(2,1)S(1)} %collective-permute-done.5.refs_1_, bf16[432,128]{1,0:T(8,128)(2,1)S(1)} %collective-permute-done.6.refs_2_, ...), custom_call_target="tpu_custom_call" | custom-call | tf_op jit(solution)/shard_map/block_3/pallas_call | solution.py:356
  77.5 1.3 collective-permute-start.7
  78.8 22.3 %collective-permute-done.7.refs_0_ = bf16[648,128]{1,0:T(8,128)(2,1)S(1)} collective-permute-done((bf16[648,128]{1,0:T(8,128)(2,1)S(1)}, bf16[648,128]{1,0:T(8,128)(2,1)S(1)}, u32[]{:S(2)}, u32[]{:S(2)}) %collective-permute-start.7) | collective-permute-done | bytes 165920 | tf_op jit(solution)/shard_map/ppermute | solution.py:433
  101.1 8.8 %block_4.1 = (bf16[648,128]{1,0:T(8,128)(2,1)S(1)}, bf16[432,128]{1,0:T(8,128)(2,1)S(1)}, bf16[432,128]{1,0:T(8,128)(2,1)S(1)}) custom-call(s32[4]{0:T(128)S(1)} %pad_add_fusion.micro_ref.place_ref, bf16[648,128]{1,0:T(8,128)(2,1)S(1)} %collective-permute-done.7.refs_0_, bf16[192,2304]{1,0:T(8,128)(2,1)S(1)} %pack_weights.1.refs_3_.refs_1_, ...), custom_call_target="tpu_custom_call" | custom-call | tf_op jit(solution)/shard_map/block_4/pallas_call | solution.py:356
  109.9 8.8 %collective-permute-start.8 = (bf16[432,128]{1,0:T(8,128)(2,1)S(1)}, bf16[432,128]{1,0:T(8,128)(2,1)S(1)}, u32[]{:S(2)}, u32[]{:S(2)}) collective-permute-start(bf16[432,128]{1,0:T(8,128)(2,1)S(1)} %get-tuple-element.31), channel_id=1, source_target_pairs={{12,20},{20,12},{13,21},{21,13},{14,22},{22,14},{15,23},{23,15},{2... | collective-permute-start | bytes 331784 | tf_op jit(solution)/shard_map/ppermute | solution.py:443
  118.7 1.9 %collective-permute-start.9 = (bf16[432,128]{1,0:T(8,128)(2,1)S(1)}, bf16[432,128]{1,0:T(8,128)(2,1)S(1)}, u32[]{:S(2)}, u32[]{:S(2)}) collective-permute-start(bf16[432,128]{1,0:T(8,128)(2,1)S(1)} %get-tuple-element.32), channel_id=1, source_target_pairs={{4,12},{12,4},{5,13},{13,5},{6,14},{14,6},{7,15},{15,7},{20,28},{2... | collective-permute-start | bytes 331784 | tf_op jit(solution)/shard_map/ppermute | solution.py:443
  120.6 3.0 %collective-permute-done.8.refs_1_ = bf16[432,128]{1,0:T(8,128)(2,1)S(1)} collective-permute-done((bf16[432,128]{1,0:T(8,128)(2,1)S(1)}, bf16[432,128]{1,0:T(8,128)(2,1)S(1)}, u32[]{:S(2)}, u32[]{:S(2)}) %collective-permute-start.8) | collective-permute-done | bytes 110624 | tf_op jit(solution)/shard_map/ppermute | solution.py:443
  123.6 0.9 collective-permute-done.9.refs_2_
  124.5 18.3 %blocks_5_6.1 = (bf16[648,128]{1,0:T(8,128)(2,1)S(1)}, bf16[648,128]{1,0:T(8,128)(2,1)S(1)}, bf16[432,128]{1,0:T(8,128)(2,1)S(1)}, bf16[432,128]{1,0:T(8,128)(2,1)S(1)}) custom-call(s32[4]{0:T(128)S(1)} %pad_add_fusion.micro_ref.place_ref, bf16[648,128]{1,0:T(8,128)(2,1)S(1)} %get-tuple-element.30.refs_0_.refs_12_, ...), custom_call_target="tpu_custom_call" | custom-call | tf_op jit(solution)/shard_map/blocks_5_6/pallas_call | solution.py:356
  142.8 7.9 %collective-permute-start.10 = (bf16[432,128]{1,0:T(8,128)(2,1)S(1)}, bf16[432,128]{1,0:T(8,128)(2,1)S(1)}, u32[]{:S(2)}, u32[]{:S(2)}) collective-permute-start(bf16[432,128]{1,0:T(8,128)(2,1)S(1)} %get-tuple-element.34), channel_id=1, source_target_pairs={{12,20},{20,12},{13,21},{21,13},{14,22},{22,14},{15,23},{23,15},{2... | collective-permute-start | bytes 331784 | tf_op jit(solution)/shard_map/ppermute | solution.py:443
  150.8 1.9 %collective-permute-start.11 = (bf16[432,128]{1,0:T(8,128)(2,1)S(1)}, bf16[432,128]{1,0:T(8,128)(2,1)S(1)}, u32[]{:S(2)}, u32[]{:S(2)}) collective-permute-start(bf16[432,128]{1,0:T(8,128)(2,1)S(1)} %get-tuple-element.35), channel_id=1, source_target_pairs={{4,12},{12,4},{5,13},{13,5},{6,14},{14,6},{7,15},{15,7},{20,28},{2... | collective-permute-start | bytes 331784 | tf_op jit(solution)/shard_map/ppermute | solution.py:443
  152.7 3.8 %collective-permute-done.10.refs_1_ = bf16[432,128]{1,0:T(8,128)(2,1)S(1)} collective-permute-done((bf16[432,128]{1,0:T(8,128)(2,1)S(1)}, bf16[432,128]{1,0:T(8,128)(2,1)S(1)}, u32[]{:S(2)}, u32[]{:S(2)}) %collective-permute-start.10) | collective-permute-done | bytes 110624 | tf_op jit(solution)/shard_map/ppermute | solution.py:443
  156.5 0.1 collective-permute-done.11.refs_2_
  156.6 10.3 %block_7.1 = (bf16[648,128]{1,0:T(8,128)(2,1)S(1)}, bf16[648,128]{1,0:T(8,128)(2,1)S(1)}, bf16[648,128]{1,0:T(8,128)(2,1)S(1)}, bf16[648,128]{1,0:T(8,128)(2,1)S(1)}) custom-call(s32[4]{0:T(128)S(1)} %pad_add_fusion.micro_ref.place_ref, bf16[648,128]{1,0:T(8,128)(2,1)S(1)} %get-tuple-element.33.refs_0_.refs_14_, ...), custom_call_target="tpu_custom_call" | custom-call | tf_op jit(solution)/shard_map/block_7/pallas_call | solution.py:356
  166.9 6.0 %collective-permute-start.14 = (bf16[648,128]{1,0:T(8,128)(2,1)S(1)}, bf16[648,128]{1,0:T(8,128)(2,1)S(1)}, u32[]{:S(2)}, u32[]{:S(2)}) collective-permute-start(bf16[648,128]{1,0:T(8,128)(2,1)S(1)} %get-tuple-element.42), channel_id=1, source_target_pairs={{0,1},{1,0},{2,3},{3,2},{4,5},{5,4},{6,7},{7,6},{8,9},{9,8},{10,11... | collective-permute-start | bytes 497672 | tf_op jit(solution)/shard_map/ppermute | solution.py:430
  172.9 5.4 %collective-permute-start.12 = (bf16[648,128]{1,0:T(8,128)(2,1)S(1)}, bf16[648,128]{1,0:T(8,128)(2,1)S(1)}, u32[]{:S(2)}, u32[]{:S(2)}) collective-permute-start(bf16[648,128]{1,0:T(8,128)(2,1)S(1)} %get-tuple-element.39), channel_id=1, source_target_pairs={{0,2},{1,3},{2,0},{3,1},{4,6},{5,7},{6,4},{7,5},{8,10},{9,11},{10,... | collective-permute-start | bytes 497672 | tf_op jit(solution)/shard_map/ppermute | solution.py:430
  178.3 1.9 %collective-permute-start.13 = (bf16[648,128]{1,0:T(8,128)(2,1)S(1)}, bf16[648,128]{1,0:T(8,128)(2,1)S(1)}, u32[]{:S(2)}, u32[]{:S(2)}) collective-permute-start(bf16[648,128]{1,0:T(8,128)(2,1)S(1)} %get-tuple-element.40), channel_id=1, source_target_pairs={{0,3},{1,2},{2,1},{3,0},{4,7},{5,6},{6,5},{7,4},{8,11},{9,10},{10,... | collective-permute-start | bytes 497672 | tf_op jit(solution)/shard_map/ppermute | solution.py:430
  180.3 0.0 collective-permute-done.14.refs_1_
  180.3 1.8 finish.2.refs_2_
  182.1 0.8 collective-permute-done.12.refs_0_
  182.9 3.5 %collective-permute-done.13.refs_1_ = bf16[648,128]{1,0:T(8,128)(2,1)S(1)} collective-permute-done((bf16[648,128]{1,0:T(8,128)(2,1)S(1)}, bf16[648,128]{1,0:T(8,128)(2,1)S(1)}, u32[]{:S(2)}, u32[]{:S(2)}) %collective-permute-start.13) | collective-permute-done | bytes 165920 | tf_op jit(solution)/shard_map/ppermute | solution.py:430
  186.4 1.8 finish.3
  (2 shorter events, 0.0 us)
Async XLA Ops:
  0.0 6.3 %copy-start.2 = (bf16[4,2,18,2304]{3,1,2,0:T(2,128)(2,1)S(1)}, bf16[4,2,18,2304]{3,1,2,0:T(2,128)(2,1)}, u32[]{:S(2)}) copy-start(bf16[4,2,18,2304]{3,1,2,0:T(2,128)(2,1)} %param.8) | copy-start | bytes 1990660
  1.4 23.4 %collective-permute-start = (bf16[192,2304]{1,0:T(8,128)(2,1)S(1)}, bf16[192,2304]{1,0:T(8,128)(2,1)S(1)}, u32[]{:S(2)}, u32[]{:S(2)}) collective-permute-start(bf16[192,2304]{1,0:T(8,128)(2,1)S(1)} %pack_weights.1.refs_3_.refs_1_), channel_id=1, source_target_pairs={{0,2},{1,3},{2,0},{3,1},{4,6},{5,7},{6,4},{7,5},{8,10},{9,11},{10,... | collective-permute-start | bytes 2654216 | tf_op jit(solution)/shard_map/ppermute | solution.py:430
  5.5 0.7 copy-start.3
  6.5 0.7 copy-start.1
  7.1 22.8 %copy-start = (f32[3,72,144]{2,1,0:T(8,128)S(1)}, f32[3,72,144]{2,1,0:T(8,128)}, u32[]{:S(2)}) copy-start(f32[3,72,144]{2,1,0:T(8,128)} %constant.48.clone.refs_7_.refs_5_) | copy-start | bytes 373252
  8.1 4.2 %collective-permute-start.2 = (bf16[648,128]{1,0:T(8,128)(2,1)S(1)}, bf16[648,128]{1,0:T(8,128)(2,1)S(1)}, u32[]{:S(2)}, u32[]{:S(2)}) collective-permute-start(bf16[648,128]{1,0:T(8,128)(2,1)S(1)} %embed.1.refs_0_), channel_id=1, source_target_pairs={{0,8},{8,0},{1,9},{9,1},{2,10},{10,2},{3,11},{11,3},{16,24},{24,16... | collective-permute-start | bytes 497672 | tf_op jit(solution)/shard_map/ppermute | solution.py:443
  8.8 3.6 %collective-permute-start.1 = (bf16[648,128]{1,0:T(8,128)(2,1)S(1)}, bf16[648,128]{1,0:T(8,128)(2,1)S(1)}, u32[]{:S(2)}, u32[]{:S(2)}) collective-permute-start(bf16[648,128]{1,0:T(8,128)(2,1)S(1)} %embed.1.refs_0_), channel_id=1, source_target_pairs={{8,16},{16,8},{9,17},{17,9},{10,18},{18,10},{11,19},{19,11},{24,32... | collective-permute-start | bytes 497672 | tf_op jit(solution)/shard_map/ppermute | solution.py:443
  9.5 18.4 %collective-permute-start.3 = (bf16[192,2304]{1,0:T(8,128)(2,1)S(1)}, bf16[192,2304]{1,0:T(8,128)(2,1)S(1)}, u32[]{:S(2)}, u32[]{:S(2)}) collective-permute-start(bf16[192,2304]{1,0:T(8,128)(2,1)S(1)} %pack_weights.1.refs_3_.refs_1_), channel_id=1, source_target_pairs={{0,1},{1,0},{2,3},{3,2},{4,5},{5,4},{6,7},{7,6},{8,9},{9,8},{10,11... | collective-permute-start | bytes 2654216 | tf_op jit(solution)/shard_map/ppermute | solution.py:430
  24.8 5.2 %collective-permute-start.4 = (bf16[192,2304]{1,0:T(8,128)(2,1)S(1)}, bf16[192,2304]{1,0:T(8,128)(2,1)S(1)}, u32[]{:S(2)}, u32[]{:S(2)}) collective-permute-start(bf16[192,2304]{1,0:T(8,128)(2,1)S(1)} %collective-permute-done.refs_5_.refs_3_), channel_id=1, source_target_pairs={{0,1},{1,0},{2,3},{3,2},{4,5},{5,4},{6,7},{7,6},{8,9},{9,8},{10,11... | collective-permute-start | bytes 2654216 | tf_op jit(solution)/shard_map/ppermute | solution.py:430
  65.7 1.4 collective-permute-start.5
  66.4 0.7 collective-permute-start.6
  77.5 23.6 %collective-permute-start.7 = (bf16[648,128]{1,0:T(8,128)(2,1)S(1)}, bf16[648,128]{1,0:T(8,128)(2,1)S(1)}, u32[]{:S(2)}, u32[]{:S(2)}) collective-permute-start(bf16[648,128]{1,0:T(8,128)(2,1)S(1)} %block_3.1.refs_11_), channel_id=1, source_target_pairs={{0,4},{1,5},{2,6},{3,7},{8,12},{9,13},{10,14},{11,15},{16,20},{17,... | collective-permute-start | bytes 497672 | tf_op jit(solution)/shard_map/ppermute | solution.py:433
  109.9 13.7 %collective-permute-start.8 = (bf16[432,128]{1,0:T(8,128)(2,1)S(1)}, bf16[432,128]{1,0:T(8,128)(2,1)S(1)}, u32[]{:S(2)}, u32[]{:S(2)}) collective-permute-start(bf16[432,128]{1,0:T(8,128)(2,1)S(1)} %get-tuple-element.31), channel_id=1, source_target_pairs={{12,20},{20,12},{13,21},{21,13},{14,22},{22,14},{15,23},{23,15},{2... | collective-permute-start | bytes 331784 | tf_op jit(solution)/shard_map/ppermute | solution.py:443
  118.7 5.8 %collective-permute-start.9 = (bf16[432,128]{1,0:T(8,128)(2,1)S(1)}, bf16[432,128]{1,0:T(8,128)(2,1)S(1)}, u32[]{:S(2)}, u32[]{:S(2)}) collective-permute-start(bf16[432,128]{1,0:T(8,128)(2,1)S(1)} %get-tuple-element.32), channel_id=1, source_target_pairs={{4,12},{12,4},{5,13},{13,5},{6,14},{14,6},{7,15},{15,7},{20,28},{2... | collective-permute-start | bytes 331784 | tf_op jit(solution)/shard_map/ppermute | solution.py:443
  142.8 13.6 %collective-permute-start.10 = (bf16[432,128]{1,0:T(8,128)(2,1)S(1)}, bf16[432,128]{1,0:T(8,128)(2,1)S(1)}, u32[]{:S(2)}, u32[]{:S(2)}) collective-permute-start(bf16[432,128]{1,0:T(8,128)(2,1)S(1)} %get-tuple-element.34), channel_id=1, source_target_pairs={{12,20},{20,12},{13,21},{21,13},{14,22},{22,14},{15,23},{23,15},{2... | collective-permute-start | bytes 331784 | tf_op jit(solution)/shard_map/ppermute | solution.py:443
  150.8 5.8 %collective-permute-start.11 = (bf16[432,128]{1,0:T(8,128)(2,1)S(1)}, bf16[432,128]{1,0:T(8,128)(2,1)S(1)}, u32[]{:S(2)}, u32[]{:S(2)}) collective-permute-start(bf16[432,128]{1,0:T(8,128)(2,1)S(1)} %get-tuple-element.35), channel_id=1, source_target_pairs={{4,12},{12,4},{5,13},{13,5},{6,14},{14,6},{7,15},{15,7},{20,28},{2... | collective-permute-start | bytes 331784 | tf_op jit(solution)/shard_map/ppermute | solution.py:443
  166.9 13.4 %collective-permute-start.14 = (bf16[648,128]{1,0:T(8,128)(2,1)S(1)}, bf16[648,128]{1,0:T(8,128)(2,1)S(1)}, u32[]{:S(2)}, u32[]{:S(2)}) collective-permute-start(bf16[648,128]{1,0:T(8,128)(2,1)S(1)} %get-tuple-element.42), channel_id=1, source_target_pairs={{0,1},{1,0},{2,3},{3,2},{4,5},{5,4},{6,7},{7,6},{8,9},{9,8},{10,11... | collective-permute-start | bytes 497672 | tf_op jit(solution)/shard_map/ppermute | solution.py:430
  172.9 10.0 %collective-permute-start.12 = (bf16[648,128]{1,0:T(8,128)(2,1)S(1)}, bf16[648,128]{1,0:T(8,128)(2,1)S(1)}, u32[]{:S(2)}, u32[]{:S(2)}) collective-permute-start(bf16[648,128]{1,0:T(8,128)(2,1)S(1)} %get-tuple-element.39), channel_id=1, source_target_pairs={{0,2},{1,3},{2,0},{3,1},{4,6},{5,7},{6,4},{7,5},{8,10},{9,11},{10,... | collective-permute-start | bytes 497672 | tf_op jit(solution)/shard_map/ppermute | solution.py:430
  178.3 8.0 %collective-permute-start.13 = (bf16[648,128]{1,0:T(8,128)(2,1)S(1)}, bf16[648,128]{1,0:T(8,128)(2,1)S(1)}, u32[]{:S(2)}, u32[]{:S(2)}) collective-permute-start(bf16[648,128]{1,0:T(8,128)(2,1)S(1)} %get-tuple-element.40), channel_id=1, source_target_pairs={{0,3},{1,2},{2,1},{3,0},{4,7},{5,6},{6,5},{7,4},{8,11},{9,10},{10,... | collective-permute-start | bytes 497672 | tf_op jit(solution)/shard_map/ppermute | solution.py:430

commit v10 on v9

--- a/solution.py
+++ b/solution.py
@@ -308,7 +308,7 @@
     def store(slot, packed):
         stage_ref[slot] = packed
 
-    flags = (place_ref[2], place_ref[3])
+    flags = (place_ref[3], place_ref[2])
     compute_blocks(mode, flags, tiles, bias_ref, w_ref, wproj_ref, store, scratch)
     for i, ref in enumerate(outs):
         ref[...] = stage_ref[i]
@@ -339,7 +339,7 @@
         def store(slot, packed):
             stage_ref[slot] = packed
 
-        flags = (place_ref[2], place_ref[3])
+        flags = (place_ref[3], place_ref[2])
         compute_blocks("odd", flags, tiles, bias_ref, w_ref, wproj_ref, store, scratch)
         route((*late, stage_ref.at[0]))
 
@@ -396,7 +396,7 @@
                 out_ref[0, 0, :, :, column * width : (column + 1) * width] = piece.astype(jnp.bfloat16)
 
 
-def finish(place, pieces, first, shape, buffer=None):
+def finish(place, pieces, first, step, shape, buffer=None):
     tokens = pieces[0].shape[0] // 3
     count = len(pieces)
     vmem = pl.BlockSpec(memory_space=pltpu.VMEM)
@@ -408,7 +408,7 @@
             num_scalar_prefetch=1,
             grid=(count,),
             in_specs=[vmem] * count + [pl.BlockSpec(memory_space=pl.ANY)] * len(more),
-            out_specs=pl.BlockSpec((1, 1) + shape[2:], lambda i, m: (0, m[0] ^ (first + i), 0, 0, 0)),
+            out_specs=pl.BlockSpec((1, 1) + shape[2:], lambda i, m: (0, m[0] ^ (first + i * step), 0, 0, 0)),
             scratch_shapes=[pltpu.VMEM((3, tokens, LANES), jnp.float32)],
         ),
         input_output_aliases={1 + count: 0} if more else {},
@@ -432,16 +432,16 @@
     def forward(value):
         return lax.ppermute(value, "section", [(s, s + STAGE) for s in range(STAGE)])
 
-    def swap(odd_value, even_value, first):
-        received = []
-        for value, phase in ((odd_value, 1), (even_value, 0)):
+    def swap(odd_value, even_value, first, fields_first=False):
+        received = {}
+        for value, phase in ((odd_value, 1), (even_value, 0))[:: 1 if fields_first else -1]:
             pairs = []
             for t in range(phase, tile_count, 2):
                 for s in range(first, first + STAGE):
                     here, there = t * section_count + s, (t + 1) % tile_count * section_count + s
                     pairs += [(here, there), (there, here)]
-            received.append(lax.ppermute(value, axes, pairs))
-        return received
+            received[phase] = lax.ppermute(value, axes, pairs)
+        return received[0], received[1]
 
     tokens = rows * levels * HALF
     tile_shape, half_shape = (3 * tokens, LANES), (2 * tokens, LANES)
@@ -451,7 +451,7 @@
     pack = pack_weights(w_qkv, w_proj, w_up, w_down.transpose(0, 2, 1))
     near, far = exchange(pack, 1), exchange(pack, 2)
     tile = embed(place, fields, land_mask, land_vector.reshape(1, width))
-    halo = swap(tile, tile, 0)
+    halo = swap(tile, tile, 0, True)
     far, halo = lax.optimization_barrier((far, halo))
     weights = (pack, near, far, exchange(far, 1))
 
@@ -467,11 +467,10 @@
     operands = (y6, *swap(o, e, STAGE), *weights, bias, y0, y1, y2, y3, y4, y5, y6)
     outs = run_part(last_kernel, "block_7", place, operands, (tile_shape,) * STAGE, 1, *sizes)
 
-    across = [exchange(outs[i], i) for i in (2, 3)]
-    mate = exchange(outs[1], 1)
+    diagonal, far_piece, mate = (exchange(outs[i], i) for i in (3, 2, 1))
     shape = (1, micro_count, rows, levels, flat_width)
-    result = finish(place, [outs[0], mate], 0, shape)
-    return finish(place, across, 2, shape, result).transpose(0, 1, 3, 2, 4)
+    result = finish(place, [outs[0], diagonal], 0, 3, shape)
+    return finish(place, [mate, far_piece], 1, 1, shape, result).transpose(0, 1, 3, 2, 4)
 
 
 def solution(mesh):

time: 189 us -> 191 us (1.011)
  starting transfers between devices: 47.9 us -> 51.7 us
  waiting for transfers between devices: 48.7 us -> 46.7 us
    ppermute x8, starting transfers between devices: 23.2 us -> 26.6 us  [swap(): received[phase] = lax.ppermute(value, axes, pairs)]
  transfers between devices with their start and end apart: 15 -> 15, of which waited for: 9 -> 6; matrix products, arithmetic and copies ran while one was open for 0% -> 0% of each run, Pallas kernels for 2% -> 1%
where the time goes in v10:
time: 191 us; the launch traced here: 190 us
  Pallas kernels  89.7 us (47%)
  starting transfers between devices  51.7 us (27%)
  waiting for transfers between devices  46.7 us (24%)
    pallas_call x5, Pallas kernels, run_part(): pl.pallas_call(kernel, out_shape=tuple((pltpu.VMEM(shape, bf16) for shape...  83.6 us
    ppermute x8, starting transfers between devices, swap(): received[phase] = lax.ppermute(value, axes, pairs)  26.6 us
    ppermute x6, starting transfers between devices, exchange(): lax.ppermute(value, 'section', [(s, s ^ bit) for s in range(section_count)])  23.9 us
    ppermute x1, waiting for transfers between devices, forward(): lax.ppermute(value, 'section', [(s, s + STAGE) for s in range(STAGE)])  21.6 us
    ppermute x6, waiting for transfers between devices, exchange(): lax.ppermute(value, 'section', [(s, s ^ bit) for s in range(section_count)])  17.8 us
    ppermute x8, waiting for transfers between devices, swap(): received[phase] = lax.ppermute(value, axes, pairs)  7.26 us
  transfers between devices with their start and end apart: 15, of which 6 were waited for; matrix products, arithmetic and copies ran while one was open for 0% of the time, Pallas kernels for 1%

profile of v10, /device:TPU:129, one launch (start us, length us, event | category | flops | bytes accessed | tf_op | source)
XLA Modules:
  0.0 190.0 jit_solution(14743671044790342994)
XLA Ops:
  0.0 0.0 copy-start.2
  0.0 1.4 pack_weights.1.refs_3_.refs_1_
  1.4 4.0 %collective-permute-start = (bf16[192,2304]{1,0:T(8,128)(2,1)S(1)}, bf16[192,2304]{1,0:T(8,128)(2,1)S(1)}, u32[]{:S(2)}, u32[]{:S(2)}) collective-permute-start(bf16[192,2304]{1,0:T(8,128)(2,1)S(1)} %pack_weights.1.refs_3_.refs_1_), channel_id=1, source_target_pairs={{0,2},{1,3},{2,0},{3,1},{4,6},{5,7},{6,4},{7,5},{8,10},{9,11},{10,... | collective-permute-start | bytes 2654216 | tf_op jit(solution)/shard_map/ppermute | solution.py:430
  5.5 0.0 copy-start.3
  5.5 0.7 copy-done.3
  6.2 0.1 copy.11.mask_ref
  6.3 0.0 copy-done.2
  6.3 0.1 copy.10.fields_ref
  6.4 0.1 pad_add_fusion.micro_ref.place_ref
  6.5 0.7 copy-done.1
  7.1 1.0 embed.1.refs_0_
  8.1 0.7 collective-permute-start.2
  8.8 0.7 collective-permute-start.1
  9.5 2.9 %collective-permute-start.3 = (bf16[192,2304]{1,0:T(8,128)(2,1)S(1)}, bf16[192,2304]{1,0:T(8,128)(2,1)S(1)}, u32[]{:S(2)}, u32[]{:S(2)}) collective-permute-start(bf16[192,2304]{1,0:T(8,128)(2,1)S(1)} %pack_weights.1.refs_3_.refs_1_), channel_id=1, source_target_pairs={{0,1},{1,0},{2,3},{3,2},{4,5},{5,4},{6,7},{7,6},{8,9},{9,8},{10,11... | collective-permute-start | bytes 2654216 | tf_op jit(solution)/shard_map/ppermute | solution.py:430
  12.4 0.0 collective-permute-done.2.refs_2_
  12.4 0.0 collective-permute-done.1.refs_1_
  12.4 12.4 %collective-permute-done.refs_5_.refs_3_ = bf16[192,2304]{1,0:T(8,128)(2,1)S(1)} collective-permute-done((bf16[192,2304]{1,0:T(8,128)(2,1)S(1)}, bf16[192,2304]{1,0:T(8,128)(2,1)S(1)}, u32[]{:S(2)}, u32[]{:S(2)}) %collective-permute-start) | collective-permute-done | bytes 884768 | tf_op jit(solution)/shard_map/ppermute | solution.py:430
  24.8 3.1 %collective-permute-start.4 = (bf16[192,2304]{1,0:T(8,128)(2,1)S(1)}, bf16[192,2304]{1,0:T(8,128)(2,1)S(1)}, u32[]{:S(2)}, u32[]{:S(2)}) collective-permute-start(bf16[192,2304]{1,0:T(8,128)(2,1)S(1)} %collective-permute-done.refs_5_.refs_3_), channel_id=1, source_target_pairs={{0,1},{1,0},{2,3},{3,2},{4,5},{5,4},{6,7},{7,6},{8,9},{9,8},{10,11... | collective-permute-start | bytes 2654216 | tf_op jit(solution)/shard_map/ppermute | solution.py:430
  27.9 0.0 collective-permute-done.3.refs_4_.refs_2_
  28.0 2.0 %collective-permute-done.4.refs_6_.refs_4_ = bf16[192,2304]{1,0:T(8,128)(2,1)S(1)} collective-permute-done((bf16[192,2304]{1,0:T(8,128)(2,1)S(1)}, bf16[192,2304]{1,0:T(8,128)(2,1)S(1)}, u32[]{:S(2)}, u32[]{:S(2)}) %collective-permute-start.4) | collective-permute-done | bytes 884768 | tf_op jit(solution)/shard_map/ppermute | solution.py:430
  30.0 0.0 copy-done
  30.0 35.8 %blocks_0_2.1 = (bf16[648,128]{1,0:T(8,128)(2,1)S(1)}, bf16[648,128]{1,0:T(8,128)(2,1)S(1)}, bf16[648,128]{1,0:T(8,128)(2,1)S(1)}, bf16[432,128]{1,0:T(8,128)(2,1)S(1)}, bf16[432,128]{1,0:T(8,128)(2,1)S(1)}) custom-call(s32[4]{0:T(128)S(1)} %pad_add_fusion.micro_ref.place_ref, bf16[648,128]{1,0:T(8,128)(2,1)S(1)} %embed.1.refs_0_, ...), custom_call_target="tpu_custom_call" | custom-call | tf_op jit(solution)/shard_map/blocks_0_2/pallas_call | solution.py:356
  65.7 0.7 collective-permute-start.5
  66.4 0.7 collective-permute-start.6
  67.1 0.0 collective-permute-done.5.refs_1_
  67.1 0.0 collective-permute-done.6.refs_2_
  67.1 10.4 %block_3.1.refs_11_ = bf16[648,128]{1,0:T(8,128)(2,1)S(1)} custom-call(s32[4]{0:T(128)S(1)} %pad_add_fusion.micro_ref.place_ref, bf16[648,128]{1,0:T(8,128)(2,1)S(1)} %get-tuple-element.27.refs_0_.refs_10_, bf16[432,128]{1,0:T(8,128)(2,1)S(1)} %collective-permute-done.5.refs_1_, bf16[432,128]{1,0:T(8,128)(2,1)S(1)} %collective-permute-done.6.refs_2_, ...), custom_call_target="tpu_custom_call" | custom-call | tf_op jit(solution)/shard_map/block_3/pallas_call | solution.py:356
  77.5 1.3 collective-permute-start.7
  78.8 21.6 %collective-permute-done.7.refs_0_ = bf16[648,128]{1,0:T(8,128)(2,1)S(1)} collective-permute-done((bf16[648,128]{1,0:T(8,128)(2,1)S(1)}, bf16[648,128]{1,0:T(8,128)(2,1)S(1)}, u32[]{:S(2)}, u32[]{:S(2)}) %collective-permute-start.7) | collective-permute-done | bytes 165920 | tf_op jit(solution)/shard_map/ppermute | solution.py:433
  100.4 8.8 %block_4.1 = (bf16[648,128]{1,0:T(8,128)(2,1)S(1)}, bf16[432,128]{1,0:T(8,128)(2,1)S(1)}, bf16[432,128]{1,0:T(8,128)(2,1)S(1)}) custom-call(s32[4]{0:T(128)S(1)} %pad_add_fusion.micro_ref.place_ref, bf16[648,128]{1,0:T(8,128)(2,1)S(1)} %collective-permute-done.7.refs_0_, bf16[192,2304]{1,0:T(8,128)(2,1)S(1)} %pack_weights.1.refs_3_.refs_1_, ...), custom_call_target="tpu_custom_call" | custom-call | tf_op jit(solution)/shard_map/block_4/pallas_call | solution.py:356
  109.3 1.9 %collective-permute-start.8 = (bf16[432,128]{1,0:T(8,128)(2,1)S(1)}, bf16[432,128]{1,0:T(8,128)(2,1)S(1)}, u32[]{:S(2)}, u32[]{:S(2)}) collective-permute-start(bf16[432,128]{1,0:T(8,128)(2,1)S(1)} %get-tuple-element.31), channel_id=1, source_target_pairs={{4,12},{12,4},{5,13},{13,5},{6,14},{14,6},{7,15},{15,7},{20,28},{2... | collective-permute-start | bytes 331784 | tf_op jit(solution)/shard_map/ppermute | solution.py:443
  111.2 10.0 %collective-permute-start.9 = (bf16[432,128]{1,0:T(8,128)(2,1)S(1)}, bf16[432,128]{1,0:T(8,128)(2,1)S(1)}, u32[]{:S(2)}, u32[]{:S(2)}) collective-permute-start(bf16[432,128]{1,0:T(8,128)(2,1)S(1)} %get-tuple-element.32), channel_id=1, source_target_pairs={{12,20},{20,12},{13,21},{21,13},{14,22},{22,14},{15,23},{23,15},{2... | collective-permute-start | bytes 331784 | tf_op jit(solution)/shard_map/ppermute | solution.py:443
  121.2 0.0 collective-permute-done.8.refs_1_
  121.3 3.7 %collective-permute-done.9.refs_2_ = bf16[432,128]{1,0:T(8,128)(2,1)S(1)} collective-permute-done((bf16[432,128]{1,0:T(8,128)(2,1)S(1)}, bf16[432,128]{1,0:T(8,128)(2,1)S(1)}, u32[]{:S(2)}, u32[]{:S(2)}) %collective-permute-start.9) | collective-permute-done | bytes 110624 | tf_op jit(solution)/shard_map/ppermute | solution.py:443
  124.9 18.3 %blocks_5_6.1 = (bf16[648,128]{1,0:T(8,128)(2,1)S(1)}, bf16[648,128]{1,0:T(8,128)(2,1)S(1)}, bf16[432,128]{1,0:T(8,128)(2,1)S(1)}, bf16[432,128]{1,0:T(8,128)(2,1)S(1)}) custom-call(s32[4]{0:T(128)S(1)} %pad_add_fusion.micro_ref.place_ref, bf16[648,128]{1,0:T(8,128)(2,1)S(1)} %get-tuple-element.30.refs_0_.refs_12_, ...), custom_call_target="tpu_custom_call" | custom-call | tf_op jit(solution)/shard_map/blocks_5_6/pallas_call | solution.py:356
  143.3 1.9 %collective-permute-start.10 = (bf16[432,128]{1,0:T(8,128)(2,1)S(1)}, bf16[432,128]{1,0:T(8,128)(2,1)S(1)}, u32[]{:S(2)}, u32[]{:S(2)}) collective-permute-start(bf16[432,128]{1,0:T(8,128)(2,1)S(1)} %get-tuple-element.34), channel_id=1, source_target_pairs={{4,12},{12,4},{5,13},{13,5},{6,14},{14,6},{7,15},{15,7},{20,28},{2... | collective-permute-start | bytes 331784 | tf_op jit(solution)/shard_map/ppermute | solution.py:443
  145.2 10.0 %collective-permute-start.11 = (bf16[432,128]{1,0:T(8,128)(2,1)S(1)}, bf16[432,128]{1,0:T(8,128)(2,1)S(1)}, u32[]{:S(2)}, u32[]{:S(2)}) collective-permute-start(bf16[432,128]{1,0:T(8,128)(2,1)S(1)} %get-tuple-element.35), channel_id=1, source_target_pairs={{12,20},{20,12},{13,21},{21,13},{14,22},{22,14},{15,23},{23,15},{2... | collective-permute-start | bytes 331784 | tf_op jit(solution)/shard_map/ppermute | solution.py:443
  155.2 0.0 collective-permute-done.10.refs_1_
  155.2 3.6 %collective-permute-done.11.refs_2_ = bf16[432,128]{1,0:T(8,128)(2,1)S(1)} collective-permute-done((bf16[432,128]{1,0:T(8,128)(2,1)S(1)}, bf16[432,128]{1,0:T(8,128)(2,1)S(1)}, u32[]{:S(2)}, u32[]{:S(2)}) %collective-permute-start.11) | collective-permute-done | bytes 110624 | tf_op jit(solution)/shard_map/ppermute | solution.py:443
  158.8 10.3 %block_7.1 = (bf16[648,128]{1,0:T(8,128)(2,1)S(1)}, bf16[648,128]{1,0:T(8,128)(2,1)S(1)}, bf16[648,128]{1,0:T(8,128)(2,1)S(1)}, bf16[648,128]{1,0:T(8,128)(2,1)S(1)}) custom-call(s32[4]{0:T(128)S(1)} %pad_add_fusion.micro_ref.place_ref, bf16[648,128]{1,0:T(8,128)(2,1)S(1)} %get-tuple-element.33.refs_0_.refs_14_, ...), custom_call_target="tpu_custom_call" | custom-call | tf_op jit(solution)/shard_map/block_7/pallas_call | solution.py:356
  169.1 9.9 %collective-permute-start.14 = (bf16[648,128]{1,0:T(8,128)(2,1)S(1)}, bf16[648,128]{1,0:T(8,128)(2,1)S(1)}, u32[]{:S(2)}, u32[]{:S(2)}) collective-permute-start(bf16[648,128]{1,0:T(8,128)(2,1)S(1)} %get-tuple-element.42), channel_id=1, source_target_pairs={{0,3},{1,2},{2,1},{3,0},{4,7},{5,6},{6,5},{7,4},{8,11},{9,10},{10,... | collective-permute-start | bytes 497672 | tf_op jit(solution)/shard_map/ppermute | solution.py:430
  179.0 1.9 %collective-permute-start.12 = (bf16[648,128]{1,0:T(8,128)(2,1)S(1)}, bf16[648,128]{1,0:T(8,128)(2,1)S(1)}, u32[]{:S(2)}, u32[]{:S(2)}) collective-permute-start(bf16[648,128]{1,0:T(8,128)(2,1)S(1)} %get-tuple-element.39), channel_id=1, source_target_pairs={{0,1},{1,0},{2,3},{3,2},{4,5},{5,4},{6,7},{7,6},{8,9},{9,8},{10,11... | collective-permute-start | bytes 497672 | tf_op jit(solution)/shard_map/ppermute | solution.py:430
  181.0 2.0 %collective-permute-start.13 = (bf16[648,128]{1,0:T(8,128)(2,1)S(1)}, bf16[648,128]{1,0:T(8,128)(2,1)S(1)}, u32[]{:S(2)}, u32[]{:S(2)}) collective-permute-start(bf16[648,128]{1,0:T(8,128)(2,1)S(1)} %get-tuple-element.40), channel_id=1, source_target_pairs={{0,2},{1,3},{2,0},{3,1},{4,6},{5,7},{6,4},{7,5},{8,10},{9,11},{10,... | collective-permute-start | bytes 497672 | tf_op jit(solution)/shard_map/ppermute | solution.py:430
  183.0 0.0 collective-permute-done.14.refs_1_
  183.0 1.8 finish.2.refs_2_
  184.9 0.0 collective-permute-done.12.refs_0_
  184.9 3.3 %collective-permute-done.13.refs_1_ = bf16[648,128]{1,0:T(8,128)(2,1)S(1)} collective-permute-done((bf16[648,128]{1,0:T(8,128)(2,1)S(1)}, bf16[648,128]{1,0:T(8,128)(2,1)S(1)}, u32[]{:S(2)}, u32[]{:S(2)}) %collective-permute-start.13) | collective-permute-done | bytes 165920 | tf_op jit(solution)/shard_map/ppermute | solution.py:430
  188.2 1.8 finish.3
  (2 shorter events, 0.0 us)
Async XLA Ops:
  0.0 6.3 %copy-start.2 = (bf16[4,2,18,2304]{3,1,2,0:T(2,128)(2,1)S(1)}, bf16[4,2,18,2304]{3,1,2,0:T(2,128)(2,1)}, u32[]{:S(2)}) copy-start(bf16[4,2,18,2304]{3,1,2,0:T(2,128)(2,1)} %param.8) | copy-start | bytes 1990660
  1.4 23.4 %collective-permute-start = (bf16[192,2304]{1,0:T(8,128)(2,1)S(1)}, bf16[192,2304]{1,0:T(8,128)(2,1)S(1)}, u32[]{:S(2)}, u32[]{:S(2)}) collective-permute-start(bf16[192,2304]{1,0:T(8,128)(2,1)S(1)} %pack_weights.1.refs_3_.refs_1_), channel_id=1, source_target_pairs={{0,2},{1,3},{2,0},{3,1},{4,6},{5,7},{6,4},{7,5},{8,10},{9,11},{10,... | collective-permute-start | bytes 2654216 | tf_op jit(solution)/shard_map/ppermute | solution.py:430
  5.5 0.7 copy-start.3
  6.5 0.7 copy-start.1
  7.1 22.8 %copy-start = (f32[3,72,144]{2,1,0:T(8,128)S(1)}, f32[3,72,144]{2,1,0:T(8,128)}, u32[]{:S(2)}) copy-start(f32[3,72,144]{2,1,0:T(8,128)} %constant.48.clone.refs_7_.refs_5_) | copy-start | bytes 373252
  8.1 4.2 %collective-permute-start.2 = (bf16[648,128]{1,0:T(8,128)(2,1)S(1)}, bf16[648,128]{1,0:T(8,128)(2,1)S(1)}, u32[]{:S(2)}, u32[]{:S(2)}) collective-permute-start(bf16[648,128]{1,0:T(8,128)(2,1)S(1)} %embed.1.refs_0_), channel_id=1, source_target_pairs={{8,16},{16,8},{9,17},{17,9},{10,18},{18,10},{11,19},{19,11},{24,32... | collective-permute-start | bytes 497672 | tf_op jit(solution)/shard_map/ppermute | solution.py:443
  8.8 3.6 %collective-permute-start.1 = (bf16[648,128]{1,0:T(8,128)(2,1)S(1)}, bf16[648,128]{1,0:T(8,128)(2,1)S(1)}, u32[]{:S(2)}, u32[]{:S(2)}) collective-permute-start(bf16[648,128]{1,0:T(8,128)(2,1)S(1)} %embed.1.refs_0_), channel_id=1, source_target_pairs={{0,8},{8,0},{1,9},{9,1},{2,10},{10,2},{3,11},{11,3},{16,24},{24,16... | collective-permute-start | bytes 497672 | tf_op jit(solution)/shard_map/ppermute | solution.py:443
  9.5 18.4 %collective-permute-start.3 = (bf16[192,2304]{1,0:T(8,128)(2,1)S(1)}, bf16[192,2304]{1,0:T(8,128)(2,1)S(1)}, u32[]{:S(2)}, u32[]{:S(2)}) collective-permute-start(bf16[192,2304]{1,0:T(8,128)(2,1)S(1)} %pack_weights.1.refs_3_.refs_1_), channel_id=1, source_target_pairs={{0,1},{1,0},{2,3},{3,2},{4,5},{5,4},{6,7},{7,6},{8,9},{9,8},{10,11... | collective-permute-start | bytes 2654216 | tf_op jit(solution)/shard_map/ppermute | solution.py:430
  24.8 5.2 %collective-permute-start.4 = (bf16[192,2304]{1,0:T(8,128)(2,1)S(1)}, bf16[192,2304]{1,0:T(8,128)(2,1)S(1)}, u32[]{:S(2)}, u32[]{:S(2)}) collective-permute-start(bf16[192,2304]{1,0:T(8,128)(2,1)S(1)} %collective-permute-done.refs_5_.refs_3_), channel_id=1, source_target_pairs={{0,1},{1,0},{2,3},{3,2},{4,5},{5,4},{6,7},{7,6},{8,9},{9,8},{10,11... | collective-permute-start | bytes 2654216 | tf_op jit(solution)/shard_map/ppermute | solution.py:430
  65.7 1.4 collective-permute-start.5
  66.4 0.7 collective-permute-start.6
  77.5 22.9 %collective-permute-start.7 = (bf16[648,128]{1,0:T(8,128)(2,1)S(1)}, bf16[648,128]{1,0:T(8,128)(2,1)S(1)}, u32[]{:S(2)}, u32[]{:S(2)}) collective-permute-start(bf16[648,128]{1,0:T(8,128)(2,1)S(1)} %block_3.1.refs_11_), channel_id=1, source_target_pairs={{0,4},{1,5},{2,6},{3,7},{8,12},{9,13},{10,14},{11,15},{16,20},{17,... | collective-permute-start | bytes 497672 | tf_op jit(solution)/shard_map/ppermute | solution.py:433
  109.3 12.0 %collective-permute-start.8 = (bf16[432,128]{1,0:T(8,128)(2,1)S(1)}, bf16[432,128]{1,0:T(8,128)(2,1)S(1)}, u32[]{:S(2)}, u32[]{:S(2)}) collective-permute-start(bf16[432,128]{1,0:T(8,128)(2,1)S(1)} %get-tuple-element.31), channel_id=1, source_target_pairs={{4,12},{12,4},{5,13},{13,5},{6,14},{14,6},{7,15},{15,7},{20,28},{2... | collective-permute-start | bytes 331784 | tf_op jit(solution)/shard_map/ppermute | solution.py:443
  111.2 13.7 %collective-permute-start.9 = (bf16[432,128]{1,0:T(8,128)(2,1)S(1)}, bf16[432,128]{1,0:T(8,128)(2,1)S(1)}, u32[]{:S(2)}, u32[]{:S(2)}) collective-permute-start(bf16[432,128]{1,0:T(8,128)(2,1)S(1)} %get-tuple-element.32), channel_id=1, source_target_pairs={{12,20},{20,12},{13,21},{21,13},{14,22},{22,14},{15,23},{23,15},{2... | collective-permute-start | bytes 331784 | tf_op jit(solution)/shard_map/ppermute | solution.py:443
  143.3 12.0 %collective-permute-start.10 = (bf16[432,128]{1,0:T(8,128)(2,1)S(1)}, bf16[432,128]{1,0:T(8,128)(2,1)S(1)}, u32[]{:S(2)}, u32[]{:S(2)}) collective-permute-start(bf16[432,128]{1,0:T(8,128)(2,1)S(1)} %get-tuple-element.34), channel_id=1, source_target_pairs={{4,12},{12,4},{5,13},{13,5},{6,14},{14,6},{7,15},{15,7},{20,28},{2... | collective-permute-start | bytes 331784 | tf_op jit(solution)/shard_map/ppermute | solution.py:443
  145.2 13.6 %collective-permute-start.11 = (bf16[432,128]{1,0:T(8,128)(2,1)S(1)}, bf16[432,128]{1,0:T(8,128)(2,1)S(1)}, u32[]{:S(2)}, u32[]{:S(2)}) collective-permute-start(bf16[432,128]{1,0:T(8,128)(2,1)S(1)} %get-tuple-element.35), channel_id=1, source_target_pairs={{12,20},{20,12},{13,21},{21,13},{14,22},{22,14},{15,23},{23,15},{2... | collective-permute-start | bytes 331784 | tf_op jit(solution)/shard_map/ppermute | solution.py:443
  169.1 13.9 %collective-permute-start.14 = (bf16[648,128]{1,0:T(8,128)(2,1)S(1)}, bf16[648,128]{1,0:T(8,128)(2,1)S(1)}, u32[]{:S(2)}, u32[]{:S(2)}) collective-permute-start(bf16[648,128]{1,0:T(8,128)(2,1)S(1)} %get-tuple-element.42), channel_id=1, source_target_pairs={{0,3},{1,2},{2,1},{3,0},{4,7},{5,6},{6,5},{7,4},{8,11},{9,10},{10,... | collective-permute-start | bytes 497672 | tf_op jit(solution)/shard_map/ppermute | solution.py:430
  179.0 5.8 %collective-permute-start.12 = (bf16[648,128]{1,0:T(8,128)(2,1)S(1)}, bf16[648,128]{1,0:T(8,128)(2,1)S(1)}, u32[]{:S(2)}, u32[]{:S(2)}) collective-permute-start(bf16[648,128]{1,0:T(8,128)(2,1)S(1)} %get-tuple-element.39), channel_id=1, source_target_pairs={{0,1},{1,0},{2,3},{3,2},{4,5},{5,4},{6,7},{7,6},{8,9},{9,8},{10,11... | collective-permute-start | bytes 497672 | tf_op jit(solution)/shard_map/ppermute | solution.py:430
  181.0 7.2 %collective-permute-start.13 = (bf16[648,128]{1,0:T(8,128)(2,1)S(1)}, bf16[648,128]{1,0:T(8,128)(2,1)S(1)}, u32[]{:S(2)}, u32[]{:S(2)}) collective-permute-start(bf16[648,128]{1,0:T(8,128)(2,1)S(1)} %get-tuple-element.40), channel_id=1, source_target_pairs={{0,2},{1,3},{2,0},{3,1},{4,6},{5,7},{6,4},{7,5},{8,10},{9,11},{10,... | collective-permute-start | bytes 497672 | tf_op jit(solution)/shard_map/ppermute | solution.py:430

commit v11 on v10

--- a/solution.py
+++ b/solution.py
@@ -308,7 +308,7 @@
     def store(slot, packed):
         stage_ref[slot] = packed
 
-    flags = (place_ref[3], place_ref[2])
+    flags = (place_ref[2], place_ref[3])
     compute_blocks(mode, flags, tiles, bias_ref, w_ref, wproj_ref, store, scratch)
     for i, ref in enumerate(outs):
         ref[...] = stage_ref[i]
@@ -339,7 +339,7 @@
         def store(slot, packed):
             stage_ref[slot] = packed
 
-        flags = (place_ref[3], place_ref[2])
+        flags = (place_ref[2], place_ref[3])
         compute_blocks("odd", flags, tiles, bias_ref, w_ref, wproj_ref, store, scratch)
         route((*late, stage_ref.at[0]))
 
@@ -441,7 +441,7 @@
                     here, there = t * section_count + s, (t + 1) % tile_count * section_count + s
                     pairs += [(here, there), (there, here)]
             received[phase] = lax.ppermute(value, axes, pairs)
-        return received[0], received[1]
+        return received[1], received[0]
 
     tokens = rows * levels * HALF
     tile_shape, half_shape = (3 * tokens, LANES), (2 * tokens, LANES)

time: 191 us -> 188 us (0.984)
  starting transfers between devices: 51.7 us -> 47.9 us
    ppermute x8, starting transfers between devices: 26.6 us -> 23.2 us  [swap(): received[phase] = lax.ppermute(value, axes, pairs)]
  transfers between devices with their start and end apart: 15 -> 15, of which waited for: 6 -> 8; matrix products, arithmetic and copies ran while one was open for 0% -> 0% of each run, Pallas kernels for 1% -> 2%
where the time goes in v11:
time: 188 us; the launch traced here: 187 us
  Pallas kernels  89.7 us (48%)
  starting transfers between devices  47.9 us (25%)
  waiting for transfers between devices  47.8 us (25%)
    pallas_call x5, Pallas kernels, run_part(): pl.pallas_call(kernel, out_shape=tuple((pltpu.VMEM(shape, bf16) for shape...  83.6 us
    ppermute x6, starting transfers between devices, exchange(): lax.ppermute(value, 'section', [(s, s ^ bit) for s in range(section_count)])  23.3 us
    ppermute x8, starting transfers between devices, swap(): received[phase] = lax.ppermute(value, axes, pairs)  23.2 us
    ppermute x1, waiting for transfers between devices, forward(): lax.ppermute(value, 'section', [(s, s + STAGE) for s in range(STAGE)])  22.3 us
    ppermute x6, waiting for transfers between devices, exchange(): lax.ppermute(value, 'section', [(s, s ^ bit) for s in range(section_count)])  17.8 us
    ppermute x8, waiting for transfers between devices, swap(): received[phase] = lax.ppermute(value, axes, pairs)  7.73 us
  transfers between devices with their start and end apart: 15, of which 8 were waited for; matrix products, arithmetic and copies ran while one was open for 0% of the time, Pallas kernels for 2%

profile of v11, /device:TPU:129, one launch (start us, length us, event | category | flops | bytes accessed | tf_op | source)
XLA Modules:
  0.0 187.3 jit_solution(1783257505498445700)
XLA Ops:
  0.0 0.0 copy-start.2
  0.0 1.4 pack_weights.1.refs_3_.refs_1_
  1.4 4.0 %collective-permute-start = (bf16[192,2304]{1,0:T(8,128)(2,1)S(1)}, bf16[192,2304]{1,0:T(8,128)(2,1)S(1)}, u32[]{:S(2)}, u32[]{:S(2)}) collective-permute-start(bf16[192,2304]{1,0:T(8,128)(2,1)S(1)} %pack_weights.1.refs_3_.refs_1_), channel_id=1, source_target_pairs={{0,2},{1,3},{2,0},{3,1},{4,6},{5,7},{6,4},{7,5},{8,10},{9,11},{10,... | collective-permute-start | bytes 2654216 | tf_op jit(solution)/shard_map/ppermute | solution.py:430
  5.5 0.0 copy-start.3
  5.5 0.7 copy-done.3
  6.2 0.1 copy.11.mask_ref
  6.3 0.0 copy-done.2
  6.3 0.1 copy.10.fields_ref
  6.4 0.1 pad_add_fusion.micro_ref.place_ref
  6.5 0.7 copy-done.1
  7.1 1.0 embed.1.refs_0_
  8.1 0.7 collective-permute-start.2
  8.8 0.7 collective-permute-start.1
  9.5 2.9 %collective-permute-start.3 = (bf16[192,2304]{1,0:T(8,128)(2,1)S(1)}, bf16[192,2304]{1,0:T(8,128)(2,1)S(1)}, u32[]{:S(2)}, u32[]{:S(2)}) collective-permute-start(bf16[192,2304]{1,0:T(8,128)(2,1)S(1)} %pack_weights.1.refs_3_.refs_1_), channel_id=1, source_target_pairs={{0,1},{1,0},{2,3},{3,2},{4,5},{5,4},{6,7},{7,6},{8,9},{9,8},{10,11... | collective-permute-start | bytes 2654216 | tf_op jit(solution)/shard_map/ppermute | solution.py:430
  12.4 0.0 collective-permute-done.2.refs_2_
  12.4 0.0 collective-permute-done.1.refs_1_
  12.4 12.4 %collective-permute-done.refs_5_.refs_3_ = bf16[192,2304]{1,0:T(8,128)(2,1)S(1)} collective-permute-done((bf16[192,2304]{1,0:T(8,128)(2,1)S(1)}, bf16[192,2304]{1,0:T(8,128)(2,1)S(1)}, u32[]{:S(2)}, u32[]{:S(2)}) %collective-permute-start) | collective-permute-done | bytes 884768 | tf_op jit(solution)/shard_map/ppermute | solution.py:430
  24.8 3.1 %collective-permute-start.4 = (bf16[192,2304]{1,0:T(8,128)(2,1)S(1)}, bf16[192,2304]{1,0:T(8,128)(2,1)S(1)}, u32[]{:S(2)}, u32[]{:S(2)}) collective-permute-start(bf16[192,2304]{1,0:T(8,128)(2,1)S(1)} %collective-permute-done.refs_5_.refs_3_), channel_id=1, source_target_pairs={{0,1},{1,0},{2,3},{3,2},{4,5},{5,4},{6,7},{7,6},{8,9},{9,8},{10,11... | collective-permute-start | bytes 2654216 | tf_op jit(solution)/shard_map/ppermute | solution.py:430
  27.9 0.0 collective-permute-done.3.refs_4_.refs_2_
  28.0 2.0 %collective-permute-done.4.refs_6_.refs_4_ = bf16[192,2304]{1,0:T(8,128)(2,1)S(1)} collective-permute-done((bf16[192,2304]{1,0:T(8,128)(2,1)S(1)}, bf16[192,2304]{1,0:T(8,128)(2,1)S(1)}, u32[]{:S(2)}, u32[]{:S(2)}) %collective-permute-start.4) | collective-permute-done | bytes 884768 | tf_op jit(solution)/shard_map/ppermute | solution.py:430
  30.0 0.0 copy-done
  30.0 35.8 %blocks_0_2.1 = (bf16[648,128]{1,0:T(8,128)(2,1)S(1)}, bf16[648,128]{1,0:T(8,128)(2,1)S(1)}, bf16[648,128]{1,0:T(8,128)(2,1)S(1)}, bf16[432,128]{1,0:T(8,128)(2,1)S(1)}, bf16[432,128]{1,0:T(8,128)(2,1)S(1)}) custom-call(s32[4]{0:T(128)S(1)} %pad_add_fusion.micro_ref.place_ref, bf16[648,128]{1,0:T(8,128)(2,1)S(1)} %embed.1.refs_0_, ...), custom_call_target="tpu_custom_call" | custom-call | tf_op jit(solution)/shard_map/blocks_0_2/pallas_call | solution.py:356
  65.7 0.7 collective-permute-start.5
  66.4 0.7 collective-permute-start.6
  67.1 0.0 collective-permute-done.5.refs_1_
  67.1 0.0 collective-permute-done.6.refs_2_
  67.1 10.4 %block_3.1.refs_11_ = bf16[648,128]{1,0:T(8,128)(2,1)S(1)} custom-call(s32[4]{0:T(128)S(1)} %pad_add_fusion.micro_ref.place_ref, bf16[648,128]{1,0:T(8,128)(2,1)S(1)} %get-tuple-element.27.refs_0_.refs_10_, bf16[432,128]{1,0:T(8,128)(2,1)S(1)} %collective-permute-done.5.refs_1_, bf16[432,128]{1,0:T(8,128)(2,1)S(1)} %collective-permute-done.6.refs_2_, ...), custom_call_target="tpu_custom_call" | custom-call | tf_op jit(solution)/shard_map/block_3/pallas_call | solution.py:356
  77.5 1.3 collective-permute-start.7
  78.8 22.3 %collective-permute-done.7.refs_0_ = bf16[648,128]{1,0:T(8,128)(2,1)S(1)} collective-permute-done((bf16[648,128]{1,0:T(8,128)(2,1)S(1)}, bf16[648,128]{1,0:T(8,128)(2,1)S(1)}, u32[]{:S(2)}, u32[]{:S(2)}) %collective-permute-start.7) | collective-permute-done | bytes 165920 | tf_op jit(solution)/shard_map/ppermute | solution.py:433
  101.1 8.8 %block_4.1 = (bf16[648,128]{1,0:T(8,128)(2,1)S(1)}, bf16[432,128]{1,0:T(8,128)(2,1)S(1)}, bf16[432,128]{1,0:T(8,128)(2,1)S(1)}) custom-call(s32[4]{0:T(128)S(1)} %pad_add_fusion.micro_ref.place_ref, bf16[648,128]{1,0:T(8,128)(2,1)S(1)} %collective-permute-done.7.refs_0_, bf16[192,2304]{1,0:T(8,128)(2,1)S(1)} %pack_weights.1.refs_3_.refs_1_, ...), custom_call_target="tpu_custom_call" | custom-call | tf_op jit(solution)/shard_map/block_4/pallas_call | solution.py:356
  109.9 8.8 %collective-permute-start.8 = (bf16[432,128]{1,0:T(8,128)(2,1)S(1)}, bf16[432,128]{1,0:T(8,128)(2,1)S(1)}, u32[]{:S(2)}, u32[]{:S(2)}) collective-permute-start(bf16[432,128]{1,0:T(8,128)(2,1)S(1)} %get-tuple-element.31), channel_id=1, source_target_pairs={{12,20},{20,12},{13,21},{21,13},{14,22},{22,14},{15,23},{23,15},{2... | collective-permute-start | bytes 331784 | tf_op jit(solution)/shard_map/ppermute | solution.py:443
  118.7 1.9 %collective-permute-start.9 = (bf16[432,128]{1,0:T(8,128)(2,1)S(1)}, bf16[432,128]{1,0:T(8,128)(2,1)S(1)}, u32[]{:S(2)}, u32[]{:S(2)}) collective-permute-start(bf16[432,128]{1,0:T(8,128)(2,1)S(1)} %get-tuple-element.32), channel_id=1, source_target_pairs={{4,12},{12,4},{5,13},{13,5},{6,14},{14,6},{7,15},{15,7},{20,28},{2... | collective-permute-start | bytes 331784 | tf_op jit(solution)/shard_map/ppermute | solution.py:443
  120.6 3.0 %collective-permute-done.8.refs_1_ = bf16[432,128]{1,0:T(8,128)(2,1)S(1)} collective-permute-done((bf16[432,128]{1,0:T(8,128)(2,1)S(1)}, bf16[432,128]{1,0:T(8,128)(2,1)S(1)}, u32[]{:S(2)}, u32[]{:S(2)}) %collective-permute-start.8) | collective-permute-done | bytes 110624 | tf_op jit(solution)/shard_map/ppermute | solution.py:443
  123.6 0.9 collective-permute-done.9.refs_2_
  124.5 18.3 %blocks_5_6.1 = (bf16[648,128]{1,0:T(8,128)(2,1)S(1)}, bf16[648,128]{1,0:T(8,128)(2,1)S(1)}, bf16[432,128]{1,0:T(8,128)(2,1)S(1)}, bf16[432,128]{1,0:T(8,128)(2,1)S(1)}) custom-call(s32[4]{0:T(128)S(1)} %pad_add_fusion.micro_ref.place_ref, bf16[648,128]{1,0:T(8,128)(2,1)S(1)} %get-tuple-element.30.refs_0_.refs_12_, ...), custom_call_target="tpu_custom_call" | custom-call | tf_op jit(solution)/shard_map/blocks_5_6/pallas_call | solution.py:356
  142.8 7.9 %collective-permute-start.10 = (bf16[432,128]{1,0:T(8,128)(2,1)S(1)}, bf16[432,128]{1,0:T(8,128)(2,1)S(1)}, u32[]{:S(2)}, u32[]{:S(2)}) collective-permute-start(bf16[432,128]{1,0:T(8,128)(2,1)S(1)} %get-tuple-element.34), channel_id=1, source_target_pairs={{12,20},{20,12},{13,21},{21,13},{14,22},{22,14},{15,23},{23,15},{2... | collective-permute-start | bytes 331784 | tf_op jit(solution)/shard_map/ppermute | solution.py:443
  150.8 1.9 %collective-permute-start.11 = (bf16[432,128]{1,0:T(8,128)(2,1)S(1)}, bf16[432,128]{1,0:T(8,128)(2,1)S(1)}, u32[]{:S(2)}, u32[]{:S(2)}) collective-permute-start(bf16[432,128]{1,0:T(8,128)(2,1)S(1)} %get-tuple-element.35), channel_id=1, source_target_pairs={{4,12},{12,4},{5,13},{13,5},{6,14},{14,6},{7,15},{15,7},{20,28},{2... | collective-permute-start | bytes 331784 | tf_op jit(solution)/shard_map/ppermute | solution.py:443
  152.7 3.8 %collective-permute-done.10.refs_1_ = bf16[432,128]{1,0:T(8,128)(2,1)S(1)} collective-permute-done((bf16[432,128]{1,0:T(8,128)(2,1)S(1)}, bf16[432,128]{1,0:T(8,128)(2,1)S(1)}, u32[]{:S(2)}, u32[]{:S(2)}) %collective-permute-start.10) | collective-permute-done | bytes 110624 | tf_op jit(solution)/shard_map/ppermute | solution.py:443
  156.5 0.1 collective-permute-done.11.refs_2_
  156.6 10.3 %block_7.1 = (bf16[648,128]{1,0:T(8,128)(2,1)S(1)}, bf16[648,128]{1,0:T(8,128)(2,1)S(1)}, bf16[648,128]{1,0:T(8,128)(2,1)S(1)}, bf16[648,128]{1,0:T(8,128)(2,1)S(1)}) custom-call(s32[4]{0:T(128)S(1)} %pad_add_fusion.micro_ref.place_ref, bf16[648,128]{1,0:T(8,128)(2,1)S(1)} %get-tuple-element.33.refs_0_.refs_14_, ...), custom_call_target="tpu_custom_call" | custom-call | tf_op jit(solution)/shard_map/block_7/pallas_call | solution.py:356
  166.9 9.4 %collective-permute-start.14 = (bf16[648,128]{1,0:T(8,128)(2,1)S(1)}, bf16[648,128]{1,0:T(8,128)(2,1)S(1)}, u32[]{:S(2)}, u32[]{:S(2)}) collective-permute-start(bf16[648,128]{1,0:T(8,128)(2,1)S(1)} %get-tuple-element.42), channel_id=1, source_target_pairs={{0,3},{1,2},{2,1},{3,0},{4,7},{5,6},{6,5},{7,4},{8,11},{9,10},{10,... | collective-permute-start | bytes 497672 | tf_op jit(solution)/shard_map/ppermute | solution.py:430
  176.3 1.9 %collective-permute-start.12 = (bf16[648,128]{1,0:T(8,128)(2,1)S(1)}, bf16[648,128]{1,0:T(8,128)(2,1)S(1)}, u32[]{:S(2)}, u32[]{:S(2)}) collective-permute-start(bf16[648,128]{1,0:T(8,128)(2,1)S(1)} %get-tuple-element.39), channel_id=1, source_target_pairs={{0,1},{1,0},{2,3},{3,2},{4,5},{5,4},{6,7},{7,6},{8,9},{9,8},{10,11... | collective-permute-start | bytes 497672 | tf_op jit(solution)/shard_map/ppermute | solution.py:430
  178.2 2.0 %collective-permute-start.13 = (bf16[648,128]{1,0:T(8,128)(2,1)S(1)}, bf16[648,128]{1,0:T(8,128)(2,1)S(1)}, u32[]{:S(2)}, u32[]{:S(2)}) collective-permute-start(bf16[648,128]{1,0:T(8,128)(2,1)S(1)} %get-tuple-element.40), channel_id=1, source_target_pairs={{0,2},{1,3},{2,0},{3,1},{4,6},{5,7},{6,4},{7,5},{8,10},{9,11},{10,... | collective-permute-start | bytes 497672 | tf_op jit(solution)/shard_map/ppermute | solution.py:430
  180.3 0.0 collective-permute-done.14.refs_1_
  180.3 1.8 finish.2.refs_2_
  182.1 0.0 collective-permute-done.12.refs_0_
  182.1 3.3 %collective-permute-done.13.refs_1_ = bf16[648,128]{1,0:T(8,128)(2,1)S(1)} collective-permute-done((bf16[648,128]{1,0:T(8,128)(2,1)S(1)}, bf16[648,128]{1,0:T(8,128)(2,1)S(1)}, u32[]{:S(2)}, u32[]{:S(2)}) %collective-permute-start.13) | collective-permute-done | bytes 165920 | tf_op jit(solution)/shard_map/ppermute | solution.py:430
  185.4 1.8 finish.3
  (2 shorter events, 0.0 us)
Async XLA Ops:
  0.0 6.3 %copy-start.2 = (bf16[4,2,18,2304]{3,1,2,0:T(2,128)(2,1)S(1)}, bf16[4,2,18,2304]{3,1,2,0:T(2,128)(2,1)}, u32[]{:S(2)}) copy-start(bf16[4,2,18,2304]{3,1,2,0:T(2,128)(2,1)} %param.8) | copy-start | bytes 1990660
  1.4 23.4 %collective-permute-start = (bf16[192,2304]{1,0:T(8,128)(2,1)S(1)}, bf16[192,2304]{1,0:T(8,128)(2,1)S(1)}, u32[]{:S(2)}, u32[]{:S(2)}) collective-permute-start(bf16[192,2304]{1,0:T(8,128)(2,1)S(1)} %pack_weights.1.refs_3_.refs_1_), channel_id=1, source_target_pairs={{0,2},{1,3},{2,0},{3,1},{4,6},{5,7},{6,4},{7,5},{8,10},{9,11},{10,... | collective-permute-start | bytes 2654216 | tf_op jit(solution)/shard_map/ppermute | solution.py:430
  5.5 0.7 copy-start.3
  6.5 0.7 copy-start.1
  7.1 22.8 %copy-start = (f32[3,72,144]{2,1,0:T(8,128)S(1)}, f32[3,72,144]{2,1,0:T(8,128)}, u32[]{:S(2)}) copy-start(f32[3,72,144]{2,1,0:T(8,128)} %constant.48.clone.refs_7_.refs_5_) | copy-start | bytes 373252
  8.1 4.2 %collective-permute-start.2 = (bf16[648,128]{1,0:T(8,128)(2,1)S(1)}, bf16[648,128]{1,0:T(8,128)(2,1)S(1)}, u32[]{:S(2)}, u32[]{:S(2)}) collective-permute-start(bf16[648,128]{1,0:T(8,128)(2,1)S(1)} %embed.1.refs_0_), channel_id=1, source_target_pairs={{0,8},{8,0},{1,9},{9,1},{2,10},{10,2},{3,11},{11,3},{16,24},{24,16... | collective-permute-start | bytes 497672 | tf_op jit(solution)/shard_map/ppermute | solution.py:443
  8.8 3.6 %collective-permute-start.1 = (bf16[648,128]{1,0:T(8,128)(2,1)S(1)}, bf16[648,128]{1,0:T(8,128)(2,1)S(1)}, u32[]{:S(2)}, u32[]{:S(2)}) collective-permute-start(bf16[648,128]{1,0:T(8,128)(2,1)S(1)} %embed.1.refs_0_), channel_id=1, source_target_pairs={{8,16},{16,8},{9,17},{17,9},{10,18},{18,10},{11,19},{19,11},{24,32... | collective-permute-start | bytes 497672 | tf_op jit(solution)/shard_map/ppermute | solution.py:443
  9.5 18.4 %collective-permute-start.3 = (bf16[192,2304]{1,0:T(8,128)(2,1)S(1)}, bf16[192,2304]{1,0:T(8,128)(2,1)S(1)}, u32[]{:S(2)}, u32[]{:S(2)}) collective-permute-start(bf16[192,2304]{1,0:T(8,128)(2,1)S(1)} %pack_weights.1.refs_3_.refs_1_), channel_id=1, source_target_pairs={{0,1},{1,0},{2,3},{3,2},{4,5},{5,4},{6,7},{7,6},{8,9},{9,8},{10,11... | collective-permute-start | bytes 2654216 | tf_op jit(solution)/shard_map/ppermute | solution.py:430
  24.8 5.2 %collective-permute-start.4 = (bf16[192,2304]{1,0:T(8,128)(2,1)S(1)}, bf16[192,2304]{1,0:T(8,128)(2,1)S(1)}, u32[]{:S(2)}, u32[]{:S(2)}) collective-permute-start(bf16[192,2304]{1,0:T(8,128)(2,1)S(1)} %collective-permute-done.refs_5_.refs_3_), channel_id=1, source_target_pairs={{0,1},{1,0},{2,3},{3,2},{4,5},{5,4},{6,7},{7,6},{8,9},{9,8},{10,11... | collective-permute-start | bytes 2654216 | tf_op jit(solution)/shard_map/ppermute | solution.py:430
  65.7 1.4 collective-permute-start.5
  66.4 0.7 collective-permute-start.6
  77.5 23.6 %collective-permute-start.7 = (bf16[648,128]{1,0:T(8,128)(2,1)S(1)}, bf16[648,128]{1,0:T(8,128)(2,1)S(1)}, u32[]{:S(2)}, u32[]{:S(2)}) collective-permute-start(bf16[648,128]{1,0:T(8,128)(2,1)S(1)} %block_3.1.refs_11_), channel_id=1, source_target_pairs={{0,4},{1,5},{2,6},{3,7},{8,12},{9,13},{10,14},{11,15},{16,20},{17,... | collective-permute-start | bytes 497672 | tf_op jit(solution)/shard_map/ppermute | solution.py:433
  109.9 13.7 %collective-permute-start.8 = (bf16[432,128]{1,0:T(8,128)(2,1)S(1)}, bf16[432,128]{1,0:T(8,128)(2,1)S(1)}, u32[]{:S(2)}, u32[]{:S(2)}) collective-permute-start(bf16[432,128]{1,0:T(8,128)(2,1)S(1)} %get-tuple-element.31), channel_id=1, source_target_pairs={{12,20},{20,12},{13,21},{21,13},{14,22},{22,14},{15,23},{23,15},{2... | collective-permute-start | bytes 331784 | tf_op jit(solution)/shard_map/ppermute | solution.py:443
  118.7 5.8 %collective-permute-start.9 = (bf16[432,128]{1,0:T(8,128)(2,1)S(1)}, bf16[432,128]{1,0:T(8,128)(2,1)S(1)}, u32[]{:S(2)}, u32[]{:S(2)}) collective-permute-start(bf16[432,128]{1,0:T(8,128)(2,1)S(1)} %get-tuple-element.32), channel_id=1, source_target_pairs={{4,12},{12,4},{5,13},{13,5},{6,14},{14,6},{7,15},{15,7},{20,28},{2... | collective-permute-start | bytes 331784 | tf_op jit(solution)/shard_map/ppermute | solution.py:443
  142.8 13.6 %collective-permute-start.10 = (bf16[432,128]{1,0:T(8,128)(2,1)S(1)}, bf16[432,128]{1,0:T(8,128)(2,1)S(1)}, u32[]{:S(2)}, u32[]{:S(2)}) collective-permute-start(bf16[432,128]{1,0:T(8,128)(2,1)S(1)} %get-tuple-element.34), channel_id=1, source_target_pairs={{12,20},{20,12},{13,21},{21,13},{14,22},{22,14},{15,23},{23,15},{2... | collective-permute-start | bytes 331784 | tf_op jit(solution)/shard_map/ppermute | solution.py:443
  150.8 5.8 %collective-permute-start.11 = (bf16[432,128]{1,0:T(8,128)(2,1)S(1)}, bf16[432,128]{1,0:T(8,128)(2,1)S(1)}, u32[]{:S(2)}, u32[]{:S(2)}) collective-permute-start(bf16[432,128]{1,0:T(8,128)(2,1)S(1)} %get-tuple-element.35), channel_id=1, source_target_pairs={{4,12},{12,4},{5,13},{13,5},{6,14},{14,6},{7,15},{15,7},{20,28},{2... | collective-permute-start | bytes 331784 | tf_op jit(solution)/shard_map/ppermute | solution.py:443
  166.9 13.4 %collective-permute-start.14 = (bf16[648,128]{1,0:T(8,128)(2,1)S(1)}, bf16[648,128]{1,0:T(8,128)(2,1)S(1)}, u32[]{:S(2)}, u32[]{:S(2)}) collective-permute-start(bf16[648,128]{1,0:T(8,128)(2,1)S(1)} %get-tuple-element.42), channel_id=1, source_target_pairs={{0,3},{1,2},{2,1},{3,0},{4,7},{5,6},{6,5},{7,4},{8,11},{9,10},{10,... | collective-permute-start | bytes 497672 | tf_op jit(solution)/shard_map/ppermute | solution.py:430
  176.3 5.8 %collective-permute-start.12 = (bf16[648,128]{1,0:T(8,128)(2,1)S(1)}, bf16[648,128]{1,0:T(8,128)(2,1)S(1)}, u32[]{:S(2)}, u32[]{:S(2)}) collective-permute-start(bf16[648,128]{1,0:T(8,128)(2,1)S(1)} %get-tuple-element.39), channel_id=1, source_target_pairs={{0,1},{1,0},{2,3},{3,2},{4,5},{5,4},{6,7},{7,6},{8,9},{9,8},{10,11... | collective-permute-start | bytes 497672 | tf_op jit(solution)/shard_map/ppermute | solution.py:430
  178.2 7.2 %collective-permute-start.13 = (bf16[648,128]{1,0:T(8,128)(2,1)S(1)}, bf16[648,128]{1,0:T(8,128)(2,1)S(1)}, u32[]{:S(2)}, u32[]{:S(2)}) collective-permute-start(bf16[648,128]{1,0:T(8,128)(2,1)S(1)} %get-tuple-element.40), channel_id=1, source_target_pairs={{0,2},{1,3},{2,0},{3,1},{4,6},{5,7},{6,4},{7,5},{8,10},{9,11},{10,... | collective-permute-start | bytes 497672 | tf_op jit(solution)/shard_map/ppermute | solution.py:430
